TPU v7x, 32 devices: a whole 2x2x4 slice. The times are simulated.
32 devices in a mesh: mp: 8 (over z, x), station: 4 (over y, core).
Axes of the slice: x: 2, y: 2, z: 4, core: 2. Of those that a mesh axis runs over, the one named last changes fastest.
Arguments:
- p_now: float32 [64, 64, 128], P('mp'), may hold values from -2.7 to 2.7
- p_prev: float32 [64, 64, 128], P('mp'), may hold values from -2.7 to 2.7
- velocity: float32 [64, 64, 128], P('mp'), may hold values from 4 to 4.5
- density: float32 [64, 64, 128], P('mp'), may hold values from -6 to 6
- wavelet: float32 [16], replicated, may hold values from -4 to 4
- source_cell: int32 [1], replicated, may hold values from 0 to 524287
- receiver_cells: int32 [256], replicated, may hold values from 0 to 4095
- station_cells: int32 [512], P('station'), may hold values from 0 to 4095
- observed: float32 [512], P('station'), may hold values from -6 to 6
Outputs:
- wavefield: float32 [64, 64, 128], P('mp')
- traces: float32 [16, 256], replicated
- gravity_residual: float32 [512], P('station')
- density_gradient: float32 [64, 64, 128], P('mp', 'station')
- cross_gradient: float32 [3, 64, 64, 128], P(None, 'mp')
All inputs are finite; a program needn't handle non-finite values.
Results may differ from a plain program's by a relative error of at most 0.0036.
The roundings to bfloat16 on the way count: a program that leaves them out, or rounds other values in their place, can miss the bound.
Values sent between devices are 32-bit elements; how exact they have to be, the bound alone decides.
No kernel may reach another device: no remote copies, remote signals or barrier semaphores. Data moves between devices by JAX's collectives and lax.ppermute only.
A program may use at most 64 MiB of HBM per device.

v0:
```python
import jax
import jax.numpy as jnp
from jax import lax
from jax.sharding import PartitionSpec as P

STENCIL = (-205.0 / 72.0, 8.0 / 5.0, -1.0 / 5.0, 8.0 / 315.0, -1.0 / 560.0)
TIME_RATIO = 0.1


def extended(cells, sides, width):
    for axis, dim in sides:
        count = lax.axis_size(axis)
        ends = count - 1
        head = lax.slice_in_dim(cells, 0, width, axis=dim)
        tail = lax.slice_in_dim(cells, cells.shape[dim] - width, cells.shape[dim], axis=dim)
        cells = jnp.concatenate(
            [
                lax.ppermute(tail, axis, [(i, (i + 1) % count) for i in range(ends)]),
                cells,
                lax.ppermute(head, axis, [((i + 1) % count, i) for i in range(ends)]),
            ],
            axis=dim,
        )
    return cells


def stencil(padded, current):
    slab, lateral, vertical = current.shape
    result = 3.0 * STENCIL[0] * current
    for distance in range(1, 5):
        pairs = padded[4 + distance : 4 + distance + slab, 4 : 4 + lateral, 4 : 4 + vertical]
        pairs = (
            pairs + padded[4 - distance : 4 - distance + slab, 4 : 4 + lateral, 4 : 4 + vertical]
        )
        pairs = (
            pairs + padded[4 : 4 + slab, 4 + distance : 4 + distance + lateral, 4 : 4 + vertical]
        )
        pairs = (
            pairs + padded[4 : 4 + slab, 4 - distance : 4 - distance + lateral, 4 : 4 + vertical]
        )
        pairs = (
            pairs + padded[4 : 4 + slab, 4 : 4 + lateral, 4 + distance : 4 + distance + vertical]
        )
        pairs = (
            pairs + padded[4 : 4 + slab, 4 : 4 + lateral, 4 - distance : 4 - distance + vertical]
        )
        result = result + STENCIL[distance] * pairs
    return result


def kernel_tile(plane_x, station_x, station_y, cell_y, cell_z):
    delta_x = plane_x - station_x
    delta_y = cell_y[None, :] - station_y[:, None]
    radius_sq = (
        delta_x[:, None] * delta_x[:, None] + delta_y * delta_y + cell_z[None, :] * cell_z[None, :]
    )
    return (cell_z[None, :] / (radius_sq * jnp.sqrt(radius_sq))).astype(jnp.bfloat16)


def cross_terms(padded, slab, lateral, vertical):
    diff_x = (
        padded[:, 2 : 2 + slab, 1 : 1 + lateral, 1 : 1 + vertical]
        - padded[:, 0:slab, 1 : 1 + lateral, 1 : 1 + vertical]
    ) * 0.5
    diff_y = (
        padded[:, 1 : 1 + slab, 2 : 2 + lateral, 1 : 1 + vertical]
        - padded[:, 1 : 1 + slab, 0:lateral, 1 : 1 + vertical]
    ) * 0.5
    diff_z = (
        padded[:, 1 : 1 + slab, 1 : 1 + lateral, 2 : 2 + vertical]
        - padded[:, 1 : 1 + slab, 1 : 1 + lateral, 0:vertical]
    ) * 0.5
    first = diff_y[0] * diff_z[1] - diff_z[0] * diff_y[1]
    second = diff_z[0] * diff_x[1] - diff_x[0] * diff_z[1]
    third = diff_x[0] * diff_y[1] - diff_y[0] * diff_x[1]
    return jnp.stack([first, second, third])


def per_device(
    p_now, p_prev, velocity, density, wavelet, source_cell, receiver_cells, station_cells, observed
):
    slab, lateral, vertical = p_now.shape
    offset_x = lax.axis_index("mp") * slab
    courant = TIME_RATIO * velocity * (TIME_RATIO * velocity)
    offset_y = 0
    global_x = offset_x + jnp.arange(slab, dtype=jnp.int32)
    global_y = offset_y + jnp.arange(lateral, dtype=jnp.int32)
    flat_index = (
        global_x[:, None, None] * lateral + global_y[None, :, None]
    ) * vertical + jnp.arange(vertical, dtype=jnp.int32)[None, None, :]
    source_mask = (flat_index == source_cell[0]).astype(jnp.float32)
    receiver_x = receiver_cells // lateral
    receiver_y = receiver_cells % lateral
    inside = (
        (receiver_x >= offset_x)
        & (receiver_x < offset_x + slab)
        & (receiver_y >= offset_y)
        & (receiver_y < offset_y + lateral)
    )
    safe_index = jnp.where(inside, (receiver_x - offset_x) * lateral + (receiver_y - offset_y), 0)

    def advance(carry, pulse):
        present, earlier = carry
        padded = extended(present, (("mp", 0),), 4)
        padded = jnp.pad(padded, ((0, 0), (4, 4), (4, 4)))
        updated = 2.0 * present - earlier + courant * stencil(padded, present) + pulse * source_mask
        surface = updated[:, :, 0].reshape(-1)
        recorded = jnp.where(inside, surface[safe_index], 0.0)
        return ((updated, present), recorded)

    (last_field, unused), recorded_all = lax.scan(advance, (p_now, p_prev), wavelet)
    traces = lax.psum(recorded_all, "mp")
    stacked = jnp.stack([velocity, density])
    padded_model = extended(stacked, (("mp", 1),), 1)
    padded_model = jnp.pad(padded_model, ((0, 0), (0, 0), (1, 1), (1, 1)))
    cross_gradient = cross_terms(padded_model, slab, lateral, vertical)
    station_x = (station_cells // lateral).astype(jnp.float32)
    station_y = (station_cells % lateral).astype(jnp.float32)
    cell_y = (jnp.arange(lateral * vertical, dtype=jnp.int32) // vertical).astype(jnp.float32)
    cell_z = (jnp.arange(lateral * vertical, dtype=jnp.int32) % vertical).astype(jnp.float32) + 1.0
    planes = density.astype(jnp.bfloat16).reshape(slab, lateral * vertical)
    plane_xs = global_x.astype(jnp.float32)

    def forward(totals, packed):
        plane_x, plane = packed
        tile = kernel_tile(plane_x, station_x, station_y, cell_y, cell_z)
        return (totals + jnp.dot(tile, plane, preferred_element_type=jnp.float32), None)

    partial_value, unused_out = lax.scan(
        forward, jnp.zeros((station_cells.shape[0],), jnp.float32), (plane_xs, planes)
    )
    predicted = lax.psum(partial_value, "mp")
    gravity_residual = predicted - observed
    residual_low = gravity_residual.astype(jnp.bfloat16)

    def adjoint(plane_x):
        tile = kernel_tile(plane_x, station_x, station_y, cell_y, cell_z)
        return jnp.dot(residual_low, tile, preferred_element_type=jnp.float32)

    local_gradient = lax.map(adjoint, plane_xs).reshape(slab, lateral, vertical)
    density_gradient = lax.psum_scatter(local_gradient, "station", scatter_dimension=1, tiled=True)
    return (last_field, traces, gravity_residual, density_gradient, cross_gradient)


def solution(mesh):
    in_specs = (
        P("mp", None, None),
        P("mp", None, None),
        P("mp", None, None),
        P("mp", None, None),
        P(),
        P(),
        P(),
        P("station"),
        P("station"),
    )
    out_specs = (
        P("mp", None, None),
        P(),
        P("station"),
        P("mp", "station", None),
        P(None, "mp", None, None),
    )
    return jax.shard_map(
        per_device, mesh=mesh, in_specs=in_specs, out_specs=out_specs, check_vma=False
    )
```

profile of v0, /device:TPU:0, one launch (start us, length us, event | category | flops | bytes accessed | tf_op | source)
XLA Modules:
  0.0 394.3 jit_solution(18170677498413099735)
XLA Ops:
  9.4 5.5 %collective-permute-start.2 = (f32[2,1,64,128]{3,2,1,0:T(8,128)S(1)}, f32[2,1,64,128]{3,2,1,0:T(8,128)S(1)}, u32[]{:S(2)}, u32[]{:S(2)}) collective-permute-start(f32[2,1,64,128]{3,2,1,0:T(8,128)S(1)} %get-tuple-element.423), channel_id=1, source_target_pairs={{0,4},{4,8},{8,12},{12,16},{16,20},{20,24},{24,28},{1,5},{5,9},{9,... | collective-permute-start | bytes 196616 | tf_op jit(solution)/shard_map/ppermute | solution.py:18
  15.3 28.2 %while.43 = (s32[]{:T(128)}, f32[128]{0:T(128)S(1)}, f32[8]{0:T(128)S(1)}, f32[128]{0:T(128)S(1)}, f32[128]{0:T(128)S(1)}, /*index=5*/bf16[8,8192]{1,0:T(8,128)(2,1)S(1)}, s32[]{:T(128)}, s32[]{:T(128)}) while((s32[]{:T(128)}, f32[128]{0:T(128)S(1)}, f32[8]{0:T(128)S(1)}, f32[128]{0:T(128)S(1)}, f32[128]{0:T(128)S(1)}, ...), condition=%wide.region_4.5_spmd.clone, body=%wide.region_3.4_spmd.clone.sunk | while | flops 9650691 | bytes 232571 | solution.py:129
  43.6 260.0 %while.41 = (s32[]{:T(128)}, f32[8,64,128]{2,1,0:T(8,128)S(1)}, f32[8,64,128]{2,1,0:T(8,128)S(1)}, f32[16,256]{1,0:T(8,128)S(1)}, f32[8,64,128]{2,1,0:T(8,128)S(...) while((s32[]{:T(128)}, f32[8,64,128]{2,1,0:T(8,128)S(1)}, ...), condition=%wide.region_1.2_spmd.clone, body=%wide.region_0.1_spmd.clone.sunk | while | flops 4776962 | bytes 12448229 | solution.py:111
  44.9 5.5 %collective-permute-start.1 = (f32[4,64,128]{2,1,0:T(8,128)S(1)}, f32[4,64,128]{2,1,0:T(8,128)S(1)}, u32[]{:S(2)}, u32[]{:S(2)}) collective-permute-start(f32[4,64,128]{2,1,0:T(8,128)S(1)} %get-tuple-element.557), channel_id=1, source_target_pairs={{0,4},{4,8},{8,12},{12,16},{16,20},{20,24},{24,28},{1,5},{5,9},{9,... | collective-permute-start | bytes 393224 | tf_op jit(solution)/shard_map/while/body/eval_jaxpr/ppermute | solution.py:18
  60.9 5.0 %collective-permute-start.1 = (f32[4,64,128]{2,1,0:T(8,128)S(1)}, f32[4,64,128]{2,1,0:T(8,128)S(1)}, u32[]{:S(2)}, u32[]{:S(2)}) collective-permute-start(f32[4,64,128]{2,1,0:T(8,128)S(1)} %get-tuple-element.557), channel_id=1, source_target_pairs={{0,4},{4,8},{8,12},{12,16},{16,20},{20,24},{24,28},{1,5},{5,9},{9,... | collective-permute-start | bytes 393224 | tf_op jit(solution)/shard_map/while/body/eval_jaxpr/ppermute | solution.py:18
  77.0 5.0 %collective-permute-start.1 = (f32[4,64,128]{2,1,0:T(8,128)S(1)}, f32[4,64,128]{2,1,0:T(8,128)S(1)}, u32[]{:S(2)}, u32[]{:S(2)}) collective-permute-start(f32[4,64,128]{2,1,0:T(8,128)S(1)} %get-tuple-element.557), channel_id=1, source_target_pairs={{0,4},{4,8},{8,12},{12,16},{16,20},{20,24},{24,28},{1,5},{5,9},{9,... | collective-permute-start | bytes 393224 | tf_op jit(solution)/shard_map/while/body/eval_jaxpr/ppermute | solution.py:18
  93.2 5.0 %collective-permute-start.1 = (f32[4,64,128]{2,1,0:T(8,128)S(1)}, f32[4,64,128]{2,1,0:T(8,128)S(1)}, u32[]{:S(2)}, u32[]{:S(2)}) collective-permute-start(f32[4,64,128]{2,1,0:T(8,128)S(1)} %get-tuple-element.557), channel_id=1, source_target_pairs={{0,4},{4,8},{8,12},{12,16},{16,20},{20,24},{24,28},{1,5},{5,9},{9,... | collective-permute-start | bytes 393224 | tf_op jit(solution)/shard_map/while/body/eval_jaxpr/ppermute | solution.py:18
  98.9 4.1 %collective-permute-done.1 = f32[4,64,128]{2,1,0:T(8,128)S(1)} collective-permute-done((f32[4,64,128]{2,1,0:T(8,128)S(1)}, f32[4,64,128]{2,1,0:T(8,128)S(1)}, u32[]{:S(2)}, u32[]{:S(2)}) %collective-permute-start.1) | collective-permute-done | bytes 131104 | tf_op jit(solution)/shard_map/while/body/eval_jaxpr/ppermute | solution.py:18
  109.5 5.0 %collective-permute-start.1 = (f32[4,64,128]{2,1,0:T(8,128)S(1)}, f32[4,64,128]{2,1,0:T(8,128)S(1)}, u32[]{:S(2)}, u32[]{:S(2)}) collective-permute-start(f32[4,64,128]{2,1,0:T(8,128)S(1)} %get-tuple-element.557), channel_id=1, source_target_pairs={{0,4},{4,8},{8,12},{12,16},{16,20},{20,24},{24,28},{1,5},{5,9},{9,... | collective-permute-start | bytes 393224 | tf_op jit(solution)/shard_map/while/body/eval_jaxpr/ppermute | solution.py:18
  115.2 4.1 %collective-permute-done.1 = f32[4,64,128]{2,1,0:T(8,128)S(1)} collective-permute-done((f32[4,64,128]{2,1,0:T(8,128)S(1)}, f32[4,64,128]{2,1,0:T(8,128)S(1)}, u32[]{:S(2)}, u32[]{:S(2)}) %collective-permute-start.1) | collective-permute-done | bytes 131104 | tf_op jit(solution)/shard_map/while/body/eval_jaxpr/ppermute | solution.py:18
  125.8 5.0 %collective-permute-start.1 = (f32[4,64,128]{2,1,0:T(8,128)S(1)}, f32[4,64,128]{2,1,0:T(8,128)S(1)}, u32[]{:S(2)}, u32[]{:S(2)}) collective-permute-start(f32[4,64,128]{2,1,0:T(8,128)S(1)} %get-tuple-element.557), channel_id=1, source_target_pairs={{0,4},{4,8},{8,12},{12,16},{16,20},{20,24},{24,28},{1,5},{5,9},{9,... | collective-permute-start | bytes 393224 | tf_op jit(solution)/shard_map/while/body/eval_jaxpr/ppermute | solution.py:18
  131.4 4.1 %collective-permute-done.1 = f32[4,64,128]{2,1,0:T(8,128)S(1)} collective-permute-done((f32[4,64,128]{2,1,0:T(8,128)S(1)}, f32[4,64,128]{2,1,0:T(8,128)S(1)}, u32[]{:S(2)}, u32[]{:S(2)}) %collective-permute-start.1) | collective-permute-done | bytes 131104 | tf_op jit(solution)/shard_map/while/body/eval_jaxpr/ppermute | solution.py:18
  142.1 5.0 %collective-permute-start.1 = (f32[4,64,128]{2,1,0:T(8,128)S(1)}, f32[4,64,128]{2,1,0:T(8,128)S(1)}, u32[]{:S(2)}, u32[]{:S(2)}) collective-permute-start(f32[4,64,128]{2,1,0:T(8,128)S(1)} %get-tuple-element.557), channel_id=1, source_target_pairs={{0,4},{4,8},{8,12},{12,16},{16,20},{20,24},{24,28},{1,5},{5,9},{9,... | collective-permute-start | bytes 393224 | tf_op jit(solution)/shard_map/while/body/eval_jaxpr/ppermute | solution.py:18
  147.7 4.1 %collective-permute-done.1 = f32[4,64,128]{2,1,0:T(8,128)S(1)} collective-permute-done((f32[4,64,128]{2,1,0:T(8,128)S(1)}, f32[4,64,128]{2,1,0:T(8,128)S(1)}, u32[]{:S(2)}, u32[]{:S(2)}) %collective-permute-start.1) | collective-permute-done | bytes 131104 | tf_op jit(solution)/shard_map/while/body/eval_jaxpr/ppermute | solution.py:18
  158.4 5.0 %collective-permute-start.1 = (f32[4,64,128]{2,1,0:T(8,128)S(1)}, f32[4,64,128]{2,1,0:T(8,128)S(1)}, u32[]{:S(2)}, u32[]{:S(2)}) collective-permute-start(f32[4,64,128]{2,1,0:T(8,128)S(1)} %get-tuple-element.557), channel_id=1, source_target_pairs={{0,4},{4,8},{8,12},{12,16},{16,20},{20,24},{24,28},{1,5},{5,9},{9,... | collective-permute-start | bytes 393224 | tf_op jit(solution)/shard_map/while/body/eval_jaxpr/ppermute | solution.py:18
  164.0 4.1 %collective-permute-done.1 = f32[4,64,128]{2,1,0:T(8,128)S(1)} collective-permute-done((f32[4,64,128]{2,1,0:T(8,128)S(1)}, f32[4,64,128]{2,1,0:T(8,128)S(1)}, u32[]{:S(2)}, u32[]{:S(2)}) %collective-permute-start.1) | collective-permute-done | bytes 131104 | tf_op jit(solution)/shard_map/while/body/eval_jaxpr/ppermute | solution.py:18
  174.6 5.0 %collective-permute-start.1 = (f32[4,64,128]{2,1,0:T(8,128)S(1)}, f32[4,64,128]{2,1,0:T(8,128)S(1)}, u32[]{:S(2)}, u32[]{:S(2)}) collective-permute-start(f32[4,64,128]{2,1,0:T(8,128)S(1)} %get-tuple-element.557), channel_id=1, source_target_pairs={{0,4},{4,8},{8,12},{12,16},{16,20},{20,24},{24,28},{1,5},{5,9},{9,... | collective-permute-start | bytes 393224 | tf_op jit(solution)/shard_map/while/body/eval_jaxpr/ppermute | solution.py:18
  180.3 4.1 %collective-permute-done.1 = f32[4,64,128]{2,1,0:T(8,128)S(1)} collective-permute-done((f32[4,64,128]{2,1,0:T(8,128)S(1)}, f32[4,64,128]{2,1,0:T(8,128)S(1)}, u32[]{:S(2)}, u32[]{:S(2)}) %collective-permute-start.1) | collective-permute-done | bytes 131104 | tf_op jit(solution)/shard_map/while/body/eval_jaxpr/ppermute | solution.py:18
  190.9 5.0 %collective-permute-start.1 = (f32[4,64,128]{2,1,0:T(8,128)S(1)}, f32[4,64,128]{2,1,0:T(8,128)S(1)}, u32[]{:S(2)}, u32[]{:S(2)}) collective-permute-start(f32[4,64,128]{2,1,0:T(8,128)S(1)} %get-tuple-element.557), channel_id=1, source_target_pairs={{0,4},{4,8},{8,12},{12,16},{16,20},{20,24},{24,28},{1,5},{5,9},{9,... | collective-permute-start | bytes 393224 | tf_op jit(solution)/shard_map/while/body/eval_jaxpr/ppermute | solution.py:18
  196.6 4.1 %collective-permute-done.1 = f32[4,64,128]{2,1,0:T(8,128)S(1)} collective-permute-done((f32[4,64,128]{2,1,0:T(8,128)S(1)}, f32[4,64,128]{2,1,0:T(8,128)S(1)}, u32[]{:S(2)}, u32[]{:S(2)}) %collective-permute-start.1) | collective-permute-done | bytes 131104 | tf_op jit(solution)/shard_map/while/body/eval_jaxpr/ppermute | solution.py:18
  207.2 5.0 %collective-permute-start.1 = (f32[4,64,128]{2,1,0:T(8,128)S(1)}, f32[4,64,128]{2,1,0:T(8,128)S(1)}, u32[]{:S(2)}, u32[]{:S(2)}) collective-permute-start(f32[4,64,128]{2,1,0:T(8,128)S(1)} %get-tuple-element.557), channel_id=1, source_target_pairs={{0,4},{4,8},{8,12},{12,16},{16,20},{20,24},{24,28},{1,5},{5,9},{9,... | collective-permute-start | bytes 393224 | tf_op jit(solution)/shard_map/while/body/eval_jaxpr/ppermute | solution.py:18
  212.8 4.1 %collective-permute-done.1 = f32[4,64,128]{2,1,0:T(8,128)S(1)} collective-permute-done((f32[4,64,128]{2,1,0:T(8,128)S(1)}, f32[4,64,128]{2,1,0:T(8,128)S(1)}, u32[]{:S(2)}, u32[]{:S(2)}) %collective-permute-start.1) | collective-permute-done | bytes 131104 | tf_op jit(solution)/shard_map/while/body/eval_jaxpr/ppermute | solution.py:18
  223.5 5.0 %collective-permute-start.1 = (f32[4,64,128]{2,1,0:T(8,128)S(1)}, f32[4,64,128]{2,1,0:T(8,128)S(1)}, u32[]{:S(2)}, u32[]{:S(2)}) collective-permute-start(f32[4,64,128]{2,1,0:T(8,128)S(1)} %get-tuple-element.557), channel_id=1, source_target_pairs={{0,4},{4,8},{8,12},{12,16},{16,20},{20,24},{24,28},{1,5},{5,9},{9,... | collective-permute-start | bytes 393224 | tf_op jit(solution)/shard_map/while/body/eval_jaxpr/ppermute | solution.py:18
  229.1 4.1 %collective-permute-done.1 = f32[4,64,128]{2,1,0:T(8,128)S(1)} collective-permute-done((f32[4,64,128]{2,1,0:T(8,128)S(1)}, f32[4,64,128]{2,1,0:T(8,128)S(1)}, u32[]{:S(2)}, u32[]{:S(2)}) %collective-permute-start.1) | collective-permute-done | bytes 131104 | tf_op jit(solution)/shard_map/while/body/eval_jaxpr/ppermute | solution.py:18
  239.8 5.0 %collective-permute-start.1 = (f32[4,64,128]{2,1,0:T(8,128)S(1)}, f32[4,64,128]{2,1,0:T(8,128)S(1)}, u32[]{:S(2)}, u32[]{:S(2)}) collective-permute-start(f32[4,64,128]{2,1,0:T(8,128)S(1)} %get-tuple-element.557), channel_id=1, source_target_pairs={{0,4},{4,8},{8,12},{12,16},{16,20},{20,24},{24,28},{1,5},{5,9},{9,... | collective-permute-start | bytes 393224 | tf_op jit(solution)/shard_map/while/body/eval_jaxpr/ppermute | solution.py:18
  245.4 4.1 %collective-permute-done.1 = f32[4,64,128]{2,1,0:T(8,128)S(1)} collective-permute-done((f32[4,64,128]{2,1,0:T(8,128)S(1)}, f32[4,64,128]{2,1,0:T(8,128)S(1)}, u32[]{:S(2)}, u32[]{:S(2)}) %collective-permute-start.1) | collective-permute-done | bytes 131104 | tf_op jit(solution)/shard_map/while/body/eval_jaxpr/ppermute | solution.py:18
  256.0 5.0 %collective-permute-start.1 = (f32[4,64,128]{2,1,0:T(8,128)S(1)}, f32[4,64,128]{2,1,0:T(8,128)S(1)}, u32[]{:S(2)}, u32[]{:S(2)}) collective-permute-start(f32[4,64,128]{2,1,0:T(8,128)S(1)} %get-tuple-element.557), channel_id=1, source_target_pairs={{0,4},{4,8},{8,12},{12,16},{16,20},{20,24},{24,28},{1,5},{5,9},{9,... | collective-permute-start | bytes 393224 | tf_op jit(solution)/shard_map/while/body/eval_jaxpr/ppermute | solution.py:18
  272.3 5.0 %collective-permute-start.1 = (f32[4,64,128]{2,1,0:T(8,128)S(1)}, f32[4,64,128]{2,1,0:T(8,128)S(1)}, u32[]{:S(2)}, u32[]{:S(2)}) collective-permute-start(f32[4,64,128]{2,1,0:T(8,128)S(1)} %get-tuple-element.557), channel_id=1, source_target_pairs={{0,4},{4,8},{8,12},{12,16},{16,20},{20,24},{24,28},{1,5},{5,9},{9,... | collective-permute-start | bytes 393224 | tf_op jit(solution)/shard_map/while/body/eval_jaxpr/ppermute | solution.py:18
  288.6 5.0 %collective-permute-start.1 = (f32[4,64,128]{2,1,0:T(8,128)S(1)}, f32[4,64,128]{2,1,0:T(8,128)S(1)}, u32[]{:S(2)}, u32[]{:S(2)}) collective-permute-start(f32[4,64,128]{2,1,0:T(8,128)S(1)} %get-tuple-element.557), channel_id=1, source_target_pairs={{0,4},{4,8},{8,12},{12,16},{16,20},{20,24},{24,28},{1,5},{5,9},{9,... | collective-permute-start | bytes 393224 | tf_op jit(solution)/shard_map/while/body/eval_jaxpr/ppermute | solution.py:18
  303.6 35.9 %all-reduce.2 = (f32[16,256]{1,0:T(8,128)}, f32[128]{0:T(128)S(1)}) all-reduce(f32[16,256]{1,0:T(8,128)S(1)} %get-tuple-element.278, f32[128]{0:T(128)S(1)} %get-tuple-element.279), channel_id=1, replica_groups=mesh['mp'=8,'station'=4] {'mp'}, use_global_device_ids=true, to_apply=%region_2.3 | all-reduce | flops 4224 | bytes 33792 | tf_op jit(solution)/shard_map/psum | solution.py:112
  340.0 29.2 %while.42 = (s32[]{:T(128)}, f32[8,8192]{1,0:T(8,128)S(1)}, f32[8]{0:T(128)S(1)}, f32[128]{0:T(128)S(1)}, f32[128]{0:T(128)S(1)}, /*index=5*/bf16[128]{0:T(256)(128)(2,1)S(1)}, s32[]{:T(128)}, s32[]{:T(128)}) while((s32[]{:T(128)}, f32[8,8192]{1,0:T(8,128)S(1)}, f32[8]{0:T(128)S(1)}, f32[128]{0:T(128)S(1)}, f32[128]{0:T(128)S(1)}, ...), condition=%wide.region_7.8_spmd.clone, body=%wide.region_6.7_spmd.clone.sunk | while | flops 9650434 | bytes 297329 | solution.py:140
  372.0 15.4 %reduce-scatter.2.cloned.1.call-done = f32[8,16,128]{2,1,0:T(8,128)} async-done(((f32[8,64,128]{2,1,0:T(8,128)}), f32[8,16,128]{2,1,0:T(8,128)}) %reduce-scatter.2.cloned.1.call-update) | async-done | bytes 65552 | tf_op jit(solution)/shard_map/reduce_scatter | solution.py:141
  (438 shorter events, 198.8 us)
Async XLA Ops:
  7.2 380.2 %reduce-scatter.2.cloned.1.call-start = ((), (), s32[]{:S(2)}) async-start(), calls=%async_computation.1 | async-start | bytes 327680 | tf_op jit(solution)/shard_map/reduce_scatter | solution.py:141
  8.1 361.8 %collective-permute-start.3 = (f32[2,1,64,128]{3,2,1,0:T(8,128)S(1)}, f32[2,1,64,128]{3,2,1,0:T(8,128)S(1)}, u32[]{:S(2)}, u32[]{:S(2)}) collective-permute-start(f32[2,1,64,128]{3,2,1,0:T(8,128)S(1)} %get-tuple-element.422), channel_id=1, source_target_pairs={{4,0},{8,4},{12,8},{16,12},{20,16},{24,20},{28,24},{5,1},{9,5},{13... | collective-permute-start | bytes 196616 | tf_op jit(solution)/shard_map/ppermute | solution.py:20
  9.4 360.5 %collective-permute-start.2 = (f32[2,1,64,128]{3,2,1,0:T(8,128)S(1)}, f32[2,1,64,128]{3,2,1,0:T(8,128)S(1)}, u32[]{:S(2)}, u32[]{:S(2)}) collective-permute-start(f32[2,1,64,128]{3,2,1,0:T(8,128)S(1)} %get-tuple-element.423), channel_id=1, source_target_pairs={{0,4},{4,8},{8,12},{12,16},{16,20},{20,24},{24,28},{1,5},{5,9},{9,... | collective-permute-start | bytes 196616 | tf_op jit(solution)/shard_map/ppermute | solution.py:18
  43.6 10.8 %collective-permute-start = (f32[4,64,128]{2,1,0:T(8,128)S(1)}, f32[4,64,128]{2,1,0:T(8,128)S(1)}, u32[]{:S(2)}, u32[]{:S(2)}) collective-permute-start(f32[4,64,128]{2,1,0:T(8,128)S(1)} %get-tuple-element.556), channel_id=1, source_target_pairs={{4,0},{8,4},{12,8},{16,12},{20,16},{24,20},{28,24},{5,1},{9,5},{13... | collective-permute-start | bytes 393224 | tf_op jit(solution)/shard_map/while/body/eval_jaxpr/ppermute | solution.py:20
  59.6 10.9 %collective-permute-start = (f32[4,64,128]{2,1,0:T(8,128)S(1)}, f32[4,64,128]{2,1,0:T(8,128)S(1)}, u32[]{:S(2)}, u32[]{:S(2)}) collective-permute-start(f32[4,64,128]{2,1,0:T(8,128)S(1)} %get-tuple-element.556), channel_id=1, source_target_pairs={{4,0},{8,4},{12,8},{16,12},{20,16},{24,20},{28,24},{5,1},{9,5},{13... | collective-permute-start | bytes 393224 | tf_op jit(solution)/shard_map/while/body/eval_jaxpr/ppermute | solution.py:20
  75.7 11.1 %collective-permute-start = (f32[4,64,128]{2,1,0:T(8,128)S(1)}, f32[4,64,128]{2,1,0:T(8,128)S(1)}, u32[]{:S(2)}, u32[]{:S(2)}) collective-permute-start(f32[4,64,128]{2,1,0:T(8,128)S(1)} %get-tuple-element.556), channel_id=1, source_target_pairs={{4,0},{8,4},{12,8},{16,12},{20,16},{24,20},{28,24},{5,1},{9,5},{13... | collective-permute-start | bytes 393224 | tf_op jit(solution)/shard_map/while/body/eval_jaxpr/ppermute | solution.py:20
  91.9 11.1 %collective-permute-start = (f32[4,64,128]{2,1,0:T(8,128)S(1)}, f32[4,64,128]{2,1,0:T(8,128)S(1)}, u32[]{:S(2)}, u32[]{:S(2)}) collective-permute-start(f32[4,64,128]{2,1,0:T(8,128)S(1)} %get-tuple-element.556), channel_id=1, source_target_pairs={{4,0},{8,4},{12,8},{16,12},{20,16},{24,20},{28,24},{5,1},{9,5},{13... | collective-permute-start | bytes 393224 | tf_op jit(solution)/shard_map/while/body/eval_jaxpr/ppermute | solution.py:20
  93.2 9.7 %collective-permute-start.1 = (f32[4,64,128]{2,1,0:T(8,128)S(1)}, f32[4,64,128]{2,1,0:T(8,128)S(1)}, u32[]{:S(2)}, u32[]{:S(2)}) collective-permute-start(f32[4,64,128]{2,1,0:T(8,128)S(1)} %get-tuple-element.557), channel_id=1, source_target_pairs={{0,4},{4,8},{8,12},{12,16},{16,20},{20,24},{24,28},{1,5},{5,9},{9,... | collective-permute-start | bytes 393224 | tf_op jit(solution)/shard_map/while/body/eval_jaxpr/ppermute | solution.py:18
  108.2 11.1 %collective-permute-start = (f32[4,64,128]{2,1,0:T(8,128)S(1)}, f32[4,64,128]{2,1,0:T(8,128)S(1)}, u32[]{:S(2)}, u32[]{:S(2)}) collective-permute-start(f32[4,64,128]{2,1,0:T(8,128)S(1)} %get-tuple-element.556), channel_id=1, source_target_pairs={{4,0},{8,4},{12,8},{16,12},{20,16},{24,20},{28,24},{5,1},{9,5},{13... | collective-permute-start | bytes 393224 | tf_op jit(solution)/shard_map/while/body/eval_jaxpr/ppermute | solution.py:20
  109.5 9.7 %collective-permute-start.1 = (f32[4,64,128]{2,1,0:T(8,128)S(1)}, f32[4,64,128]{2,1,0:T(8,128)S(1)}, u32[]{:S(2)}, u32[]{:S(2)}) collective-permute-start(f32[4,64,128]{2,1,0:T(8,128)S(1)} %get-tuple-element.557), channel_id=1, source_target_pairs={{0,4},{4,8},{8,12},{12,16},{16,20},{20,24},{24,28},{1,5},{5,9},{9,... | collective-permute-start | bytes 393224 | tf_op jit(solution)/shard_map/while/body/eval_jaxpr/ppermute | solution.py:18
  124.5 11.1 %collective-permute-start = (f32[4,64,128]{2,1,0:T(8,128)S(1)}, f32[4,64,128]{2,1,0:T(8,128)S(1)}, u32[]{:S(2)}, u32[]{:S(2)}) collective-permute-start(f32[4,64,128]{2,1,0:T(8,128)S(1)} %get-tuple-element.556), channel_id=1, source_target_pairs={{4,0},{8,4},{12,8},{16,12},{20,16},{24,20},{28,24},{5,1},{9,5},{13... | collective-permute-start | bytes 393224 | tf_op jit(solution)/shard_map/while/body/eval_jaxpr/ppermute | solution.py:20
  125.8 9.7 %collective-permute-start.1 = (f32[4,64,128]{2,1,0:T(8,128)S(1)}, f32[4,64,128]{2,1,0:T(8,128)S(1)}, u32[]{:S(2)}, u32[]{:S(2)}) collective-permute-start(f32[4,64,128]{2,1,0:T(8,128)S(1)} %get-tuple-element.557), channel_id=1, source_target_pairs={{0,4},{4,8},{8,12},{12,16},{16,20},{20,24},{24,28},{1,5},{5,9},{9,... | collective-permute-start | bytes 393224 | tf_op jit(solution)/shard_map/while/body/eval_jaxpr/ppermute | solution.py:18
  140.8 11.1 %collective-permute-start = (f32[4,64,128]{2,1,0:T(8,128)S(1)}, f32[4,64,128]{2,1,0:T(8,128)S(1)}, u32[]{:S(2)}, u32[]{:S(2)}) collective-permute-start(f32[4,64,128]{2,1,0:T(8,128)S(1)} %get-tuple-element.556), channel_id=1, source_target_pairs={{4,0},{8,4},{12,8},{16,12},{20,16},{24,20},{28,24},{5,1},{9,5},{13... | collective-permute-start | bytes 393224 | tf_op jit(solution)/shard_map/while/body/eval_jaxpr/ppermute | solution.py:20
  142.1 9.7 %collective-permute-start.1 = (f32[4,64,128]{2,1,0:T(8,128)S(1)}, f32[4,64,128]{2,1,0:T(8,128)S(1)}, u32[]{:S(2)}, u32[]{:S(2)}) collective-permute-start(f32[4,64,128]{2,1,0:T(8,128)S(1)} %get-tuple-element.557), channel_id=1, source_target_pairs={{0,4},{4,8},{8,12},{12,16},{16,20},{20,24},{24,28},{1,5},{5,9},{9,... | collective-permute-start | bytes 393224 | tf_op jit(solution)/shard_map/while/body/eval_jaxpr/ppermute | solution.py:18
  157.1 11.1 %collective-permute-start = (f32[4,64,128]{2,1,0:T(8,128)S(1)}, f32[4,64,128]{2,1,0:T(8,128)S(1)}, u32[]{:S(2)}, u32[]{:S(2)}) collective-permute-start(f32[4,64,128]{2,1,0:T(8,128)S(1)} %get-tuple-element.556), channel_id=1, source_target_pairs={{4,0},{8,4},{12,8},{16,12},{20,16},{24,20},{28,24},{5,1},{9,5},{13... | collective-permute-start | bytes 393224 | tf_op jit(solution)/shard_map/while/body/eval_jaxpr/ppermute | solution.py:20
  158.4 9.7 %collective-permute-start.1 = (f32[4,64,128]{2,1,0:T(8,128)S(1)}, f32[4,64,128]{2,1,0:T(8,128)S(1)}, u32[]{:S(2)}, u32[]{:S(2)}) collective-permute-start(f32[4,64,128]{2,1,0:T(8,128)S(1)} %get-tuple-element.557), channel_id=1, source_target_pairs={{0,4},{4,8},{8,12},{12,16},{16,20},{20,24},{24,28},{1,5},{5,9},{9,... | collective-permute-start | bytes 393224 | tf_op jit(solution)/shard_map/while/body/eval_jaxpr/ppermute | solution.py:18
  173.3 11.1 %collective-permute-start = (f32[4,64,128]{2,1,0:T(8,128)S(1)}, f32[4,64,128]{2,1,0:T(8,128)S(1)}, u32[]{:S(2)}, u32[]{:S(2)}) collective-permute-start(f32[4,64,128]{2,1,0:T(8,128)S(1)} %get-tuple-element.556), channel_id=1, source_target_pairs={{4,0},{8,4},{12,8},{16,12},{20,16},{24,20},{28,24},{5,1},{9,5},{13... | collective-permute-start | bytes 393224 | tf_op jit(solution)/shard_map/while/body/eval_jaxpr/ppermute | solution.py:20
  174.6 9.7 %collective-permute-start.1 = (f32[4,64,128]{2,1,0:T(8,128)S(1)}, f32[4,64,128]{2,1,0:T(8,128)S(1)}, u32[]{:S(2)}, u32[]{:S(2)}) collective-permute-start(f32[4,64,128]{2,1,0:T(8,128)S(1)} %get-tuple-element.557), channel_id=1, source_target_pairs={{0,4},{4,8},{8,12},{12,16},{16,20},{20,24},{24,28},{1,5},{5,9},{9,... | collective-permute-start | bytes 393224 | tf_op jit(solution)/shard_map/while/body/eval_jaxpr/ppermute | solution.py:18
  189.6 11.1 %collective-permute-start = (f32[4,64,128]{2,1,0:T(8,128)S(1)}, f32[4,64,128]{2,1,0:T(8,128)S(1)}, u32[]{:S(2)}, u32[]{:S(2)}) collective-permute-start(f32[4,64,128]{2,1,0:T(8,128)S(1)} %get-tuple-element.556), channel_id=1, source_target_pairs={{4,0},{8,4},{12,8},{16,12},{20,16},{24,20},{28,24},{5,1},{9,5},{13... | collective-permute-start | bytes 393224 | tf_op jit(solution)/shard_map/while/body/eval_jaxpr/ppermute | solution.py:20
  190.9 9.7 %collective-permute-start.1 = (f32[4,64,128]{2,1,0:T(8,128)S(1)}, f32[4,64,128]{2,1,0:T(8,128)S(1)}, u32[]{:S(2)}, u32[]{:S(2)}) collective-permute-start(f32[4,64,128]{2,1,0:T(8,128)S(1)} %get-tuple-element.557), channel_id=1, source_target_pairs={{0,4},{4,8},{8,12},{12,16},{16,20},{20,24},{24,28},{1,5},{5,9},{9,... | collective-permute-start | bytes 393224 | tf_op jit(solution)/shard_map/while/body/eval_jaxpr/ppermute | solution.py:18
  205.9 11.1 %collective-permute-start = (f32[4,64,128]{2,1,0:T(8,128)S(1)}, f32[4,64,128]{2,1,0:T(8,128)S(1)}, u32[]{:S(2)}, u32[]{:S(2)}) collective-permute-start(f32[4,64,128]{2,1,0:T(8,128)S(1)} %get-tuple-element.556), channel_id=1, source_target_pairs={{4,0},{8,4},{12,8},{16,12},{20,16},{24,20},{28,24},{5,1},{9,5},{13... | collective-permute-start | bytes 393224 | tf_op jit(solution)/shard_map/while/body/eval_jaxpr/ppermute | solution.py:20
  207.2 9.7 %collective-permute-start.1 = (f32[4,64,128]{2,1,0:T(8,128)S(1)}, f32[4,64,128]{2,1,0:T(8,128)S(1)}, u32[]{:S(2)}, u32[]{:S(2)}) collective-permute-start(f32[4,64,128]{2,1,0:T(8,128)S(1)} %get-tuple-element.557), channel_id=1, source_target_pairs={{0,4},{4,8},{8,12},{12,16},{16,20},{20,24},{24,28},{1,5},{5,9},{9,... | collective-permute-start | bytes 393224 | tf_op jit(solution)/shard_map/while/body/eval_jaxpr/ppermute | solution.py:18
  222.2 11.1 %collective-permute-start = (f32[4,64,128]{2,1,0:T(8,128)S(1)}, f32[4,64,128]{2,1,0:T(8,128)S(1)}, u32[]{:S(2)}, u32[]{:S(2)}) collective-permute-start(f32[4,64,128]{2,1,0:T(8,128)S(1)} %get-tuple-element.556), channel_id=1, source_target_pairs={{4,0},{8,4},{12,8},{16,12},{20,16},{24,20},{28,24},{5,1},{9,5},{13... | collective-permute-start | bytes 393224 | tf_op jit(solution)/shard_map/while/body/eval_jaxpr/ppermute | solution.py:20
  223.5 9.7 %collective-permute-start.1 = (f32[4,64,128]{2,1,0:T(8,128)S(1)}, f32[4,64,128]{2,1,0:T(8,128)S(1)}, u32[]{:S(2)}, u32[]{:S(2)}) collective-permute-start(f32[4,64,128]{2,1,0:T(8,128)S(1)} %get-tuple-element.557), channel_id=1, source_target_pairs={{0,4},{4,8},{8,12},{12,16},{16,20},{20,24},{24,28},{1,5},{5,9},{9,... | collective-permute-start | bytes 393224 | tf_op jit(solution)/shard_map/while/body/eval_jaxpr/ppermute | solution.py:18
  238.5 11.1 %collective-permute-start = (f32[4,64,128]{2,1,0:T(8,128)S(1)}, f32[4,64,128]{2,1,0:T(8,128)S(1)}, u32[]{:S(2)}, u32[]{:S(2)}) collective-permute-start(f32[4,64,128]{2,1,0:T(8,128)S(1)} %get-tuple-element.556), channel_id=1, source_target_pairs={{4,0},{8,4},{12,8},{16,12},{20,16},{24,20},{28,24},{5,1},{9,5},{13... | collective-permute-start | bytes 393224 | tf_op jit(solution)/shard_map/while/body/eval_jaxpr/ppermute | solution.py:20
  239.8 9.7 %collective-permute-start.1 = (f32[4,64,128]{2,1,0:T(8,128)S(1)}, f32[4,64,128]{2,1,0:T(8,128)S(1)}, u32[]{:S(2)}, u32[]{:S(2)}) collective-permute-start(f32[4,64,128]{2,1,0:T(8,128)S(1)} %get-tuple-element.557), channel_id=1, source_target_pairs={{0,4},{4,8},{8,12},{12,16},{16,20},{20,24},{24,28},{1,5},{5,9},{9,... | collective-permute-start | bytes 393224 | tf_op jit(solution)/shard_map/while/body/eval_jaxpr/ppermute | solution.py:18
  254.7 11.1 %collective-permute-start = (f32[4,64,128]{2,1,0:T(8,128)S(1)}, f32[4,64,128]{2,1,0:T(8,128)S(1)}, u32[]{:S(2)}, u32[]{:S(2)}) collective-permute-start(f32[4,64,128]{2,1,0:T(8,128)S(1)} %get-tuple-element.556), channel_id=1, source_target_pairs={{4,0},{8,4},{12,8},{16,12},{20,16},{24,20},{28,24},{5,1},{9,5},{13... | collective-permute-start | bytes 393224 | tf_op jit(solution)/shard_map/while/body/eval_jaxpr/ppermute | solution.py:20
  256.0 9.7 %collective-permute-start.1 = (f32[4,64,128]{2,1,0:T(8,128)S(1)}, f32[4,64,128]{2,1,0:T(8,128)S(1)}, u32[]{:S(2)}, u32[]{:S(2)}) collective-permute-start(f32[4,64,128]{2,1,0:T(8,128)S(1)} %get-tuple-element.557), channel_id=1, source_target_pairs={{0,4},{4,8},{8,12},{12,16},{16,20},{20,24},{24,28},{1,5},{5,9},{9,... | collective-permute-start | bytes 393224 | tf_op jit(solution)/shard_map/while/body/eval_jaxpr/ppermute | solution.py:18
  271.0 11.1 %collective-permute-start = (f32[4,64,128]{2,1,0:T(8,128)S(1)}, f32[4,64,128]{2,1,0:T(8,128)S(1)}, u32[]{:S(2)}, u32[]{:S(2)}) collective-permute-start(f32[4,64,128]{2,1,0:T(8,128)S(1)} %get-tuple-element.556), channel_id=1, source_target_pairs={{4,0},{8,4},{12,8},{16,12},{20,16},{24,20},{28,24},{5,1},{9,5},{13... | collective-permute-start | bytes 393224 | tf_op jit(solution)/shard_map/while/body/eval_jaxpr/ppermute | solution.py:20
  272.3 9.7 %collective-permute-start.1 = (f32[4,64,128]{2,1,0:T(8,128)S(1)}, f32[4,64,128]{2,1,0:T(8,128)S(1)}, u32[]{:S(2)}, u32[]{:S(2)}) collective-permute-start(f32[4,64,128]{2,1,0:T(8,128)S(1)} %get-tuple-element.557), channel_id=1, source_target_pairs={{0,4},{4,8},{8,12},{12,16},{16,20},{20,24},{24,28},{1,5},{5,9},{9,... | collective-permute-start | bytes 393224 | tf_op jit(solution)/shard_map/while/body/eval_jaxpr/ppermute | solution.py:18
  287.3 11.1 %collective-permute-start = (f32[4,64,128]{2,1,0:T(8,128)S(1)}, f32[4,64,128]{2,1,0:T(8,128)S(1)}, u32[]{:S(2)}, u32[]{:S(2)}) collective-permute-start(f32[4,64,128]{2,1,0:T(8,128)S(1)} %get-tuple-element.556), channel_id=1, source_target_pairs={{4,0},{8,4},{12,8},{16,12},{20,16},{24,20},{28,24},{5,1},{9,5},{13... | collective-permute-start | bytes 393224 | tf_op jit(solution)/shard_map/while/body/eval_jaxpr/ppermute | solution.py:20
  288.6 9.7 %collective-permute-start.1 = (f32[4,64,128]{2,1,0:T(8,128)S(1)}, f32[4,64,128]{2,1,0:T(8,128)S(1)}, u32[]{:S(2)}, u32[]{:S(2)}) collective-permute-start(f32[4,64,128]{2,1,0:T(8,128)S(1)} %get-tuple-element.557), channel_id=1, source_target_pairs={{0,4},{4,8},{8,12},{12,16},{16,20},{20,24},{24,28},{1,5},{5,9},{9,... | collective-permute-start | bytes 393224 | tf_op jit(solution)/shard_map/while/body/eval_jaxpr/ppermute | solution.py:18
  (12 other events, 497.6 us)
Sparse Core Ops, SparseCore 0:
  370.1 17.3 reduce-scatter.1
where the time goes:
time: 396 us; the launch traced here: 394 us
  starting transfers between devices  108 us (27%)
  waiting for transfers between devices  80 us (20%)
  other arithmetic  60.4 us (15%)
  local copies, waits for them, and re-layouts  58 us (15%)
  blocking collectives  35.9 us (9%)
  matrix products  34.7 us (9%)
  between operations  14.3 us (4%)
    ppermute x17, starting transfers between devices, extended(): lax.ppermute(tail, axis, [(i, (i + 1) % count) for i in range(ends)])  86.3 us
    ppermute x17, waiting for transfers between devices, extended(): lax.ppermute(tail, axis, [(i, (i + 1) % count) for i in range(ends)])  64.5 us
    add x16, other arithmetic, advance(): 2.0 * present - earlier + courant * stencil(padded, present)  39.2 us
    psum x1, blocking collectives, per_device(): traces = lax.psum(recorded_all, 'mp')  35.9 us
    gather x16, local copies, waits for them, and re-layouts, advance(): recorded = jnp.where(inside, surface[safe_index], 0.0)  31.1 us
    ppermute x17, starting transfers between devices, extended(): lax.ppermute(head, axis, [((i + 1) % count, i) for i in range(ends)])  22 us
    dot_general x8, matrix products, forward(): jnp.dot(tile, plane, preferred_element_type=jnp.float32)  17.5 us
    dot_general x8, matrix products, adjoint(): return jnp.dot(residual_low, tile, preferred_element_type=jnp.float32)  17.2 us
  transfers between devices with their start and end apart: 35, of which 17 were waited for; matrix products, arithmetic and copies ran while one was open for 39% of the time, Pallas kernels for 0%

commit v1 on v0

v1 whole, which is shorter than its diff:
```python
import functools

import jax
import jax.numpy as jnp
from jax import lax
from jax.experimental import pallas as pl
from jax.experimental.pallas import tpu as pltpu
from jax.sharding import PartitionSpec as P

STENCIL = (-205.0 / 72.0, 8.0 / 5.0, -1.0 / 5.0, 8.0 / 315.0, -1.0 / 560.0)
TIME_RATIO = 0.1
REACH = 4
AXES = ("mp", "station")
VMEM = pl.BlockSpec(memory_space=pltpu.VMEM)
SMEM = pl.BlockSpec(memory_space=pltpu.SMEM)
SRC_PLANE, SRC_ROW, SRC_LANE, X_LOW, HALF_LOW, ROW_LOW, LEFT_OK, RIGHT_OK, OUTER_OK, FLIPPED = range(10)
F32 = jnp.float32


def shape(dims):
    return jax.ShapeDtypeStruct(dims, F32)


def pairs_of(count, stations, partner):
    return [
        (m * stations + s, (lambda t: t[0] * stations + t[1])(partner(m, s)))
        for m in range(count)
        for s in range(stations)
    ]


def chain_partner(count):
    def partner(m, s):
        if s % 2 == 0:
            return (m ^ 1, s)
        other = m + 1 if m % 2 else m - 1
        if other < 0 or other >= count:
            return (m, s ^ 2)
        return (other, s)

    return partner


def divmod_static(value, divisor):
    if divisor & (divisor - 1) == 0:
        return value >> (divisor.bit_length() - 1), value & (divisor - 1)
    return value // divisor, value % divisor


def local_kernel(step, meta, wavelet, cur, prev, cour, surf_in, base, surf, pad):
    planes, rows, lanes = cur.shape
    lane = lax.broadcasted_iota(jnp.int32, (rows, lanes), 1)
    weights = {}
    for d in range(1, REACH + 1):
        weights[d] = jnp.where(lane >= d, STENCIL[d], 0.0)
        weights[-d] = jnp.where(lane < lanes - d, STENCIL[d], 0.0)
    for j in range(planes):
        pad[j, 0:8, :] = jnp.zeros((8, lanes), F32)
        pad[j, 8 + rows : 16 + rows, :] = jnp.zeros((8, lanes), F32)
        pad[j, 8 : 8 + rows, :] = cur[j]
    for j in range(planes):
        c = cur[j]
        acc = 3.0 * STENCIL[0] * c
        for d in range(1, REACH + 1):
            acc = acc + weights[d] * pltpu.roll(c, d, 1) + weights[-d] * pltpu.roll(c, lanes - d, 1)
            near = pad[j, 8 + d : 8 + d + rows, :] + pad[j, 8 - d : 8 - d + rows, :]
            for i in (j - d, j + d):
                if 0 <= i < planes:
                    near = near + cur[i]
            acc = acc + STENCIL[d] * near
        base[j] = 2.0 * c - prev[j] + cour[j] * acc
        if step == 0:
            surf[j] = jnp.zeros((rows, lanes), F32)
        else:
            surf[j] = jnp.where(
                lane == step - 1, jnp.broadcast_to(c[:, 0:1], (rows, lanes)), surf_in[j]
            )

    @pl.when(meta[SRC_PLANE] >= 0)
    def _():
        j, row = meta[SRC_PLANE], meta[SRC_ROW]
        hit = lax.broadcasted_iota(jnp.int32, (1, lanes), 1) == meta[SRC_LANE]
        line = base[j, pl.ds(row, 1), :]
        base[j, pl.ds(row, 1), :] = line + jnp.where(hit, wavelet[step], 0.0)


def local_step(step, meta, wavelet, cur, prev, cour, surf):
    planes, rows, lanes = cur.shape
    return pl.pallas_call(
        functools.partial(local_kernel, step),
        out_shape=(shape(cur.shape), shape(cur.shape)),
        in_specs=[SMEM, SMEM, VMEM, VMEM, VMEM, VMEM],
        out_specs=(VMEM, VMEM),
        scratch_shapes=[pltpu.VMEM((planes, rows + 16, lanes), F32)],
        cost_estimate=pl.CostEstimate(
            flops=60 * cur.size, bytes_accessed=24 * cur.size, transcendentals=0
        ),
        name="wave_local",
    )(meta, wavelet, cur, prev, cour, surf)


def halo_kernel(meta, base, cour, outer, inner, out):
    planes = base.shape[0]
    ok = jnp.where(meta[OUTER_OK] > 0, 1.0, 0.0)
    for j in range(planes):
        far = None
        for d in range(j + 1, REACH + 1):
            term = (STENCIL[d] * ok) * outer[d - j - 1]
            far = term if far is None else far + term
        for d in range(planes - j, REACH + 1):
            far = far + STENCIL[d] * inner[2 * planes - 1 - j - d]
        out[j] = base[j] + cour[j] * far


def halo_step(meta, base, cour, outer, inner):
    return pl.pallas_call(
        halo_kernel,
        out_shape=shape(base.shape),
        in_specs=[SMEM, VMEM, VMEM, VMEM, VMEM],
        out_specs=VMEM,
        cost_estimate=pl.CostEstimate(
            flops=12 * base.size, bytes_accessed=20 * base.size, transcendentals=0
        ),
        name="wave_halo",
    )(meta, base, cour, outer, inner)


def trace_kernel(step, place, cur, surf, out):
    planes, rows, lanes = cur.shape
    receivers = place.shape[0]
    steps = out.shape[0]
    lane = lax.broadcasted_iota(jnp.int32, (rows, lanes), 1)
    columns = jnp.concatenate(
        [
            jnp.where(lane == step, jnp.broadcast_to(cur[j, :, 0:1], (rows, lanes)), surf[j])
            for j in range(planes)
        ],
        0,
    )
    where = lax.broadcasted_iota(jnp.int32, (receivers, planes * rows), 1)
    pick = jnp.where(place[...] == where, 1.0, 0.0).astype(jnp.bfloat16)
    total = None
    for _ in range(3):
        part = columns.astype(jnp.bfloat16)
        columns = columns - part.astype(F32)
        term = jnp.dot(pick, part, preferred_element_type=F32)
        total = term if total is None else total + term
    out[...] = total.T[:steps, :]


def table_kernel(low, out):
    spread = out.shape[1]
    lanes = out.shape[2]
    dy = (lax.broadcasted_iota(jnp.int32, (spread, lanes), 0) - (spread // 2 - 1)).astype(F32)
    dz = (lax.broadcasted_iota(jnp.int32, (spread, lanes), 1) + 1).astype(F32)
    side = dy * dy
    deep = dz * dz

    def one(t, carry):
        dx = (t + low[0]).astype(F32)
        square = dx * dx + side + deep
        value = dz / (square * jnp.sqrt(square))
        out[t] = value.astype(jnp.bfloat16).astype(F32)
        return carry

    lax.fori_loop(0, out.shape[0], one, 0)


def gravity_table(low, depth, lateral, vertical):
    size = depth * 2 * lateral * vertical
    return pl.pallas_call(
        table_kernel,
        out_shape=shape((depth, 2 * lateral, vertical)),
        in_specs=[SMEM],
        out_specs=VMEM,
        cost_estimate=pl.CostEstimate(
            flops=20 * size, bytes_accessed=4 * size, transcendentals=2 * size
        ),
        name="gravity_table",
    )(low)


def forward_kernel(first, guard, lateral, low, meta, stations, table, dens, out):
    planes, rows, lanes = dens.shape
    count = out.shape[0]
    spread = 2 * lateral
    if guard:
        out[...] = jnp.zeros_like(out)

    def one(s, carry):
        sx, sy = divmod_static(stations[first + s], lateral)
        shift = meta[X_LOW] - sx - low[0]
        start = (shift + meta[HALF_LOW]) * spread + (lateral - 1 - sy)

        def accumulate():
            acc = None
            for p in range(planes):
                term = table[pl.ds(start + p * spread, rows), :] * dens[p]
                acc = term if acc is None else acc + term
            out[pl.ds(s, 1), :] = jnp.sum(acc, axis=0, keepdims=True)

        if guard:
            pl.when((shift >= 0) & (shift < guard))(accumulate)
        else:
            accumulate()
        return carry

    lax.fori_loop(0, count, one, 0, unroll=4)


def gravity_forward(first, count, guard, lateral, low, meta, stations, table, dens):
    flat = table.reshape(-1, table.shape[2])
    work = count * dens.size
    return pl.pallas_call(
        functools.partial(forward_kernel, first, guard, lateral),
        out_shape=shape((count, dens.shape[2])),
        in_specs=[SMEM, SMEM, SMEM, VMEM, VMEM],
        out_specs=VMEM,
        cost_estimate=pl.CostEstimate(
            flops=4 * work, bytes_accessed=4 * (flat.size + dens.size), transcendentals=0
        ),
        name="gravity_forward",
    )(low, meta, stations, flat, dens)


def adjoint_kernel(guard, lateral, slab, low, meta, stations, weights, table, out):
    rows = out.shape[1]
    spread = 2 * lateral

    def one(s, acc):
        sx, sy = divmod_static(stations[s], lateral)
        shift = meta[X_LOW] - sx - low[0]
        weight = weights[s]
        if guard:
            keep = (shift >= 0) & (shift < guard)
            shift = jnp.where(keep, shift, 0)
            weight = jnp.where(keep, weight, 0.0)
        start = shift * spread + (lateral - 1 - sy + meta[ROW_LOW])
        return tuple(
            acc[x] + weight * table[pl.ds(start + x * spread, rows), :] for x in range(slab)
        )

    zero = jnp.zeros((rows, out.shape[2]), F32)
    acc = lax.fori_loop(0, stations.shape[0], one, (zero,) * slab, unroll=4)
    for x in range(slab):
        out[x] = acc[x]


def gravity_adjoint(guard, lateral, slab, rows, low, meta, stations, weights, table):
    flat = table.reshape(-1, table.shape[2])
    return pl.pallas_call(
        functools.partial(adjoint_kernel, guard, lateral, slab),
        out_shape=shape((slab, rows, table.shape[2])),
        in_specs=[SMEM, SMEM, SMEM, SMEM, VMEM],
        out_specs=VMEM,
        name="gravity_adjoint",
    )(low, meta, stations, weights, flat)


def cross_kernel(meta, velocity, density, outer, inner, out):
    slab, rows, lanes = velocity.shape
    lane = lax.broadcasted_iota(jnp.int32, (rows, lanes), 1)
    row = lax.broadcasted_iota(jnp.int32, (rows, lanes), 0)
    flipped = meta[FLIPPED] > 0
    left_ok = jnp.where(meta[LEFT_OK] > 0, 0.5, 0.0)
    right_ok = jnp.where(meta[RIGHT_OK] > 0, 0.5, 0.0)

    def slopes(field, side, x):
        f = field[x]
        if x > 0:
            below = 0.5 * field[x - 1]
        else:
            below = left_ok * jnp.where(flipped, inner[side], outer[side])
        if x < slab - 1:
            above = 0.5 * field[x + 1]
        else:
            above = right_ok * jnp.where(flipped, outer[side], inner[side])
        up = jnp.where(row < rows - 1, pltpu.roll(f, rows - 1, 0), 0.0)
        down = jnp.where(row > 0, pltpu.roll(f, 1, 0), 0.0)
        ahead = jnp.where(lane < lanes - 1, pltpu.roll(f, lanes - 1, 1), 0.0)
        back = jnp.where(lane > 0, pltpu.roll(f, 1, 1), 0.0)
        return above - below, (up - down) * 0.5, (ahead - back) * 0.5

    for x in range(slab):
        v = slopes(velocity, 0, x)
        q = slopes(density, 1, x)
        out[0, x] = v[1] * q[2] - v[2] * q[1]
        out[1, x] = v[2] * q[0] - v[0] * q[2]
        out[2, x] = v[0] * q[1] - v[1] * q[0]


def cross_gradient_of(meta, velocity, density, outer, inner):
    return pl.pallas_call(
        cross_kernel,
        out_shape=shape((3,) + velocity.shape),
        in_specs=[SMEM, VMEM, VMEM, VMEM, VMEM],
        out_specs=VMEM,
        cost_estimate=pl.CostEstimate(
            flops=60 * velocity.size, bytes_accessed=24 * velocity.size, transcendentals=0
        ),
        name="cross_gradient",
    )(meta, velocity, density, outer, inner)


def per_device(
    p_now, p_prev, velocity, density, wavelet, source_cell, receiver_cells, station_cells, observed
):
    slab, lateral, vertical = p_now.shape
    count = lax.axis_size("mp")
    stations = lax.axis_size("station")
    steps = wavelet.shape[0]
    half = slab // 2
    assert half == REACH and count % 2 == 0 and stations % 4 == 0
    total_x = slab * count
    m = lax.axis_index("mp")
    s = lax.axis_index("station")
    core = s % 2
    x_low = m * slab
    flipped = (m + core) % 2 == 0
    outer_ok = jnp.where(flipped, m < count - 1, m > 0)

    chain = pairs_of(count, stations, chain_partner(count))

    def across(value):
        return lax.ppermute(value, AXES, chain)

    def swap_station(value, bit):
        return lax.ppermute(value, AXES, pairs_of(count, stations, lambda i, k: (i, k ^ bit)))

    def swap_slab(value, bit):
        return lax.ppermute(value, AXES, pairs_of(count, stations, lambda i, k: (i ^ bit, k)))

    def owned(field):
        return jnp.where(flipped, jnp.flip(field[half:], 0), field[:half])

    source_plane, source_lane = divmod_static(source_cell[0], vertical)
    source_x, source_row = divmod_static(source_plane, lateral)
    offset = source_x - x_low
    source_j = jnp.where(flipped, slab - 1 - offset, offset)
    source_j = jnp.where((source_j >= 0) & (source_j < half), source_j, -1)
    block = lateral // stations
    meta = jnp.stack(
        [
            source_j,
            source_row,
            source_lane,
            x_low,
            core * half,
            s * block,
            (m > 0).astype(jnp.int32),
            (m < count - 1).astype(jnp.int32),
            outer_ok.astype(jnp.int32),
            flipped.astype(jnp.int32),
        ]
    ).astype(jnp.int32)

    receiver_x, receiver_y = divmod_static(receiver_cells, lateral)
    receiver_j = receiver_x - x_low
    receiver_j = jnp.where(flipped, slab - 1 - receiver_j, receiver_j)
    inside = (receiver_j >= 0) & (receiver_j < half)
    place = jnp.where(inside, receiver_j * lateral + receiver_y, -1)[:, None]

    known = jnp.stack([station_cells.astype(F32), observed])[:, None, :]
    bit = 1
    while bit < stations:
        other = swap_station(known, bit)
        upper = (s // bit) % 2 == 1
        known = jnp.concatenate(
            [jnp.where(upper, other, known), jnp.where(upper, known, other)], 1
        )
        bit *= 2
    all_stations = known[0].reshape(-1).astype(jnp.int32)
    all_observed = known[1].reshape(-1)
    n_stations = all_stations.shape[0]

    reach = min(total_x, 64)
    chunks = -(-total_x // reach)
    guard = 0 if chunks == 1 else reach
    rounded = density.astype(jnp.bfloat16).astype(F32)
    half_density = jnp.where(core == 0, rounded[:half], rounded[half:])
    span = reach + slab - 1
    base_low = x_low - (total_x - 1)

    def table_at(low):
        return gravity_table(low, span, lateral, vertical)

    if chunks == 1:
        low = base_low[None].astype(jnp.int32)
        table = table_at(low)
        pieces = 4
        part = n_stations // pieces
        sums = jnp.concatenate(
            [
                gravity_forward(i * part, part, 0, lateral, low, meta, all_stations, table, half_density)
                for i in range(pieces)
            ]
        )
    else:

        def add_chunk(i, total):
            low = (base_low + i * reach)[None].astype(jnp.int32)
            return total + gravity_forward(
                0, n_stations, guard, lateral, low, meta, all_stations, table_at(low), half_density
            )

        sums = lax.fori_loop(0, chunks, add_chunk, jnp.zeros((n_stations, vertical), F32))
    predicted = jnp.sum(sums, axis=1)

    cour_full = TIME_RATIO * velocity * (TIME_RATIO * velocity)
    cour = owned(cour_full)
    cur = owned(p_now)
    prev = owned(p_prev)
    surf = cour
    edges = jnp.stack([owned(velocity)[0], owned(density)[0]])
    outer_edges = inner_edges = None
    for step in range(steps):
        if step == 0:
            received = across(jnp.concatenate([cur, edges]))
            outer, outer_edges = received[:half], received[half:]
        else:
            outer = across(cur)
        inner = swap_station(cur, 1)
        base, surf = local_step(step, meta, wavelet, cur, prev, cour, surf)
        if step == 1:
            inner_edges = swap_station(outer_edges, 1)
        cur, prev = halo_step(meta, base, cour, outer, inner), cur

    cross_gradient = cross_gradient_of(meta, velocity, density, outer_edges, inner_edges)

    sibling = swap_station(cur, 1)
    swapped = core == (m % 2)
    left = jnp.where(swapped, sibling, cur)
    right = jnp.where(swapped, cur, sibling)
    wavefield = jnp.concatenate([left, jnp.flip(right, 0)])

    recorded = pl.pallas_call(
        functools.partial(trace_kernel, steps - 1),
        out_shape=shape((steps, receiver_cells.shape[0])),
        in_specs=[VMEM] * 3,
        out_specs=VMEM,
        name="traces",
    )(place, cur, surf)
    packed = jnp.concatenate([recorded.reshape(-1, 128), predicted.reshape(-1, 128)])
    packed = packed + swap_station(packed, 1)
    if count & (count - 1) == 0:
        bit = 1
        while bit < count:
            packed = packed + swap_slab(packed, bit)
            bit *= 2
    else:
        packed = lax.psum(packed, "mp")
    trace_rows = recorded.size // 128
    traces = packed[:trace_rows].reshape(recorded.shape)
    residual = packed[trace_rows:].reshape(-1) - all_observed
    own_stations = station_cells.shape[0]
    gravity_residual = lax.dynamic_slice(residual, (s * own_stations,), (own_stations,))
    weights = residual.astype(jnp.bfloat16).astype(F32)

    if chunks == 1:
        density_gradient = gravity_adjoint(
            0, lateral, slab, block, low, meta, all_stations, weights, table
        )
    else:

        def back_chunk(i, total):
            low = (base_low + i * reach)[None].astype(jnp.int32)
            return total + gravity_adjoint(
                guard, lateral, slab, block, low, meta, all_stations, weights, table_at(low)
            )

        density_gradient = lax.fori_loop(
            0, chunks, back_chunk, jnp.zeros((slab, block, vertical), F32)
        )
    return (wavefield, traces, gravity_residual, density_gradient, cross_gradient)


def solution(mesh):
    in_specs = (
        P("mp", None, None),
        P("mp", None, None),
        P("mp", None, None),
        P("mp", None, None),
        P(),
        P(),
        P(),
        P("station"),
        P("station"),
    )
    out_specs = (
        P("mp", None, None),
        P(),
        P("station"),
        P("mp", "station", None),
        P(None, "mp", None, None),
    )
    return jax.shard_map(
        per_device, mesh=mesh, in_specs=in_specs, out_specs=out_specs, check_vma=False
    )
```

time: 396 us -> 189 us (0.48)
  Pallas kernels: 0 us -> 99.4 us
  starting transfers between devices: 108 us -> 40.6 us
  waiting for transfers between devices: 80 us -> 18.9 us
  other arithmetic: 60.4 us -> 7.22 us
  local copies, waits for them, and re-layouts: 58 us -> 19.9 us
  blocking collectives: 35.9 us -> 0 us
  matrix products: 34.7 us -> 0 us
  between operations: 14.3 us -> 1.65 us
    pallas_call x0 -> x40, Pallas kernels: none -> 99.4 us  [the longest x16 34.9 us: local_step(): pl.pallas_call(functools.partial(local_kernel, step), out_shape=(shape(cu...]
    ppermute x34 -> x40, starting transfers between devices: 108 us -> 40.6 us  [the longest x16 31.4 us: across(): return lax.ppermute(value, AXES, chain)]
    ppermute x34 -> x40, waiting for transfers between devices: 64.6 us -> 18.9 us  [the longest x16 13.3 us: across(): return lax.ppermute(value, AXES, chain)]
    add x32 -> x4, other arithmetic: 39.3 us -> 0.02 us  [the longest x3 0.01 us: per_device(): packed = packed + swap_slab(packed, bit)]
    psum x1 -> x0, blocking collectives: 35.9 us -> none  [per_device(): traces = lax.psum(recorded_all, 'mp')]
    dot_general x16 -> x0, matrix products: 34.7 us -> none  [the longest x8 17.5 us: forward(): jnp.dot(tile, plane, preferred_element_type=jnp.float32)]
    gather x16 -> x0, local copies, waits for them, and re-layouts: 31.1 us -> none  [advance(): recorded = jnp.where(inside, surface[safe_index], 0.0)]
    dynamic_slice x32 -> x1, local copies, waits for them, and re-layouts: 18.8 us -> 0.58 us  [per_device(): lax.dynamic_slice(residual, (s * own_stations,), (own_stations,))]
  transfers between devices with their start and end apart: 35 -> 40, of which waited for: 17 -> 16; matrix products, arithmetic and copies ran while one was open for 39% -> 6% of each run, Pallas kernels for 0% -> 41%
where the time goes in v1:
time: 189 us; the launch traced here: 188 us
  Pallas kernels  99.4 us (53%)
  starting transfers between devices  40.6 us (21%)
  local copies, waits for them, and re-layouts  19.9 us (11%)
  waiting for transfers between devices  18.9 us (10%)
  other arithmetic  7.22 us (4%)
    pallas_call x16, Pallas kernels, local_step(): pl.pallas_call(functools.partial(local_kernel, step), out_shape=(shape(cu...  34.9 us
    ppermute x16, starting transfers between devices, across(): return lax.ppermute(value, AXES, chain)  31.4 us
    pallas_call x16, Pallas kernels, halo_step(): pl.pallas_call(halo_kernel, out_shape=shape(base.shape), in_specs=[SMEM,...  29 us
    pallas_call x4, Pallas kernels, gravity_forward(): pl.pallas_call(functools.partial(forward_kernel, first, guard, lateral),...  19.3 us
    ppermute x16, waiting for transfers between devices, across(): return lax.ppermute(value, AXES, chain)  13.3 us
    unnamed x84, local copies, waits for them, and re-layouts  12 us
    pallas_call x1, Pallas kernels, gravity_adjoint(): pl.pallas_call(functools.partial(adjoint_kernel, guard, lateral, slab), o...  6.53 us
    ppermute x3, starting transfers between devices, swap_slab(): lax.ppermute(value, AXES, pairs_of(count, stations, lambda i, k: (i ^ bit...  5.8 us
  transfers between devices with their start and end apart: 40, of which 16 were waited for; matrix products, arithmetic and copies ran while one was open for 6% of the time, Pallas kernels for 41%

profile of v1, /device:TPU:0, one launch (start us, length us, event | category | flops | bytes accessed | tf_op | source)
XLA Modules:
  0.0 187.6 jit_solution(61935197564778820)
XLA Ops:
  5.1 2.6 %collective-permute-start = (f32[6,64,128]{2,1,0:T(8,128)S(1)}, f32[6,64,128]{2,1,0:T(8,128)S(1)}, u32[]{:S(2)}, u32[]{:S(2)}) collective-permute-start(f32[6,64,128]{2,1,0:T(8,128)S(1)} %pad_maximum_fusion.1), channel_id=1, source_target_pairs={{0,4},{1,3},{2,6},{3,1},{4,0},{5,9},{6,2},{7,11},{8,12},{9,5},{10,... | collective-permute-start | bytes 589832 | tf_op jit(solution)/shard_map/ppermute | solution.py:325
  12.6 2.1 %wave_local.16 = (f32[4,64,128]{2,1,0:T(8,128)}, f32[4,64,128]{2,1,0:T(8,128)}) custom-call(s32[10]{0:T(128)} %stack.62.meta, f32[16]{0:T(128)} %wavelet.31, f32[4,64,128]{2,1,0:T(8,128)} %copy-done.1, f32[4,64,128]{2,1,0:T(8,128)} %get-tuple-element.84.prev, f32[4,64,128]{2,1,0:T(8,128)} %get-tuple-element.83.cour.surf_in, ...), custom_call_target="tpu_custom_call" | custom-call | flops 1966080 | bytes 786432 | tf_op jit(solution)/shard_map/wave_local/pallas_call | solution.py:89
  18.6 2.2 %wave_local.17 = (f32[4,64,128]{2,1,0:T(8,128)}, f32[4,64,128]{2,1,0:T(8,128)}) custom-call(s32[10]{0:T(128)} %stack.62.meta, f32[16]{0:T(128)} %wavelet.31, f32[4,64,128]{2,1,0:T(8,128)} %wave_halo.16.cur.prev, f32[4,64,128]{2,1,0:T(8,128)} %copy-done.1, f32[4,64,128]{2,1,0:T(8,128)} %get-tuple-element.83.cour.surf_in, f32[4,64,128]{2,1,0:T(8,128)} %get-tuple-element.38.surf_in), custom_call_target="tpu_custom_call" | custom-call | flops 1966080 | bytes 786432 | tf_op jit(solution)/shard_map/wave_local/pallas_call | solution.py:89
  20.9 2.3 %collective-permute-done.2.outer = f32[4,64,128]{2,1,0:T(8,128)S(1)} collective-permute-done((f32[4,64,128]{2,1,0:T(8,128)}, f32[4,64,128]{2,1,0:T(8,128)S(1)}, u32[]{:S(2)}, u32[]{:S(2)}) %collective-permute-start.2) | collective-permute-done | bytes 131104 | tf_op jit(solution)/shard_map/ppermute | solution.py:325
  25.6 2.1 %collective-permute-start.4 = (f32[4,64,128]{2,1,0:T(8,128)}, f32[4,64,128]{2,1,0:T(8,128)S(1)}, u32[]{:S(2)}, u32[]{:S(2)}) collective-permute-start(f32[4,64,128]{2,1,0:T(8,128)} %wave_halo.17.cur.prev), channel_id=1, source_target_pairs={{0,4},{1,3},{2,6},{3,1},{4,0},{5,9},{6,2},{7,11},{8,12},{9,5},{10,... | collective-permute-start | bytes 393224 | tf_op jit(solution)/shard_map/ppermute | solution.py:325
  27.7 2.2 %wave_local.18 = (f32[4,64,128]{2,1,0:T(8,128)}, f32[4,64,128]{2,1,0:T(8,128)}) custom-call(s32[10]{0:T(128)} %stack.62.meta, f32[16]{0:T(128)} %wavelet.31, f32[4,64,128]{2,1,0:T(8,128)} %wave_halo.17.cur.prev, f32[4,64,128]{2,1,0:T(8,128)} %wave_halo.16.cur.prev, f32[4,64,128]{2,1,0:T(8,128)} %get-tuple-element.83.cour.surf_in, ...), custom_call_target="tpu_custom_call" | custom-call | flops 1966080 | bytes 786432 | tf_op jit(solution)/shard_map/wave_local/pallas_call | solution.py:89
  33.9 2.4 %collective-permute-start.6 = (f32[4,64,128]{2,1,0:T(8,128)}, f32[4,64,128]{2,1,0:T(8,128)S(1)}, u32[]{:S(2)}, u32[]{:S(2)}) collective-permute-start(f32[4,64,128]{2,1,0:T(8,128)} %wave_halo.18.cur.prev), channel_id=1, source_target_pairs={{0,4},{1,3},{2,6},{3,1},{4,0},{5,9},{6,2},{7,11},{8,12},{9,5},{10,... | collective-permute-start | bytes 393224 | tf_op jit(solution)/shard_map/ppermute | solution.py:325
  36.3 2.2 %wave_local.19 = (f32[4,64,128]{2,1,0:T(8,128)}, f32[4,64,128]{2,1,0:T(8,128)}) custom-call(s32[10]{0:T(128)} %stack.62.meta, f32[16]{0:T(128)} %wavelet.31, f32[4,64,128]{2,1,0:T(8,128)} %wave_halo.18.cur.prev, f32[4,64,128]{2,1,0:T(8,128)} %wave_halo.17.cur.prev, f32[4,64,128]{2,1,0:T(8,128)} %get-tuple-element.83.cour.surf_in, ...), custom_call_target="tpu_custom_call" | custom-call | flops 1966080 | bytes 786432 | tf_op jit(solution)/shard_map/wave_local/pallas_call | solution.py:89
  44.0 2.2 %wave_local.20 = (f32[4,64,128]{2,1,0:T(8,128)}, f32[4,64,128]{2,1,0:T(8,128)}) custom-call(s32[10]{0:T(128)} %stack.62.meta, f32[16]{0:T(128)} %wavelet.31, f32[4,64,128]{2,1,0:T(8,128)} %wave_halo.19.cur.prev, f32[4,64,128]{2,1,0:T(8,128)} %wave_halo.18.cur.prev, f32[4,64,128]{2,1,0:T(8,128)} %get-tuple-element.83.cour.surf_in, ...), custom_call_target="tpu_custom_call" | custom-call | flops 1966080 | bytes 786432 | tf_op jit(solution)/shard_map/wave_local/pallas_call | solution.py:89
  51.7 2.2 %wave_local.21 = (f32[4,64,128]{2,1,0:T(8,128)}, f32[4,64,128]{2,1,0:T(8,128)}) custom-call(s32[10]{0:T(128)} %stack.62.meta, f32[16]{0:T(128)} %wavelet.31, f32[4,64,128]{2,1,0:T(8,128)} %wave_halo.20.cur.prev, f32[4,64,128]{2,1,0:T(8,128)} %wave_halo.19.cur.prev, f32[4,64,128]{2,1,0:T(8,128)} %get-tuple-element.83.cour.surf_in, ...), custom_call_target="tpu_custom_call" | custom-call | flops 1966080 | bytes 786432 | tf_op jit(solution)/shard_map/wave_local/pallas_call | solution.py:89
  59.4 2.2 %wave_local.22 = (f32[4,64,128]{2,1,0:T(8,128)}, f32[4,64,128]{2,1,0:T(8,128)}) custom-call(s32[10]{0:T(128)} %stack.62.meta, f32[16]{0:T(128)} %wavelet.31, f32[4,64,128]{2,1,0:T(8,128)} %wave_halo.21.cur.prev, f32[4,64,128]{2,1,0:T(8,128)} %wave_halo.20.cur.prev, f32[4,64,128]{2,1,0:T(8,128)} %get-tuple-element.83.cour.surf_in, ...), custom_call_target="tpu_custom_call" | custom-call | flops 1966080 | bytes 786432 | tf_op jit(solution)/shard_map/wave_local/pallas_call | solution.py:89
  67.2 2.2 %wave_local.23 = (f32[4,64,128]{2,1,0:T(8,128)}, f32[4,64,128]{2,1,0:T(8,128)}) custom-call(s32[10]{0:T(128)} %stack.62.meta, f32[16]{0:T(128)} %wavelet.31, f32[4,64,128]{2,1,0:T(8,128)} %wave_halo.22.cur.prev, f32[4,64,128]{2,1,0:T(8,128)} %wave_halo.21.cur.prev, f32[4,64,128]{2,1,0:T(8,128)} %get-tuple-element.83.cour.surf_in, ...), custom_call_target="tpu_custom_call" | custom-call | flops 1966080 | bytes 786432 | tf_op jit(solution)/shard_map/wave_local/pallas_call | solution.py:89
  74.9 2.2 %wave_local.24 = (f32[4,64,128]{2,1,0:T(8,128)}, f32[4,64,128]{2,1,0:T(8,128)}) custom-call(s32[10]{0:T(128)} %stack.62.meta, f32[16]{0:T(128)} %wavelet.31, f32[4,64,128]{2,1,0:T(8,128)} %wave_halo.23.cur.prev, f32[4,64,128]{2,1,0:T(8,128)} %wave_halo.22.cur.prev, f32[4,64,128]{2,1,0:T(8,128)} %get-tuple-element.83.cour.surf_in, ...), custom_call_target="tpu_custom_call" | custom-call | flops 1966080 | bytes 786432 | tf_op jit(solution)/shard_map/wave_local/pallas_call | solution.py:89
  83.2 2.2 %wave_local.25 = (f32[4,64,128]{2,1,0:T(8,128)}, f32[4,64,128]{2,1,0:T(8,128)}) custom-call(s32[10]{0:T(128)} %stack.62.meta, f32[16]{0:T(128)} %wavelet.31, f32[4,64,128]{2,1,0:T(8,128)} %wave_halo.24.cur.prev, f32[4,64,128]{2,1,0:T(8,128)} %wave_halo.23.cur.prev, f32[4,64,128]{2,1,0:T(8,128)} %get-tuple-element.83.cour.surf_in, ...), custom_call_target="tpu_custom_call" | custom-call | flops 1966080 | bytes 786432 | tf_op jit(solution)/shard_map/wave_local/pallas_call | solution.py:89
  90.3 2.2 %wave_local.26 = (f32[4,64,128]{2,1,0:T(8,128)}, f32[4,64,128]{2,1,0:T(8,128)}) custom-call(s32[10]{0:T(128)} %stack.62.meta, f32[16]{0:T(128)} %wavelet.31, f32[4,64,128]{2,1,0:T(8,128)} %wave_halo.25.cur.prev, f32[4,64,128]{2,1,0:T(8,128)} %wave_halo.24.cur.prev, f32[4,64,128]{2,1,0:T(8,128)} %get-tuple-element.83.cour.surf_in, ...), custom_call_target="tpu_custom_call" | custom-call | flops 1966080 | bytes 786432 | tf_op jit(solution)/shard_map/wave_local/pallas_call | solution.py:89
  98.7 2.2 %wave_local.27 = (f32[4,64,128]{2,1,0:T(8,128)}, f32[4,64,128]{2,1,0:T(8,128)}) custom-call(s32[10]{0:T(128)} %stack.62.meta, f32[16]{0:T(128)} %wavelet.31, f32[4,64,128]{2,1,0:T(8,128)} %wave_halo.26.cur.prev, f32[4,64,128]{2,1,0:T(8,128)} %wave_halo.25.cur.prev, f32[4,64,128]{2,1,0:T(8,128)} %get-tuple-element.83.cour.surf_in, ...), custom_call_target="tpu_custom_call" | custom-call | flops 1966080 | bytes 786432 | tf_op jit(solution)/shard_map/wave_local/pallas_call | solution.py:89
  106.6 2.2 %wave_local.28 = (f32[4,64,128]{2,1,0:T(8,128)}, f32[4,64,128]{2,1,0:T(8,128)}) custom-call(s32[10]{0:T(128)} %stack.62.meta, f32[16]{0:T(128)} %wavelet.31, f32[4,64,128]{2,1,0:T(8,128)} %wave_halo.27.cur.prev, f32[4,64,128]{2,1,0:T(8,128)} %wave_halo.26.cur.prev, f32[4,64,128]{2,1,0:T(8,128)} %get-tuple-element.83.cour.surf_in, ...), custom_call_target="tpu_custom_call" | custom-call | flops 1966080 | bytes 786432 | tf_op jit(solution)/shard_map/wave_local/pallas_call | solution.py:89
  115.0 5.3 %gravity_table.1 = f32[71,128,128]{2,1,0:T(8,128)} custom-call(s32[1]{0:T(128)} %bitcast.10.low), custom_call_target="tpu_custom_call" | custom-call | flops 23265280 | bytes 4653056 | tf_op jit(solution)/shard_map/gravity_table/pallas_call | solution.py:171
  120.3 2.2 %wave_local.29 = (f32[4,64,128]{2,1,0:T(8,128)}, f32[4,64,128]{2,1,0:T(8,128)}) custom-call(s32[10]{0:T(128)} %stack.62.meta, f32[16]{0:T(128)} %wavelet.31, f32[4,64,128]{2,1,0:T(8,128)} %wave_halo.28.cur.prev, f32[4,64,128]{2,1,0:T(8,128)} %wave_halo.27.cur.prev, f32[4,64,128]{2,1,0:T(8,128)} %get-tuple-element.83.cour.surf_in, ...), custom_call_target="tpu_custom_call" | custom-call | flops 1966080 | bytes 786432 | tf_op jit(solution)/shard_map/wave_local/pallas_call | solution.py:89
  126.1 2.2 %wave_local.30 = (f32[4,64,128]{2,1,0:T(8,128)}, f32[4,64,128]{2,1,0:T(8,128)}) custom-call(s32[10]{0:T(128)} %stack.62.meta, f32[16]{0:T(128)} %wavelet.31, f32[4,64,128]{2,1,0:T(8,128)} %wave_halo.29.cur.prev, f32[4,64,128]{2,1,0:T(8,128)} %wave_halo.28.cur.prev, f32[4,64,128]{2,1,0:T(8,128)} %get-tuple-element.83.cour.surf_in, ...), custom_call_target="tpu_custom_call" | custom-call | flops 1966080 | bytes 786432 | tf_op jit(solution)/shard_map/wave_local/pallas_call | solution.py:89
  132.8 2.4 %collective-permute-start.30 = (f32[4,64,128]{2,1,0:T(8,128)}, f32[4,64,128]{2,1,0:T(8,128)S(1)}, u32[]{:S(2)}, u32[]{:S(2)}) collective-permute-start(f32[4,64,128]{2,1,0:T(8,128)} %wave_halo.30.cur), channel_id=1, source_target_pairs={{0,4},{1,3},{2,6},{3,1},{4,0},{5,9},{6,2},{7,11},{8,12},{9,5},{10,... | collective-permute-start | bytes 393224 | tf_op jit(solution)/shard_map/ppermute | solution.py:325
  135.8 4.8 %gravity_forward.4 = f32[128,128]{1,0:T(8,128)} custom-call(s32[1]{0:T(128)} %bitcast.10.low, s32[10]{0:T(128)} %stack.62.meta, s32[512]{0:T(512)} %bitcast.34, f32[9088,128]{1,0:T(8,128)} %bitcast.29, f32[4,64,128]{2,1,0:T(8,128)} %slice_select_fusion.dens), custom_call_target="tpu_custom_call" | custom-call | flops 16777216 | bytes 4784128 | tf_op jit(solution)/shard_map/gravity_forward/pallas_call | solution.py:214
  140.6 4.8 %gravity_forward.5 = f32[128,128]{1,0:T(8,128)} custom-call(s32[1]{0:T(128)} %bitcast.10.low, s32[10]{0:T(128)} %stack.62.meta, s32[512]{0:T(512)} %bitcast.35, f32[9088,128]{1,0:T(8,128)} %bitcast.30, f32[4,64,128]{2,1,0:T(8,128)} %slice_select_fusion.dens), custom_call_target="tpu_custom_call" | custom-call | flops 16777216 | bytes 4784128 | tf_op jit(solution)/shard_map/gravity_forward/pallas_call | solution.py:214
  145.4 4.8 %gravity_forward.6 = f32[128,128]{1,0:T(8,128)} custom-call(s32[1]{0:T(128)} %bitcast.10.low, s32[10]{0:T(128)} %stack.62.meta, s32[512]{0:T(512)} %bitcast.36, f32[9088,128]{1,0:T(8,128)} %bitcast.31, f32[4,64,128]{2,1,0:T(8,128)} %slice_select_fusion.dens), custom_call_target="tpu_custom_call" | custom-call | flops 16777216 | bytes 4784128 | tf_op jit(solution)/shard_map/gravity_forward/pallas_call | solution.py:214
  150.3 4.8 %gravity_forward.7 = f32[128,128]{1,0:T(8,128)} custom-call(s32[1]{0:T(128)} %bitcast.10.low, s32[10]{0:T(128)} %stack.62.meta, s32[512]{0:T(512)} %bitcast.37, f32[9088,128]{1,0:T(8,128)} %bitcast.32, f32[4,64,128]{2,1,0:T(8,128)} %slice_select_fusion.dens), custom_call_target="tpu_custom_call" | custom-call | flops 16777216 | bytes 4784128 | tf_op jit(solution)/shard_map/gravity_forward/pallas_call | solution.py:214
  156.1 2.2 %wave_local.31 = (f32[4,64,128]{2,1,0:T(8,128)}, f32[4,64,128]{2,1,0:T(8,128)}) custom-call(s32[10]{0:T(128)} %stack.62.meta, f32[16]{0:T(128)} %wavelet.31, f32[4,64,128]{2,1,0:T(8,128)} %wave_halo.30.cur, f32[4,64,128]{2,1,0:T(8,128)} %wave_halo.29.cur.prev, f32[4,64,128]{2,1,0:T(8,128)} %get-tuple-element.83.cour.surf_in, ...), custom_call_target="tpu_custom_call" | custom-call | flops 1966080 | bytes 786432 | tf_op jit(solution)/shard_map/wave_local/pallas_call | solution.py:89
  160.8 2.1 %traces.1 = f32[16,256]{1,0:T(8,128)} custom-call(s32[256,1]{1,0:T(8,128)} %copy.14.place, f32[4,64,128]{2,1,0:T(8,128)} %wave_halo.31.cur, f32[4,64,128]{2,1,0:T(8,128)} %get-tuple-element.68.surf), custom_call_target="tpu_custom_call" | custom-call | tf_op jit(solution)/shard_map/traces/pallas_call | solution.py:436
  165.7 3.1 %collective-permute-done.36 = f32[36,128]{1,0:T(8,128)S(1)} collective-permute-done((f32[36,128]{1,0:T(8,128)S(1)}, f32[36,128]{1,0:T(8,128)S(1)}, u32[]{:S(2)}, u32[]{:S(2)}) %collective-permute-start.36) | collective-permute-done | bytes 18464 | tf_op jit(solution)/shard_map/ppermute | solution.py:331
  168.7 2.0 %collective-permute-start.37 = (f32[36,128]{1,0:T(8,128)S(1)}, f32[36,128]{1,0:T(8,128)S(1)}, u32[]{:S(2)}, u32[]{:S(2)}) collective-permute-start(f32[36,128]{1,0:T(8,128)S(1)} %add.45), channel_id=1, source_target_pairs={{0,8},{1,9},{2,10},{3,11},{4,12},{5,13},{6,14},{7,15},{8,0},{9,1},... | collective-permute-start | bytes 55304 | tf_op jit(solution)/shard_map/ppermute | solution.py:331
  172.5 3.0 %collective-permute-start.38 = (f32[36,128]{1,0:T(8,128)S(1)}, f32[36,128]{1,0:T(8,128)S(1)}, u32[]{:S(2)}, u32[]{:S(2)}) collective-permute-start(f32[36,128]{1,0:T(8,128)S(1)} %add.46), channel_id=1, source_target_pairs={{0,16},{1,17},{2,18},{3,19},{4,20},{5,21},{6,22},{7,23},{8,24},{9,... | collective-permute-start | bytes 55304 | tf_op jit(solution)/shard_map/ppermute | solution.py:331
  176.2 2.3 %cross_gradient.1 = f32[3,8,64,128]{3,2,1,0:T(8,128)} custom-call(s32[10]{0:T(128)} %stack.62.meta, f32[8,64,128]{2,1,0:T(8,128)} %velocity.1, f32[8,64,128]{2,1,0:T(8,128)} %density.1, f32[2,64,128]{2,1,0:T(8,128)} %copy-done.6, f32[2,64,128]{2,1,0:T(8,128)} %copy-done.38), custom_call_target="tpu_custom_call" | custom-call | flops 3932160 | bytes 1572864 | tf_op jit(solution)/shard_map/cross_gradient/pallas_call | solution.py:293
  179.1 6.5 %gravity_adjoint.1 = f32[8,16,128]{2,1,0:T(8,128)} custom-call(s32[1]{0:T(128)} %bitcast.10.low, s32[10]{0:T(128)} %stack.62.meta, s32[512]{0:T(512)} %bitcast.38, f32[512]{0:T(512)} %get-tuple-element.69.weights, f32[9088,128]{1,0:T(8,128)} %bitcast.33), custom_call_target="tpu_custom_call" | custom-call | tf_op jit(solution)/shard_map/gravity_adjoint/pallas_call | solution.py:251
  (211 shorter events, 95.8 us)
Async XLA Ops:
  2.5 12.9 %collective-permute-start.1 = (f32[4,64,128]{2,1,0:T(8,128)S(1)}, f32[4,64,128]{2,1,0:T(8,128)S(1)}, u32[]{:S(2)}, u32[]{:S(2)}) collective-permute-start(f32[4,64,128]{2,1,0:T(8,128)S(1)} %slice_select_fusion.3.cur.prev), channel_id=1, source_target_pairs={{0,1},{1,0},{2,3},{3,2},{4,5},{5,4},{6,7},{7,6},{8,9},{9,8},{10,11... | collective-permute-start | bytes 393224 | tf_op jit(solution)/shard_map/ppermute | solution.py:328
  5.1 9.6 %collective-permute-start = (f32[6,64,128]{2,1,0:T(8,128)S(1)}, f32[6,64,128]{2,1,0:T(8,128)S(1)}, u32[]{:S(2)}, u32[]{:S(2)}) collective-permute-start(f32[6,64,128]{2,1,0:T(8,128)S(1)} %pad_maximum_fusion.1), channel_id=1, source_target_pairs={{0,4},{1,3},{2,6},{3,1},{4,0},{5,9},{6,2},{7,11},{8,12},{9,5},{10,... | collective-permute-start | bytes 589832 | tf_op jit(solution)/shard_map/ppermute | solution.py:325
  17.9 5.2 %collective-permute-start.2 = (f32[4,64,128]{2,1,0:T(8,128)}, f32[4,64,128]{2,1,0:T(8,128)S(1)}, u32[]{:S(2)}, u32[]{:S(2)}) collective-permute-start(f32[4,64,128]{2,1,0:T(8,128)} %wave_halo.16.cur.prev), channel_id=1, source_target_pairs={{0,4},{1,3},{2,6},{3,1},{4,0},{5,9},{6,2},{7,11},{8,12},{9,5},{10,... | collective-permute-start | bytes 393224 | tf_op jit(solution)/shard_map/ppermute | solution.py:325
  18.6 4.5 %collective-permute-start.3 = (f32[4,64,128]{2,1,0:T(8,128)}, f32[4,64,128]{2,1,0:T(8,128)S(1)}, u32[]{:S(2)}, u32[]{:S(2)}) collective-permute-start(f32[4,64,128]{2,1,0:T(8,128)} %wave_halo.16.cur.prev), channel_id=1, source_target_pairs={{0,1},{1,0},{2,3},{3,2},{4,5},{5,4},{6,7},{7,6},{8,9},{9,8},{10,11... | collective-permute-start | bytes 393224 | tf_op jit(solution)/shard_map/ppermute | solution.py:328
  25.6 5.7 %collective-permute-start.4 = (f32[4,64,128]{2,1,0:T(8,128)}, f32[4,64,128]{2,1,0:T(8,128)S(1)}, u32[]{:S(2)}, u32[]{:S(2)}) collective-permute-start(f32[4,64,128]{2,1,0:T(8,128)} %wave_halo.17.cur.prev), channel_id=1, source_target_pairs={{0,4},{1,3},{2,6},{3,1},{4,0},{5,9},{6,2},{7,11},{8,12},{9,5},{10,... | collective-permute-start | bytes 393224 | tf_op jit(solution)/shard_map/ppermute | solution.py:325
  27.7 3.6 %collective-permute-start.5 = (f32[4,64,128]{2,1,0:T(8,128)}, f32[4,64,128]{2,1,0:T(8,128)S(1)}, u32[]{:S(2)}, u32[]{:S(2)}) collective-permute-start(f32[4,64,128]{2,1,0:T(8,128)} %wave_halo.17.cur.prev), channel_id=1, source_target_pairs={{0,1},{1,0},{2,3},{3,2},{4,5},{5,4},{6,7},{7,6},{8,9},{9,8},{10,11... | collective-permute-start | bytes 393224 | tf_op jit(solution)/shard_map/ppermute | solution.py:328
  33.9 5.5 %collective-permute-start.6 = (f32[4,64,128]{2,1,0:T(8,128)}, f32[4,64,128]{2,1,0:T(8,128)S(1)}, u32[]{:S(2)}, u32[]{:S(2)}) collective-permute-start(f32[4,64,128]{2,1,0:T(8,128)} %wave_halo.18.cur.prev), channel_id=1, source_target_pairs={{0,4},{1,3},{2,6},{3,1},{4,0},{5,9},{6,2},{7,11},{8,12},{9,5},{10,... | collective-permute-start | bytes 393224 | tf_op jit(solution)/shard_map/ppermute | solution.py:325
  42.0 5.2 %collective-permute-start.8 = (f32[4,64,128]{2,1,0:T(8,128)}, f32[4,64,128]{2,1,0:T(8,128)S(1)}, u32[]{:S(2)}, u32[]{:S(2)}) collective-permute-start(f32[4,64,128]{2,1,0:T(8,128)} %wave_halo.19.cur.prev), channel_id=1, source_target_pairs={{0,4},{1,3},{2,6},{3,1},{4,0},{5,9},{6,2},{7,11},{8,12},{9,5},{10,... | collective-permute-start | bytes 393224 | tf_op jit(solution)/shard_map/ppermute | solution.py:325
  49.7 5.2 %collective-permute-start.10 = (f32[4,64,128]{2,1,0:T(8,128)}, f32[4,64,128]{2,1,0:T(8,128)S(1)}, u32[]{:S(2)}, u32[]{:S(2)}) collective-permute-start(f32[4,64,128]{2,1,0:T(8,128)} %wave_halo.20.cur.prev), channel_id=1, source_target_pairs={{0,4},{1,3},{2,6},{3,1},{4,0},{5,9},{6,2},{7,11},{8,12},{9,5},{10,... | collective-permute-start | bytes 393224 | tf_op jit(solution)/shard_map/ppermute | solution.py:325
  51.7 3.2 %collective-permute-start.11 = (f32[4,64,128]{2,1,0:T(8,128)}, f32[4,64,128]{2,1,0:T(8,128)S(1)}, u32[]{:S(2)}, u32[]{:S(2)}) collective-permute-start(f32[4,64,128]{2,1,0:T(8,128)} %wave_halo.20.cur.prev), channel_id=1, source_target_pairs={{0,1},{1,0},{2,3},{3,2},{4,5},{5,4},{6,7},{7,6},{8,9},{9,8},{10,11... | collective-permute-start | bytes 393224 | tf_op jit(solution)/shard_map/ppermute | solution.py:328
  57.4 5.2 %collective-permute-start.12 = (f32[4,64,128]{2,1,0:T(8,128)}, f32[4,64,128]{2,1,0:T(8,128)S(1)}, u32[]{:S(2)}, u32[]{:S(2)}) collective-permute-start(f32[4,64,128]{2,1,0:T(8,128)} %wave_halo.21.cur.prev), channel_id=1, source_target_pairs={{0,4},{1,3},{2,6},{3,1},{4,0},{5,9},{6,2},{7,11},{8,12},{9,5},{10,... | collective-permute-start | bytes 393224 | tf_op jit(solution)/shard_map/ppermute | solution.py:325
  59.4 3.2 %collective-permute-start.13 = (f32[4,64,128]{2,1,0:T(8,128)}, f32[4,64,128]{2,1,0:T(8,128)S(1)}, u32[]{:S(2)}, u32[]{:S(2)}) collective-permute-start(f32[4,64,128]{2,1,0:T(8,128)} %wave_halo.21.cur.prev), channel_id=1, source_target_pairs={{0,1},{1,0},{2,3},{3,2},{4,5},{5,4},{6,7},{7,6},{8,9},{9,8},{10,11... | collective-permute-start | bytes 393224 | tf_op jit(solution)/shard_map/ppermute | solution.py:328
  65.1 5.2 %collective-permute-start.14 = (f32[4,64,128]{2,1,0:T(8,128)}, f32[4,64,128]{2,1,0:T(8,128)S(1)}, u32[]{:S(2)}, u32[]{:S(2)}) collective-permute-start(f32[4,64,128]{2,1,0:T(8,128)} %wave_halo.22.cur.prev), channel_id=1, source_target_pairs={{0,4},{1,3},{2,6},{3,1},{4,0},{5,9},{6,2},{7,11},{8,12},{9,5},{10,... | collective-permute-start | bytes 393224 | tf_op jit(solution)/shard_map/ppermute | solution.py:325
  67.2 3.2 %collective-permute-start.15 = (f32[4,64,128]{2,1,0:T(8,128)}, f32[4,64,128]{2,1,0:T(8,128)S(1)}, u32[]{:S(2)}, u32[]{:S(2)}) collective-permute-start(f32[4,64,128]{2,1,0:T(8,128)} %wave_halo.22.cur.prev), channel_id=1, source_target_pairs={{0,1},{1,0},{2,3},{3,2},{4,5},{5,4},{6,7},{7,6},{8,9},{9,8},{10,11... | collective-permute-start | bytes 393224 | tf_op jit(solution)/shard_map/ppermute | solution.py:328
  72.8 5.2 %collective-permute-start.16 = (f32[4,64,128]{2,1,0:T(8,128)}, f32[4,64,128]{2,1,0:T(8,128)S(1)}, u32[]{:S(2)}, u32[]{:S(2)}) collective-permute-start(f32[4,64,128]{2,1,0:T(8,128)} %wave_halo.23.cur.prev), channel_id=1, source_target_pairs={{0,4},{1,3},{2,6},{3,1},{4,0},{5,9},{6,2},{7,11},{8,12},{9,5},{10,... | collective-permute-start | bytes 393224 | tf_op jit(solution)/shard_map/ppermute | solution.py:325
  80.6 5.2 %collective-permute-start.18 = (f32[4,64,128]{2,1,0:T(8,128)}, f32[4,64,128]{2,1,0:T(8,128)S(1)}, u32[]{:S(2)}, u32[]{:S(2)}) collective-permute-start(f32[4,64,128]{2,1,0:T(8,128)} %wave_halo.24.cur.prev), channel_id=1, source_target_pairs={{0,4},{1,3},{2,6},{3,1},{4,0},{5,9},{6,2},{7,11},{8,12},{9,5},{10,... | collective-permute-start | bytes 393224 | tf_op jit(solution)/shard_map/ppermute | solution.py:325
  82.6 30.8 %collective-permute-start.33 = (f32[2,1,128]{2,0,1:T(2,128)S(1)}, f32[2,1,128]{2,0,1:T(2,128)S(1)}, u32[]{:S(2)}, u32[]{:S(2)}) collective-permute-start(f32[2,1,128]{2,0,1:T(2,128)S(1)} %maximum_bitcast_fusion), channel_id=1, source_target_pairs={{0,1},{1,0},{2,3},{3,2},{4,5},{5,4},{6,7},{7,6},{8,9},{9,8},{10,11... | collective-permute-start | bytes 3080 | tf_op jit(solution)/shard_map/ppermute | solution.py:328
  88.3 5.2 %collective-permute-start.20 = (f32[4,64,128]{2,1,0:T(8,128)}, f32[4,64,128]{2,1,0:T(8,128)S(1)}, u32[]{:S(2)}, u32[]{:S(2)}) collective-permute-start(f32[4,64,128]{2,1,0:T(8,128)} %wave_halo.25.cur.prev), channel_id=1, source_target_pairs={{0,4},{1,3},{2,6},{3,1},{4,0},{5,9},{6,2},{7,11},{8,12},{9,5},{10,... | collective-permute-start | bytes 393224 | tf_op jit(solution)/shard_map/ppermute | solution.py:325
  96.0 5.2 %collective-permute-start.22 = (f32[4,64,128]{2,1,0:T(8,128)}, f32[4,64,128]{2,1,0:T(8,128)S(1)}, u32[]{:S(2)}, u32[]{:S(2)}) collective-permute-start(f32[4,64,128]{2,1,0:T(8,128)} %wave_halo.26.cur.prev), channel_id=1, source_target_pairs={{0,4},{1,3},{2,6},{3,1},{4,0},{5,9},{6,2},{7,11},{8,12},{9,5},{10,... | collective-permute-start | bytes 393224 | tf_op jit(solution)/shard_map/ppermute | solution.py:325
  103.7 5.2 %collective-permute-start.24 = (f32[4,64,128]{2,1,0:T(8,128)}, f32[4,64,128]{2,1,0:T(8,128)S(1)}, u32[]{:S(2)}, u32[]{:S(2)}) collective-permute-start(f32[4,64,128]{2,1,0:T(8,128)} %wave_halo.27.cur.prev), channel_id=1, source_target_pairs={{0,4},{1,3},{2,6},{3,1},{4,0},{5,9},{6,2},{7,11},{8,12},{9,5},{10,... | collective-permute-start | bytes 393224 | tf_op jit(solution)/shard_map/ppermute | solution.py:325
  111.4 11.1 %collective-permute-start.26 = (f32[4,64,128]{2,1,0:T(8,128)}, f32[4,64,128]{2,1,0:T(8,128)S(1)}, u32[]{:S(2)}, u32[]{:S(2)}) collective-permute-start(f32[4,64,128]{2,1,0:T(8,128)} %wave_halo.28.cur.prev), channel_id=1, source_target_pairs={{0,4},{1,3},{2,6},{3,1},{4,0},{5,9},{6,2},{7,11},{8,12},{9,5},{10,... | collective-permute-start | bytes 393224 | tf_op jit(solution)/shard_map/ppermute | solution.py:325
  113.4 9.1 %collective-permute-start.27 = (f32[4,64,128]{2,1,0:T(8,128)}, f32[4,64,128]{2,1,0:T(8,128)S(1)}, u32[]{:S(2)}, u32[]{:S(2)}) collective-permute-start(f32[4,64,128]{2,1,0:T(8,128)} %wave_halo.28.cur.prev), channel_id=1, source_target_pairs={{0,1},{1,0},{2,3},{3,2},{4,5},{5,4},{6,7},{7,6},{8,9},{9,8},{10,11... | collective-permute-start | bytes 393224 | tf_op jit(solution)/shard_map/ppermute | solution.py:328
  113.5 12.7 %collective-permute-start.34 = (f32[2,2,128]{2,0,1:T(2,128)S(1)}, f32[2,2,128]{2,0,1:T(2,128)S(1)}, u32[]{:S(2)}, u32[]{:S(2)}) collective-permute-start(f32[2,2,128]{2,0,1:T(2,128)S(1)} %pad_maximum_fusion.4), channel_id=1, source_target_pairs={{0,2},{1,3},{2,0},{3,1},{4,6},{5,7},{6,4},{7,5},{8,10},{9,11},{10,... | collective-permute-start | bytes 6152 | tf_op jit(solution)/shard_map/ppermute | solution.py:328
  125.0 5.3 %collective-permute-start.28 = (f32[4,64,128]{2,1,0:T(8,128)}, f32[4,64,128]{2,1,0:T(8,128)S(1)}, u32[]{:S(2)}, u32[]{:S(2)}) collective-permute-start(f32[4,64,128]{2,1,0:T(8,128)} %wave_halo.29.cur.prev), channel_id=1, source_target_pairs={{0,4},{1,3},{2,6},{3,1},{4,0},{5,9},{6,2},{7,11},{8,12},{9,5},{10,... | collective-permute-start | bytes 393224 | tf_op jit(solution)/shard_map/ppermute | solution.py:325
  126.1 4.2 %collective-permute-start.29 = (f32[4,64,128]{2,1,0:T(8,128)}, f32[4,64,128]{2,1,0:T(8,128)S(1)}, u32[]{:S(2)}, u32[]{:S(2)}) collective-permute-start(f32[4,64,128]{2,1,0:T(8,128)} %wave_halo.29.cur.prev), channel_id=1, source_target_pairs={{0,1},{1,0},{2,3},{3,2},{4,5},{5,4},{6,7},{7,6},{8,9},{9,8},{10,11... | collective-permute-start | bytes 393224 | tf_op jit(solution)/shard_map/ppermute | solution.py:328
  132.8 25.4 %collective-permute-start.30 = (f32[4,64,128]{2,1,0:T(8,128)}, f32[4,64,128]{2,1,0:T(8,128)S(1)}, u32[]{:S(2)}, u32[]{:S(2)}) collective-permute-start(f32[4,64,128]{2,1,0:T(8,128)} %wave_halo.30.cur), channel_id=1, source_target_pairs={{0,4},{1,3},{2,6},{3,1},{4,0},{5,9},{6,2},{7,11},{8,12},{9,5},{10,... | collective-permute-start | bytes 393224 | tf_op jit(solution)/shard_map/ppermute | solution.py:325
  135.2 23.1 %collective-permute-start.31 = (f32[4,64,128]{2,1,0:T(8,128)}, f32[4,64,128]{2,1,0:T(8,128)S(1)}, u32[]{:S(2)}, u32[]{:S(2)}) collective-permute-start(f32[4,64,128]{2,1,0:T(8,128)} %wave_halo.30.cur), channel_id=1, source_target_pairs={{0,1},{1,0},{2,3},{3,2},{4,5},{5,4},{6,7},{7,6},{8,9},{9,8},{10,11... | collective-permute-start | bytes 393224 | tf_op jit(solution)/shard_map/ppermute | solution.py:328
  164.1 11.5 %collective-permute-start.39 = (f32[2,64,128]{2,1,0:T(8,128)S(1)}, f32[2,64,128]{2,1,0:T(8,128)S(1)}, u32[]{:S(2)}, u32[]{:S(2)}) collective-permute-start(f32[2,64,128]{2,1,0:T(8,128)S(1)} %slice.93.outer), channel_id=1, source_target_pairs={{0,1},{1,0},{2,3},{3,2},{4,5},{5,4},{6,7},{7,6},{8,9},{9,8},{10,11... | collective-permute-start | bytes 196616 | tf_op jit(solution)/shard_map/ppermute | solution.py:328
  164.9 3.8 %collective-permute-start.36 = (f32[36,128]{1,0:T(8,128)S(1)}, f32[36,128]{1,0:T(8,128)S(1)}, u32[]{:S(2)}, u32[]{:S(2)}) collective-permute-start(f32[36,128]{1,0:T(8,128)S(1)} %fusion.3), channel_id=1, source_target_pairs={{0,4},{1,5},{2,6},{3,7},{4,0},{5,1},{6,2},{7,3},{8,12},{9,13},{10,... | collective-permute-start | bytes 55304 | tf_op jit(solution)/shard_map/ppermute | solution.py:331
  168.7 3.8 %collective-permute-start.37 = (f32[36,128]{1,0:T(8,128)S(1)}, f32[36,128]{1,0:T(8,128)S(1)}, u32[]{:S(2)}, u32[]{:S(2)}) collective-permute-start(f32[36,128]{1,0:T(8,128)S(1)} %add.45), channel_id=1, source_target_pairs={{0,8},{1,9},{2,10},{3,11},{4,12},{5,13},{6,14},{7,15},{8,0},{9,1},... | collective-permute-start | bytes 55304 | tf_op jit(solution)/shard_map/ppermute | solution.py:331
  172.5 6.0 %collective-permute-start.38 = (f32[36,128]{1,0:T(8,128)S(1)}, f32[36,128]{1,0:T(8,128)S(1)}, u32[]{:S(2)}, u32[]{:S(2)}) collective-permute-start(f32[36,128]{1,0:T(8,128)S(1)} %add.46), channel_id=1, source_target_pairs={{0,16},{1,17},{2,18},{3,19},{4,20},{5,21},{6,22},{7,23},{8,24},{9,... | collective-permute-start | bytes 55304 | tf_op jit(solution)/shard_map/ppermute | solution.py:331
  178.5 8.3 %collective-permute-start.32 = (f32[4,64,128]{2,1,0:T(8,128)}, f32[4,64,128]{2,1,0:T(8,128)S(1)}, u32[]{:S(2)}, u32[]{:S(2)}) collective-permute-start(f32[4,64,128]{2,1,0:T(8,128)} %wave_halo.31.cur), channel_id=1, source_target_pairs={{0,1},{1,0},{2,3},{3,2},{4,5},{5,4},{6,7},{7,6},{8,9},{9,8},{10,11... | collective-permute-start | bytes 393224 | tf_op jit(solution)/shard_map/ppermute | solution.py:328
  (50 other events, 363.7 us)

commit v2 on v1

--- a/solution.py
+++ b/solution.py
@@ -13,8 +13,13 @@
 AXES = ("mp", "station")
 VMEM = pl.BlockSpec(memory_space=pltpu.VMEM)
 SMEM = pl.BlockSpec(memory_space=pltpu.SMEM)
-SRC_PLANE, SRC_ROW, SRC_LANE, X_LOW, HALF_LOW, ROW_LOW, LEFT_OK, RIGHT_OK, OUTER_OK, FLIPPED = range(10)
+SRC_PLANE, SRC_ROW, SRC_LANE, X_LOW, HALF_LOW, ROW_LOW, LEFT_OK, RIGHT_OK, FLIPPED = range(9)
 F32 = jnp.float32
+MIB = 1 << 20
+
+
+def room(mib):
+    return pltpu.CompilerParams(vmem_limit_bytes=mib * MIB)
 
 
 def shape(dims):
@@ -92,6 +97,7 @@
         in_specs=[SMEM, SMEM, VMEM, VMEM, VMEM, VMEM],
         out_specs=(VMEM, VMEM),
         scratch_shapes=[pltpu.VMEM((planes, rows + 16, lanes), F32)],
+        compiler_params=room(2),
         cost_estimate=pl.CostEstimate(
             flops=60 * cur.size, bytes_accessed=24 * cur.size, transcendentals=0
         ),
@@ -99,30 +105,31 @@
     )(meta, wavelet, cur, prev, cour, surf)
 
 
-def halo_kernel(meta, base, cour, outer, inner, out):
+def halo_kernel(base, cour, cour_outer, outer, inner, out):
     planes = base.shape[0]
-    ok = jnp.where(meta[OUTER_OK] > 0, 1.0, 0.0)
     for j in range(planes):
-        far = None
+        far = near = None
         for d in range(j + 1, REACH + 1):
-            term = (STENCIL[d] * ok) * outer[d - j - 1]
+            term = STENCIL[d] * outer[d - j - 1]
             far = term if far is None else far + term
         for d in range(planes - j, REACH + 1):
-            far = far + STENCIL[d] * inner[2 * planes - 1 - j - d]
-        out[j] = base[j] + cour[j] * far
-
-
-def halo_step(meta, base, cour, outer, inner):
+            term = STENCIL[d] * inner[2 * planes - 1 - j - d]
+            near = term if near is None else near + term
+        out[j] = base[j] + (cour[j] * near + cour_outer[j] * far)
+
+
+def halo_step(base, cour, cour_outer, outer, inner):
     return pl.pallas_call(
         halo_kernel,
         out_shape=shape(base.shape),
-        in_specs=[SMEM, VMEM, VMEM, VMEM, VMEM],
+        in_specs=[VMEM] * 5,
         out_specs=VMEM,
+        compiler_params=room(2),
         cost_estimate=pl.CostEstimate(
             flops=12 * base.size, bytes_accessed=20 * base.size, transcendentals=0
         ),
         name="wave_halo",
-    )(meta, base, cour, outer, inner)
+    )(base, cour, cour_outer, outer, inner)
 
 
 def trace_kernel(step, place, cur, surf, out):
@@ -176,6 +183,7 @@
         cost_estimate=pl.CostEstimate(
             flops=20 * size, bytes_accessed=4 * size, transcendentals=2 * size
         ),
+        compiler_params=room(8),
         name="gravity_table",
     )(low)
 
@@ -219,6 +227,7 @@
         cost_estimate=pl.CostEstimate(
             flops=4 * work, bytes_accessed=4 * (flat.size + dens.size), transcendentals=0
         ),
+        compiler_params=room(8),
         name="gravity_forward",
     )(low, meta, stations, flat, dens)
 
@@ -253,6 +262,7 @@
         out_shape=shape((slab, rows, table.shape[2])),
         in_specs=[SMEM, SMEM, SMEM, SMEM, VMEM],
         out_specs=VMEM,
+        compiler_params=room(8),
         name="gravity_adjoint",
     )(low, meta, stations, weights, flat)
 
@@ -298,6 +308,7 @@
         cost_estimate=pl.CostEstimate(
             flops=60 * velocity.size, bytes_accessed=24 * velocity.size, transcendentals=0
         ),
+        compiler_params=room(8),
         name="cross_gradient",
     )(meta, velocity, density, outer, inner)
 
@@ -349,7 +360,6 @@
             s * block,
             (m > 0).astype(jnp.int32),
             (m < count - 1).astype(jnp.int32),
-            outer_ok.astype(jnp.int32),
             flipped.astype(jnp.int32),
         ]
     ).astype(jnp.int32)
@@ -408,6 +418,7 @@
 
     cour_full = TIME_RATIO * velocity * (TIME_RATIO * velocity)
     cour = owned(cour_full)
+    cour_outer = jnp.where(outer_ok, cour, 0.0)
     cur = owned(p_now)
     prev = owned(p_prev)
     surf = cour
@@ -423,7 +434,7 @@
         base, surf = local_step(step, meta, wavelet, cur, prev, cour, surf)
         if step == 1:
             inner_edges = swap_station(outer_edges, 1)
-        cur, prev = halo_step(meta, base, cour, outer, inner), cur
+        cur, prev = halo_step(base, cour, cour_outer, outer, inner), cur
 
     cross_gradient = cross_gradient_of(meta, velocity, density, outer_edges, inner_edges)
 
@@ -438,6 +449,7 @@
         out_shape=shape((steps, receiver_cells.shape[0])),
         in_specs=[VMEM] * 3,
         out_specs=VMEM,
+        compiler_params=room(4),
         name="traces",
     )(place, cur, surf)
     packed = jnp.concatenate([recorded.reshape(-1, 128), predicted.reshape(-1, 128)])

time: 189 us -> 124 us (0.66)
  Pallas kernels: 99.4 us -> 35.4 us
  waiting for transfers between devices: 18.9 us -> 32.8 us
  local copies, waits for them, and re-layouts: 19.9 us -> 7.64 us
  other arithmetic: 7.22 us -> 3.88 us
    pallas_call x16, Pallas kernels: 29 us -> 1.02 us  [halo_step(): pl.pallas_call(halo_kernel, out_shape=shape(base.shape), in_specs=[VMEM]...]
    pallas_call x16, Pallas kernels: 34.9 us -> 14.8 us  [local_step(): pl.pallas_call(functools.partial(local_kernel, step), out_shape=(shape(cu...]
    ppermute x16, waiting for transfers between devices: 13.3 us -> 27.6 us  [across(): return lax.ppermute(value, AXES, chain)]
    pallas_call x4, Pallas kernels: 19.3 us -> 9.65 us  [gravity_forward(): pl.pallas_call(functools.partial(forward_kernel, first, guard, lateral),...]
    unnamed x84 -> x16, local copies, waits for them, and re-layouts: 12 us -> 2.35 us
    pallas_call x1, Pallas kernels: 5.27 us -> 3.03 us  [gravity_table(): pl.pallas_call(table_kernel, out_shape=shape((depth, 2 * lateral, vertica...]
  transfers between devices with their start and end apart: 40 -> 40, of which waited for: 16 -> 17; matrix products, arithmetic and copies ran while one was open for 6% -> 5% of each run, Pallas kernels for 41% -> 28%
where the time goes in v2:
time: 124 us; the launch traced here: 123 us
  starting transfers between devices  41.8 us (34%)
  Pallas kernels  35.4 us (29%)
  waiting for transfers between devices  32.8 us (26%)
  local copies, waits for them, and re-layouts  7.64 us (6%)
  other arithmetic  3.88 us (3%)
  between operations  1.89 us (2%)
    ppermute x16, starting transfers between devices, across(): return lax.ppermute(value, AXES, chain)  31.9 us
    ppermute x16, waiting for transfers between devices, across(): return lax.ppermute(value, AXES, chain)  27.6 us
    pallas_call x16, Pallas kernels, local_step(): pl.pallas_call(functools.partial(local_kernel, step), out_shape=(shape(cu...  14.8 us
    pallas_call x4, Pallas kernels, gravity_forward(): pl.pallas_call(functools.partial(forward_kernel, first, guard, lateral),...  9.65 us
    ppermute x3, starting transfers between devices, swap_slab(): lax.ppermute(value, AXES, pairs_of(count, stations, lambda i, k: (i ^ bit...  6.21 us
    pallas_call x1, Pallas kernels, gravity_adjoint(): pl.pallas_call(functools.partial(adjoint_kernel, guard, lateral, slab), o...  4.74 us
    ppermute x3, waiting for transfers between devices, swap_slab(): lax.ppermute(value, AXES, pairs_of(count, stations, lambda i, k: (i ^ bit...  4.39 us
    slice x5, local copies, waits for them, and re-layouts, owned(): return jnp.where(flipped, jnp.flip(field[half:], 0), field[:half])  3.82 us
  transfers between devices with their start and end apart: 40, of which 17 were waited for; matrix products, arithmetic and copies ran while one was open for 5% of the time, Pallas kernels for 28%

profile of v2, /device:TPU:0, one launch (start us, length us, event | category | flops | bytes accessed | tf_op | source)
XLA Modules:
  0.0 123.4 jit_solution(2307790390500505199)
XLA Ops:
  5.1 2.6 %collective-permute-start = (f32[6,64,128]{2,1,0:T(8,128)S(1)}, f32[6,64,128]{2,1,0:T(8,128)S(1)}, u32[]{:S(2)}, u32[]{:S(2)}) collective-permute-start(f32[6,64,128]{2,1,0:T(8,128)S(1)} %pad_maximum_fusion.1), channel_id=1, source_target_pairs={{0,4},{1,3},{2,6},{3,1},{4,0},{5,9},{6,2},{7,11},{8,12},{9,5},{10,... | collective-permute-start | bytes 589832 | tf_op jit(solution)/shard_map/ppermute | solution.py:336
  13.1 2.5 %collective-permute-start.2 = (f32[4,64,128]{2,1,0:T(8,128)S(1)}, f32[4,64,128]{2,1,0:T(8,128)S(1)}, u32[]{:S(2)}, u32[]{:S(2)}) collective-permute-start(f32[4,64,128]{2,1,0:T(8,128)S(1)} %wave_halo.16.cur.prev), channel_id=1, source_target_pairs={{0,4},{1,3},{2,6},{3,1},{4,0},{5,9},{6,2},{7,11},{8,12},{9,5},{10,... | collective-permute-start | bytes 393224 | tf_op jit(solution)/shard_map/ppermute | solution.py:336
  16.6 2.0 %collective-permute-done.2.outer = f32[4,64,128]{2,1,0:T(8,128)S(1)} collective-permute-done((f32[4,64,128]{2,1,0:T(8,128)S(1)}, f32[4,64,128]{2,1,0:T(8,128)S(1)}, u32[]{:S(2)}, u32[]{:S(2)}) %collective-permute-start.2) | collective-permute-done | bytes 131104 | tf_op jit(solution)/shard_map/ppermute | solution.py:336
  18.7 2.1 %collective-permute-start.4 = (f32[4,64,128]{2,1,0:T(8,128)S(1)}, f32[4,64,128]{2,1,0:T(8,128)S(1)}, u32[]{:S(2)}, u32[]{:S(2)}) collective-permute-start(f32[4,64,128]{2,1,0:T(8,128)S(1)} %wave_halo.17.cur.prev), channel_id=1, source_target_pairs={{0,4},{1,3},{2,6},{3,1},{4,0},{5,9},{6,2},{7,11},{8,12},{9,5},{10,... | collective-permute-start | bytes 393224 | tf_op jit(solution)/shard_map/ppermute | solution.py:336
  23.8 2.1 %collective-permute-start.6 = (f32[4,64,128]{2,1,0:T(8,128)S(1)}, f32[4,64,128]{2,1,0:T(8,128)S(1)}, u32[]{:S(2)}, u32[]{:S(2)}) collective-permute-start(f32[4,64,128]{2,1,0:T(8,128)S(1)} %wave_halo.18.cur.prev), channel_id=1, source_target_pairs={{0,4},{1,3},{2,6},{3,1},{4,0},{5,9},{6,2},{7,11},{8,12},{9,5},{10,... | collective-permute-start | bytes 393224 | tf_op jit(solution)/shard_map/ppermute | solution.py:336
  26.8 2.0 %collective-permute-done.6.outer = f32[4,64,128]{2,1,0:T(8,128)S(1)} collective-permute-done((f32[4,64,128]{2,1,0:T(8,128)S(1)}, f32[4,64,128]{2,1,0:T(8,128)S(1)}, u32[]{:S(2)}, u32[]{:S(2)}) %collective-permute-start.6) | collective-permute-done | bytes 131104 | tf_op jit(solution)/shard_map/ppermute | solution.py:336
  28.9 2.1 %collective-permute-start.8 = (f32[4,64,128]{2,1,0:T(8,128)S(1)}, f32[4,64,128]{2,1,0:T(8,128)S(1)}, u32[]{:S(2)}, u32[]{:S(2)}) collective-permute-start(f32[4,64,128]{2,1,0:T(8,128)S(1)} %wave_halo.19.cur.prev), channel_id=1, source_target_pairs={{0,4},{1,3},{2,6},{3,1},{4,0},{5,9},{6,2},{7,11},{8,12},{9,5},{10,... | collective-permute-start | bytes 393224 | tf_op jit(solution)/shard_map/ppermute | solution.py:336
  31.9 2.0 %collective-permute-done.8.outer = f32[4,64,128]{2,1,0:T(8,128)S(1)} collective-permute-done((f32[4,64,128]{2,1,0:T(8,128)S(1)}, f32[4,64,128]{2,1,0:T(8,128)S(1)}, u32[]{:S(2)}, u32[]{:S(2)}) %collective-permute-start.8) | collective-permute-done | bytes 131104 | tf_op jit(solution)/shard_map/ppermute | solution.py:336
  34.0 2.1 %collective-permute-start.10 = (f32[4,64,128]{2,1,0:T(8,128)S(1)}, f32[4,64,128]{2,1,0:T(8,128)S(1)}, u32[]{:S(2)}, u32[]{:S(2)}) collective-permute-start(f32[4,64,128]{2,1,0:T(8,128)S(1)} %wave_halo.20.cur.prev), channel_id=1, source_target_pairs={{0,4},{1,3},{2,6},{3,1},{4,0},{5,9},{6,2},{7,11},{8,12},{9,5},{10,... | collective-permute-start | bytes 393224 | tf_op jit(solution)/shard_map/ppermute | solution.py:336
  37.0 2.0 %collective-permute-done.10.outer = f32[4,64,128]{2,1,0:T(8,128)S(1)} collective-permute-done((f32[4,64,128]{2,1,0:T(8,128)S(1)}, f32[4,64,128]{2,1,0:T(8,128)S(1)}, u32[]{:S(2)}, u32[]{:S(2)}) %collective-permute-start.10) | collective-permute-done | bytes 131104 | tf_op jit(solution)/shard_map/ppermute | solution.py:336
  39.1 2.1 %collective-permute-start.12 = (f32[4,64,128]{2,1,0:T(8,128)S(1)}, f32[4,64,128]{2,1,0:T(8,128)S(1)}, u32[]{:S(2)}, u32[]{:S(2)}) collective-permute-start(f32[4,64,128]{2,1,0:T(8,128)S(1)} %wave_halo.21.cur.prev), channel_id=1, source_target_pairs={{0,4},{1,3},{2,6},{3,1},{4,0},{5,9},{6,2},{7,11},{8,12},{9,5},{10,... | collective-permute-start | bytes 393224 | tf_op jit(solution)/shard_map/ppermute | solution.py:336
  44.2 2.1 %collective-permute-start.14 = (f32[4,64,128]{2,1,0:T(8,128)S(1)}, f32[4,64,128]{2,1,0:T(8,128)S(1)}, u32[]{:S(2)}, u32[]{:S(2)}) collective-permute-start(f32[4,64,128]{2,1,0:T(8,128)S(1)} %wave_halo.22.cur.prev), channel_id=1, source_target_pairs={{0,4},{1,3},{2,6},{3,1},{4,0},{5,9},{6,2},{7,11},{8,12},{9,5},{10,... | collective-permute-start | bytes 393224 | tf_op jit(solution)/shard_map/ppermute | solution.py:336
  47.2 2.0 %collective-permute-done.14.outer = f32[4,64,128]{2,1,0:T(8,128)S(1)} collective-permute-done((f32[4,64,128]{2,1,0:T(8,128)S(1)}, f32[4,64,128]{2,1,0:T(8,128)S(1)}, u32[]{:S(2)}, u32[]{:S(2)}) %collective-permute-start.14) | collective-permute-done | bytes 131104 | tf_op jit(solution)/shard_map/ppermute | solution.py:336
  49.3 2.1 %collective-permute-start.16 = (f32[4,64,128]{2,1,0:T(8,128)S(1)}, f32[4,64,128]{2,1,0:T(8,128)S(1)}, u32[]{:S(2)}, u32[]{:S(2)}) collective-permute-start(f32[4,64,128]{2,1,0:T(8,128)S(1)} %wave_halo.23.cur.prev), channel_id=1, source_target_pairs={{0,4},{1,3},{2,6},{3,1},{4,0},{5,9},{6,2},{7,11},{8,12},{9,5},{10,... | collective-permute-start | bytes 393224 | tf_op jit(solution)/shard_map/ppermute | solution.py:336
  52.3 2.0 %collective-permute-done.16.outer = f32[4,64,128]{2,1,0:T(8,128)S(1)} collective-permute-done((f32[4,64,128]{2,1,0:T(8,128)S(1)}, f32[4,64,128]{2,1,0:T(8,128)S(1)}, u32[]{:S(2)}, u32[]{:S(2)}) %collective-permute-start.16) | collective-permute-done | bytes 131104 | tf_op jit(solution)/shard_map/ppermute | solution.py:336
  54.4 2.1 %collective-permute-start.18 = (f32[4,64,128]{2,1,0:T(8,128)S(1)}, f32[4,64,128]{2,1,0:T(8,128)S(1)}, u32[]{:S(2)}, u32[]{:S(2)}) collective-permute-start(f32[4,64,128]{2,1,0:T(8,128)S(1)} %wave_halo.24.cur.prev), channel_id=1, source_target_pairs={{0,4},{1,3},{2,6},{3,1},{4,0},{5,9},{6,2},{7,11},{8,12},{9,5},{10,... | collective-permute-start | bytes 393224 | tf_op jit(solution)/shard_map/ppermute | solution.py:336
  59.5 2.1 %collective-permute-start.20 = (f32[4,64,128]{2,1,0:T(8,128)S(1)}, f32[4,64,128]{2,1,0:T(8,128)S(1)}, u32[]{:S(2)}, u32[]{:S(2)}) collective-permute-start(f32[4,64,128]{2,1,0:T(8,128)S(1)} %wave_halo.25.cur.prev), channel_id=1, source_target_pairs={{0,4},{1,3},{2,6},{3,1},{4,0},{5,9},{6,2},{7,11},{8,12},{9,5},{10,... | collective-permute-start | bytes 393224 | tf_op jit(solution)/shard_map/ppermute | solution.py:336
  64.6 2.1 %collective-permute-start.22 = (f32[4,64,128]{2,1,0:T(8,128)S(1)}, f32[4,64,128]{2,1,0:T(8,128)S(1)}, u32[]{:S(2)}, u32[]{:S(2)}) collective-permute-start(f32[4,64,128]{2,1,0:T(8,128)S(1)} %wave_halo.26.cur.prev), channel_id=1, source_target_pairs={{0,4},{1,3},{2,6},{3,1},{4,0},{5,9},{6,2},{7,11},{8,12},{9,5},{10,... | collective-permute-start | bytes 393224 | tf_op jit(solution)/shard_map/ppermute | solution.py:336
  67.7 2.0 %collective-permute-done.22.outer = f32[4,64,128]{2,1,0:T(8,128)S(1)} collective-permute-done((f32[4,64,128]{2,1,0:T(8,128)S(1)}, f32[4,64,128]{2,1,0:T(8,128)S(1)}, u32[]{:S(2)}, u32[]{:S(2)}) %collective-permute-start.22) | collective-permute-done | bytes 131104 | tf_op jit(solution)/shard_map/ppermute | solution.py:336
  69.7 2.1 %collective-permute-start.24 = (f32[4,64,128]{2,1,0:T(8,128)S(1)}, f32[4,64,128]{2,1,0:T(8,128)S(1)}, u32[]{:S(2)}, u32[]{:S(2)}) collective-permute-start(f32[4,64,128]{2,1,0:T(8,128)S(1)} %wave_halo.27.cur.prev), channel_id=1, source_target_pairs={{0,4},{1,3},{2,6},{3,1},{4,0},{5,9},{6,2},{7,11},{8,12},{9,5},{10,... | collective-permute-start | bytes 393224 | tf_op jit(solution)/shard_map/ppermute | solution.py:336
  74.8 2.1 %collective-permute-start.26 = (f32[4,64,128]{2,1,0:T(8,128)S(1)}, f32[4,64,128]{2,1,0:T(8,128)S(1)}, u32[]{:S(2)}, u32[]{:S(2)}) collective-permute-start(f32[4,64,128]{2,1,0:T(8,128)S(1)} %wave_halo.28.cur.prev), channel_id=1, source_target_pairs={{0,4},{1,3},{2,6},{3,1},{4,0},{5,9},{6,2},{7,11},{8,12},{9,5},{10,... | collective-permute-start | bytes 393224 | tf_op jit(solution)/shard_map/ppermute | solution.py:336
  78.5 3.0 %gravity_table.1 = f32[71,128,128]{2,1,0:T(8,128)S(1)} custom-call(s32[1]{0:T(128)} %bitcast.9.low), custom_call_target="tpu_custom_call" | custom-call | flops 23265280 | bytes 4653056 | tf_op jit(solution)/shard_map/gravity_table/pallas_call | solution.py:178
  84.1 3.6 %collective-permute-done.28.outer = f32[4,64,128]{2,1,0:T(8,128)S(1)} collective-permute-done((f32[4,64,128]{2,1,0:T(8,128)S(1)}, f32[4,64,128]{2,1,0:T(8,128)S(1)}, u32[]{:S(2)}, u32[]{:S(2)}) %collective-permute-start.28) | collective-permute-done | bytes 131104 | tf_op jit(solution)/shard_map/ppermute | solution.py:336
  89.3 2.4 %gravity_forward.4 = f32[128,128]{1,0:T(8,128)S(1)} custom-call(s32[1]{0:T(128)} %bitcast.9.low, s32[9]{0:T(128)S(1)} %stack.54.meta, s32[512]{0:T(512)S(1)} %bitcast.33, f32[9088,128]{1,0:T(8,128)S(1)} %bitcast.28, f32[4,64,128]{2,1,0:T(8,128)S(1)} %slice_select_fusion.dens), custom_call_target="tpu_custom_call" | custom-call | flops 16777216 | bytes 4784128 | tf_op jit(solution)/shard_map/gravity_forward/pallas_call | solution.py:222
  91.7 2.4 %gravity_forward.5 = f32[128,128]{1,0:T(8,128)S(1)} custom-call(s32[1]{0:T(128)} %bitcast.9.low, s32[9]{0:T(128)S(1)} %stack.54.meta, s32[512]{0:T(512)S(1)} %bitcast.34, f32[9088,128]{1,0:T(8,128)S(1)} %bitcast.29, f32[4,64,128]{2,1,0:T(8,128)S(1)} %slice_select_fusion.dens), custom_call_target="tpu_custom_call" | custom-call | flops 16777216 | bytes 4784128 | tf_op jit(solution)/shard_map/gravity_forward/pallas_call | solution.py:222
  94.1 2.4 %gravity_forward.6 = f32[128,128]{1,0:T(8,128)S(1)} custom-call(s32[1]{0:T(128)} %bitcast.9.low, s32[9]{0:T(128)S(1)} %stack.54.meta, s32[512]{0:T(512)S(1)} %bitcast.35, f32[9088,128]{1,0:T(8,128)S(1)} %bitcast.30, f32[4,64,128]{2,1,0:T(8,128)S(1)} %slice_select_fusion.dens), custom_call_target="tpu_custom_call" | custom-call | flops 16777216 | bytes 4784128 | tf_op jit(solution)/shard_map/gravity_forward/pallas_call | solution.py:222
  96.6 2.4 %gravity_forward.7 = f32[128,128]{1,0:T(8,128)S(1)} custom-call(s32[1]{0:T(128)} %bitcast.9.low, s32[9]{0:T(128)S(1)} %stack.54.meta, s32[512]{0:T(512)S(1)} %bitcast.36, f32[9088,128]{1,0:T(8,128)S(1)} %bitcast.31, f32[4,64,128]{2,1,0:T(8,128)S(1)} %slice_select_fusion.dens), custom_call_target="tpu_custom_call" | custom-call | flops 16777216 | bytes 4784128 | tf_op jit(solution)/shard_map/gravity_forward/pallas_call | solution.py:222
  103.1 2.6 %collective-permute-done.36 = f32[36,128]{1,0:T(8,128)S(1)} collective-permute-done((f32[36,128]{1,0:T(8,128)S(1)}, f32[36,128]{1,0:T(8,128)S(1)}, u32[]{:S(2)}, u32[]{:S(2)}) %collective-permute-start.36) | collective-permute-done | bytes 18464 | tf_op jit(solution)/shard_map/ppermute | solution.py:342
  105.8 2.0 %collective-permute-start.37 = (f32[36,128]{1,0:T(8,128)S(1)}, f32[36,128]{1,0:T(8,128)S(1)}, u32[]{:S(2)}, u32[]{:S(2)}) collective-permute-start(f32[36,128]{1,0:T(8,128)S(1)} %add.45), channel_id=1, source_target_pairs={{0,8},{1,9},{2,10},{3,11},{4,12},{5,13},{6,14},{7,15},{8,0},{9,1},... | collective-permute-start | bytes 55304 | tf_op jit(solution)/shard_map/ppermute | solution.py:342
  109.5 3.0 %collective-permute-start.38 = (f32[36,128]{1,0:T(8,128)S(1)}, f32[36,128]{1,0:T(8,128)S(1)}, u32[]{:S(2)}, u32[]{:S(2)}) collective-permute-start(f32[36,128]{1,0:T(8,128)S(1)} %add.46), channel_id=1, source_target_pairs={{0,16},{1,17},{2,18},{3,19},{4,20},{5,21},{6,22},{7,23},{8,24},{9,... | collective-permute-start | bytes 55304 | tf_op jit(solution)/shard_map/ppermute | solution.py:342
  114.4 2.3 %copy-done.1 = f32[71,128,128]{2,1,0:T(8,128)S(1)} copy-done((f32[71,128,128]{2,1,0:T(8,128)S(1)}, f32[71,128,128]{2,1,0:T(8,128)}, u32[]{:S(2)}) %copy-start.1) | copy-done | bytes 4653080
  116.7 4.7 %gravity_adjoint.1 = f32[8,16,128]{2,1,0:T(8,128)} custom-call(s32[1]{0:T(128)} %bitcast.9.low, s32[9]{0:T(128)S(1)} %stack.54.meta, s32[512]{0:T(512)S(1)} %bitcast.37, f32[512]{0:T(512)S(1)} %get-tuple-element.69.weights, f32[9088,128]{1,0:T(8,128)S(1)} %bitcast.32), custom_call_target="tpu_custom_call" | custom-call | tf_op jit(solution)/shard_map/gravity_adjoint/pallas_call | solution.py:260
  (143 shorter events, 46.4 us)
Async XLA Ops:
  2.5 10.5 %collective-permute-start.1 = (f32[4,64,128]{2,1,0:T(8,128)S(1)}, f32[4,64,128]{2,1,0:T(8,128)S(1)}, u32[]{:S(2)}, u32[]{:S(2)}) collective-permute-start(f32[4,64,128]{2,1,0:T(8,128)S(1)} %slice_select_fusion.3.cur.prev), channel_id=1, source_target_pairs={{0,1},{1,0},{2,3},{3,2},{4,5},{5,4},{6,7},{7,6},{8,9},{9,8},{10,11... | collective-permute-start | bytes 393224 | tf_op jit(solution)/shard_map/ppermute | solution.py:339
  5.1 7.9 %collective-permute-start = (f32[6,64,128]{2,1,0:T(8,128)S(1)}, f32[6,64,128]{2,1,0:T(8,128)S(1)}, u32[]{:S(2)}, u32[]{:S(2)}) collective-permute-start(f32[6,64,128]{2,1,0:T(8,128)S(1)} %pad_maximum_fusion.1), channel_id=1, source_target_pairs={{0,4},{1,3},{2,6},{3,1},{4,0},{5,9},{6,2},{7,11},{8,12},{9,5},{10,... | collective-permute-start | bytes 589832 | tf_op jit(solution)/shard_map/ppermute | solution.py:336
  13.1 5.5 %collective-permute-start.2 = (f32[4,64,128]{2,1,0:T(8,128)S(1)}, f32[4,64,128]{2,1,0:T(8,128)S(1)}, u32[]{:S(2)}, u32[]{:S(2)}) collective-permute-start(f32[4,64,128]{2,1,0:T(8,128)S(1)} %wave_halo.16.cur.prev), channel_id=1, source_target_pairs={{0,4},{1,3},{2,6},{3,1},{4,0},{5,9},{6,2},{7,11},{8,12},{9,5},{10,... | collective-permute-start | bytes 393224 | tf_op jit(solution)/shard_map/ppermute | solution.py:336
  15.6 3.0 %collective-permute-start.3 = (f32[4,64,128]{2,1,0:T(8,128)S(1)}, f32[4,64,128]{2,1,0:T(8,128)S(1)}, u32[]{:S(2)}, u32[]{:S(2)}) collective-permute-start(f32[4,64,128]{2,1,0:T(8,128)S(1)} %wave_halo.16.cur.prev), channel_id=1, source_target_pairs={{0,1},{1,0},{2,3},{3,2},{4,5},{5,4},{6,7},{7,6},{8,9},{9,8},{10,11... | collective-permute-start | bytes 393224 | tf_op jit(solution)/shard_map/ppermute | solution.py:339
  18.7 5.0 %collective-permute-start.4 = (f32[4,64,128]{2,1,0:T(8,128)S(1)}, f32[4,64,128]{2,1,0:T(8,128)S(1)}, u32[]{:S(2)}, u32[]{:S(2)}) collective-permute-start(f32[4,64,128]{2,1,0:T(8,128)S(1)} %wave_halo.17.cur.prev), channel_id=1, source_target_pairs={{0,4},{1,3},{2,6},{3,1},{4,0},{5,9},{6,2},{7,11},{8,12},{9,5},{10,... | collective-permute-start | bytes 393224 | tf_op jit(solution)/shard_map/ppermute | solution.py:336
  23.8 5.0 %collective-permute-start.6 = (f32[4,64,128]{2,1,0:T(8,128)S(1)}, f32[4,64,128]{2,1,0:T(8,128)S(1)}, u32[]{:S(2)}, u32[]{:S(2)}) collective-permute-start(f32[4,64,128]{2,1,0:T(8,128)S(1)} %wave_halo.18.cur.prev), channel_id=1, source_target_pairs={{0,4},{1,3},{2,6},{3,1},{4,0},{5,9},{6,2},{7,11},{8,12},{9,5},{10,... | collective-permute-start | bytes 393224 | tf_op jit(solution)/shard_map/ppermute | solution.py:336
  25.9 3.0 %collective-permute-start.7 = (f32[4,64,128]{2,1,0:T(8,128)S(1)}, f32[4,64,128]{2,1,0:T(8,128)S(1)}, u32[]{:S(2)}, u32[]{:S(2)}) collective-permute-start(f32[4,64,128]{2,1,0:T(8,128)S(1)} %wave_halo.18.cur.prev), channel_id=1, source_target_pairs={{0,1},{1,0},{2,3},{3,2},{4,5},{5,4},{6,7},{7,6},{8,9},{9,8},{10,11... | collective-permute-start | bytes 393224 | tf_op jit(solution)/shard_map/ppermute | solution.py:339
  28.9 5.0 %collective-permute-start.8 = (f32[4,64,128]{2,1,0:T(8,128)S(1)}, f32[4,64,128]{2,1,0:T(8,128)S(1)}, u32[]{:S(2)}, u32[]{:S(2)}) collective-permute-start(f32[4,64,128]{2,1,0:T(8,128)S(1)} %wave_halo.19.cur.prev), channel_id=1, source_target_pairs={{0,4},{1,3},{2,6},{3,1},{4,0},{5,9},{6,2},{7,11},{8,12},{9,5},{10,... | collective-permute-start | bytes 393224 | tf_op jit(solution)/shard_map/ppermute | solution.py:336
  31.0 3.0 %collective-permute-start.9 = (f32[4,64,128]{2,1,0:T(8,128)S(1)}, f32[4,64,128]{2,1,0:T(8,128)S(1)}, u32[]{:S(2)}, u32[]{:S(2)}) collective-permute-start(f32[4,64,128]{2,1,0:T(8,128)S(1)} %wave_halo.19.cur.prev), channel_id=1, source_target_pairs={{0,1},{1,0},{2,3},{3,2},{4,5},{5,4},{6,7},{7,6},{8,9},{9,8},{10,11... | collective-permute-start | bytes 393224 | tf_op jit(solution)/shard_map/ppermute | solution.py:339
  34.0 5.0 %collective-permute-start.10 = (f32[4,64,128]{2,1,0:T(8,128)S(1)}, f32[4,64,128]{2,1,0:T(8,128)S(1)}, u32[]{:S(2)}, u32[]{:S(2)}) collective-permute-start(f32[4,64,128]{2,1,0:T(8,128)S(1)} %wave_halo.20.cur.prev), channel_id=1, source_target_pairs={{0,4},{1,3},{2,6},{3,1},{4,0},{5,9},{6,2},{7,11},{8,12},{9,5},{10,... | collective-permute-start | bytes 393224 | tf_op jit(solution)/shard_map/ppermute | solution.py:336
  39.1 5.0 %collective-permute-start.12 = (f32[4,64,128]{2,1,0:T(8,128)S(1)}, f32[4,64,128]{2,1,0:T(8,128)S(1)}, u32[]{:S(2)}, u32[]{:S(2)}) collective-permute-start(f32[4,64,128]{2,1,0:T(8,128)S(1)} %wave_halo.21.cur.prev), channel_id=1, source_target_pairs={{0,4},{1,3},{2,6},{3,1},{4,0},{5,9},{6,2},{7,11},{8,12},{9,5},{10,... | collective-permute-start | bytes 393224 | tf_op jit(solution)/shard_map/ppermute | solution.py:336
  44.2 5.0 %collective-permute-start.14 = (f32[4,64,128]{2,1,0:T(8,128)S(1)}, f32[4,64,128]{2,1,0:T(8,128)S(1)}, u32[]{:S(2)}, u32[]{:S(2)}) collective-permute-start(f32[4,64,128]{2,1,0:T(8,128)S(1)} %wave_halo.22.cur.prev), channel_id=1, source_target_pairs={{0,4},{1,3},{2,6},{3,1},{4,0},{5,9},{6,2},{7,11},{8,12},{9,5},{10,... | collective-permute-start | bytes 393224 | tf_op jit(solution)/shard_map/ppermute | solution.py:336
  49.3 5.0 %collective-permute-start.16 = (f32[4,64,128]{2,1,0:T(8,128)S(1)}, f32[4,64,128]{2,1,0:T(8,128)S(1)}, u32[]{:S(2)}, u32[]{:S(2)}) collective-permute-start(f32[4,64,128]{2,1,0:T(8,128)S(1)} %wave_halo.23.cur.prev), channel_id=1, source_target_pairs={{0,4},{1,3},{2,6},{3,1},{4,0},{5,9},{6,2},{7,11},{8,12},{9,5},{10,... | collective-permute-start | bytes 393224 | tf_op jit(solution)/shard_map/ppermute | solution.py:336
  51.4 3.0 %collective-permute-start.17 = (f32[4,64,128]{2,1,0:T(8,128)S(1)}, f32[4,64,128]{2,1,0:T(8,128)S(1)}, u32[]{:S(2)}, u32[]{:S(2)}) collective-permute-start(f32[4,64,128]{2,1,0:T(8,128)S(1)} %wave_halo.23.cur.prev), channel_id=1, source_target_pairs={{0,1},{1,0},{2,3},{3,2},{4,5},{5,4},{6,7},{7,6},{8,9},{9,8},{10,11... | collective-permute-start | bytes 393224 | tf_op jit(solution)/shard_map/ppermute | solution.py:339
  54.4 5.0 %collective-permute-start.18 = (f32[4,64,128]{2,1,0:T(8,128)S(1)}, f32[4,64,128]{2,1,0:T(8,128)S(1)}, u32[]{:S(2)}, u32[]{:S(2)}) collective-permute-start(f32[4,64,128]{2,1,0:T(8,128)S(1)} %wave_halo.24.cur.prev), channel_id=1, source_target_pairs={{0,4},{1,3},{2,6},{3,1},{4,0},{5,9},{6,2},{7,11},{8,12},{9,5},{10,... | collective-permute-start | bytes 393224 | tf_op jit(solution)/shard_map/ppermute | solution.py:336
  56.5 3.0 %collective-permute-start.19 = (f32[4,64,128]{2,1,0:T(8,128)S(1)}, f32[4,64,128]{2,1,0:T(8,128)S(1)}, u32[]{:S(2)}, u32[]{:S(2)}) collective-permute-start(f32[4,64,128]{2,1,0:T(8,128)S(1)} %wave_halo.24.cur.prev), channel_id=1, source_target_pairs={{0,1},{1,0},{2,3},{3,2},{4,5},{5,4},{6,7},{7,6},{8,9},{9,8},{10,11... | collective-permute-start | bytes 393224 | tf_op jit(solution)/shard_map/ppermute | solution.py:339
  56.5 20.4 %collective-permute-start.33 = (f32[2,1,128]{2,0,1:T(2,128)S(1)}, f32[2,1,128]{2,0,1:T(2,128)S(1)}, u32[]{:S(2)}, u32[]{:S(2)}) collective-permute-start(f32[2,1,128]{2,0,1:T(2,128)S(1)} %maximum_bitcast_fusion), channel_id=1, source_target_pairs={{0,1},{1,0},{2,3},{3,2},{4,5},{5,4},{6,7},{7,6},{8,9},{9,8},{10,11... | collective-permute-start | bytes 3080 | tf_op jit(solution)/shard_map/ppermute | solution.py:339
  59.5 5.0 %collective-permute-start.20 = (f32[4,64,128]{2,1,0:T(8,128)S(1)}, f32[4,64,128]{2,1,0:T(8,128)S(1)}, u32[]{:S(2)}, u32[]{:S(2)}) collective-permute-start(f32[4,64,128]{2,1,0:T(8,128)S(1)} %wave_halo.25.cur.prev), channel_id=1, source_target_pairs={{0,4},{1,3},{2,6},{3,1},{4,0},{5,9},{6,2},{7,11},{8,12},{9,5},{10,... | collective-permute-start | bytes 393224 | tf_op jit(solution)/shard_map/ppermute | solution.py:336
  64.6 5.0 %collective-permute-start.22 = (f32[4,64,128]{2,1,0:T(8,128)S(1)}, f32[4,64,128]{2,1,0:T(8,128)S(1)}, u32[]{:S(2)}, u32[]{:S(2)}) collective-permute-start(f32[4,64,128]{2,1,0:T(8,128)S(1)} %wave_halo.26.cur.prev), channel_id=1, source_target_pairs={{0,4},{1,3},{2,6},{3,1},{4,0},{5,9},{6,2},{7,11},{8,12},{9,5},{10,... | collective-permute-start | bytes 393224 | tf_op jit(solution)/shard_map/ppermute | solution.py:336
  69.7 5.0 %collective-permute-start.24 = (f32[4,64,128]{2,1,0:T(8,128)S(1)}, f32[4,64,128]{2,1,0:T(8,128)S(1)}, u32[]{:S(2)}, u32[]{:S(2)}) collective-permute-start(f32[4,64,128]{2,1,0:T(8,128)S(1)} %wave_halo.27.cur.prev), channel_id=1, source_target_pairs={{0,4},{1,3},{2,6},{3,1},{4,0},{5,9},{6,2},{7,11},{8,12},{9,5},{10,... | collective-permute-start | bytes 393224 | tf_op jit(solution)/shard_map/ppermute | solution.py:336
  74.8 7.7 %collective-permute-start.26 = (f32[4,64,128]{2,1,0:T(8,128)S(1)}, f32[4,64,128]{2,1,0:T(8,128)S(1)}, u32[]{:S(2)}, u32[]{:S(2)}) collective-permute-start(f32[4,64,128]{2,1,0:T(8,128)S(1)} %wave_halo.28.cur.prev), channel_id=1, source_target_pairs={{0,4},{1,3},{2,6},{3,1},{4,0},{5,9},{6,2},{7,11},{8,12},{9,5},{10,... | collective-permute-start | bytes 393224 | tf_op jit(solution)/shard_map/ppermute | solution.py:336
  76.9 5.6 %collective-permute-start.27 = (f32[4,64,128]{2,1,0:T(8,128)S(1)}, f32[4,64,128]{2,1,0:T(8,128)S(1)}, u32[]{:S(2)}, u32[]{:S(2)}) collective-permute-start(f32[4,64,128]{2,1,0:T(8,128)S(1)} %wave_halo.28.cur.prev), channel_id=1, source_target_pairs={{0,1},{1,0},{2,3},{3,2},{4,5},{5,4},{6,7},{7,6},{8,9},{9,8},{10,11... | collective-permute-start | bytes 393224 | tf_op jit(solution)/shard_map/ppermute | solution.py:339
  77.0 6.2 %collective-permute-start.34 = (f32[2,2,128]{2,0,1:T(2,128)S(1)}, f32[2,2,128]{2,0,1:T(2,128)S(1)}, u32[]{:S(2)}, u32[]{:S(2)}) collective-permute-start(f32[2,2,128]{2,0,1:T(2,128)S(1)} %pad_maximum_fusion.4), channel_id=1, source_target_pairs={{0,2},{1,3},{2,0},{3,1},{4,6},{5,7},{6,4},{7,5},{8,10},{9,11},{10,... | collective-permute-start | bytes 6152 | tf_op jit(solution)/shard_map/ppermute | solution.py:339
  82.6 5.0 %collective-permute-start.28 = (f32[4,64,128]{2,1,0:T(8,128)S(1)}, f32[4,64,128]{2,1,0:T(8,128)S(1)}, u32[]{:S(2)}, u32[]{:S(2)}) collective-permute-start(f32[4,64,128]{2,1,0:T(8,128)S(1)} %wave_halo.29.cur.prev), channel_id=1, source_target_pairs={{0,4},{1,3},{2,6},{3,1},{4,0},{5,9},{6,2},{7,11},{8,12},{9,5},{10,... | collective-permute-start | bytes 393224 | tf_op jit(solution)/shard_map/ppermute | solution.py:336
  82.8 4.9 %collective-permute-start.29 = (f32[4,64,128]{2,1,0:T(8,128)S(1)}, f32[4,64,128]{2,1,0:T(8,128)S(1)}, u32[]{:S(2)}, u32[]{:S(2)}) collective-permute-start(f32[4,64,128]{2,1,0:T(8,128)S(1)} %wave_halo.29.cur.prev), channel_id=1, source_target_pairs={{0,1},{1,0},{2,3},{3,2},{4,5},{5,4},{6,7},{7,6},{8,9},{9,8},{10,11... | collective-permute-start | bytes 393224 | tf_op jit(solution)/shard_map/ppermute | solution.py:339
  87.7 12.4 %collective-permute-start.30 = (f32[4,64,128]{2,1,0:T(8,128)S(1)}, f32[4,64,128]{2,1,0:T(8,128)S(1)}, u32[]{:S(2)}, u32[]{:S(2)}) collective-permute-start(f32[4,64,128]{2,1,0:T(8,128)S(1)} %wave_halo.30.cur), channel_id=1, source_target_pairs={{0,4},{1,3},{2,6},{3,1},{4,0},{5,9},{6,2},{7,11},{8,12},{9,5},{10,... | collective-permute-start | bytes 393224 | tf_op jit(solution)/shard_map/ppermute | solution.py:336
  89.3 10.8 %collective-permute-start.31 = (f32[4,64,128]{2,1,0:T(8,128)S(1)}, f32[4,64,128]{2,1,0:T(8,128)S(1)}, u32[]{:S(2)}, u32[]{:S(2)}) collective-permute-start(f32[4,64,128]{2,1,0:T(8,128)S(1)} %wave_halo.30.cur), channel_id=1, source_target_pairs={{0,1},{1,0},{2,3},{3,2},{4,5},{5,4},{6,7},{7,6},{8,9},{9,8},{10,11... | collective-permute-start | bytes 393224 | tf_op jit(solution)/shard_map/ppermute | solution.py:339
  101.1 11.5 %collective-permute-start.39 = (f32[2,64,128]{2,1,0:T(8,128)S(1)}, f32[2,64,128]{2,1,0:T(8,128)S(1)}, u32[]{:S(2)}, u32[]{:S(2)}) collective-permute-start(f32[2,64,128]{2,1,0:T(8,128)S(1)} %slice.93.outer), channel_id=1, source_target_pairs={{0,1},{1,0},{2,3},{3,2},{4,5},{5,4},{6,7},{7,6},{8,9},{9,8},{10,11... | collective-permute-start | bytes 196616 | tf_op jit(solution)/shard_map/ppermute | solution.py:339
  102.0 3.8 %collective-permute-start.36 = (f32[36,128]{1,0:T(8,128)S(1)}, f32[36,128]{1,0:T(8,128)S(1)}, u32[]{:S(2)}, u32[]{:S(2)}) collective-permute-start(f32[36,128]{1,0:T(8,128)S(1)} %fusion.3), channel_id=1, source_target_pairs={{0,4},{1,5},{2,6},{3,7},{4,0},{5,1},{6,2},{7,3},{8,12},{9,13},{10,... | collective-permute-start | bytes 55304 | tf_op jit(solution)/shard_map/ppermute | solution.py:342
  105.8 3.8 %collective-permute-start.37 = (f32[36,128]{1,0:T(8,128)S(1)}, f32[36,128]{1,0:T(8,128)S(1)}, u32[]{:S(2)}, u32[]{:S(2)}) collective-permute-start(f32[36,128]{1,0:T(8,128)S(1)} %add.45), channel_id=1, source_target_pairs={{0,8},{1,9},{2,10},{3,11},{4,12},{5,13},{6,14},{7,15},{8,0},{9,1},... | collective-permute-start | bytes 55304 | tf_op jit(solution)/shard_map/ppermute | solution.py:342
  109.5 4.8 %collective-permute-start.38 = (f32[36,128]{1,0:T(8,128)S(1)}, f32[36,128]{1,0:T(8,128)S(1)}, u32[]{:S(2)}, u32[]{:S(2)}) collective-permute-start(f32[36,128]{1,0:T(8,128)S(1)} %add.46), channel_id=1, source_target_pairs={{0,16},{1,17},{2,18},{3,19},{4,20},{5,21},{6,22},{7,23},{8,24},{9,... | collective-permute-start | bytes 55304 | tf_op jit(solution)/shard_map/ppermute | solution.py:342
  114.4 8.3 %collective-permute-start.32 = (f32[4,64,128]{2,1,0:T(8,128)S(1)}, f32[4,64,128]{2,1,0:T(8,128)S(1)}, u32[]{:S(2)}, u32[]{:S(2)}) collective-permute-start(f32[4,64,128]{2,1,0:T(8,128)S(1)} %wave_halo.31.cur), channel_id=1, source_target_pairs={{0,1},{1,0},{2,3},{3,2},{4,5},{5,4},{6,7},{7,6},{8,9},{9,8},{10,11... | collective-permute-start | bytes 393224 | tf_op jit(solution)/shard_map/ppermute | solution.py:339
  (16 other events, 212.4 us)

commit v3 on v2

v3 whole, which is shorter than its diff:
```python
import functools

import jax
import jax.numpy as jnp
from jax import lax
from jax.experimental import pallas as pl
from jax.experimental.pallas import tpu as pltpu
from jax.sharding import PartitionSpec as P

STENCIL = (-205.0 / 72.0, 8.0 / 5.0, -1.0 / 5.0, 8.0 / 315.0, -1.0 / 560.0)
TIME_RATIO = 0.1
REACH = 4
AXES = ("mp", "station")
VMEM = pl.BlockSpec(memory_space=pltpu.VMEM)
SMEM = pl.BlockSpec(memory_space=pltpu.SMEM)
ANY = pl.BlockSpec(memory_space=pl.ANY)
F32 = jnp.float32
MIB = 1 << 20


def room(mib):
    return pltpu.CompilerParams(vmem_limit_bytes=mib * MIB)


def shape(dims):
    return jax.ShapeDtypeStruct(dims, F32)


def pairs_of(count, stations, partner):
    return [
        (m * stations + s, (lambda t: t[0] * stations + t[1])(partner(m, s)))
        for m in range(count)
        for s in range(stations)
    ]


def chain_partner(count):
    def partner(m, s):
        other = m + 1 if s % 2 == 0 else m - 1
        if other < 0 or other >= count:
            return (m, s ^ 2)
        return (other, s ^ 1)

    return partner


def position():
    return lax.axis_index("mp"), lax.axis_index("station") % 2


def divmod_static(value, divisor):
    if divisor & (divisor - 1) == 0:
        return value >> (divisor.bit_length() - 1), value & (divisor - 1)
    return value // divisor, value % divisor


def run_copies(pairs, sems):
    copies = [pltpu.make_async_copy(a, b, sems.at[i]) for i, (a, b) in enumerate(pairs)]
    for copy in copies:
        copy.start()
    for copy in copies:
        copy.wait()


def plane_of(core, j, slab):
    return jnp.where(core == 0, slab - 1 - j, j)


def first_kernel(now, velocity, density, cur, message, sems):
    slab = now.shape[0]
    half = slab // 2
    _, core = position()
    pairs = []
    for j in range(half):
        plane = plane_of(core, j, slab)
        pairs += [(now.at[plane], cur.at[j]), (now.at[plane], message.at[j])]
    edge = plane_of(core, 0, slab)
    pairs += [(velocity.at[edge], message.at[half]), (density.at[edge], message.at[half + 1])]
    run_copies(pairs, sems)


def first_message(p_now, velocity, density):
    slab, rows, lanes = p_now.shape
    half = slab // 2
    return pl.pallas_call(
        first_kernel,
        out_shape=(shape((half, rows, lanes)), shape((half + 2, rows, lanes))),
        in_specs=[ANY] * 3,
        out_specs=(VMEM, VMEM),
        scratch_shapes=[pltpu.SemaphoreType.DMA((2 * half + 2,))],
        compiler_params=room(2),
        name="first_message",
    )(p_now, velocity, density)


def setup_kernel(count, source, p_prev, velocity, density, prev, cour, cour_outer, mask, dens, vel, raw, sems):
    slab = p_prev.shape[0]
    half, rows, lanes = prev.shape
    m, core = position()
    pairs = []
    for j in range(half):
        plane = plane_of(core, j, slab)
        pairs += [(p_prev.at[plane], prev.at[j]), (velocity.at[plane], vel.at[j])]
    pairs += [(density.at[pl.ds(core * half, half)], raw)]
    run_copies(pairs, sems)
    outer_ok = jnp.where(jnp.where(core == 0, m < count - 1, m > 0), 1.0, 0.0)
    column, source_lane = divmod_static(source[0], lanes)
    source_x, source_row = divmod_static(column, rows)
    row = lax.broadcasted_iota(jnp.int32, (rows, lanes), 0)
    lane = lax.broadcasted_iota(jnp.int32, (rows, lanes), 1)
    spot = jnp.where((row == source_row) & (lane == source_lane), 1.0, 0.0)
    for j in range(half):
        scaled = TIME_RATIO * vel[j]
        square = scaled * scaled
        cour[j] = square
        cour_outer[j] = square * outer_ok
        here = m * slab + plane_of(core, j, slab) == source_x
        mask[j] = spot * jnp.where(here, 1.0, 0.0)
        dens[j] = raw[j].astype(jnp.bfloat16).astype(F32)


def setup(count, source_cell, p_prev, velocity, density):
    slab, rows, lanes = p_prev.shape
    half = slab // 2
    part = shape((half, rows, lanes))
    held = pltpu.VMEM((half, rows, lanes), F32)
    return pl.pallas_call(
        functools.partial(setup_kernel, count),
        out_shape=(part,) * 5,
        in_specs=[SMEM] + [ANY] * 3,
        out_specs=(VMEM,) * 5,
        scratch_shapes=[held, held, pltpu.SemaphoreType.DMA((2 * half + 1,))],
        compiler_params=room(4),
        cost_estimate=pl.CostEstimate(
            flops=20 * half * rows * lanes, bytes_accessed=32 * half * rows * lanes, transcendentals=0
        ),
        name="setup",
    )(source_cell, p_prev, velocity, density)


def local_kernel(step, pulses, mask, cur, prev, cour, surf_in, base, surf, pad):
    planes, rows, lanes = prev.shape
    lane = lax.broadcasted_iota(jnp.int32, (rows, lanes), 1)
    weights = {}
    for d in range(1, REACH + 1):
        weights[d] = jnp.where(lane >= d, STENCIL[d], 0.0)
        weights[-d] = jnp.where(lane < lanes - d, STENCIL[d], 0.0)
    pulse = pulses[step : step + 1, :]
    for j in range(planes):
        pad[j, 0:8, :] = jnp.zeros((8, lanes), F32)
        pad[j, 8 + rows : 16 + rows, :] = jnp.zeros((8, lanes), F32)
        pad[j, 8 : 8 + rows, :] = cur[j]
    for j in range(planes):
        c = cur[j]
        acc = 3.0 * STENCIL[0] * c
        for d in range(1, REACH + 1):
            acc = acc + weights[d] * pltpu.roll(c, d, 1) + weights[-d] * pltpu.roll(c, lanes - d, 1)
            near = pad[j, 8 + d : 8 + d + rows, :] + pad[j, 8 - d : 8 - d + rows, :]
            for i in (j - d, j + d):
                if 0 <= i < planes:
                    near = near + cur[i]
            acc = acc + STENCIL[d] * near
        base[j] = 2.0 * c - prev[j] + cour[j] * acc + pulse * mask[j]
        if step == 0:
            surf[j] = jnp.zeros((rows, lanes), F32)
        else:
            surf[j] = jnp.where(
                lane == step - 1, jnp.broadcast_to(c[:, 0:1], (rows, lanes)), surf_in[j]
            )


def local_step(step, pulses, mask, cur, prev, cour, surf):
    planes, rows, lanes = cur.shape
    return pl.pallas_call(
        functools.partial(local_kernel, step),
        out_shape=(shape(cur.shape), shape(cur.shape)),
        in_specs=[VMEM] * 6,
        out_specs=(VMEM, VMEM),
        scratch_shapes=[pltpu.VMEM((planes, rows + 16, lanes), F32)],
        compiler_params=room(2),
        cost_estimate=pl.CostEstimate(
            flops=60 * cur.size, bytes_accessed=24 * cur.size, transcendentals=0
        ),
        name="wave_local",
    )(pulses, mask, cur, prev, cour, surf)


def halo_kernel(base, cour, cour_outer, outer, inner, out):
    planes = base.shape[0]
    for j in range(planes):
        far = near = None
        for d in range(j + 1, REACH + 1):
            term = STENCIL[d] * outer[d - j - 1]
            far = term if far is None else far + term
        for d in range(planes - j, REACH + 1):
            term = STENCIL[d] * inner[2 * planes - 1 - j - d]
            near = term if near is None else near + term
        out[j] = base[j] + (cour[j] * near + cour_outer[j] * far)


def halo_step(base, cour, cour_outer, outer, inner):
    return pl.pallas_call(
        halo_kernel,
        out_shape=shape(base.shape),
        in_specs=[VMEM] * 5,
        out_specs=VMEM,
        compiler_params=room(2),
        cost_estimate=pl.CostEstimate(
            flops=12 * base.size, bytes_accessed=20 * base.size, transcendentals=0
        ),
        name="wave_halo",
    )(base, cour, cour_outer, outer, inner)


def trace_kernel(step, place, cur, surf, predicted, out):
    planes, rows, lanes = cur.shape
    receivers = place.shape[0]
    steps = step + 1
    lane = lax.broadcasted_iota(jnp.int32, (rows, lanes), 1)
    columns = jnp.concatenate(
        [
            jnp.where(lane == step, jnp.broadcast_to(cur[j, :, 0:1], (rows, lanes)), surf[j])
            for j in range(planes)
        ],
        0,
    )
    where = lax.broadcasted_iota(jnp.int32, (receivers, planes * rows), 1)
    pick = jnp.where(place[...] == where, 1.0, 0.0).astype(jnp.bfloat16)
    total = None
    for _ in range(3):
        part = columns.astype(jnp.bfloat16)
        columns = columns - part.astype(F32)
        term = jnp.dot(pick, part, preferred_element_type=F32)
        total = term if total is None else total + term
    total = total.T
    for b in range(receivers // 128):
        out[b * steps : (b + 1) * steps, :] = total[:steps, b * 128 : (b + 1) * 128]
    out[steps * (receivers // 128) :, :] = predicted[...]


def recorded_traces(step, place, cur, surf, predicted):
    rows = (step + 1) * (place.shape[0] // 128) + predicted.shape[0]
    return pl.pallas_call(
        functools.partial(trace_kernel, step),
        out_shape=shape((rows, 128)),
        in_specs=[VMEM] * 4,
        out_specs=VMEM,
        compiler_params=room(4),
        name="traces",
    )(place, cur, surf, predicted)


def join_kernel(own, sibling, out, sems):
    slab = out.shape[0]
    _, core = position()
    pairs = []
    for j in range(slab // 2):
        pairs += [
            (own.at[j], out.at[plane_of(core, j, slab)]),
            (sibling.at[j], out.at[plane_of(1 - core, j, slab)]),
        ]
    run_copies(pairs, sems)


def join(own, sibling):
    half, rows, lanes = own.shape
    return pl.pallas_call(
        join_kernel,
        out_shape=shape((2 * half, rows, lanes)),
        in_specs=[VMEM, VMEM],
        out_specs=ANY,
        scratch_shapes=[pltpu.SemaphoreType.DMA((2 * half,))],
        compiler_params=room(2),
        name="join",
    )(own, sibling)


def table_low(total_x, slab, offset):
    m, _ = position()
    return m * slab - (total_x - 1) + offset


def table_kernel(total_x, slab, head, out):
    spread, lanes = out.shape[1:]
    low = table_low(total_x, slab, head[0])
    dy = (lax.broadcasted_iota(jnp.int32, (spread, lanes), 0) - (spread // 2 - 1)).astype(F32)
    dz = (lax.broadcasted_iota(jnp.int32, (spread, lanes), 1) + 1).astype(F32)
    side = dy * dy
    deep = dz * dz

    def one(t, carry):
        dx = (t + low).astype(F32)
        square = dx * dx + side + deep
        value = dz / (square * jnp.sqrt(square))
        out[t] = value.astype(jnp.bfloat16).astype(F32)
        return carry

    lax.fori_loop(0, out.shape[0], one, 0)


def gravity_table(total_x, slab, depth, lateral, vertical, head):
    size = depth * 2 * lateral * vertical
    return pl.pallas_call(
        functools.partial(table_kernel, total_x, slab),
        out_shape=shape((depth, 2 * lateral, vertical)),
        in_specs=[SMEM],
        out_specs=VMEM,
        cost_estimate=pl.CostEstimate(
            flops=20 * size, bytes_accessed=4 * size, transcendentals=2 * size
        ),
        compiler_params=room(8),
        name="gravity_table",
    )(head)


def forward_kernel(first, guard, total_x, slab, lateral, head, table, dens, out):
    planes, rows, lanes = dens.shape
    count = out.shape[0]
    spread = 2 * lateral
    m, core = position()
    lead = total_x - 1 - head[0]
    if guard:
        out[...] = jnp.zeros_like(out)

    def one(s, carry):
        sx, sy = divmod_static(head[1 + first + s], lateral)
        shift = lead - sx
        start = (shift + core * planes) * spread + (lateral - 1 - sy)

        def accumulate():
            acc = None
            for p in range(planes):
                term = table[pl.ds(start + p * spread, rows), :] * dens[p]
                acc = term if acc is None else acc + term
            out[pl.ds(s, 1), :] = jnp.sum(acc, axis=0, keepdims=True)

        if guard:
            pl.when((shift >= 0) & (shift < guard))(accumulate)
        else:
            accumulate()
        return carry

    lax.fori_loop(0, count, one, 0, unroll=4)


def gravity_forward(first, count, guard, total_x, slab, lateral, head, table, dens):
    flat = table.reshape(-1, table.shape[2])
    work = count * dens.size
    return pl.pallas_call(
        functools.partial(forward_kernel, first, guard, total_x, slab, lateral),
        out_shape=shape((count, dens.shape[2])),
        in_specs=[SMEM, VMEM, VMEM],
        out_specs=VMEM,
        cost_estimate=pl.CostEstimate(
            flops=4 * work, bytes_accessed=4 * dens.size, transcendentals=0
        ),
        compiler_params=room(8),
        name="gravity_forward",
    )(head, flat, dens)


def spread_back(guard, total_x, lateral, row_low, head, weights, table, out):
    slab, rows, lanes = out.shape
    spread = 2 * lateral
    lead = total_x - 1 - head[0]

    def one(s, acc):
        sx, sy = divmod_static(head[1 + s], lateral)
        shift = lead - sx
        weight = weights(s)
        if guard:
            keep = (shift >= 0) & (shift < guard)
            shift = jnp.where(keep, shift, 0)
            weight = jnp.where(keep, weight, 0.0)
        start = shift * spread + (lateral - 1 - sy + row_low)
        return tuple(
            acc[x] + weight * table[pl.ds(start + x * spread, rows), :] for x in range(slab)
        )

    zero = jnp.zeros((rows, lanes), F32)
    acc = lax.fori_loop(0, head.shape[0] - 1, one, (zero,) * slab, unroll=4)
    for x in range(slab):
        out[x] = acc[x]


def adjoint_kernel(guard, total_x, lateral, head, weights, table, out):
    row_low = lax.axis_index("station") * out.shape[1]
    spread_back(guard, total_x, lateral, row_low, head, lambda s: weights[s], table, out)


def gravity_adjoint(guard, total_x, slab, rows, lateral, head, weights, table):
    flat = table.reshape(-1, table.shape[2])
    return pl.pallas_call(
        functools.partial(adjoint_kernel, guard, total_x, lateral),
        out_shape=shape((slab, rows, table.shape[2])),
        in_specs=[SMEM, SMEM, VMEM],
        out_specs=VMEM,
        compiler_params=room(8),
        name="gravity_adjoint",
    )(head, weights, flat)


def last_kernel(total_x, lateral, head, packed, other, observed, table, traces, own, out, held, scalars, sem):
    steps, receivers = traces.shape
    blocks = receivers // 128
    total = packed[...] + other[...]
    residual = total[steps * blocks :, :] - observed[...]
    held[...] = residual.astype(jnp.bfloat16).astype(F32)
    copy = pltpu.make_async_copy(held, scalars, sem)
    copy.start()
    for b in range(blocks):
        traces[:, b * 128 : (b + 1) * 128] = total[b * steps : (b + 1) * steps, :]
    s = lax.axis_index("station")
    mine = own.shape[0]
    for k in range(residual.shape[0] // mine):

        @pl.when(s == k)
        def _(k=k):
            own[...] = residual[k * mine : (k + 1) * mine, :]

    copy.wait()
    spread_back(
        0,
        total_x,
        lateral,
        s * out.shape[1],
        head,
        lambda i: scalars[i // 128, i % 128],
        table,
        out,
    )


def gravity_last(steps, receivers, total_x, slab, rows, lateral, head, packed, other, observed, table):
    flat = table.reshape(-1, table.shape[2])
    count = lax.axis_size("station")
    lines = observed.shape[0]
    return pl.pallas_call(
        functools.partial(last_kernel, total_x, lateral),
        out_shape=(
            shape((steps, receivers)),
            shape((lines // count, 128)),
            shape((slab, rows, table.shape[2])),
        ),
        in_specs=[SMEM] + [VMEM] * 4,
        out_specs=(VMEM,) * 3,
        scratch_shapes=[
            pltpu.VMEM((lines, 128), F32),
            pltpu.SMEM((lines, 128), F32),
            pltpu.SemaphoreType.DMA,
        ],
        compiler_params=room(8),
        name="gravity_last",
    )(head, packed, other, observed, flat)


def cross_kernel(count, velocity, density, outer, inner, out):
    slab, rows, lanes = velocity.shape
    half = slab // 2
    lane = lax.broadcasted_iota(jnp.int32, (rows, lanes), 1)
    row = lax.broadcasted_iota(jnp.int32, (rows, lanes), 0)
    m, core = position()
    flipped = core == 0
    left_ok = jnp.where(m > 0, 0.5, 0.0)
    right_ok = jnp.where(m < count - 1, 0.5, 0.0)

    def slopes(field, side, x):
        f = field[x]
        if x > 0:
            below = 0.5 * field[x - 1]
        else:
            below = left_ok * jnp.where(flipped, inner[side], outer[side])
        if x < slab - 1:
            above = 0.5 * field[x + 1]
        else:
            above = right_ok * jnp.where(flipped, outer[side], inner[side])
        up = jnp.where(row < rows - 1, pltpu.roll(f, rows - 1, 0), 0.0)
        down = jnp.where(row > 0, pltpu.roll(f, 1, 0), 0.0)
        ahead = jnp.where(lane < lanes - 1, pltpu.roll(f, lanes - 1, 1), 0.0)
        back = jnp.where(lane > 0, pltpu.roll(f, 1, 1), 0.0)
        return above - below, (up - down) * 0.5, (ahead - back) * 0.5

    for x in range(slab):
        v = slopes(velocity, half, x)
        q = slopes(density, half + 1, x)
        out[0, x] = v[1] * q[2] - v[2] * q[1]
        out[1, x] = v[2] * q[0] - v[0] * q[2]
        out[2, x] = v[0] * q[1] - v[1] * q[0]


def cross_gradient_of(count, velocity, density, outer, inner):
    return pl.pallas_call(
        functools.partial(cross_kernel, count),
        out_shape=shape((3,) + velocity.shape),
        in_specs=[VMEM] * 4,
        out_specs=VMEM,
        cost_estimate=pl.CostEstimate(
            flops=60 * velocity.size, bytes_accessed=24 * velocity.size, transcendentals=0
        ),
        compiler_params=room(8),
        name="cross_gradient",
    )(velocity, density, outer, inner)


def per_device(
    p_now, p_prev, velocity, density, wavelet, source_cell, receiver_cells, station_cells, observed
):
    slab, lateral, vertical = p_now.shape
    count = lax.axis_size("mp")
    stations = lax.axis_size("station")
    steps = wavelet.shape[0]
    half = slab // 2
    assert half == REACH and count % 2 == 0 and stations % 4 == 0
    total_x = slab * count
    m, core = position()
    s = lax.axis_index("station")
    block = lateral // stations
    chain = pairs_of(count, stations, chain_partner(count))
    together = lax.optimization_barrier

    def across(value):
        return lax.ppermute(value, AXES, chain)

    def swap(value, slab_bit, station_bit):
        pairs = pairs_of(count, stations, lambda i, k: (i ^ slab_bit, k ^ station_bit))
        return lax.ppermute(value, AXES, pairs)

    cur, message = first_message(p_now, velocity, density)
    outer = across(message)
    inner = swap(cur, 0, 1)
    edges = outer
    prev, cour, cour_outer, mask, dens = setup(count, source_cell, p_prev, velocity, density)
    pulses = jnp.broadcast_to(wavelet[:, None], (steps, 128))

    receiver_x, receiver_y = divmod_static(receiver_cells, lateral)
    receiver_j = receiver_x - m * slab
    receiver_j = jnp.where(core == 0, slab - 1 - receiver_j, receiver_j)
    inside = (receiver_j >= 0) & (receiver_j < half)
    place = jnp.where(inside, receiver_j * lateral + receiver_y, -1)[:, None]

    reach = min(total_x, 64)
    chunks = -(-total_x // reach)
    span = reach + slab - 1
    own_stations = station_cells.shape[0]
    n_stations = own_stations * stations

    def head_of(offset, cells):
        return jnp.concatenate([jnp.reshape(offset, (1,)).astype(jnp.int32), cells])

    def table_of(head):
        return gravity_table(total_x, slab, span, lateral, vertical, head)

    state = {"known": jnp.stack([station_cells.astype(F32), observed])[:, None, :]}

    def exchange(bit):
        def work(gate):
            known = gate(state["known"])
            other = swap(known, 0, bit)
            upper = (s // bit) % 2 == 1
            state["known"] = jnp.concatenate(
                [jnp.where(upper, other, known), jnp.where(upper, known, other)], 1
            )
            return "known"

        return work

    def share_edges(gate):
        state["inner"] = swap(gate(edges), 0, 1)
        return "inner"

    def cross(gate):
        state["cross"] = cross_gradient_of(count, velocity, density, edges, gate(state["inner"]))
        return "cross"

    def build_table(gate):
        cells = state["known"][0].reshape(-1).astype(jnp.int32)
        state["head"] = head_of(0, cells)
        state["table"] = table_of(gate(jnp.zeros((1,), jnp.int32)))
        return "table"

    pieces = 8
    part = n_stations // pieces

    def forward(i):
        def work(gate):
            state[i] = gravity_forward(
                i * part, part, 0, total_x, slab, lateral, gate(state["head"]), state["table"], dens
            )
            return i

        return work

    def gather_sums(gate):
        sums = jnp.concatenate([state[i] for i in range(pieces)])
        state["predicted"] = jnp.sum(gate(sums), axis=1).reshape(-1, 128)
        return "predicted"

    jobs = [exchange(1 << b) for b in range(stations.bit_length() - 1)]
    jobs.insert(1, share_edges)
    jobs.append(cross)
    if chunks == 1:
        jobs += [build_table] + [forward(i) for i in range(pieces)] + [gather_sums]

    surf = cour
    for step in range(steps):
        job = jobs.pop(0) if step and jobs else None
        done = None
        if step:
            if job is not None:
                gated = []

                def gate(value):
                    nonlocal cur
                    cur, value = together((cur, value))
                    gated.append(value)
                    return value

                done = job(gate)
            outer = across(cur)
            inner = swap(cur, 0, 1)
        base, surf = local_step(step, pulses, mask, cur, prev, cour, surf)
        cur, prev = halo_step(base, cour, cour_outer, outer, inner), cur
        if done is not None:
            cur, state[done] = together((cur, state[done]))
    assert not jobs

    all_observed = state["known"][1].reshape(-1, 128)
    cells = state["known"][0].reshape(-1).astype(jnp.int32)
    if chunks == 1:
        predicted = state["predicted"]
    else:

        def add_chunk(i, total):
            head = head_of(i * reach, cells)
            return total + gravity_forward(
                0, n_stations, reach, total_x, slab, lateral, head, table_of(head[:1]), dens
            )

        sums = lax.fori_loop(0, chunks, add_chunk, jnp.zeros((n_stations, vertical), F32))
        predicted = jnp.sum(sums, axis=1).reshape(-1, 128)

    sibling = swap(cur, 0, 1)
    packed = recorded_traces(steps - 1, place, cur, surf, predicted)
    other = swap(packed, 0, 1)
    if count & (count - 1) == 0:
        bit = 1
        while bit < count:
            packed = packed + other
            other = swap(packed, bit, 1)
            if bit == 1:
                wavefield = join(cur, sibling)
                other, wavefield = together((other, wavefield))
            bit *= 2
    else:
        wavefield = join(cur, sibling)
        packed = lax.psum(packed + other, "mp")
        other = jnp.zeros_like(packed)

    receivers = receiver_cells.shape[0]
    if chunks == 1:
        traces, own, density_gradient = gravity_last(
            steps,
            receivers,
            total_x,
            slab,
            block,
            lateral,
            state["head"],
            packed,
            other,
            all_observed,
            state["table"],
        )
        gravity_residual = own.reshape(-1)
    else:
        packed = packed + other
        blocks = receivers // 128
        traces = jnp.concatenate(
            [packed[b * steps : (b + 1) * steps] for b in range(blocks)], axis=1
        )
        residual = (packed[steps * blocks :] - all_observed).reshape(-1)
        gravity_residual = lax.dynamic_slice(residual, (s * own_stations,), (own_stations,))
        weights = residual.astype(jnp.bfloat16).astype(F32)

        def back_chunk(i, total):
            head = head_of(i * reach, cells)
            return total + gravity_adjoint(
                reach, total_x, slab, block, lateral, head, weights, table_of(head[:1])
            )

        density_gradient = lax.fori_loop(
            0, chunks, back_chunk, jnp.zeros((slab, block, vertical), F32)
        )
    return (wavefield, traces, gravity_residual, density_gradient, state["cross"])


def solution(mesh):
    in_specs = (
        P("mp", None, None),
        P("mp", None, None),
        P("mp", None, None),
        P("mp", None, None),
        P(),
        P(),
        P(),
        P("station"),
        P("station"),
    )
    out_specs = (
        P("mp", None, None),
        P(),
        P("station"),
        P("mp", "station", None),
        P(None, "mp", None, None),
    )
    return jax.shard_map(
        per_device, mesh=mesh, in_specs=in_specs, out_specs=out_specs, check_vma=False
    )
```

time: 124 us -> 124 us (level)
  waiting for transfers between devices: 32.8 us -> 36 us
  other arithmetic: 3.88 us -> 1.6 us
  Pallas kernels: 35.4 us -> 33.6 us
  local copies, waits for them, and re-layouts: 7.64 us -> 8.91 us
    pallas_call x16, Pallas kernels: 14.8 us -> 6.31 us  [local_step(): pl.pallas_call(functools.partial(local_kernel, step), out_shape=(shape(cu...]
    pallas_call x8 -> x15, Pallas kernels: 19.6 us -> 26.2 us  [the longest x8 12 us: gravity_forward(): pl.pallas_call(functools.partial(forward_kernel, first, guard, total_x, s...]
    unnamed x16 -> x29, local copies, waits for them, and re-layouts: 2.35 us -> 8.05 us
    slice x8 -> x0, local copies, waits for them, and re-layouts: 3.84 us -> none  [the longest x5 3.82 us: owned(): return jnp.where(flipped, jnp.flip(field[half:], 0), field[:half])]
    ppermute x16, waiting for transfers between devices: 27.6 us -> 31.3 us  [across(): return lax.ppermute(value, AXES, chain)]
    select_n x7 -> x2, other arithmetic: 1.93 us -> 0.01 us  [work(): jnp.where(upper, other, known)]
    another operation x1 -> x2, other arithmetic: 0.01 us -> 1.32 us  [per_device(): jnp.stack([station_cells.astype(F32), observed])[:, None, :]]
  transfers between devices with their start and end apart: 40 -> 40, of which waited for: 17 -> 19; matrix products, arithmetic and copies ran while one was open for 5% -> 2% of each run, Pallas kernels for 28% -> 20%
where the time goes in v3:
time: 124 us; the launch traced here: 123 us
  starting transfers between devices  41.7 us (34%)
  waiting for transfers between devices  36 us (29%)
  Pallas kernels  33.6 us (27%)
  local copies, waits for them, and re-layouts  8.91 us (7%)
  between operations  1.71 us (1%)
  other arithmetic  1.6 us (1%)
    ppermute x16, waiting for transfers between devices, across(): return lax.ppermute(value, AXES, chain)  31.3 us
    ppermute x16, starting transfers between devices, across(): return lax.ppermute(value, AXES, chain)  31 us
    pallas_call x8, Pallas kernels, gravity_forward(): pl.pallas_call(functools.partial(forward_kernel, first, guard, total_x, s...  12 us
    ppermute x24, starting transfers between devices, swap(): return lax.ppermute(value, AXES, pairs)  10.7 us
    unnamed x29, local copies, waits for them, and re-layouts  8.05 us
    pallas_call x1, Pallas kernels, gravity_last(): pl.pallas_call(functools.partial(last_kernel, total_x, lateral), out_shap...  7.92 us
    pallas_call x16, Pallas kernels, local_step(): pl.pallas_call(functools.partial(local_kernel, step), out_shape=(shape(cu...  6.31 us
    ppermute x24, waiting for transfers between devices, swap(): return lax.ppermute(value, AXES, pairs)  4.62 us
  transfers between devices with their start and end apart: 40, of which 19 were waited for; matrix products, arithmetic and copies ran while one was open for 2% of the time, Pallas kernels for 20%

profile of v3, /device:TPU:0, one launch (start us, length us, event | category | flops | bytes accessed | tf_op | source)
XLA Modules:
  0.0 123.4 jit_solution(6638541730020761923)
XLA Ops:
  4.0 2.5 %collective-permute-start = (f32[6,64,128]{2,1,0:T(8,128)S(1)}, f32[6,64,128]{2,1,0:T(8,128)S(1)}, u32[]{:S(2)}, u32[]{:S(2)}) collective-permute-start(f32[6,64,128]{2,1,0:T(8,128)S(1)} %get-tuple-element.111), channel_id=1, source_target_pairs={{0,5},{1,3},{2,7},{3,1},{4,9},{5,0},{6,11},{7,2},{8,13},{9,4},{10,... | collective-permute-start | bytes 589832 | tf_op jit(solution)/shard_map/ppermute | solution.py:522
  15.5 3.4 %collective-permute-done.2.outer = f32[4,64,128]{2,1,0:T(8,128)S(1)} collective-permute-done((f32[4,64,128]{2,1,0:T(8,128)S(1)}, f32[4,64,128]{2,1,0:T(8,128)S(1)}, u32[]{:S(2)}, u32[]{:S(2)}) %collective-permute-start.2) | collective-permute-done | bytes 131104 | tf_op jit(solution)/shard_map/ppermute | solution.py:522
  19.0 2.0 %collective-permute-start.5 = (f32[4,64,128]{2,1,0:T(8,128)S(1)}, f32[4,64,128]{2,1,0:T(8,128)S(1)}, u32[]{:S(2)}, u32[]{:S(2)}) collective-permute-start(f32[4,64,128]{2,1,0:T(8,128)S(1)} %wave_halo.17.cur.prev), channel_id=1, source_target_pairs={{0,5},{1,3},{2,7},{3,1},{4,9},{5,0},{6,11},{7,2},{8,13},{9,4},{10,... | collective-permute-start | bytes 393224 | tf_op jit(solution)/shard_map/ppermute | solution.py:522
  21.4 3.5 %collective-permute-done.5.outer = f32[4,64,128]{2,1,0:T(8,128)S(1)} collective-permute-done((f32[4,64,128]{2,1,0:T(8,128)S(1)}, f32[4,64,128]{2,1,0:T(8,128)S(1)}, u32[]{:S(2)}, u32[]{:S(2)}) %collective-permute-start.5) | collective-permute-done | bytes 131104 | tf_op jit(solution)/shard_map/ppermute | solution.py:522
  24.9 1.6 %collective-permute-start.10 = (f32[2,2,128]{2,1,0:T(2,128)S(1)}, f32[2,2,128]{2,1,0:T(2,128)S(1)}, u32[]{:S(2)}, u32[]{:S(2)}) collective-permute-start(f32[2,2,128]{2,1,0:T(2,128)S(1)} %pad_maximum_fusion.1), channel_id=1, source_target_pairs={{0,2},{1,3},{2,0},{3,1},{4,6},{5,7},{6,4},{7,5},{8,10},{9,11},{10,... | collective-permute-start | bytes 6152 | tf_op jit(solution)/shard_map/ppermute | solution.py:526
  26.5 1.6 %collective-permute-start.8 = (f32[4,64,128]{2,1,0:T(8,128)S(1)}, f32[4,64,128]{2,1,0:T(8,128)S(1)}, u32[]{:S(2)}, u32[]{:S(2)}) collective-permute-start(f32[4,64,128]{2,1,0:T(8,128)S(1)} %wave_halo.18.cur.prev), channel_id=1, source_target_pairs={{0,5},{1,3},{2,7},{3,1},{4,9},{5,0},{6,11},{7,2},{8,13},{9,4},{10,... | collective-permute-start | bytes 393224 | tf_op jit(solution)/shard_map/ppermute | solution.py:522
  28.6 3.4 %collective-permute-done.8.outer = f32[4,64,128]{2,1,0:T(8,128)S(1)} collective-permute-done((f32[4,64,128]{2,1,0:T(8,128)S(1)}, f32[4,64,128]{2,1,0:T(8,128)S(1)}, u32[]{:S(2)}, u32[]{:S(2)}) %collective-permute-start.8) | collective-permute-done | bytes 131104 | tf_op jit(solution)/shard_map/ppermute | solution.py:522
  32.1 2.0 %collective-permute-start.11 = (f32[4,64,128]{2,1,0:T(8,128)S(1)}, f32[4,64,128]{2,1,0:T(8,128)S(1)}, u32[]{:S(2)}, u32[]{:S(2)}) collective-permute-start(f32[4,64,128]{2,1,0:T(8,128)S(1)} %wave_halo.19.cur.prev), channel_id=1, source_target_pairs={{0,5},{1,3},{2,7},{3,1},{4,9},{5,0},{6,11},{7,2},{8,13},{9,4},{10,... | collective-permute-start | bytes 393224 | tf_op jit(solution)/shard_map/ppermute | solution.py:522
  35.8 2.2 %collective-permute-done.11.outer = f32[4,64,128]{2,1,0:T(8,128)S(1)} collective-permute-done((f32[4,64,128]{2,1,0:T(8,128)S(1)}, f32[4,64,128]{2,1,0:T(8,128)S(1)}, u32[]{:S(2)}, u32[]{:S(2)}) %collective-permute-start.11) | collective-permute-done | bytes 131104 | tf_op jit(solution)/shard_map/ppermute | solution.py:522
  38.0 2.0 %collective-permute-start.13 = (f32[4,64,128]{2,1,0:T(8,128)S(1)}, f32[4,64,128]{2,1,0:T(8,128)S(1)}, u32[]{:S(2)}, u32[]{:S(2)}) collective-permute-start(f32[4,64,128]{2,1,0:T(8,128)S(1)} %wave_halo.20.cur.prev), channel_id=1, source_target_pairs={{0,5},{1,3},{2,7},{3,1},{4,9},{5,0},{6,11},{7,2},{8,13},{9,4},{10,... | collective-permute-start | bytes 393224 | tf_op jit(solution)/shard_map/ppermute | solution.py:522
  40.5 2.8 %gravity_table.1 = f32[71,128,128]{2,1,0:T(8,128)S(1)} custom-call(s32[1]{0:T(128)} %constant.67.clone.1.head), custom_call_target="tpu_custom_call" | custom-call | flops 23265280 | bytes 4653056 | tf_op jit(solution)/shard_map/gravity_table/pallas_call | solution.py:303
  43.7 2.0 %collective-permute-start.15 = (f32[4,64,128]{2,1,0:T(8,128)S(1)}, f32[4,64,128]{2,1,0:T(8,128)S(1)}, u32[]{:S(2)}, u32[]{:S(2)}) collective-permute-start(f32[4,64,128]{2,1,0:T(8,128)S(1)} %wave_halo.21.cur.prev), channel_id=1, source_target_pairs={{0,5},{1,3},{2,7},{3,1},{4,9},{5,0},{6,11},{7,2},{8,13},{9,4},{10,... | collective-permute-start | bytes 393224 | tf_op jit(solution)/shard_map/ppermute | solution.py:522
  47.5 1.6 %collective-permute-done.15.outer = f32[4,64,128]{2,1,0:T(8,128)S(1)} collective-permute-done((f32[4,64,128]{2,1,0:T(8,128)S(1)}, f32[4,64,128]{2,1,0:T(8,128)S(1)}, u32[]{:S(2)}, u32[]{:S(2)}) %collective-permute-start.15) | collective-permute-done | bytes 131104 | tf_op jit(solution)/shard_map/ppermute | solution.py:522
  49.2 2.0 %collective-permute-start.17 = (f32[4,64,128]{2,1,0:T(8,128)S(1)}, f32[4,64,128]{2,1,0:T(8,128)S(1)}, u32[]{:S(2)}, u32[]{:S(2)}) collective-permute-start(f32[4,64,128]{2,1,0:T(8,128)S(1)} %wave_halo.22.cur.prev), channel_id=1, source_target_pairs={{0,5},{1,3},{2,7},{3,1},{4,9},{5,0},{6,11},{7,2},{8,13},{9,4},{10,... | collective-permute-start | bytes 393224 | tf_op jit(solution)/shard_map/ppermute | solution.py:522
  53.1 1.6 %collective-permute-done.17.outer = f32[4,64,128]{2,1,0:T(8,128)S(1)} collective-permute-done((f32[4,64,128]{2,1,0:T(8,128)S(1)}, f32[4,64,128]{2,1,0:T(8,128)S(1)}, u32[]{:S(2)}, u32[]{:S(2)}) %collective-permute-start.17) | collective-permute-done | bytes 131104 | tf_op jit(solution)/shard_map/ppermute | solution.py:522
  54.7 2.0 %collective-permute-start.19 = (f32[4,64,128]{2,1,0:T(8,128)S(1)}, f32[4,64,128]{2,1,0:T(8,128)S(1)}, u32[]{:S(2)}, u32[]{:S(2)}) collective-permute-start(f32[4,64,128]{2,1,0:T(8,128)S(1)} %wave_halo.23.cur.prev), channel_id=1, source_target_pairs={{0,5},{1,3},{2,7},{3,1},{4,9},{5,0},{6,11},{7,2},{8,13},{9,4},{10,... | collective-permute-start | bytes 393224 | tf_op jit(solution)/shard_map/ppermute | solution.py:522
  58.6 1.6 %collective-permute-done.19.outer = f32[4,64,128]{2,1,0:T(8,128)S(1)} collective-permute-done((f32[4,64,128]{2,1,0:T(8,128)S(1)}, f32[4,64,128]{2,1,0:T(8,128)S(1)}, u32[]{:S(2)}, u32[]{:S(2)}) %collective-permute-start.19) | collective-permute-done | bytes 131104 | tf_op jit(solution)/shard_map/ppermute | solution.py:522
  60.3 2.0 %collective-permute-start.21 = (f32[4,64,128]{2,1,0:T(8,128)S(1)}, f32[4,64,128]{2,1,0:T(8,128)S(1)}, u32[]{:S(2)}, u32[]{:S(2)}) collective-permute-start(f32[4,64,128]{2,1,0:T(8,128)S(1)} %wave_halo.24.cur.prev), channel_id=1, source_target_pairs={{0,5},{1,3},{2,7},{3,1},{4,9},{5,0},{6,11},{7,2},{8,13},{9,4},{10,... | collective-permute-start | bytes 393224 | tf_op jit(solution)/shard_map/ppermute | solution.py:522
  64.1 1.6 %collective-permute-done.21.outer = f32[4,64,128]{2,1,0:T(8,128)S(1)} collective-permute-done((f32[4,64,128]{2,1,0:T(8,128)S(1)}, f32[4,64,128]{2,1,0:T(8,128)S(1)}, u32[]{:S(2)}, u32[]{:S(2)}) %collective-permute-start.21) | collective-permute-done | bytes 131104 | tf_op jit(solution)/shard_map/ppermute | solution.py:522
  65.8 2.0 %collective-permute-start.23 = (f32[4,64,128]{2,1,0:T(8,128)S(1)}, f32[4,64,128]{2,1,0:T(8,128)S(1)}, u32[]{:S(2)}, u32[]{:S(2)}) collective-permute-start(f32[4,64,128]{2,1,0:T(8,128)S(1)} %wave_halo.25.cur.prev), channel_id=1, source_target_pairs={{0,5},{1,3},{2,7},{3,1},{4,9},{5,0},{6,11},{7,2},{8,13},{9,4},{10,... | collective-permute-start | bytes 393224 | tf_op jit(solution)/shard_map/ppermute | solution.py:522
  71.3 2.0 %collective-permute-start.25 = (f32[4,64,128]{2,1,0:T(8,128)S(1)}, f32[4,64,128]{2,1,0:T(8,128)S(1)}, u32[]{:S(2)}, u32[]{:S(2)}) collective-permute-start(f32[4,64,128]{2,1,0:T(8,128)S(1)} %wave_halo.26.cur.prev), channel_id=1, source_target_pairs={{0,5},{1,3},{2,7},{3,1},{4,9},{5,0},{6,11},{7,2},{8,13},{9,4},{10,... | collective-permute-start | bytes 393224 | tf_op jit(solution)/shard_map/ppermute | solution.py:522
  76.8 2.0 %collective-permute-start.27 = (f32[4,64,128]{2,1,0:T(8,128)S(1)}, f32[4,64,128]{2,1,0:T(8,128)S(1)}, u32[]{:S(2)}, u32[]{:S(2)}) collective-permute-start(f32[4,64,128]{2,1,0:T(8,128)S(1)} %wave_halo.27.cur.prev), channel_id=1, source_target_pairs={{0,5},{1,3},{2,7},{3,1},{4,9},{5,0},{6,11},{7,2},{8,13},{9,4},{10,... | collective-permute-start | bytes 393224 | tf_op jit(solution)/shard_map/ppermute | solution.py:522
  82.4 2.0 %collective-permute-start.29 = (f32[4,64,128]{2,1,0:T(8,128)S(1)}, f32[4,64,128]{2,1,0:T(8,128)S(1)}, u32[]{:S(2)}, u32[]{:S(2)}) collective-permute-start(f32[4,64,128]{2,1,0:T(8,128)S(1)} %wave_halo.28.cur.prev), channel_id=1, source_target_pairs={{0,5},{1,3},{2,7},{3,1},{4,9},{5,0},{6,11},{7,2},{8,13},{9,4},{10,... | collective-permute-start | bytes 393224 | tf_op jit(solution)/shard_map/ppermute | solution.py:522
  87.9 2.0 %collective-permute-start.31 = (f32[4,64,128]{2,1,0:T(8,128)S(1)}, f32[4,64,128]{2,1,0:T(8,128)S(1)}, u32[]{:S(2)}, u32[]{:S(2)}) collective-permute-start(f32[4,64,128]{2,1,0:T(8,128)S(1)} %wave_halo.29.cur.prev), channel_id=1, source_target_pairs={{0,5},{1,3},{2,7},{3,1},{4,9},{5,0},{6,11},{7,2},{8,13},{9,4},{10,... | collective-permute-start | bytes 393224 | tf_op jit(solution)/shard_map/ppermute | solution.py:522
  90.4 2.9 %collective-permute-done.31.outer = f32[4,64,128]{2,1,0:T(8,128)S(1)} collective-permute-done((f32[4,64,128]{2,1,0:T(8,128)S(1)}, f32[4,64,128]{2,1,0:T(8,128)S(1)}, u32[]{:S(2)}, u32[]{:S(2)}) %collective-permute-start.31) | collective-permute-done | bytes 131104 | tf_op jit(solution)/shard_map/ppermute | solution.py:522
  93.4 2.0 %collective-permute-start.33 = (f32[4,64,128]{2,1,0:T(8,128)S(1)}, f32[4,64,128]{2,1,0:T(8,128)S(1)}, u32[]{:S(2)}, u32[]{:S(2)}) collective-permute-start(f32[4,64,128]{2,1,0:T(8,128)S(1)} %wave_halo.30.cur), channel_id=1, source_target_pairs={{0,5},{1,3},{2,7},{3,1},{4,9},{5,0},{6,11},{7,2},{8,13},{9,4},{10,... | collective-permute-start | bytes 393224 | tf_op jit(solution)/shard_map/ppermute | solution.py:522
  95.8 3.1 %collective-permute-done.33.outer = f32[4,64,128]{2,1,0:T(8,128)S(1)} collective-permute-done((f32[4,64,128]{2,1,0:T(8,128)S(1)}, f32[4,64,128]{2,1,0:T(8,128)S(1)}, u32[]{:S(2)}, u32[]{:S(2)}) %collective-permute-start.33) | collective-permute-done | bytes 131104 | tf_op jit(solution)/shard_map/ppermute | solution.py:522
  101.0 1.9 %collective-permute-start.36 = (f32[36,128]{1,0:T(8,128)S(1)}, f32[36,128]{1,0:T(8,128)S(1)}, u32[]{:S(2)}, u32[]{:S(2)}) collective-permute-start(f32[36,128]{1,0:T(8,128)S(1)} %add.25), channel_id=1, source_target_pairs={{0,5},{1,4},{2,7},{3,6},{4,1},{5,0},{6,3},{7,2},{8,13},{9,12},{10,... | collective-permute-start | bytes 55304 | tf_op jit(solution)/shard_map/ppermute | solution.py:526
  104.4 3.1 %collective-permute-start.38 = (f32[36,128]{1,0:T(8,128)S(1)}, f32[36,128]{1,0:T(8,128)S(1)}, u32[]{:S(2)}, u32[]{:S(2)}) collective-permute-start(f32[36,128]{1,0:T(8,128)S(1)} %add.26), channel_id=1, source_target_pairs={{0,9},{1,8},{2,11},{3,10},{4,13},{5,12},{6,15},{7,14},{8,1},{9,0},... | collective-permute-start | bytes 55304 | tf_op jit(solution)/shard_map/ppermute | solution.py:526
  108.9 2.7 %collective-permute-start.39 = (f32[36,128]{1,0:T(8,128)S(1)}, f32[36,128]{1,0:T(8,128)S(1)}, u32[]{:S(2)}, u32[]{:S(2)}) collective-permute-start(f32[36,128]{1,0:T(8,128)S(1)} %add.27.packed), channel_id=1, source_target_pairs={{0,17},{1,16},{2,19},{3,18},{4,21},{5,20},{6,23},{7,22},{8,25},{9,... | collective-permute-start | bytes 55304 | tf_op jit(solution)/shard_map/ppermute | solution.py:526
  113.2 2.3 %copy-done.1 = f32[71,128,128]{2,1,0:T(8,128)S(1)} copy-done((f32[71,128,128]{2,1,0:T(8,128)S(1)}, f32[71,128,128]{2,1,0:T(8,128)}, u32[]{:S(2)}) %copy-start.1) | copy-done | bytes 4653080
  115.5 7.9 %gravity_last.1 = (f32[16,256]{1,0:T(8,128)}, f32[1,128]{1,0:T(1,128)}, f32[8,16,128]{2,1,0:T(8,128)}) custom-call(s32[513]{0:T(1024)S(1)} %pad_add_fusion.head, f32[36,128]{1,0:T(8,128)S(1)} %add.27.packed, f32[36,128]{1,0:T(8,128)S(1)} %collective-permute-done.39.other, f32[4,128]{1,0:T(4,128)S(1)} %get-tuple-element.205.observed, f32[9088,128]{1,0:T(8,128)S(1)} %bitcast.20), custom_call_target="tpu_custom_call" | custom-call | tf_op jit(solution)/shard_map/gravity_last/pallas_call | solution.py:438
  (140 shorter events, 44.8 us)
Async XLA Ops:
  4.0 9.2 %collective-permute-start = (f32[6,64,128]{2,1,0:T(8,128)S(1)}, f32[6,64,128]{2,1,0:T(8,128)S(1)}, u32[]{:S(2)}, u32[]{:S(2)}) collective-permute-start(f32[6,64,128]{2,1,0:T(8,128)S(1)} %get-tuple-element.111), channel_id=1, source_target_pairs={{0,5},{1,3},{2,7},{3,1},{4,9},{5,0},{6,11},{7,2},{8,13},{9,4},{10,... | collective-permute-start | bytes 589832 | tf_op jit(solution)/shard_map/ppermute | solution.py:522
  6.5 6.7 %collective-permute-start.1 = (f32[4,64,128]{2,1,0:T(8,128)S(1)}, f32[4,64,128]{2,1,0:T(8,128)S(1)}, u32[]{:S(2)}, u32[]{:S(2)}) collective-permute-start(f32[4,64,128]{2,1,0:T(8,128)S(1)} %get-tuple-element.106.cur.prev), channel_id=1, source_target_pairs={{0,1},{1,0},{2,3},{3,2},{4,5},{5,4},{6,7},{7,6},{8,9},{9,8},{10,11... | collective-permute-start | bytes 393224 | tf_op jit(solution)/shard_map/ppermute | solution.py:526
  13.7 5.1 %collective-permute-start.2 = (f32[4,64,128]{2,1,0:T(8,128)S(1)}, f32[4,64,128]{2,1,0:T(8,128)S(1)}, u32[]{:S(2)}, u32[]{:S(2)}) collective-permute-start(f32[4,64,128]{2,1,0:T(8,128)S(1)} %wave_halo.16.cur.prev), channel_id=1, source_target_pairs={{0,5},{1,3},{2,7},{3,1},{4,9},{5,0},{6,11},{7,2},{8,13},{9,4},{10,... | collective-permute-start | bytes 393224 | tf_op jit(solution)/shard_map/ppermute | solution.py:522
  15.0 3.9 %collective-permute-start.3 = (f32[4,64,128]{2,1,0:T(8,128)S(1)}, f32[4,64,128]{2,1,0:T(8,128)S(1)}, u32[]{:S(2)}, u32[]{:S(2)}) collective-permute-start(f32[4,64,128]{2,1,0:T(8,128)S(1)} %wave_halo.16.cur.prev), channel_id=1, source_target_pairs={{0,1},{1,0},{2,3},{3,2},{4,5},{5,4},{6,7},{7,6},{8,9},{9,8},{10,11... | collective-permute-start | bytes 393224 | tf_op jit(solution)/shard_map/ppermute | solution.py:526
  18.9 6.0 %collective-permute-start.7 = (f32[6,64,128]{2,1,0:T(8,128)S(1)}, f32[6,64,128]{2,1,0:T(8,128)S(1)}, u32[]{:S(2)}, u32[]{:S(2)}) collective-permute-start(f32[6,64,128]{2,1,0:T(8,128)S(1)} %collective-permute-done.outer), channel_id=1, source_target_pairs={{0,1},{1,0},{2,3},{3,2},{4,5},{5,4},{6,7},{7,6},{8,9},{9,8},{10,11... | collective-permute-start | bytes 589832 | tf_op jit(solution)/shard_map/ppermute | solution.py:526
  19.0 5.9 %collective-permute-start.5 = (f32[4,64,128]{2,1,0:T(8,128)S(1)}, f32[4,64,128]{2,1,0:T(8,128)S(1)}, u32[]{:S(2)}, u32[]{:S(2)}) collective-permute-start(f32[4,64,128]{2,1,0:T(8,128)S(1)} %wave_halo.17.cur.prev), channel_id=1, source_target_pairs={{0,5},{1,3},{2,7},{3,1},{4,9},{5,0},{6,11},{7,2},{8,13},{9,4},{10,... | collective-permute-start | bytes 393224 | tf_op jit(solution)/shard_map/ppermute | solution.py:522
  21.0 3.9 %collective-permute-start.6 = (f32[4,64,128]{2,1,0:T(8,128)S(1)}, f32[4,64,128]{2,1,0:T(8,128)S(1)}, u32[]{:S(2)}, u32[]{:S(2)}) collective-permute-start(f32[4,64,128]{2,1,0:T(8,128)S(1)} %wave_halo.17.cur.prev), channel_id=1, source_target_pairs={{0,1},{1,0},{2,3},{3,2},{4,5},{5,4},{6,7},{7,6},{8,9},{9,8},{10,11... | collective-permute-start | bytes 393224 | tf_op jit(solution)/shard_map/ppermute | solution.py:526
  24.9 3.7 %collective-permute-start.10 = (f32[2,2,128]{2,1,0:T(2,128)S(1)}, f32[2,2,128]{2,1,0:T(2,128)S(1)}, u32[]{:S(2)}, u32[]{:S(2)}) collective-permute-start(f32[2,2,128]{2,1,0:T(2,128)S(1)} %pad_maximum_fusion.1), channel_id=1, source_target_pairs={{0,2},{1,3},{2,0},{3,1},{4,6},{5,7},{6,4},{7,5},{8,10},{9,11},{10,... | collective-permute-start | bytes 6152 | tf_op jit(solution)/shard_map/ppermute | solution.py:526
  26.5 5.5 %collective-permute-start.8 = (f32[4,64,128]{2,1,0:T(8,128)S(1)}, f32[4,64,128]{2,1,0:T(8,128)S(1)}, u32[]{:S(2)}, u32[]{:S(2)}) collective-permute-start(f32[4,64,128]{2,1,0:T(8,128)S(1)} %wave_halo.18.cur.prev), channel_id=1, source_target_pairs={{0,5},{1,3},{2,7},{3,1},{4,9},{5,0},{6,11},{7,2},{8,13},{9,4},{10,... | collective-permute-start | bytes 393224 | tf_op jit(solution)/shard_map/ppermute | solution.py:522
  28.1 3.9 %collective-permute-start.9 = (f32[4,64,128]{2,1,0:T(8,128)S(1)}, f32[4,64,128]{2,1,0:T(8,128)S(1)}, u32[]{:S(2)}, u32[]{:S(2)}) collective-permute-start(f32[4,64,128]{2,1,0:T(8,128)S(1)} %wave_halo.18.cur.prev), channel_id=1, source_target_pairs={{0,1},{1,0},{2,3},{3,2},{4,5},{5,4},{6,7},{7,6},{8,9},{9,8},{10,11... | collective-permute-start | bytes 393224 | tf_op jit(solution)/shard_map/ppermute | solution.py:526
  32.1 5.9 %collective-permute-start.11 = (f32[4,64,128]{2,1,0:T(8,128)S(1)}, f32[4,64,128]{2,1,0:T(8,128)S(1)}, u32[]{:S(2)}, u32[]{:S(2)}) collective-permute-start(f32[4,64,128]{2,1,0:T(8,128)S(1)} %wave_halo.19.cur.prev), channel_id=1, source_target_pairs={{0,5},{1,3},{2,7},{3,1},{4,9},{5,0},{6,11},{7,2},{8,13},{9,4},{10,... | collective-permute-start | bytes 393224 | tf_op jit(solution)/shard_map/ppermute | solution.py:522
  34.1 3.9 %collective-permute-start.12 = (f32[4,64,128]{2,1,0:T(8,128)S(1)}, f32[4,64,128]{2,1,0:T(8,128)S(1)}, u32[]{:S(2)}, u32[]{:S(2)}) collective-permute-start(f32[4,64,128]{2,1,0:T(8,128)S(1)} %wave_halo.19.cur.prev), channel_id=1, source_target_pairs={{0,1},{1,0},{2,3},{3,2},{4,5},{5,4},{6,7},{7,6},{8,9},{9,8},{10,11... | collective-permute-start | bytes 393224 | tf_op jit(solution)/shard_map/ppermute | solution.py:526
  38.0 5.6 %collective-permute-start.13 = (f32[4,64,128]{2,1,0:T(8,128)S(1)}, f32[4,64,128]{2,1,0:T(8,128)S(1)}, u32[]{:S(2)}, u32[]{:S(2)}) collective-permute-start(f32[4,64,128]{2,1,0:T(8,128)S(1)} %wave_halo.20.cur.prev), channel_id=1, source_target_pairs={{0,5},{1,3},{2,7},{3,1},{4,9},{5,0},{6,11},{7,2},{8,13},{9,4},{10,... | collective-permute-start | bytes 393224 | tf_op jit(solution)/shard_map/ppermute | solution.py:522
  40.0 3.6 %collective-permute-start.14 = (f32[4,64,128]{2,1,0:T(8,128)S(1)}, f32[4,64,128]{2,1,0:T(8,128)S(1)}, u32[]{:S(2)}, u32[]{:S(2)}) collective-permute-start(f32[4,64,128]{2,1,0:T(8,128)S(1)} %wave_halo.20.cur.prev), channel_id=1, source_target_pairs={{0,1},{1,0},{2,3},{3,2},{4,5},{5,4},{6,7},{7,6},{8,9},{9,8},{10,11... | collective-permute-start | bytes 393224 | tf_op jit(solution)/shard_map/ppermute | solution.py:526
  43.7 5.5 %collective-permute-start.15 = (f32[4,64,128]{2,1,0:T(8,128)S(1)}, f32[4,64,128]{2,1,0:T(8,128)S(1)}, u32[]{:S(2)}, u32[]{:S(2)}) collective-permute-start(f32[4,64,128]{2,1,0:T(8,128)S(1)} %wave_halo.21.cur.prev), channel_id=1, source_target_pairs={{0,5},{1,3},{2,7},{3,1},{4,9},{5,0},{6,11},{7,2},{8,13},{9,4},{10,... | collective-permute-start | bytes 393224 | tf_op jit(solution)/shard_map/ppermute | solution.py:522
  45.6 3.5 %collective-permute-start.16 = (f32[4,64,128]{2,1,0:T(8,128)S(1)}, f32[4,64,128]{2,1,0:T(8,128)S(1)}, u32[]{:S(2)}, u32[]{:S(2)}) collective-permute-start(f32[4,64,128]{2,1,0:T(8,128)S(1)} %wave_halo.21.cur.prev), channel_id=1, source_target_pairs={{0,1},{1,0},{2,3},{3,2},{4,5},{5,4},{6,7},{7,6},{8,9},{9,8},{10,11... | collective-permute-start | bytes 393224 | tf_op jit(solution)/shard_map/ppermute | solution.py:526
  49.2 5.5 %collective-permute-start.17 = (f32[4,64,128]{2,1,0:T(8,128)S(1)}, f32[4,64,128]{2,1,0:T(8,128)S(1)}, u32[]{:S(2)}, u32[]{:S(2)}) collective-permute-start(f32[4,64,128]{2,1,0:T(8,128)S(1)} %wave_halo.22.cur.prev), channel_id=1, source_target_pairs={{0,5},{1,3},{2,7},{3,1},{4,9},{5,0},{6,11},{7,2},{8,13},{9,4},{10,... | collective-permute-start | bytes 393224 | tf_op jit(solution)/shard_map/ppermute | solution.py:522
  51.2 3.5 %collective-permute-start.18 = (f32[4,64,128]{2,1,0:T(8,128)S(1)}, f32[4,64,128]{2,1,0:T(8,128)S(1)}, u32[]{:S(2)}, u32[]{:S(2)}) collective-permute-start(f32[4,64,128]{2,1,0:T(8,128)S(1)} %wave_halo.22.cur.prev), channel_id=1, source_target_pairs={{0,1},{1,0},{2,3},{3,2},{4,5},{5,4},{6,7},{7,6},{8,9},{9,8},{10,11... | collective-permute-start | bytes 393224 | tf_op jit(solution)/shard_map/ppermute | solution.py:526
  54.7 5.5 %collective-permute-start.19 = (f32[4,64,128]{2,1,0:T(8,128)S(1)}, f32[4,64,128]{2,1,0:T(8,128)S(1)}, u32[]{:S(2)}, u32[]{:S(2)}) collective-permute-start(f32[4,64,128]{2,1,0:T(8,128)S(1)} %wave_halo.23.cur.prev), channel_id=1, source_target_pairs={{0,5},{1,3},{2,7},{3,1},{4,9},{5,0},{6,11},{7,2},{8,13},{9,4},{10,... | collective-permute-start | bytes 393224 | tf_op jit(solution)/shard_map/ppermute | solution.py:522
  60.3 5.5 %collective-permute-start.21 = (f32[4,64,128]{2,1,0:T(8,128)S(1)}, f32[4,64,128]{2,1,0:T(8,128)S(1)}, u32[]{:S(2)}, u32[]{:S(2)}) collective-permute-start(f32[4,64,128]{2,1,0:T(8,128)S(1)} %wave_halo.24.cur.prev), channel_id=1, source_target_pairs={{0,5},{1,3},{2,7},{3,1},{4,9},{5,0},{6,11},{7,2},{8,13},{9,4},{10,... | collective-permute-start | bytes 393224 | tf_op jit(solution)/shard_map/ppermute | solution.py:522
  65.8 5.5 %collective-permute-start.23 = (f32[4,64,128]{2,1,0:T(8,128)S(1)}, f32[4,64,128]{2,1,0:T(8,128)S(1)}, u32[]{:S(2)}, u32[]{:S(2)}) collective-permute-start(f32[4,64,128]{2,1,0:T(8,128)S(1)} %wave_halo.25.cur.prev), channel_id=1, source_target_pairs={{0,5},{1,3},{2,7},{3,1},{4,9},{5,0},{6,11},{7,2},{8,13},{9,4},{10,... | collective-permute-start | bytes 393224 | tf_op jit(solution)/shard_map/ppermute | solution.py:522
  67.8 3.5 %collective-permute-start.24 = (f32[4,64,128]{2,1,0:T(8,128)S(1)}, f32[4,64,128]{2,1,0:T(8,128)S(1)}, u32[]{:S(2)}, u32[]{:S(2)}) collective-permute-start(f32[4,64,128]{2,1,0:T(8,128)S(1)} %wave_halo.25.cur.prev), channel_id=1, source_target_pairs={{0,1},{1,0},{2,3},{3,2},{4,5},{5,4},{6,7},{7,6},{8,9},{9,8},{10,11... | collective-permute-start | bytes 393224 | tf_op jit(solution)/shard_map/ppermute | solution.py:526
  71.3 5.5 %collective-permute-start.25 = (f32[4,64,128]{2,1,0:T(8,128)S(1)}, f32[4,64,128]{2,1,0:T(8,128)S(1)}, u32[]{:S(2)}, u32[]{:S(2)}) collective-permute-start(f32[4,64,128]{2,1,0:T(8,128)S(1)} %wave_halo.26.cur.prev), channel_id=1, source_target_pairs={{0,5},{1,3},{2,7},{3,1},{4,9},{5,0},{6,11},{7,2},{8,13},{9,4},{10,... | collective-permute-start | bytes 393224 | tf_op jit(solution)/shard_map/ppermute | solution.py:522
  73.3 3.5 %collective-permute-start.26 = (f32[4,64,128]{2,1,0:T(8,128)S(1)}, f32[4,64,128]{2,1,0:T(8,128)S(1)}, u32[]{:S(2)}, u32[]{:S(2)}) collective-permute-start(f32[4,64,128]{2,1,0:T(8,128)S(1)} %wave_halo.26.cur.prev), channel_id=1, source_target_pairs={{0,1},{1,0},{2,3},{3,2},{4,5},{5,4},{6,7},{7,6},{8,9},{9,8},{10,11... | collective-permute-start | bytes 393224 | tf_op jit(solution)/shard_map/ppermute | solution.py:526
  76.8 5.5 %collective-permute-start.27 = (f32[4,64,128]{2,1,0:T(8,128)S(1)}, f32[4,64,128]{2,1,0:T(8,128)S(1)}, u32[]{:S(2)}, u32[]{:S(2)}) collective-permute-start(f32[4,64,128]{2,1,0:T(8,128)S(1)} %wave_halo.27.cur.prev), channel_id=1, source_target_pairs={{0,5},{1,3},{2,7},{3,1},{4,9},{5,0},{6,11},{7,2},{8,13},{9,4},{10,... | collective-permute-start | bytes 393224 | tf_op jit(solution)/shard_map/ppermute | solution.py:522
  82.4 5.5 %collective-permute-start.29 = (f32[4,64,128]{2,1,0:T(8,128)S(1)}, f32[4,64,128]{2,1,0:T(8,128)S(1)}, u32[]{:S(2)}, u32[]{:S(2)}) collective-permute-start(f32[4,64,128]{2,1,0:T(8,128)S(1)} %wave_halo.28.cur.prev), channel_id=1, source_target_pairs={{0,5},{1,3},{2,7},{3,1},{4,9},{5,0},{6,11},{7,2},{8,13},{9,4},{10,... | collective-permute-start | bytes 393224 | tf_op jit(solution)/shard_map/ppermute | solution.py:522
  87.9 5.5 %collective-permute-start.31 = (f32[4,64,128]{2,1,0:T(8,128)S(1)}, f32[4,64,128]{2,1,0:T(8,128)S(1)}, u32[]{:S(2)}, u32[]{:S(2)}) collective-permute-start(f32[4,64,128]{2,1,0:T(8,128)S(1)} %wave_halo.29.cur.prev), channel_id=1, source_target_pairs={{0,5},{1,3},{2,7},{3,1},{4,9},{5,0},{6,11},{7,2},{8,13},{9,4},{10,... | collective-permute-start | bytes 393224 | tf_op jit(solution)/shard_map/ppermute | solution.py:522
  89.9 3.5 %collective-permute-start.32 = (f32[4,64,128]{2,1,0:T(8,128)S(1)}, f32[4,64,128]{2,1,0:T(8,128)S(1)}, u32[]{:S(2)}, u32[]{:S(2)}) collective-permute-start(f32[4,64,128]{2,1,0:T(8,128)S(1)} %wave_halo.29.cur.prev), channel_id=1, source_target_pairs={{0,1},{1,0},{2,3},{3,2},{4,5},{5,4},{6,7},{7,6},{8,9},{9,8},{10,11... | collective-permute-start | bytes 393224 | tf_op jit(solution)/shard_map/ppermute | solution.py:526
  93.4 5.5 %collective-permute-start.33 = (f32[4,64,128]{2,1,0:T(8,128)S(1)}, f32[4,64,128]{2,1,0:T(8,128)S(1)}, u32[]{:S(2)}, u32[]{:S(2)}) collective-permute-start(f32[4,64,128]{2,1,0:T(8,128)S(1)} %wave_halo.30.cur), channel_id=1, source_target_pairs={{0,5},{1,3},{2,7},{3,1},{4,9},{5,0},{6,11},{7,2},{8,13},{9,4},{10,... | collective-permute-start | bytes 393224 | tf_op jit(solution)/shard_map/ppermute | solution.py:522
  99.0 3.9 %collective-permute-start.37 = (f32[4,64,128]{2,1,0:T(8,128)S(1)}, f32[4,64,128]{2,1,0:T(8,128)S(1)}, u32[]{:S(2)}, u32[]{:S(2)}) collective-permute-start(f32[4,64,128]{2,1,0:T(8,128)S(1)} %wave_halo.31.cur.own), channel_id=1, source_target_pairs={{0,1},{1,0},{2,3},{3,2},{4,5},{5,4},{6,7},{7,6},{8,9},{9,8},{10,11... | collective-permute-start | bytes 393224 | tf_op jit(solution)/shard_map/ppermute | solution.py:526
  104.4 4.6 %collective-permute-start.38 = (f32[36,128]{1,0:T(8,128)S(1)}, f32[36,128]{1,0:T(8,128)S(1)}, u32[]{:S(2)}, u32[]{:S(2)}) collective-permute-start(f32[36,128]{1,0:T(8,128)S(1)} %add.26), channel_id=1, source_target_pairs={{0,9},{1,8},{2,11},{3,10},{4,13},{5,12},{6,15},{7,14},{8,1},{9,0},... | collective-permute-start | bytes 55304 | tf_op jit(solution)/shard_map/ppermute | solution.py:526
  108.9 4.2 %collective-permute-start.39 = (f32[36,128]{1,0:T(8,128)S(1)}, f32[36,128]{1,0:T(8,128)S(1)}, u32[]{:S(2)}, u32[]{:S(2)}) collective-permute-start(f32[36,128]{1,0:T(8,128)S(1)} %add.27.packed), channel_id=1, source_target_pairs={{0,17},{1,16},{2,19},{3,18},{4,21},{5,20},{6,23},{7,22},{8,25},{9,... | collective-permute-start | bytes 55304 | tf_op jit(solution)/shard_map/ppermute | solution.py:526
  (19 other events, 150.6 us)

commit v4 on v3

--- a/solution.py
+++ b/solution.py
@@ -13,7 +13,7 @@
 AXES = ("mp", "station")
 VMEM = pl.BlockSpec(memory_space=pltpu.VMEM)
 SMEM = pl.BlockSpec(memory_space=pltpu.SMEM)
-ANY = pl.BlockSpec(memory_space=pl.ANY)
+HBM = pl.BlockSpec(memory_space=pltpu.HBM)
 F32 = jnp.float32
 MIB = 1 << 20
 
@@ -36,22 +36,29 @@
 
 def chain_partner(count):
     def partner(m, s):
-        other = m + 1 if s % 2 == 0 else m - 1
+        if s % 2 == 0:
+            return (m ^ 1, s)
+        other = m + 1 if m % 2 else m - 1
         if other < 0 or other >= count:
             return (m, s ^ 2)
-        return (other, s ^ 1)
+        return (other, s)
 
     return partner
 
 
 def position():
-    return lax.axis_index("mp"), lax.axis_index("station") % 2
+    m = lax.axis_index("mp")
+    return m, (m + lax.axis_index("station")) % 2 == 0
 
 
 def divmod_static(value, divisor):
     if divisor & (divisor - 1) == 0:
         return value >> (divisor.bit_length() - 1), value & (divisor - 1)
     return value // divisor, value % divisor
+
+
+def in_place(*values):
+    return [pltpu.with_memory_space_constraint(value, pltpu.HBM) for value in values]
 
 
 def run_copies(pairs, sems):
@@ -62,19 +69,19 @@
         copy.wait()
 
 
-def plane_of(core, j, slab):
-    return jnp.where(core == 0, slab - 1 - j, j)
+def plane_of(upper, j, slab):
+    return jnp.where(upper, slab - 1 - j, j)
 
 
 def first_kernel(now, velocity, density, cur, message, sems):
     slab = now.shape[0]
     half = slab // 2
-    _, core = position()
+    _, upper = position()
     pairs = []
     for j in range(half):
-        plane = plane_of(core, j, slab)
+        plane = plane_of(upper, j, slab)
         pairs += [(now.at[plane], cur.at[j]), (now.at[plane], message.at[j])]
-    edge = plane_of(core, 0, slab)
+    edge = plane_of(upper, 0, slab)
     pairs += [(velocity.at[edge], message.at[half]), (density.at[edge], message.at[half + 1])]
     run_copies(pairs, sems)
 
@@ -85,25 +92,31 @@
     return pl.pallas_call(
         first_kernel,
         out_shape=(shape((half, rows, lanes)), shape((half + 2, rows, lanes))),
-        in_specs=[ANY] * 3,
+        in_specs=[HBM] * 3,
         out_specs=(VMEM, VMEM),
         scratch_shapes=[pltpu.SemaphoreType.DMA((2 * half + 2,))],
         compiler_params=room(2),
         name="first_message",
-    )(p_now, velocity, density)
-
-
-def setup_kernel(count, source, p_prev, velocity, density, prev, cour, cour_outer, mask, dens, vel, raw, sems):
+    )(*in_place(p_now, velocity, density))
+
+
+def setup_kernel(
+    count, source, wavelet, p_prev, velocity, density, prev, cour, cour_outer, mask, dens, pulses, vel, raw, sems
+):
     slab = p_prev.shape[0]
     half, rows, lanes = prev.shape
-    m, core = position()
+    m, upper = position()
     pairs = []
     for j in range(half):
-        plane = plane_of(core, j, slab)
+        plane = plane_of(upper, j, slab)
         pairs += [(p_prev.at[plane], prev.at[j]), (velocity.at[plane], vel.at[j])]
-    pairs += [(density.at[pl.ds(core * half, half)], raw)]
+    low = half * (lax.axis_index("station") % 2)
+    pairs += [(density.at[pl.ds(low, half)], raw)]
     run_copies(pairs, sems)
-    outer_ok = jnp.where(jnp.where(core == 0, m < count - 1, m > 0), 1.0, 0.0)
+    for n in range(pulses.shape[0]):
+        pulses[n : n + 1, :] = jnp.full((1, lanes), wavelet[n], F32)
+    outer_ok = jnp.where(upper, m < count - 1, m > 0)
+    outer_ok = jnp.where(outer_ok, 1.0, 0.0)
     column, source_lane = divmod_static(source[0], lanes)
     source_x, source_row = divmod_static(column, rows)
     row = lax.broadcasted_iota(jnp.int32, (rows, lanes), 0)
@@ -114,28 +127,28 @@
         square = scaled * scaled
         cour[j] = square
         cour_outer[j] = square * outer_ok
-        here = m * slab + plane_of(core, j, slab) == source_x
+        here = m * slab + plane_of(upper, j, slab) == source_x
         mask[j] = spot * jnp.where(here, 1.0, 0.0)
         dens[j] = raw[j].astype(jnp.bfloat16).astype(F32)
 
 
-def setup(count, source_cell, p_prev, velocity, density):
+def setup(count, source_cell, wavelet, p_prev, velocity, density):
     slab, rows, lanes = p_prev.shape
     half = slab // 2
     part = shape((half, rows, lanes))
     held = pltpu.VMEM((half, rows, lanes), F32)
     return pl.pallas_call(
         functools.partial(setup_kernel, count),
-        out_shape=(part,) * 5,
-        in_specs=[SMEM] + [ANY] * 3,
-        out_specs=(VMEM,) * 5,
+        out_shape=(part,) * 5 + (shape((wavelet.shape[0], lanes)),),
+        in_specs=[SMEM, SMEM] + [HBM] * 3,
+        out_specs=(VMEM,) * 6,
         scratch_shapes=[held, held, pltpu.SemaphoreType.DMA((2 * half + 1,))],
         compiler_params=room(4),
         cost_estimate=pl.CostEstimate(
             flops=20 * half * rows * lanes, bytes_accessed=32 * half * rows * lanes, transcendentals=0
         ),
         name="setup",
-    )(source_cell, p_prev, velocity, density)
+    )(source_cell, wavelet, *in_place(p_prev, velocity, density))
 
 
 def local_kernel(step, pulses, mask, cur, prev, cour, surf_in, base, surf, pad):
@@ -212,7 +225,8 @@
     )(base, cour, cour_outer, outer, inner)
 
 
-def trace_kernel(step, place, cur, surf, predicted, out):
+def trace_kernel(step, place, cur, surf, predicted, kept, out):
+    del kept
     planes, rows, lanes = cur.shape
     receivers = place.shape[0]
     steps = step + 1
@@ -238,41 +252,44 @@
     out[steps * (receivers // 128) :, :] = predicted[...]
 
 
-def recorded_traces(step, place, cur, surf, predicted):
+def recorded_traces(step, place, cur, surf, predicted, kept):
     rows = (step + 1) * (place.shape[0] // 128) + predicted.shape[0]
     return pl.pallas_call(
         functools.partial(trace_kernel, step),
         out_shape=shape((rows, 128)),
-        in_specs=[VMEM] * 4,
+        in_specs=[VMEM] * 5,
         out_specs=VMEM,
         compiler_params=room(4),
         name="traces",
-    )(place, cur, surf, predicted)
-
-
-def join_kernel(own, sibling, out, sems):
+    )(place, cur, surf, predicted, kept)
+
+
+def join_kernel(own, sibling, kept, out, sems):
+    del kept
     slab = out.shape[0]
-    _, core = position()
+    _, upper = position()
     pairs = []
     for j in range(slab // 2):
-        pairs += [
-            (own.at[j], out.at[plane_of(core, j, slab)]),
-            (sibling.at[j], out.at[plane_of(1 - core, j, slab)]),
-        ]
+        here = plane_of(upper, j, slab)
+        pairs += [(own.at[j], out.at[here]), (sibling.at[j], out.at[slab - 1 - here])]
     run_copies(pairs, sems)
 
 
-def join(own, sibling):
+def join(own, sibling, kept):
     half, rows, lanes = own.shape
     return pl.pallas_call(
         join_kernel,
         out_shape=shape((2 * half, rows, lanes)),
-        in_specs=[VMEM, VMEM],
-        out_specs=ANY,
+        in_specs=[VMEM] * 3,
+        out_specs=HBM,
         scratch_shapes=[pltpu.SemaphoreType.DMA((2 * half,))],
         compiler_params=room(2),
         name="join",
-    )(own, sibling)
+    )(own, sibling, kept)
+
+
+def on_chip(value):
+    return pltpu.with_memory_space_constraint(value, pltpu.VMEM)
 
 
 def table_low(total_x, slab, offset):
@@ -280,8 +297,8 @@
     return m * slab - (total_x - 1) + offset
 
 
-def table_kernel(total_x, slab, head, out):
-    spread, lanes = out.shape[1:]
+def table_kernel(total_x, slab, spread, head, out):
+    lanes = out.shape[1]
     low = table_low(total_x, slab, head[0])
     dy = (lax.broadcasted_iota(jnp.int32, (spread, lanes), 0) - (spread // 2 - 1)).astype(F32)
     dz = (lax.broadcasted_iota(jnp.int32, (spread, lanes), 1) + 1).astype(F32)
@@ -292,17 +309,18 @@
         dx = (t + low).astype(F32)
         square = dx * dx + side + deep
         value = dz / (square * jnp.sqrt(square))
-        out[t] = value.astype(jnp.bfloat16).astype(F32)
+        start = pl.multiple_of(t * spread, spread)
+        out[pl.ds(start, spread), :] = value.astype(jnp.bfloat16).astype(F32)
         return carry
 
-    lax.fori_loop(0, out.shape[0], one, 0)
+    lax.fori_loop(0, out.shape[0] // spread, one, 0)
 
 
 def gravity_table(total_x, slab, depth, lateral, vertical, head):
     size = depth * 2 * lateral * vertical
     return pl.pallas_call(
-        functools.partial(table_kernel, total_x, slab),
-        out_shape=shape((depth, 2 * lateral, vertical)),
+        functools.partial(table_kernel, total_x, slab, 2 * lateral),
+        out_shape=shape((depth * 2 * lateral, vertical)),
         in_specs=[SMEM],
         out_specs=VMEM,
         cost_estimate=pl.CostEstimate(
@@ -317,7 +335,7 @@
     planes, rows, lanes = dens.shape
     count = out.shape[0]
     spread = 2 * lateral
-    m, core = position()
+    core = lax.axis_index("station") % 2
     lead = total_x - 1 - head[0]
     if guard:
         out[...] = jnp.zeros_like(out)
@@ -344,7 +362,6 @@
 
 
 def gravity_forward(first, count, guard, total_x, slab, lateral, head, table, dens):
-    flat = table.reshape(-1, table.shape[2])
     work = count * dens.size
     return pl.pallas_call(
         functools.partial(forward_kernel, first, guard, total_x, slab, lateral),
@@ -356,18 +373,19 @@
         ),
         compiler_params=room(8),
         name="gravity_forward",
-    )(head, flat, dens)
+    )(head, on_chip(table), dens)
 
 
 def spread_back(guard, total_x, lateral, row_low, head, weights, table, out):
     slab, rows, lanes = out.shape
+    groups = (head.shape[0] - 1) // 128
     spread = 2 * lateral
     lead = total_x - 1 - head[0]
 
-    def one(s, acc):
-        sx, sy = divmod_static(head[1 + s], lateral)
+    def one(k, i, acc):
+        sx, sy = divmod_static(head[1 + 128 * k + i], lateral)
         shift = lead - sx
-        weight = weights(s)
+        weight = weights(k, i)
         if guard:
             keep = (shift >= 0) & (shift < guard)
             shift = jnp.where(keep, shift, 0)
@@ -378,26 +396,27 @@
         )
 
     zero = jnp.zeros((rows, lanes), F32)
-    acc = lax.fori_loop(0, head.shape[0] - 1, one, (zero,) * slab, unroll=4)
+    acc = (zero,) * slab
+    for k in range(groups):
+        acc = lax.fori_loop(0, 128, functools.partial(one, k), acc, unroll=4)
     for x in range(slab):
         out[x] = acc[x]
 
 
 def adjoint_kernel(guard, total_x, lateral, head, weights, table, out):
     row_low = lax.axis_index("station") * out.shape[1]
-    spread_back(guard, total_x, lateral, row_low, head, lambda s: weights[s], table, out)
+    spread_back(guard, total_x, lateral, row_low, head, lambda k, i: weights[128 * k + i], table, out)
 
 
 def gravity_adjoint(guard, total_x, slab, rows, lateral, head, weights, table):
-    flat = table.reshape(-1, table.shape[2])
     return pl.pallas_call(
         functools.partial(adjoint_kernel, guard, total_x, lateral),
-        out_shape=shape((slab, rows, table.shape[2])),
+        out_shape=shape((slab, rows, table.shape[1])),
         in_specs=[SMEM, SMEM, VMEM],
         out_specs=VMEM,
         compiler_params=room(8),
         name="gravity_adjoint",
-    )(head, weights, flat)
+    )(head, weights, table)
 
 
 def last_kernel(total_x, lateral, head, packed, other, observed, table, traces, own, out, held, scalars, sem):
@@ -425,14 +444,13 @@
         lateral,
         s * out.shape[1],
         head,
-        lambda i: scalars[i // 128, i % 128],
+        lambda k, i: scalars[k, i],
         table,
         out,
     )
 
 
 def gravity_last(steps, receivers, total_x, slab, rows, lateral, head, packed, other, observed, table):
-    flat = table.reshape(-1, table.shape[2])
     count = lax.axis_size("station")
     lines = observed.shape[0]
     return pl.pallas_call(
@@ -440,7 +458,7 @@
         out_shape=(
             shape((steps, receivers)),
             shape((lines // count, 128)),
-            shape((slab, rows, table.shape[2])),
+            shape((slab, rows, table.shape[1])),
         ),
         in_specs=[SMEM] + [VMEM] * 4,
         out_specs=(VMEM,) * 3,
@@ -451,7 +469,7 @@
         ],
         compiler_params=room(8),
         name="gravity_last",
-    )(head, packed, other, observed, flat)
+    )(head, packed, other, observed, on_chip(table))
 
 
 def cross_kernel(count, velocity, density, outer, inner, out):
@@ -459,8 +477,7 @@
     half = slab // 2
     lane = lax.broadcasted_iota(jnp.int32, (rows, lanes), 1)
     row = lax.broadcasted_iota(jnp.int32, (rows, lanes), 0)
-    m, core = position()
-    flipped = core == 0
+    m, flipped = position()
     left_ok = jnp.where(m > 0, 0.5, 0.0)
     right_ok = jnp.where(m < count - 1, 0.5, 0.0)
 
@@ -512,7 +529,7 @@
     half = slab // 2
     assert half == REACH and count % 2 == 0 and stations % 4 == 0
     total_x = slab * count
-    m, core = position()
+    m, upper = position()
     s = lax.axis_index("station")
     block = lateral // stations
     chain = pairs_of(count, stations, chain_partner(count))
@@ -529,12 +546,13 @@
     outer = across(message)
     inner = swap(cur, 0, 1)
     edges = outer
-    prev, cour, cour_outer, mask, dens = setup(count, source_cell, p_prev, velocity, density)
-    pulses = jnp.broadcast_to(wavelet[:, None], (steps, 128))
+    prev, cour, cour_outer, mask, dens, pulses = setup(
+        count, source_cell, wavelet, p_prev, velocity, density
+    )
 
     receiver_x, receiver_y = divmod_static(receiver_cells, lateral)
     receiver_j = receiver_x - m * slab
-    receiver_j = jnp.where(core == 0, slab - 1 - receiver_j, receiver_j)
+    receiver_j = jnp.where(upper, slab - 1 - receiver_j, receiver_j)
     inside = (receiver_j >= 0) & (receiver_j < half)
     place = jnp.where(inside, receiver_j * lateral + receiver_y, -1)[:, None]
 
@@ -550,11 +568,14 @@
     def table_of(head):
         return gravity_table(total_x, slab, span, lateral, vertical, head)
 
-    state = {"known": jnp.stack([station_cells.astype(F32), observed])[:, None, :]}
+    state = {}
 
     def exchange(bit):
         def work(gate):
-            known = gate(state["known"])
+            if bit == 1:
+                known = jnp.stack([gate(station_cells).astype(F32), observed])[:, None, :]
+            else:
+                known = gate(state["known"])
             other = swap(known, 0, bit)
             upper = (s // bit) % 2 == 1
             state["known"] = jnp.concatenate(
@@ -597,7 +618,7 @@
 
     jobs = [exchange(1 << b) for b in range(stations.bit_length() - 1)]
     jobs.insert(1, share_edges)
-    jobs.append(cross)
+    jobs += [cross, None]
     if chunks == 1:
         jobs += [build_table] + [forward(i) for i in range(pieces)] + [gather_sums]
 
@@ -622,7 +643,7 @@
         cur, prev = halo_step(base, cour, cour_outer, outer, inner), cur
         if done is not None:
             cur, state[done] = together((cur, state[done]))
-    assert not jobs
+    assert not any(jobs)
 
     all_observed = state["known"][1].reshape(-1, 128)
     cells = state["known"][0].reshape(-1).astype(jnp.int32)
@@ -639,8 +660,9 @@
         sums = lax.fori_loop(0, chunks, add_chunk, jnp.zeros((n_stations, vertical), F32))
         predicted = jnp.sum(sums, axis=1).reshape(-1, 128)
 
+    kept = state["table"] if chunks == 1 else predicted
     sibling = swap(cur, 0, 1)
-    packed = recorded_traces(steps - 1, place, cur, surf, predicted)
+    packed = recorded_traces(steps - 1, place, cur, surf, predicted, kept)
     other = swap(packed, 0, 1)
     if count & (count - 1) == 0:
         bit = 1
@@ -648,11 +670,11 @@
             packed = packed + other
             other = swap(packed, bit, 1)
             if bit == 1:
-                wavefield = join(cur, sibling)
+                wavefield = join(cur, sibling, kept)
                 other, wavefield = together((other, wavefield))
             bit *= 2
     else:
-        wavefield = join(cur, sibling)
+        wavefield = join(cur, sibling, kept)
         packed = lax.psum(packed + other, "mp")
         other = jnp.zeros_like(packed)
 

time: 124 us -> 115 us (0.927)
  local copies, waits for them, and re-layouts: 8.91 us -> 3.16 us
  waiting for transfers between devices: 36 us -> 30.6 us
  starting transfers between devices: 41.7 us -> 45.2 us
    ppermute x16, waiting for transfers between devices: 31.3 us -> 26.1 us  [across(): return lax.ppermute(value, AXES, chain)]
    unnamed x29 -> x21, local copies, waits for them, and re-layouts: 8.05 us -> 3.02 us
    ppermute x16, starting transfers between devices: 31 us -> 35.5 us  [across(): return lax.ppermute(value, AXES, chain)]
    pallas_call x1, Pallas kernels: 7.92 us -> 5.31 us  [gravity_last(): pl.pallas_call(functools.partial(last_kernel, total_x, lateral), out_shap...]
  transfers between devices with their start and end apart: 40 -> 40, of which waited for: 19 -> 19; matrix products, arithmetic and copies ran while one was open for 2% -> 0% of each run, Pallas kernels for 20% -> 22%
where the time goes in v4:
time: 115 us
  starting transfers between devices  45.2 us (39%)
  Pallas kernels  32.4 us (28%)
  waiting for transfers between devices  30.6 us (27%)
  local copies, waits for them, and re-layouts  3.16 us (3%)
  between operations  1.78 us (2%)
  other arithmetic  1.6 us (1%)
    ppermute x16, starting transfers between devices, across(): return lax.ppermute(value, AXES, chain)  35.5 us
    ppermute x16, waiting for transfers between devices, across(): return lax.ppermute(value, AXES, chain)  26.1 us
    pallas_call x8, Pallas kernels, gravity_forward(): pl.pallas_call(functools.partial(forward_kernel, first, guard, total_x, s...  12 us
    ppermute x24, starting transfers between devices, swap(): return lax.ppermute(value, AXES, pairs)  9.75 us
    pallas_call x16, Pallas kernels, local_step(): pl.pallas_call(functools.partial(local_kernel, step), out_shape=(shape(cu...  6.12 us
    pallas_call x1, Pallas kernels, gravity_last(): pl.pallas_call(functools.partial(last_kernel, total_x, lateral), out_shap...  5.31 us
    ppermute x24, waiting for transfers between devices, swap(): return lax.ppermute(value, AXES, pairs)  4.57 us
    unnamed x21, local copies, waits for them, and re-layouts  3.02 us
  transfers between devices with their start and end apart: 40, of which 19 were waited for; matrix products, arithmetic and copies ran while one was open for 0% of the time, Pallas kernels for 22%

profile of v4, /device:TPU:0, one launch (start us, length us, event | category | flops | bytes accessed | tf_op | source)
XLA Modules:
  0.0 114.8 jit_solution(16545520982246120002)
XLA Ops:
  1.7 3.0 %collective-permute-start = (f32[6,64,128]{2,1,0:T(8,128)S(1)}, f32[6,64,128]{2,1,0:T(8,128)S(1)}, u32[]{:S(2)}, u32[]{:S(2)}) collective-permute-start(f32[6,64,128]{2,1,0:T(8,128)S(1)} %get-tuple-element.113), channel_id=1, source_target_pairs={{0,4},{1,3},{2,6},{3,1},{4,0},{5,9},{6,2},{7,11},{8,12},{9,5},{10,... | collective-permute-start | bytes 589832 | tf_op jit(solution)/shard_map/ppermute | solution.py:539
  6.1 1.7 %setup.1 = (f32[4,64,128]{2,1,0:T(8,128)S(1)}, f32[4,64,128]{2,1,0:T(8,128)S(1)}, f32[4,64,128]{2,1,0:T(8,128)S(1)}, f32[4,64,128]{2,1,0:T(8,128)S(1)}, f32[4,64...) custom-call(s32[1]{0:T(128)S(6)} %copy.22.source, f32[16]{0:T(128)S(1)} %copy-done.5, f32[8,64,128]{2,1,0:T(8,128)} %p_prev.1, ...), custom_call_target="tpu_custom_call" | custom-call | flops 655360 | bytes 1048576 | tf_op jit(solution)/shard_map/setup/pallas_call | solution.py:140
  8.2 1.6 %collective-permute-done.outer = f32[6,64,128]{2,1,0:T(8,128)S(1)} collective-permute-done((f32[6,64,128]{2,1,0:T(8,128)S(1)}, f32[6,64,128]{2,1,0:T(8,128)S(1)}, u32[]{:S(2)}, u32[]{:S(2)}) %collective-permute-start) | collective-permute-done | bytes 196640 | tf_op jit(solution)/shard_map/ppermute | solution.py:539
  11.2 2.5 %collective-permute-start.2 = (f32[4,64,128]{2,1,0:T(8,128)S(1)}, f32[4,64,128]{2,1,0:T(8,128)S(1)}, u32[]{:S(2)}, u32[]{:S(2)}) collective-permute-start(f32[4,64,128]{2,1,0:T(8,128)S(1)} %wave_halo.16.cur.prev), channel_id=1, source_target_pairs={{0,4},{1,3},{2,6},{3,1},{4,0},{5,9},{6,2},{7,11},{8,12},{9,5},{10,... | collective-permute-start | bytes 393224 | tf_op jit(solution)/shard_map/ppermute | solution.py:539
  14.2 3.4 %collective-permute-done.2.outer = f32[4,64,128]{2,1,0:T(8,128)S(1)} collective-permute-done((f32[4,64,128]{2,1,0:T(8,128)S(1)}, f32[4,64,128]{2,1,0:T(8,128)S(1)}, u32[]{:S(2)}, u32[]{:S(2)}) %collective-permute-start.2) | collective-permute-done | bytes 131104 | tf_op jit(solution)/shard_map/ppermute | solution.py:539
  17.8 2.5 %collective-permute-start.5 = (f32[4,64,128]{2,1,0:T(8,128)S(1)}, f32[4,64,128]{2,1,0:T(8,128)S(1)}, u32[]{:S(2)}, u32[]{:S(2)}) collective-permute-start(f32[4,64,128]{2,1,0:T(8,128)S(1)} %wave_halo.17.cur.prev), channel_id=1, source_target_pairs={{0,4},{1,3},{2,6},{3,1},{4,0},{5,9},{6,2},{7,11},{8,12},{9,5},{10,... | collective-permute-start | bytes 393224 | tf_op jit(solution)/shard_map/ppermute | solution.py:539
  20.8 3.5 %collective-permute-done.5.outer = f32[4,64,128]{2,1,0:T(8,128)S(1)} collective-permute-done((f32[4,64,128]{2,1,0:T(8,128)S(1)}, f32[4,64,128]{2,1,0:T(8,128)S(1)}, u32[]{:S(2)}, u32[]{:S(2)}) %collective-permute-start.5) | collective-permute-done | bytes 131104 | tf_op jit(solution)/shard_map/ppermute | solution.py:539
  24.3 1.6 %collective-permute-start.10 = (f32[2,2,128]{2,1,0:T(2,128)S(1)}, f32[2,2,128]{2,1,0:T(2,128)S(1)}, u32[]{:S(2)}, u32[]{:S(2)}) collective-permute-start(f32[2,2,128]{2,1,0:T(2,128)S(1)} %pad_maximum_fusion.1), channel_id=1, source_target_pairs={{0,2},{1,3},{2,0},{3,1},{4,6},{5,7},{6,4},{7,5},{8,10},{9,11},{10,... | collective-permute-start | bytes 6152 | tf_op jit(solution)/shard_map/ppermute | solution.py:543
  25.9 2.5 %collective-permute-start.8 = (f32[4,64,128]{2,1,0:T(8,128)S(1)}, f32[4,64,128]{2,1,0:T(8,128)S(1)}, u32[]{:S(2)}, u32[]{:S(2)}) collective-permute-start(f32[4,64,128]{2,1,0:T(8,128)S(1)} %wave_halo.18.cur.prev), channel_id=1, source_target_pairs={{0,4},{1,3},{2,6},{3,1},{4,0},{5,9},{6,2},{7,11},{8,12},{9,5},{10,... | collective-permute-start | bytes 393224 | tf_op jit(solution)/shard_map/ppermute | solution.py:539
  28.8 2.5 %collective-permute-done.8.outer = f32[4,64,128]{2,1,0:T(8,128)S(1)} collective-permute-done((f32[4,64,128]{2,1,0:T(8,128)S(1)}, f32[4,64,128]{2,1,0:T(8,128)S(1)}, u32[]{:S(2)}, u32[]{:S(2)}) %collective-permute-start.8) | collective-permute-done | bytes 131104 | tf_op jit(solution)/shard_map/ppermute | solution.py:539
  31.4 2.1 %collective-permute-start.11 = (f32[4,64,128]{2,1,0:T(8,128)S(1)}, f32[4,64,128]{2,1,0:T(8,128)S(1)}, u32[]{:S(2)}, u32[]{:S(2)}) collective-permute-start(f32[4,64,128]{2,1,0:T(8,128)S(1)} %wave_halo.19.cur.prev), channel_id=1, source_target_pairs={{0,4},{1,3},{2,6},{3,1},{4,0},{5,9},{6,2},{7,11},{8,12},{9,5},{10,... | collective-permute-start | bytes 393224 | tf_op jit(solution)/shard_map/ppermute | solution.py:539
  36.5 2.1 %collective-permute-start.13 = (f32[4,64,128]{2,1,0:T(8,128)S(1)}, f32[4,64,128]{2,1,0:T(8,128)S(1)}, u32[]{:S(2)}, u32[]{:S(2)}) collective-permute-start(f32[4,64,128]{2,1,0:T(8,128)S(1)} %wave_halo.20.cur.prev), channel_id=1, source_target_pairs={{0,4},{1,3},{2,6},{3,1},{4,0},{5,9},{6,2},{7,11},{8,12},{9,5},{10,... | collective-permute-start | bytes 393224 | tf_op jit(solution)/shard_map/ppermute | solution.py:539
  39.0 2.6 %collective-permute-done.13.outer = f32[4,64,128]{2,1,0:T(8,128)S(1)} collective-permute-done((f32[4,64,128]{2,1,0:T(8,128)S(1)}, f32[4,64,128]{2,1,0:T(8,128)S(1)}, u32[]{:S(2)}, u32[]{:S(2)}) %collective-permute-start.13) | collective-permute-done | bytes 131104 | tf_op jit(solution)/shard_map/ppermute | solution.py:539
  41.6 2.1 %collective-permute-start.15 = (f32[4,64,128]{2,1,0:T(8,128)S(1)}, f32[4,64,128]{2,1,0:T(8,128)S(1)}, u32[]{:S(2)}, u32[]{:S(2)}) collective-permute-start(f32[4,64,128]{2,1,0:T(8,128)S(1)} %wave_halo.21.cur.prev), channel_id=1, source_target_pairs={{0,4},{1,3},{2,6},{3,1},{4,0},{5,9},{6,2},{7,11},{8,12},{9,5},{10,... | collective-permute-start | bytes 393224 | tf_op jit(solution)/shard_map/ppermute | solution.py:539
  44.2 2.8 %gravity_table.1.table.kept = f32[9088,128]{1,0:T(8,128)S(1)} custom-call(s32[1]{0:T(128)} %constant.67.clone.1.head), custom_call_target="tpu_custom_call" | custom-call | flops 23265280 | bytes 4653056 | tf_op jit(solution)/shard_map/gravity_table/pallas_call | solution.py:321
  47.1 1.7 %collective-permute-start.17 = (f32[4,64,128]{2,1,0:T(8,128)S(1)}, f32[4,64,128]{2,1,0:T(8,128)S(1)}, u32[]{:S(2)}, u32[]{:S(2)}) collective-permute-start(f32[4,64,128]{2,1,0:T(8,128)S(1)} %wave_halo.22.cur.prev), channel_id=1, source_target_pairs={{0,4},{1,3},{2,6},{3,1},{4,0},{5,9},{6,2},{7,11},{8,12},{9,5},{10,... | collective-permute-start | bytes 393224 | tf_op jit(solution)/shard_map/ppermute | solution.py:539
  49.2 1.5 %gravity_forward.8 = f32[64,128]{1,0:T(8,128)S(1)} custom-call(s32[513]{0:T(1024)S(1)} %pad_add_fusion.head, f32[9088,128]{1,0:T(8,128)S(1)} %gravity_table.1.table.kept, f32[4,64,128]{2,1,0:T(8,128)S(1)} %get-tuple-element.149.dens), custom_call_target="tpu_custom_call" | custom-call | flops 8388608 | bytes 131072 | tf_op jit(solution)/shard_map/gravity_forward/pallas_call | solution.py:366
  52.2 2.3 %collective-permute-start.19 = (f32[4,64,128]{2,1,0:T(8,128)S(1)}, f32[4,64,128]{2,1,0:T(8,128)S(1)}, u32[]{:S(2)}, u32[]{:S(2)}) collective-permute-start(f32[4,64,128]{2,1,0:T(8,128)S(1)} %wave_halo.23.cur.prev), channel_id=1, source_target_pairs={{0,4},{1,3},{2,6},{3,1},{4,0},{5,9},{6,2},{7,11},{8,12},{9,5},{10,... | collective-permute-start | bytes 393224 | tf_op jit(solution)/shard_map/ppermute | solution.py:539
  57.5 2.1 %collective-permute-start.21 = (f32[4,64,128]{2,1,0:T(8,128)S(1)}, f32[4,64,128]{2,1,0:T(8,128)S(1)}, u32[]{:S(2)}, u32[]{:S(2)}) collective-permute-start(f32[4,64,128]{2,1,0:T(8,128)S(1)} %wave_halo.24.cur.prev), channel_id=1, source_target_pairs={{0,4},{1,3},{2,6},{3,1},{4,0},{5,9},{6,2},{7,11},{8,12},{9,5},{10,... | collective-permute-start | bytes 393224 | tf_op jit(solution)/shard_map/ppermute | solution.py:539
  62.6 2.1 %collective-permute-start.23 = (f32[4,64,128]{2,1,0:T(8,128)S(1)}, f32[4,64,128]{2,1,0:T(8,128)S(1)}, u32[]{:S(2)}, u32[]{:S(2)}) collective-permute-start(f32[4,64,128]{2,1,0:T(8,128)S(1)} %wave_halo.25.cur.prev), channel_id=1, source_target_pairs={{0,4},{1,3},{2,6},{3,1},{4,0},{5,9},{6,2},{7,11},{8,12},{9,5},{10,... | collective-permute-start | bytes 393224 | tf_op jit(solution)/shard_map/ppermute | solution.py:539
  67.7 2.1 %collective-permute-start.25 = (f32[4,64,128]{2,1,0:T(8,128)S(1)}, f32[4,64,128]{2,1,0:T(8,128)S(1)}, u32[]{:S(2)}, u32[]{:S(2)}) collective-permute-start(f32[4,64,128]{2,1,0:T(8,128)S(1)} %wave_halo.26.cur.prev), channel_id=1, source_target_pairs={{0,4},{1,3},{2,6},{3,1},{4,0},{5,9},{6,2},{7,11},{8,12},{9,5},{10,... | collective-permute-start | bytes 393224 | tf_op jit(solution)/shard_map/ppermute | solution.py:539
  72.8 2.1 %collective-permute-start.27 = (f32[4,64,128]{2,1,0:T(8,128)S(1)}, f32[4,64,128]{2,1,0:T(8,128)S(1)}, u32[]{:S(2)}, u32[]{:S(2)}) collective-permute-start(f32[4,64,128]{2,1,0:T(8,128)S(1)} %wave_halo.27.cur.prev), channel_id=1, source_target_pairs={{0,4},{1,3},{2,6},{3,1},{4,0},{5,9},{6,2},{7,11},{8,12},{9,5},{10,... | collective-permute-start | bytes 393224 | tf_op jit(solution)/shard_map/ppermute | solution.py:539
  77.9 2.1 %collective-permute-start.29 = (f32[4,64,128]{2,1,0:T(8,128)S(1)}, f32[4,64,128]{2,1,0:T(8,128)S(1)}, u32[]{:S(2)}, u32[]{:S(2)}) collective-permute-start(f32[4,64,128]{2,1,0:T(8,128)S(1)} %wave_halo.28.cur.prev), channel_id=1, source_target_pairs={{0,4},{1,3},{2,6},{3,1},{4,0},{5,9},{6,2},{7,11},{8,12},{9,5},{10,... | collective-permute-start | bytes 393224 | tf_op jit(solution)/shard_map/ppermute | solution.py:539
  83.0 2.1 %collective-permute-start.31 = (f32[4,64,128]{2,1,0:T(8,128)S(1)}, f32[4,64,128]{2,1,0:T(8,128)S(1)}, u32[]{:S(2)}, u32[]{:S(2)}) collective-permute-start(f32[4,64,128]{2,1,0:T(8,128)S(1)} %wave_halo.29.cur.prev), channel_id=1, source_target_pairs={{0,4},{1,3},{2,6},{3,1},{4,0},{5,9},{6,2},{7,11},{8,12},{9,5},{10,... | collective-permute-start | bytes 393224 | tf_op jit(solution)/shard_map/ppermute | solution.py:539
  85.5 1.5 %gravity_forward.15 = f32[64,128]{1,0:T(8,128)S(1)} custom-call(s32[513]{0:T(1024)S(1)} %pad_add_fusion.head, f32[9088,128]{1,0:T(8,128)S(1)} %gravity_table.1.table.kept, f32[4,64,128]{2,1,0:T(8,128)S(1)} %get-tuple-element.149.dens), custom_call_target="tpu_custom_call" | custom-call | flops 8388608 | bytes 131072 | tf_op jit(solution)/shard_map/gravity_forward/pallas_call | solution.py:366
  88.1 2.1 %collective-permute-start.33 = (f32[4,64,128]{2,1,0:T(8,128)S(1)}, f32[4,64,128]{2,1,0:T(8,128)S(1)}, u32[]{:S(2)}, u32[]{:S(2)}) collective-permute-start(f32[4,64,128]{2,1,0:T(8,128)S(1)} %wave_halo.30.cur), channel_id=1, source_target_pairs={{0,4},{1,3},{2,6},{3,1},{4,0},{5,9},{6,2},{7,11},{8,12},{9,5},{10,... | collective-permute-start | bytes 393224 | tf_op jit(solution)/shard_map/ppermute | solution.py:539
  90.8 2.4 %collective-permute-done.33.outer = f32[4,64,128]{2,1,0:T(8,128)S(1)} collective-permute-done((f32[4,64,128]{2,1,0:T(8,128)S(1)}, f32[4,64,128]{2,1,0:T(8,128)S(1)}, u32[]{:S(2)}, u32[]{:S(2)}) %collective-permute-start.33) | collective-permute-done | bytes 131104 | tf_op jit(solution)/shard_map/ppermute | solution.py:539
  93.5 2.3 %copy-done.1 = f32[9088,128]{1,0:T(8,128)S(1)} copy-done((f32[9088,128]{1,0:T(8,128)S(1)}, f32[9088,128]{1,0:T(8,128)}, u32[]{:S(2)}) %copy-start.1) | copy-done | bytes 4653080
  97.6 2.0 %collective-permute-start.36 = (f32[36,128]{1,0:T(8,128)S(1)}, f32[36,128]{1,0:T(8,128)S(1)}, u32[]{:S(2)}, u32[]{:S(2)}) collective-permute-start(f32[36,128]{1,0:T(8,128)S(1)} %add.32), channel_id=1, source_target_pairs={{0,5},{1,4},{2,7},{3,6},{4,1},{5,0},{6,3},{7,2},{8,13},{9,12},{10,... | collective-permute-start | bytes 55304 | tf_op jit(solution)/shard_map/ppermute | solution.py:543
  101.0 2.8 %collective-permute-start.38 = (f32[36,128]{1,0:T(8,128)S(1)}, f32[36,128]{1,0:T(8,128)S(1)}, u32[]{:S(2)}, u32[]{:S(2)}) collective-permute-start(f32[36,128]{1,0:T(8,128)S(1)} %add.33), channel_id=1, source_target_pairs={{0,9},{1,8},{2,11},{3,10},{4,13},{5,12},{6,15},{7,14},{8,1},{9,0},... | collective-permute-start | bytes 55304 | tf_op jit(solution)/shard_map/ppermute | solution.py:543
  105.3 2.7 %collective-permute-start.39 = (f32[36,128]{1,0:T(8,128)S(1)}, f32[36,128]{1,0:T(8,128)S(1)}, u32[]{:S(2)}, u32[]{:S(2)}) collective-permute-start(f32[36,128]{1,0:T(8,128)S(1)} %add.34.packed), channel_id=1, source_target_pairs={{0,17},{1,16},{2,19},{3,18},{4,21},{5,20},{6,23},{7,22},{8,25},{9,... | collective-permute-start | bytes 55304 | tf_op jit(solution)/shard_map/ppermute | solution.py:543
  109.5 5.3 %gravity_last.1 = (f32[16,256]{1,0:T(8,128)}, f32[1,128]{1,0:T(1,128)}, f32[8,16,128]{2,1,0:T(8,128)}) custom-call(s32[513]{0:T(1024)S(1)} %pad_add_fusion.head, f32[36,128]{1,0:T(8,128)S(1)} %add.34.packed, f32[36,128]{1,0:T(8,128)S(1)} %collective-permute-done.39.other, f32[4,128]{1,0:T(4,128)S(1)} %get-tuple-element.207.observed, f32[9088,128]{1,0:T(8,128)S(1)} %copy-done.2), custom_call_target="tpu_custom_call" | custom-call | tf_op jit(solution)/shard_map/gravity_last/pallas_call | solution.py:456
  (131 shorter events, 37.3 us)
Async XLA Ops:
  1.7 8.1 %collective-permute-start = (f32[6,64,128]{2,1,0:T(8,128)S(1)}, f32[6,64,128]{2,1,0:T(8,128)S(1)}, u32[]{:S(2)}, u32[]{:S(2)}) collective-permute-start(f32[6,64,128]{2,1,0:T(8,128)S(1)} %get-tuple-element.113), channel_id=1, source_target_pairs={{0,4},{1,3},{2,6},{3,1},{4,0},{5,9},{6,2},{7,11},{8,12},{9,5},{10,... | collective-permute-start | bytes 589832 | tf_op jit(solution)/shard_map/ppermute | solution.py:539
  4.8 3.4 %collective-permute-start.1 = (f32[4,64,128]{2,1,0:T(8,128)S(1)}, f32[4,64,128]{2,1,0:T(8,128)S(1)}, u32[]{:S(2)}, u32[]{:S(2)}) collective-permute-start(f32[4,64,128]{2,1,0:T(8,128)S(1)} %get-tuple-element.108.cur.prev), channel_id=1, source_target_pairs={{0,1},{1,0},{2,3},{3,2},{4,5},{5,4},{6,7},{7,6},{8,9},{9,8},{10,11... | collective-permute-start | bytes 393224 | tf_op jit(solution)/shard_map/ppermute | solution.py:543
  11.2 3.0 %collective-permute-start.4 = (f32[2,1,128]{2,1,0:T(1,128)S(1)}, f32[2,1,128]{2,1,0:T(1,128)S(1)}, u32[]{:S(2)}, u32[]{:S(2)}) collective-permute-start(f32[2,1,128]{2,1,0:T(1,128)S(1)} %bitcast.13), channel_id=1, source_target_pairs={{0,1},{1,0},{2,3},{3,2},{4,5},{5,4},{6,7},{7,6},{8,9},{9,8},{10,11... | collective-permute-start | bytes 3080 | tf_op jit(solution)/shard_map/ppermute | solution.py:543
  11.2 6.4 %collective-permute-start.2 = (f32[4,64,128]{2,1,0:T(8,128)S(1)}, f32[4,64,128]{2,1,0:T(8,128)S(1)}, u32[]{:S(2)}, u32[]{:S(2)}) collective-permute-start(f32[4,64,128]{2,1,0:T(8,128)S(1)} %wave_halo.16.cur.prev), channel_id=1, source_target_pairs={{0,4},{1,3},{2,6},{3,1},{4,0},{5,9},{6,2},{7,11},{8,12},{9,5},{10,... | collective-permute-start | bytes 393224 | tf_op jit(solution)/shard_map/ppermute | solution.py:539
  13.8 3.9 %collective-permute-start.3 = (f32[4,64,128]{2,1,0:T(8,128)S(1)}, f32[4,64,128]{2,1,0:T(8,128)S(1)}, u32[]{:S(2)}, u32[]{:S(2)}) collective-permute-start(f32[4,64,128]{2,1,0:T(8,128)S(1)} %wave_halo.16.cur.prev), channel_id=1, source_target_pairs={{0,1},{1,0},{2,3},{3,2},{4,5},{5,4},{6,7},{7,6},{8,9},{9,8},{10,11... | collective-permute-start | bytes 393224 | tf_op jit(solution)/shard_map/ppermute | solution.py:543
  17.7 6.6 %collective-permute-start.7 = (f32[6,64,128]{2,1,0:T(8,128)S(1)}, f32[6,64,128]{2,1,0:T(8,128)S(1)}, u32[]{:S(2)}, u32[]{:S(2)}) collective-permute-start(f32[6,64,128]{2,1,0:T(8,128)S(1)} %collective-permute-done.outer), channel_id=1, source_target_pairs={{0,1},{1,0},{2,3},{3,2},{4,5},{5,4},{6,7},{7,6},{8,9},{9,8},{10,11... | collective-permute-start | bytes 589832 | tf_op jit(solution)/shard_map/ppermute | solution.py:543
  17.8 6.4 %collective-permute-start.5 = (f32[4,64,128]{2,1,0:T(8,128)S(1)}, f32[4,64,128]{2,1,0:T(8,128)S(1)}, u32[]{:S(2)}, u32[]{:S(2)}) collective-permute-start(f32[4,64,128]{2,1,0:T(8,128)S(1)} %wave_halo.17.cur.prev), channel_id=1, source_target_pairs={{0,4},{1,3},{2,6},{3,1},{4,0},{5,9},{6,2},{7,11},{8,12},{9,5},{10,... | collective-permute-start | bytes 393224 | tf_op jit(solution)/shard_map/ppermute | solution.py:539
  20.4 3.9 %collective-permute-start.6 = (f32[4,64,128]{2,1,0:T(8,128)S(1)}, f32[4,64,128]{2,1,0:T(8,128)S(1)}, u32[]{:S(2)}, u32[]{:S(2)}) collective-permute-start(f32[4,64,128]{2,1,0:T(8,128)S(1)} %wave_halo.17.cur.prev), channel_id=1, source_target_pairs={{0,1},{1,0},{2,3},{3,2},{4,5},{5,4},{6,7},{7,6},{8,9},{9,8},{10,11... | collective-permute-start | bytes 393224 | tf_op jit(solution)/shard_map/ppermute | solution.py:543
  24.3 4.5 %collective-permute-start.10 = (f32[2,2,128]{2,1,0:T(2,128)S(1)}, f32[2,2,128]{2,1,0:T(2,128)S(1)}, u32[]{:S(2)}, u32[]{:S(2)}) collective-permute-start(f32[2,2,128]{2,1,0:T(2,128)S(1)} %pad_maximum_fusion.1), channel_id=1, source_target_pairs={{0,2},{1,3},{2,0},{3,1},{4,6},{5,7},{6,4},{7,5},{8,10},{9,11},{10,... | collective-permute-start | bytes 6152 | tf_op jit(solution)/shard_map/ppermute | solution.py:543
  25.9 5.4 %collective-permute-start.8 = (f32[4,64,128]{2,1,0:T(8,128)S(1)}, f32[4,64,128]{2,1,0:T(8,128)S(1)}, u32[]{:S(2)}, u32[]{:S(2)}) collective-permute-start(f32[4,64,128]{2,1,0:T(8,128)S(1)} %wave_halo.18.cur.prev), channel_id=1, source_target_pairs={{0,4},{1,3},{2,6},{3,1},{4,0},{5,9},{6,2},{7,11},{8,12},{9,5},{10,... | collective-permute-start | bytes 393224 | tf_op jit(solution)/shard_map/ppermute | solution.py:539
  31.4 5.0 %collective-permute-start.11 = (f32[4,64,128]{2,1,0:T(8,128)S(1)}, f32[4,64,128]{2,1,0:T(8,128)S(1)}, u32[]{:S(2)}, u32[]{:S(2)}) collective-permute-start(f32[4,64,128]{2,1,0:T(8,128)S(1)} %wave_halo.19.cur.prev), channel_id=1, source_target_pairs={{0,4},{1,3},{2,6},{3,1},{4,0},{5,9},{6,2},{7,11},{8,12},{9,5},{10,... | collective-permute-start | bytes 393224 | tf_op jit(solution)/shard_map/ppermute | solution.py:539
  33.5 3.0 %collective-permute-start.12 = (f32[4,64,128]{2,1,0:T(8,128)S(1)}, f32[4,64,128]{2,1,0:T(8,128)S(1)}, u32[]{:S(2)}, u32[]{:S(2)}) collective-permute-start(f32[4,64,128]{2,1,0:T(8,128)S(1)} %wave_halo.19.cur.prev), channel_id=1, source_target_pairs={{0,1},{1,0},{2,3},{3,2},{4,5},{5,4},{6,7},{7,6},{8,9},{9,8},{10,11... | collective-permute-start | bytes 393224 | tf_op jit(solution)/shard_map/ppermute | solution.py:543
  36.5 5.0 %collective-permute-start.13 = (f32[4,64,128]{2,1,0:T(8,128)S(1)}, f32[4,64,128]{2,1,0:T(8,128)S(1)}, u32[]{:S(2)}, u32[]{:S(2)}) collective-permute-start(f32[4,64,128]{2,1,0:T(8,128)S(1)} %wave_halo.20.cur.prev), channel_id=1, source_target_pairs={{0,4},{1,3},{2,6},{3,1},{4,0},{5,9},{6,2},{7,11},{8,12},{9,5},{10,... | collective-permute-start | bytes 393224 | tf_op jit(solution)/shard_map/ppermute | solution.py:539
  41.6 5.4 %collective-permute-start.15 = (f32[4,64,128]{2,1,0:T(8,128)S(1)}, f32[4,64,128]{2,1,0:T(8,128)S(1)}, u32[]{:S(2)}, u32[]{:S(2)}) collective-permute-start(f32[4,64,128]{2,1,0:T(8,128)S(1)} %wave_halo.21.cur.prev), channel_id=1, source_target_pairs={{0,4},{1,3},{2,6},{3,1},{4,0},{5,9},{6,2},{7,11},{8,12},{9,5},{10,... | collective-permute-start | bytes 393224 | tf_op jit(solution)/shard_map/ppermute | solution.py:539
  43.7 3.3 %collective-permute-start.16 = (f32[4,64,128]{2,1,0:T(8,128)S(1)}, f32[4,64,128]{2,1,0:T(8,128)S(1)}, u32[]{:S(2)}, u32[]{:S(2)}) collective-permute-start(f32[4,64,128]{2,1,0:T(8,128)S(1)} %wave_halo.21.cur.prev), channel_id=1, source_target_pairs={{0,1},{1,0},{2,3},{3,2},{4,5},{5,4},{6,7},{7,6},{8,9},{9,8},{10,11... | collective-permute-start | bytes 393224 | tf_op jit(solution)/shard_map/ppermute | solution.py:543
  47.1 5.0 %collective-permute-start.17 = (f32[4,64,128]{2,1,0:T(8,128)S(1)}, f32[4,64,128]{2,1,0:T(8,128)S(1)}, u32[]{:S(2)}, u32[]{:S(2)}) collective-permute-start(f32[4,64,128]{2,1,0:T(8,128)S(1)} %wave_halo.22.cur.prev), channel_id=1, source_target_pairs={{0,4},{1,3},{2,6},{3,1},{4,0},{5,9},{6,2},{7,11},{8,12},{9,5},{10,... | collective-permute-start | bytes 393224 | tf_op jit(solution)/shard_map/ppermute | solution.py:539
  48.8 3.3 %collective-permute-start.18 = (f32[4,64,128]{2,1,0:T(8,128)S(1)}, f32[4,64,128]{2,1,0:T(8,128)S(1)}, u32[]{:S(2)}, u32[]{:S(2)}) collective-permute-start(f32[4,64,128]{2,1,0:T(8,128)S(1)} %wave_halo.22.cur.prev), channel_id=1, source_target_pairs={{0,1},{1,0},{2,3},{3,2},{4,5},{5,4},{6,7},{7,6},{8,9},{9,8},{10,11... | collective-permute-start | bytes 393224 | tf_op jit(solution)/shard_map/ppermute | solution.py:543
  52.2 5.3 %collective-permute-start.19 = (f32[4,64,128]{2,1,0:T(8,128)S(1)}, f32[4,64,128]{2,1,0:T(8,128)S(1)}, u32[]{:S(2)}, u32[]{:S(2)}) collective-permute-start(f32[4,64,128]{2,1,0:T(8,128)S(1)} %wave_halo.23.cur.prev), channel_id=1, source_target_pairs={{0,4},{1,3},{2,6},{3,1},{4,0},{5,9},{6,2},{7,11},{8,12},{9,5},{10,... | collective-permute-start | bytes 393224 | tf_op jit(solution)/shard_map/ppermute | solution.py:539
  54.5 3.0 %collective-permute-start.20 = (f32[4,64,128]{2,1,0:T(8,128)S(1)}, f32[4,64,128]{2,1,0:T(8,128)S(1)}, u32[]{:S(2)}, u32[]{:S(2)}) collective-permute-start(f32[4,64,128]{2,1,0:T(8,128)S(1)} %wave_halo.23.cur.prev), channel_id=1, source_target_pairs={{0,1},{1,0},{2,3},{3,2},{4,5},{5,4},{6,7},{7,6},{8,9},{9,8},{10,11... | collective-permute-start | bytes 393224 | tf_op jit(solution)/shard_map/ppermute | solution.py:543
  57.5 5.0 %collective-permute-start.21 = (f32[4,64,128]{2,1,0:T(8,128)S(1)}, f32[4,64,128]{2,1,0:T(8,128)S(1)}, u32[]{:S(2)}, u32[]{:S(2)}) collective-permute-start(f32[4,64,128]{2,1,0:T(8,128)S(1)} %wave_halo.24.cur.prev), channel_id=1, source_target_pairs={{0,4},{1,3},{2,6},{3,1},{4,0},{5,9},{6,2},{7,11},{8,12},{9,5},{10,... | collective-permute-start | bytes 393224 | tf_op jit(solution)/shard_map/ppermute | solution.py:539
  62.6 5.0 %collective-permute-start.23 = (f32[4,64,128]{2,1,0:T(8,128)S(1)}, f32[4,64,128]{2,1,0:T(8,128)S(1)}, u32[]{:S(2)}, u32[]{:S(2)}) collective-permute-start(f32[4,64,128]{2,1,0:T(8,128)S(1)} %wave_halo.25.cur.prev), channel_id=1, source_target_pairs={{0,4},{1,3},{2,6},{3,1},{4,0},{5,9},{6,2},{7,11},{8,12},{9,5},{10,... | collective-permute-start | bytes 393224 | tf_op jit(solution)/shard_map/ppermute | solution.py:539
  67.7 5.0 %collective-permute-start.25 = (f32[4,64,128]{2,1,0:T(8,128)S(1)}, f32[4,64,128]{2,1,0:T(8,128)S(1)}, u32[]{:S(2)}, u32[]{:S(2)}) collective-permute-start(f32[4,64,128]{2,1,0:T(8,128)S(1)} %wave_halo.26.cur.prev), channel_id=1, source_target_pairs={{0,4},{1,3},{2,6},{3,1},{4,0},{5,9},{6,2},{7,11},{8,12},{9,5},{10,... | collective-permute-start | bytes 393224 | tf_op jit(solution)/shard_map/ppermute | solution.py:539
  72.8 5.0 %collective-permute-start.27 = (f32[4,64,128]{2,1,0:T(8,128)S(1)}, f32[4,64,128]{2,1,0:T(8,128)S(1)}, u32[]{:S(2)}, u32[]{:S(2)}) collective-permute-start(f32[4,64,128]{2,1,0:T(8,128)S(1)} %wave_halo.27.cur.prev), channel_id=1, source_target_pairs={{0,4},{1,3},{2,6},{3,1},{4,0},{5,9},{6,2},{7,11},{8,12},{9,5},{10,... | collective-permute-start | bytes 393224 | tf_op jit(solution)/shard_map/ppermute | solution.py:539
  77.9 5.0 %collective-permute-start.29 = (f32[4,64,128]{2,1,0:T(8,128)S(1)}, f32[4,64,128]{2,1,0:T(8,128)S(1)}, u32[]{:S(2)}, u32[]{:S(2)}) collective-permute-start(f32[4,64,128]{2,1,0:T(8,128)S(1)} %wave_halo.28.cur.prev), channel_id=1, source_target_pairs={{0,4},{1,3},{2,6},{3,1},{4,0},{5,9},{6,2},{7,11},{8,12},{9,5},{10,... | collective-permute-start | bytes 393224 | tf_op jit(solution)/shard_map/ppermute | solution.py:539
  83.0 5.0 %collective-permute-start.31 = (f32[4,64,128]{2,1,0:T(8,128)S(1)}, f32[4,64,128]{2,1,0:T(8,128)S(1)}, u32[]{:S(2)}, u32[]{:S(2)}) collective-permute-start(f32[4,64,128]{2,1,0:T(8,128)S(1)} %wave_halo.29.cur.prev), channel_id=1, source_target_pairs={{0,4},{1,3},{2,6},{3,1},{4,0},{5,9},{6,2},{7,11},{8,12},{9,5},{10,... | collective-permute-start | bytes 393224 | tf_op jit(solution)/shard_map/ppermute | solution.py:539
  85.1 3.0 %collective-permute-start.32 = (f32[4,64,128]{2,1,0:T(8,128)S(1)}, f32[4,64,128]{2,1,0:T(8,128)S(1)}, u32[]{:S(2)}, u32[]{:S(2)}) collective-permute-start(f32[4,64,128]{2,1,0:T(8,128)S(1)} %wave_halo.29.cur.prev), channel_id=1, source_target_pairs={{0,1},{1,0},{2,3},{3,2},{4,5},{5,4},{6,7},{7,6},{8,9},{9,8},{10,11... | collective-permute-start | bytes 393224 | tf_op jit(solution)/shard_map/ppermute | solution.py:543
  88.1 5.0 %collective-permute-start.33 = (f32[4,64,128]{2,1,0:T(8,128)S(1)}, f32[4,64,128]{2,1,0:T(8,128)S(1)}, u32[]{:S(2)}, u32[]{:S(2)}) collective-permute-start(f32[4,64,128]{2,1,0:T(8,128)S(1)} %wave_halo.30.cur), channel_id=1, source_target_pairs={{0,4},{1,3},{2,6},{3,1},{4,0},{5,9},{6,2},{7,11},{8,12},{9,5},{10,... | collective-permute-start | bytes 393224 | tf_op jit(solution)/shard_map/ppermute | solution.py:539
  90.2 3.0 %collective-permute-start.34 = (f32[4,64,128]{2,1,0:T(8,128)S(1)}, f32[4,64,128]{2,1,0:T(8,128)S(1)}, u32[]{:S(2)}, u32[]{:S(2)}) collective-permute-start(f32[4,64,128]{2,1,0:T(8,128)S(1)} %wave_halo.30.cur), channel_id=1, source_target_pairs={{0,1},{1,0},{2,3},{3,2},{4,5},{5,4},{6,7},{7,6},{8,9},{9,8},{10,11... | collective-permute-start | bytes 393224 | tf_op jit(solution)/shard_map/ppermute | solution.py:543
  93.3 6.3 %collective-permute-start.37 = (f32[4,64,128]{2,1,0:T(8,128)S(1)}, f32[4,64,128]{2,1,0:T(8,128)S(1)}, u32[]{:S(2)}, u32[]{:S(2)}) collective-permute-start(f32[4,64,128]{2,1,0:T(8,128)S(1)} %wave_halo.31.cur.own), channel_id=1, source_target_pairs={{0,1},{1,0},{2,3},{3,2},{4,5},{5,4},{6,7},{7,6},{8,9},{9,8},{10,11... | collective-permute-start | bytes 393224 | tf_op jit(solution)/shard_map/ppermute | solution.py:543
  97.6 3.5 %collective-permute-start.36 = (f32[36,128]{1,0:T(8,128)S(1)}, f32[36,128]{1,0:T(8,128)S(1)}, u32[]{:S(2)}, u32[]{:S(2)}) collective-permute-start(f32[36,128]{1,0:T(8,128)S(1)} %add.32), channel_id=1, source_target_pairs={{0,5},{1,4},{2,7},{3,6},{4,1},{5,0},{6,3},{7,2},{8,13},{9,12},{10,... | collective-permute-start | bytes 55304 | tf_op jit(solution)/shard_map/ppermute | solution.py:543
  101.0 4.2 %collective-permute-start.38 = (f32[36,128]{1,0:T(8,128)S(1)}, f32[36,128]{1,0:T(8,128)S(1)}, u32[]{:S(2)}, u32[]{:S(2)}) collective-permute-start(f32[36,128]{1,0:T(8,128)S(1)} %add.33), channel_id=1, source_target_pairs={{0,9},{1,8},{2,11},{3,10},{4,13},{5,12},{6,15},{7,14},{8,1},{9,0},... | collective-permute-start | bytes 55304 | tf_op jit(solution)/shard_map/ppermute | solution.py:543
  105.3 4.2 %collective-permute-start.39 = (f32[36,128]{1,0:T(8,128)S(1)}, f32[36,128]{1,0:T(8,128)S(1)}, u32[]{:S(2)}, u32[]{:S(2)}) collective-permute-start(f32[36,128]{1,0:T(8,128)S(1)} %add.34.packed), channel_id=1, source_target_pairs={{0,17},{1,16},{2,19},{3,18},{4,21},{5,20},{6,23},{7,22},{8,25},{9,... | collective-permute-start | bytes 55304 | tf_op jit(solution)/shard_map/ppermute | solution.py:543
  (15 other events, 145.2 us)

commit v5 on v4

--- a/solution.py
+++ b/solution.py
@@ -225,8 +225,7 @@
     )(base, cour, cour_outer, outer, inner)
 
 
-def trace_kernel(step, place, cur, surf, predicted, kept, out):
-    del kept
+def trace_kernel(step, place, cur, surf, predicted, out):
     planes, rows, lanes = cur.shape
     receivers = place.shape[0]
     steps = step + 1
@@ -252,16 +251,16 @@
     out[steps * (receivers // 128) :, :] = predicted[...]
 
 
-def recorded_traces(step, place, cur, surf, predicted, kept):
+def recorded_traces(step, place, cur, surf, predicted):
     rows = (step + 1) * (place.shape[0] // 128) + predicted.shape[0]
     return pl.pallas_call(
         functools.partial(trace_kernel, step),
         out_shape=shape((rows, 128)),
-        in_specs=[VMEM] * 5,
+        in_specs=[VMEM] * 4,
         out_specs=VMEM,
         compiler_params=room(4),
         name="traces",
-    )(place, cur, surf, predicted, kept)
+    )(place, cur, surf, predicted)
 
 
 def join_kernel(own, sibling, kept, out, sems):
@@ -581,13 +580,11 @@
             state["known"] = jnp.concatenate(
                 [jnp.where(upper, other, known), jnp.where(upper, known, other)], 1
             )
-            return "known"
 
         return work
 
     def share_edges(gate):
         state["inner"] = swap(gate(edges), 0, 1)
-        return "inner"
 
     def cross(gate):
         state["cross"] = cross_gradient_of(count, velocity, density, edges, gate(state["inner"]))
@@ -624,22 +621,20 @@
 
     surf = cour
     for step in range(steps):
-        job = jobs.pop(0) if step and jobs else None
-        done = None
         if step:
-            if job is not None:
-                gated = []
-
-                def gate(value):
-                    nonlocal cur
-                    cur, value = together((cur, value))
-                    gated.append(value)
-                    return value
-
-                done = job(gate)
             outer = across(cur)
             inner = swap(cur, 0, 1)
         base, surf = local_step(step, pulses, mask, cur, prev, cour, surf)
+        job = jobs.pop(0) if step and jobs else None
+        done = None
+        if job is not None:
+
+            def gate(value):
+                nonlocal base
+                base, value = together((base, value))
+                return value
+
+            done = job(gate)
         cur, prev = halo_step(base, cour, cour_outer, outer, inner), cur
         if done is not None:
             cur, state[done] = together((cur, state[done]))
@@ -662,7 +657,7 @@
 
     kept = state["table"] if chunks == 1 else predicted
     sibling = swap(cur, 0, 1)
-    packed = recorded_traces(steps - 1, place, cur, surf, predicted, kept)
+    packed = recorded_traces(steps - 1, place, cur, surf, predicted)
     other = swap(packed, 0, 1)
     if count & (count - 1) == 0:
         bit = 1

time: 115 us -> 112 us (0.974)
  waiting for transfers between devices: 30.6 us -> 23.3 us
  local copies, waits for them, and re-layouts: 3.16 us -> 7.79 us
    ppermute x16, waiting for transfers between devices: 26.1 us -> 19.4 us  [across(): return lax.ppermute(value, AXES, chain)]
    unnamed x21 -> x25, local copies, waits for them, and re-layouts: 3.02 us -> 7.65 us
    ppermute x16, starting transfers between devices: 35.5 us -> 33.8 us  [across(): return lax.ppermute(value, AXES, chain)]
    ppermute x24, starting transfers between devices: 9.75 us -> 11.1 us  [swap(): return lax.ppermute(value, AXES, pairs)]
  transfers between devices with their start and end apart: 40 -> 40, of which waited for: 19 -> 17; matrix products, arithmetic and copies ran while one was open for 0% -> 2% of each run, Pallas kernels for 22% -> 23%
where the time goes in v5:
time: 112 us
  starting transfers between devices  44.9 us (40%)
  Pallas kernels  32.4 us (29%)
  waiting for transfers between devices  23.3 us (21%)
  local copies, waits for them, and re-layouts  7.79 us (7%)
  between operations  1.75 us (2%)
  other arithmetic  1.6 us (1%)
    ppermute x16, starting transfers between devices, across(): return lax.ppermute(value, AXES, chain)  33.8 us
    ppermute x16, waiting for transfers between devices, across(): return lax.ppermute(value, AXES, chain)  19.4 us
    pallas_call x8, Pallas kernels, gravity_forward(): pl.pallas_call(functools.partial(forward_kernel, first, guard, total_x, s...  12 us
    ppermute x24, starting transfers between devices, swap(): return lax.ppermute(value, AXES, pairs)  11.1 us
    unnamed x25, local copies, waits for them, and re-layouts  7.65 us
    pallas_call x16, Pallas kernels, local_step(): pl.pallas_call(functools.partial(local_kernel, step), out_shape=(shape(cu...  6.13 us
    pallas_call x1, Pallas kernels, gravity_last(): pl.pallas_call(functools.partial(last_kernel, total_x, lateral), out_shap...  5.31 us
    ppermute x24, waiting for transfers between devices, swap(): return lax.ppermute(value, AXES, pairs)  3.86 us
  transfers between devices with their start and end apart: 40, of which 17 were waited for; matrix products, arithmetic and copies ran while one was open for 2% of the time, Pallas kernels for 23%

profile of v5, /device:TPU:0, one launch (start us, length us, event | category | flops | bytes accessed | tf_op | source)
XLA Modules:
  0.0 111.7 jit_solution(15571744644282114297)
XLA Ops:
  1.7 3.0 %collective-permute-start = (f32[6,64,128]{2,1,0:T(8,128)S(1)}, f32[6,64,128]{2,1,0:T(8,128)S(1)}, u32[]{:S(2)}, u32[]{:S(2)}) collective-permute-start(f32[6,64,128]{2,1,0:T(8,128)S(1)} %get-tuple-element.107), channel_id=1, source_target_pairs={{0,4},{1,3},{2,6},{3,1},{4,0},{5,9},{6,2},{7,11},{8,12},{9,5},{10,... | collective-permute-start | bytes 589832 | tf_op jit(solution)/shard_map/ppermute | solution.py:538
  6.1 1.7 %setup.1 = (f32[4,64,128]{2,1,0:T(8,128)S(1)}, f32[4,64,128]{2,1,0:T(8,128)S(1)}, f32[4,64,128]{2,1,0:T(8,128)S(1)}, f32[4,64,128]{2,1,0:T(8,128)S(1)}, f32[4,64...) custom-call(s32[1]{0:T(128)S(6)} %copy.22.source, f32[16]{0:T(128)S(1)} %copy-done.7, f32[8,64,128]{2,1,0:T(8,128)} %p_prev.1, ...), custom_call_target="tpu_custom_call" | custom-call | flops 655360 | bytes 1048576 | tf_op jit(solution)/shard_map/setup/pallas_call | solution.py:140
  8.2 1.6 %collective-permute-done.outer = f32[6,64,128]{2,1,0:T(8,128)S(1)} collective-permute-done((f32[6,64,128]{2,1,0:T(8,128)S(1)}, f32[6,64,128]{2,1,0:T(8,128)S(1)}, u32[]{:S(2)}, u32[]{:S(2)}) %collective-permute-start) | collective-permute-done | bytes 196640 | tf_op jit(solution)/shard_map/ppermute | solution.py:538
  9.9 2.5 %collective-permute-start.2 = (f32[4,64,128]{2,1,0:T(8,128)S(1)}, f32[4,64,128]{2,1,0:T(8,128)S(1)}, u32[]{:S(2)}, u32[]{:S(2)}) collective-permute-start(f32[4,64,128]{2,1,0:T(8,128)S(1)} %wave_halo.16.cur.prev), channel_id=1, source_target_pairs={{0,4},{1,3},{2,6},{3,1},{4,0},{5,9},{6,2},{7,11},{8,12},{9,5},{10,... | collective-permute-start | bytes 393224 | tf_op jit(solution)/shard_map/ppermute | solution.py:538
  12.8 2.5 %collective-permute-done.2.outer = f32[4,64,128]{2,1,0:T(8,128)S(1)} collective-permute-done((f32[4,64,128]{2,1,0:T(8,128)S(1)}, f32[4,64,128]{2,1,0:T(8,128)S(1)}, u32[]{:S(2)}, u32[]{:S(2)}) %collective-permute-start.2) | collective-permute-done | bytes 131104 | tf_op jit(solution)/shard_map/ppermute | solution.py:538
  15.4 2.1 %collective-permute-start.4 = (f32[4,64,128]{2,1,0:T(8,128)S(1)}, f32[4,64,128]{2,1,0:T(8,128)S(1)}, u32[]{:S(2)}, u32[]{:S(2)}) collective-permute-start(f32[4,64,128]{2,1,0:T(8,128)S(1)} %wave_halo.17.cur.prev), channel_id=1, source_target_pairs={{0,4},{1,3},{2,6},{3,1},{4,0},{5,9},{6,2},{7,11},{8,12},{9,5},{10,... | collective-permute-start | bytes 393224 | tf_op jit(solution)/shard_map/ppermute | solution.py:538
  20.6 2.1 %collective-permute-start.7 = (f32[4,64,128]{2,1,0:T(8,128)S(1)}, f32[4,64,128]{2,1,0:T(8,128)S(1)}, u32[]{:S(2)}, u32[]{:S(2)}) collective-permute-start(f32[4,64,128]{2,1,0:T(8,128)S(1)} %wave_halo.18.cur.prev), channel_id=1, source_target_pairs={{0,4},{1,3},{2,6},{3,1},{4,0},{5,9},{6,2},{7,11},{8,12},{9,5},{10,... | collective-permute-start | bytes 393224 | tf_op jit(solution)/shard_map/ppermute | solution.py:538
  23.6 2.0 %collective-permute-done.7.outer = f32[4,64,128]{2,1,0:T(8,128)S(1)} collective-permute-done((f32[4,64,128]{2,1,0:T(8,128)S(1)}, f32[4,64,128]{2,1,0:T(8,128)S(1)}, u32[]{:S(2)}, u32[]{:S(2)}) %collective-permute-start.7) | collective-permute-done | bytes 131104 | tf_op jit(solution)/shard_map/ppermute | solution.py:538
  25.7 2.1 %collective-permute-start.10 = (f32[4,64,128]{2,1,0:T(8,128)S(1)}, f32[4,64,128]{2,1,0:T(8,128)S(1)}, u32[]{:S(2)}, u32[]{:S(2)}) collective-permute-start(f32[4,64,128]{2,1,0:T(8,128)S(1)} %wave_halo.19.cur.prev), channel_id=1, source_target_pairs={{0,4},{1,3},{2,6},{3,1},{4,0},{5,9},{6,2},{7,11},{8,12},{9,5},{10,... | collective-permute-start | bytes 393224 | tf_op jit(solution)/shard_map/ppermute | solution.py:538
  30.8 2.1 %collective-permute-start.12 = (f32[4,64,128]{2,1,0:T(8,128)S(1)}, f32[4,64,128]{2,1,0:T(8,128)S(1)}, u32[]{:S(2)}, u32[]{:S(2)}) collective-permute-start(f32[4,64,128]{2,1,0:T(8,128)S(1)} %wave_halo.20.cur.prev), channel_id=1, source_target_pairs={{0,4},{1,3},{2,6},{3,1},{4,0},{5,9},{6,2},{7,11},{8,12},{9,5},{10,... | collective-permute-start | bytes 393224 | tf_op jit(solution)/shard_map/ppermute | solution.py:538
  32.9 1.5 %collective-permute-start.16 = (f32[2,2,128]{2,1,0:T(2,128)S(1)}, f32[2,2,128]{2,1,0:T(2,128)S(1)}, u32[]{:S(2)}, u32[]{:S(2)}) collective-permute-start(f32[2,2,128]{2,1,0:T(2,128)S(1)} %pad_maximum_fusion.1), channel_id=1, source_target_pairs={{0,2},{1,3},{2,0},{3,1},{4,6},{5,7},{6,4},{7,5},{8,10},{9,11},{10,... | collective-permute-start | bytes 6152 | tf_op jit(solution)/shard_map/ppermute | solution.py:542
  35.9 2.1 %collective-permute-start.14 = (f32[4,64,128]{2,1,0:T(8,128)S(1)}, f32[4,64,128]{2,1,0:T(8,128)S(1)}, u32[]{:S(2)}, u32[]{:S(2)}) collective-permute-start(f32[4,64,128]{2,1,0:T(8,128)S(1)} %wave_halo.21.cur.prev), channel_id=1, source_target_pairs={{0,4},{1,3},{2,6},{3,1},{4,0},{5,9},{6,2},{7,11},{8,12},{9,5},{10,... | collective-permute-start | bytes 393224 | tf_op jit(solution)/shard_map/ppermute | solution.py:538
  38.3 2.8 %gravity_table.1.table.kept = f32[9088,128]{1,0:T(8,128)S(1)} custom-call(s32[1]{0:T(128)} %constant.67.clone.1.head), custom_call_target="tpu_custom_call" | custom-call | flops 23265280 | bytes 4653056 | tf_op jit(solution)/shard_map/gravity_table/pallas_call | solution.py:320
  41.3 1.8 %collective-permute-start.17 = (f32[4,64,128]{2,1,0:T(8,128)S(1)}, f32[4,64,128]{2,1,0:T(8,128)S(1)}, u32[]{:S(2)}, u32[]{:S(2)}) collective-permute-start(f32[4,64,128]{2,1,0:T(8,128)S(1)} %wave_halo.22.cur.prev), channel_id=1, source_target_pairs={{0,4},{1,3},{2,6},{3,1},{4,0},{5,9},{6,2},{7,11},{8,12},{9,5},{10,... | collective-permute-start | bytes 393224 | tf_op jit(solution)/shard_map/ppermute | solution.py:538
  46.4 2.3 %collective-permute-start.19 = (f32[4,64,128]{2,1,0:T(8,128)S(1)}, f32[4,64,128]{2,1,0:T(8,128)S(1)}, u32[]{:S(2)}, u32[]{:S(2)}) collective-permute-start(f32[4,64,128]{2,1,0:T(8,128)S(1)} %wave_halo.23.cur.prev), channel_id=1, source_target_pairs={{0,4},{1,3},{2,6},{3,1},{4,0},{5,9},{6,2},{7,11},{8,12},{9,5},{10,... | collective-permute-start | bytes 393224 | tf_op jit(solution)/shard_map/ppermute | solution.py:538
  49.1 1.5 %gravity_forward.9 = f32[64,128]{1,0:T(8,128)S(1)} custom-call(s32[513]{0:T(1024)S(1)} %pad_add_fusion.head, f32[9088,128]{1,0:T(8,128)S(1)} %gravity_table.1.table.kept, f32[4,64,128]{2,1,0:T(8,128)S(1)} %get-tuple-element.137.dens), custom_call_target="tpu_custom_call" | custom-call | flops 8388608 | bytes 131072 | tf_op jit(solution)/shard_map/gravity_forward/pallas_call | solution.py:365
  51.7 2.1 %collective-permute-start.21 = (f32[4,64,128]{2,1,0:T(8,128)S(1)}, f32[4,64,128]{2,1,0:T(8,128)S(1)}, u32[]{:S(2)}, u32[]{:S(2)}) collective-permute-start(f32[4,64,128]{2,1,0:T(8,128)S(1)} %wave_halo.24.cur.prev), channel_id=1, source_target_pairs={{0,4},{1,3},{2,6},{3,1},{4,0},{5,9},{6,2},{7,11},{8,12},{9,5},{10,... | collective-permute-start | bytes 393224 | tf_op jit(solution)/shard_map/ppermute | solution.py:538
  56.8 2.1 %collective-permute-start.23 = (f32[4,64,128]{2,1,0:T(8,128)S(1)}, f32[4,64,128]{2,1,0:T(8,128)S(1)}, u32[]{:S(2)}, u32[]{:S(2)}) collective-permute-start(f32[4,64,128]{2,1,0:T(8,128)S(1)} %wave_halo.25.cur.prev), channel_id=1, source_target_pairs={{0,4},{1,3},{2,6},{3,1},{4,0},{5,9},{6,2},{7,11},{8,12},{9,5},{10,... | collective-permute-start | bytes 393224 | tf_op jit(solution)/shard_map/ppermute | solution.py:538
  61.9 2.1 %collective-permute-start.25 = (f32[4,64,128]{2,1,0:T(8,128)S(1)}, f32[4,64,128]{2,1,0:T(8,128)S(1)}, u32[]{:S(2)}, u32[]{:S(2)}) collective-permute-start(f32[4,64,128]{2,1,0:T(8,128)S(1)} %wave_halo.26.cur.prev), channel_id=1, source_target_pairs={{0,4},{1,3},{2,6},{3,1},{4,0},{5,9},{6,2},{7,11},{8,12},{9,5},{10,... | collective-permute-start | bytes 393224 | tf_op jit(solution)/shard_map/ppermute | solution.py:538
  64.4 2.3 %copy-done.1 = f32[9088,128]{1,0:T(8,128)S(1)} copy-done((f32[9088,128]{1,0:T(8,128)S(1)}, f32[9088,128]{1,0:T(8,128)}, u32[]{:S(2)}) %copy-start.1) | copy-done | bytes 4653080
  66.7 1.5 %gravity_forward.12 = f32[64,128]{1,0:T(8,128)S(1)} custom-call(s32[513]{0:T(1024)S(1)} %pad_add_fusion.head, f32[9088,128]{1,0:T(8,128)S(1)} %copy-done.1, f32[4,64,128]{2,1,0:T(8,128)S(1)} %get-tuple-element.137.dens), custom_call_target="tpu_custom_call" | custom-call | flops 8388608 | bytes 131072 | tf_op jit(solution)/shard_map/gravity_forward/pallas_call | solution.py:365
  70.5 1.5 %gravity_forward.13 = f32[64,128]{1,0:T(8,128)S(1)} custom-call(s32[513]{0:T(1024)S(1)} %pad_add_fusion.head, f32[9088,128]{1,0:T(8,128)S(1)} %copy-done.2, f32[4,64,128]{2,1,0:T(8,128)S(1)} %get-tuple-element.137.dens), custom_call_target="tpu_custom_call" | custom-call | flops 8388608 | bytes 131072 | tf_op jit(solution)/shard_map/gravity_forward/pallas_call | solution.py:365
  73.4 2.2 %collective-permute-start.29 = (f32[4,64,128]{2,1,0:T(8,128)S(1)}, f32[4,64,128]{2,1,0:T(8,128)S(1)}, u32[]{:S(2)}, u32[]{:S(2)}) collective-permute-start(f32[4,64,128]{2,1,0:T(8,128)S(1)} %wave_halo.28.cur.prev), channel_id=1, source_target_pairs={{0,4},{1,3},{2,6},{3,1},{4,0},{5,9},{6,2},{7,11},{8,12},{9,5},{10,... | collective-permute-start | bytes 393224 | tf_op jit(solution)/shard_map/ppermute | solution.py:538
  78.6 2.4 %collective-permute-start.31 = (f32[4,64,128]{2,1,0:T(8,128)S(1)}, f32[4,64,128]{2,1,0:T(8,128)S(1)}, u32[]{:S(2)}, u32[]{:S(2)}) collective-permute-start(f32[4,64,128]{2,1,0:T(8,128)S(1)} %wave_halo.29.cur.prev), channel_id=1, source_target_pairs={{0,4},{1,3},{2,6},{3,1},{4,0},{5,9},{6,2},{7,11},{8,12},{9,5},{10,... | collective-permute-start | bytes 393224 | tf_op jit(solution)/shard_map/ppermute | solution.py:538
  84.0 2.1 %collective-permute-start.33 = (f32[4,64,128]{2,1,0:T(8,128)S(1)}, f32[4,64,128]{2,1,0:T(8,128)S(1)}, u32[]{:S(2)}, u32[]{:S(2)}) collective-permute-start(f32[4,64,128]{2,1,0:T(8,128)S(1)} %wave_halo.30.cur), channel_id=1, source_target_pairs={{0,4},{1,3},{2,6},{3,1},{4,0},{5,9},{6,2},{7,11},{8,12},{9,5},{10,... | collective-permute-start | bytes 393224 | tf_op jit(solution)/shard_map/ppermute | solution.py:538
  86.6 2.4 %collective-permute-done.33.outer = f32[4,64,128]{2,1,0:T(8,128)S(1)} collective-permute-done((f32[4,64,128]{2,1,0:T(8,128)S(1)}, f32[4,64,128]{2,1,0:T(8,128)S(1)}, u32[]{:S(2)}, u32[]{:S(2)}) %collective-permute-start.33) | collective-permute-done | bytes 131104 | tf_op jit(solution)/shard_map/ppermute | solution.py:538
  91.1 2.0 %collective-permute-start.36 = (f32[36,128]{1,0:T(8,128)S(1)}, f32[36,128]{1,0:T(8,128)S(1)}, u32[]{:S(2)}, u32[]{:S(2)}) collective-permute-start(f32[36,128]{1,0:T(8,128)S(1)} %add.32), channel_id=1, source_target_pairs={{0,5},{1,4},{2,7},{3,6},{4,1},{5,0},{6,3},{7,2},{8,13},{9,12},{10,... | collective-permute-start | bytes 55304 | tf_op jit(solution)/shard_map/ppermute | solution.py:542
  93.1 2.3 %copy-done.3 = f32[9088,128]{1,0:T(8,128)S(1)} copy-done((f32[9088,128]{1,0:T(8,128)S(1)}, f32[9088,128]{1,0:T(8,128)}, u32[]{:S(2)}) %copy-start.3) | copy-done | bytes 4653080
  96.2 2.2 %collective-permute-start.38 = (f32[36,128]{1,0:T(8,128)S(1)}, f32[36,128]{1,0:T(8,128)S(1)}, u32[]{:S(2)}, u32[]{:S(2)}) collective-permute-start(f32[36,128]{1,0:T(8,128)S(1)} %add.33), channel_id=1, source_target_pairs={{0,9},{1,8},{2,11},{3,10},{4,13},{5,12},{6,15},{7,14},{8,1},{9,0},... | collective-permute-start | bytes 55304 | tf_op jit(solution)/shard_map/ppermute | solution.py:542
  99.9 2.7 %collective-permute-start.39 = (f32[36,128]{1,0:T(8,128)S(1)}, f32[36,128]{1,0:T(8,128)S(1)}, u32[]{:S(2)}, u32[]{:S(2)}) collective-permute-start(f32[36,128]{1,0:T(8,128)S(1)} %add.34.packed), channel_id=1, source_target_pairs={{0,17},{1,16},{2,19},{3,18},{4,21},{5,20},{6,23},{7,22},{8,25},{9,... | collective-permute-start | bytes 55304 | tf_op jit(solution)/shard_map/ppermute | solution.py:542
  104.1 2.3 %copy-done.4 = f32[9088,128]{1,0:T(8,128)S(1)} copy-done((f32[9088,128]{1,0:T(8,128)S(1)}, f32[9088,128]{1,0:T(8,128)}, u32[]{:S(2)}) %copy-start.4) | copy-done | bytes 4653080
  106.4 5.3 %gravity_last.1 = (f32[16,256]{1,0:T(8,128)}, f32[1,128]{1,0:T(1,128)}, f32[8,16,128]{2,1,0:T(8,128)}) custom-call(s32[513]{0:T(1024)S(1)} %pad_add_fusion.head, f32[36,128]{1,0:T(8,128)S(1)} %add.34.packed, f32[36,128]{1,0:T(8,128)S(1)} %collective-permute-done.39.other, f32[4,128]{1,0:T(4,128)S(1)} %get-tuple-element.195.observed, f32[9088,128]{1,0:T(8,128)S(1)} %copy-done.4), custom_call_target="tpu_custom_call" | custom-call | tf_op jit(solution)/shard_map/gravity_last/pallas_call | solution.py:455
  (134 shorter events, 38.7 us)
Async XLA Ops:
  1.7 8.1 %collective-permute-start = (f32[6,64,128]{2,1,0:T(8,128)S(1)}, f32[6,64,128]{2,1,0:T(8,128)S(1)}, u32[]{:S(2)}, u32[]{:S(2)}) collective-permute-start(f32[6,64,128]{2,1,0:T(8,128)S(1)} %get-tuple-element.107), channel_id=1, source_target_pairs={{0,4},{1,3},{2,6},{3,1},{4,0},{5,9},{6,2},{7,11},{8,12},{9,5},{10,... | collective-permute-start | bytes 589832 | tf_op jit(solution)/shard_map/ppermute | solution.py:538
  4.8 3.4 %collective-permute-start.1 = (f32[4,64,128]{2,1,0:T(8,128)S(1)}, f32[4,64,128]{2,1,0:T(8,128)S(1)}, u32[]{:S(2)}, u32[]{:S(2)}) collective-permute-start(f32[4,64,128]{2,1,0:T(8,128)S(1)} %get-tuple-element.102.cur.prev), channel_id=1, source_target_pairs={{0,1},{1,0},{2,3},{3,2},{4,5},{5,4},{6,7},{7,6},{8,9},{9,8},{10,11... | collective-permute-start | bytes 393224 | tf_op jit(solution)/shard_map/ppermute | solution.py:542
  9.9 5.5 %collective-permute-start.2 = (f32[4,64,128]{2,1,0:T(8,128)S(1)}, f32[4,64,128]{2,1,0:T(8,128)S(1)}, u32[]{:S(2)}, u32[]{:S(2)}) collective-permute-start(f32[4,64,128]{2,1,0:T(8,128)S(1)} %wave_halo.16.cur.prev), channel_id=1, source_target_pairs={{0,4},{1,3},{2,6},{3,1},{4,0},{5,9},{6,2},{7,11},{8,12},{9,5},{10,... | collective-permute-start | bytes 393224 | tf_op jit(solution)/shard_map/ppermute | solution.py:538
  12.4 3.0 %collective-permute-start.3 = (f32[4,64,128]{2,1,0:T(8,128)S(1)}, f32[4,64,128]{2,1,0:T(8,128)S(1)}, u32[]{:S(2)}, u32[]{:S(2)}) collective-permute-start(f32[4,64,128]{2,1,0:T(8,128)S(1)} %wave_halo.16.cur.prev), channel_id=1, source_target_pairs={{0,1},{1,0},{2,3},{3,2},{4,5},{5,4},{6,7},{7,6},{8,9},{9,8},{10,11... | collective-permute-start | bytes 393224 | tf_op jit(solution)/shard_map/ppermute | solution.py:542
  15.4 5.0 %collective-permute-start.4 = (f32[4,64,128]{2,1,0:T(8,128)S(1)}, f32[4,64,128]{2,1,0:T(8,128)S(1)}, u32[]{:S(2)}, u32[]{:S(2)}) collective-permute-start(f32[4,64,128]{2,1,0:T(8,128)S(1)} %wave_halo.17.cur.prev), channel_id=1, source_target_pairs={{0,4},{1,3},{2,6},{3,1},{4,0},{5,9},{6,2},{7,11},{8,12},{9,5},{10,... | collective-permute-start | bytes 393224 | tf_op jit(solution)/shard_map/ppermute | solution.py:538
  18.9 3.8 %collective-permute-start.6 = (f32[2,1,128]{2,1,0:T(1,128)S(1)}, f32[2,1,128]{2,1,0:T(1,128)S(1)}, u32[]{:S(2)}, u32[]{:S(2)}) collective-permute-start(f32[2,1,128]{2,1,0:T(1,128)S(1)} %bitcast.13), channel_id=1, source_target_pairs={{0,1},{1,0},{2,3},{3,2},{4,5},{5,4},{6,7},{7,6},{8,9},{9,8},{10,11... | collective-permute-start | bytes 3080 | tf_op jit(solution)/shard_map/ppermute | solution.py:542
  20.6 5.0 %collective-permute-start.7 = (f32[4,64,128]{2,1,0:T(8,128)S(1)}, f32[4,64,128]{2,1,0:T(8,128)S(1)}, u32[]{:S(2)}, u32[]{:S(2)}) collective-permute-start(f32[4,64,128]{2,1,0:T(8,128)S(1)} %wave_halo.18.cur.prev), channel_id=1, source_target_pairs={{0,4},{1,3},{2,6},{3,1},{4,0},{5,9},{6,2},{7,11},{8,12},{9,5},{10,... | collective-permute-start | bytes 393224 | tf_op jit(solution)/shard_map/ppermute | solution.py:538
  22.7 5.5 %collective-permute-start.9 = (f32[6,64,128]{2,1,0:T(8,128)S(1)}, f32[6,64,128]{2,1,0:T(8,128)S(1)}, u32[]{:S(2)}, u32[]{:S(2)}) collective-permute-start(f32[6,64,128]{2,1,0:T(8,128)S(1)} %collective-permute-done.outer), channel_id=1, source_target_pairs={{0,1},{1,0},{2,3},{3,2},{4,5},{5,4},{6,7},{7,6},{8,9},{9,8},{10,11... | collective-permute-start | bytes 589832 | tf_op jit(solution)/shard_map/ppermute | solution.py:542
  25.7 5.0 %collective-permute-start.10 = (f32[4,64,128]{2,1,0:T(8,128)S(1)}, f32[4,64,128]{2,1,0:T(8,128)S(1)}, u32[]{:S(2)}, u32[]{:S(2)}) collective-permute-start(f32[4,64,128]{2,1,0:T(8,128)S(1)} %wave_halo.19.cur.prev), channel_id=1, source_target_pairs={{0,4},{1,3},{2,6},{3,1},{4,0},{5,9},{6,2},{7,11},{8,12},{9,5},{10,... | collective-permute-start | bytes 393224 | tf_op jit(solution)/shard_map/ppermute | solution.py:538
  30.8 5.0 %collective-permute-start.12 = (f32[4,64,128]{2,1,0:T(8,128)S(1)}, f32[4,64,128]{2,1,0:T(8,128)S(1)}, u32[]{:S(2)}, u32[]{:S(2)}) collective-permute-start(f32[4,64,128]{2,1,0:T(8,128)S(1)} %wave_halo.20.cur.prev), channel_id=1, source_target_pairs={{0,4},{1,3},{2,6},{3,1},{4,0},{5,9},{6,2},{7,11},{8,12},{9,5},{10,... | collective-permute-start | bytes 393224 | tf_op jit(solution)/shard_map/ppermute | solution.py:538
  32.8 3.0 %collective-permute-start.13 = (f32[4,64,128]{2,1,0:T(8,128)S(1)}, f32[4,64,128]{2,1,0:T(8,128)S(1)}, u32[]{:S(2)}, u32[]{:S(2)}) collective-permute-start(f32[4,64,128]{2,1,0:T(8,128)S(1)} %wave_halo.20.cur.prev), channel_id=1, source_target_pairs={{0,1},{1,0},{2,3},{3,2},{4,5},{5,4},{6,7},{7,6},{8,9},{9,8},{10,11... | collective-permute-start | bytes 393224 | tf_op jit(solution)/shard_map/ppermute | solution.py:542
  32.9 5.1 %collective-permute-start.16 = (f32[2,2,128]{2,1,0:T(2,128)S(1)}, f32[2,2,128]{2,1,0:T(2,128)S(1)}, u32[]{:S(2)}, u32[]{:S(2)}) collective-permute-start(f32[2,2,128]{2,1,0:T(2,128)S(1)} %pad_maximum_fusion.1), channel_id=1, source_target_pairs={{0,2},{1,3},{2,0},{3,1},{4,6},{5,7},{6,4},{7,5},{8,10},{9,11},{10,... | collective-permute-start | bytes 6152 | tf_op jit(solution)/shard_map/ppermute | solution.py:542
  35.9 5.3 %collective-permute-start.14 = (f32[4,64,128]{2,1,0:T(8,128)S(1)}, f32[4,64,128]{2,1,0:T(8,128)S(1)}, u32[]{:S(2)}, u32[]{:S(2)}) collective-permute-start(f32[4,64,128]{2,1,0:T(8,128)S(1)} %wave_halo.21.cur.prev), channel_id=1, source_target_pairs={{0,4},{1,3},{2,6},{3,1},{4,0},{5,9},{6,2},{7,11},{8,12},{9,5},{10,... | collective-permute-start | bytes 393224 | tf_op jit(solution)/shard_map/ppermute | solution.py:538
  37.9 3.2 %collective-permute-start.15 = (f32[4,64,128]{2,1,0:T(8,128)S(1)}, f32[4,64,128]{2,1,0:T(8,128)S(1)}, u32[]{:S(2)}, u32[]{:S(2)}) collective-permute-start(f32[4,64,128]{2,1,0:T(8,128)S(1)} %wave_halo.21.cur.prev), channel_id=1, source_target_pairs={{0,1},{1,0},{2,3},{3,2},{4,5},{5,4},{6,7},{7,6},{8,9},{9,8},{10,11... | collective-permute-start | bytes 393224 | tf_op jit(solution)/shard_map/ppermute | solution.py:542
  41.3 5.0 %collective-permute-start.17 = (f32[4,64,128]{2,1,0:T(8,128)S(1)}, f32[4,64,128]{2,1,0:T(8,128)S(1)}, u32[]{:S(2)}, u32[]{:S(2)}) collective-permute-start(f32[4,64,128]{2,1,0:T(8,128)S(1)} %wave_halo.22.cur.prev), channel_id=1, source_target_pairs={{0,4},{1,3},{2,6},{3,1},{4,0},{5,9},{6,2},{7,11},{8,12},{9,5},{10,... | collective-permute-start | bytes 393224 | tf_op jit(solution)/shard_map/ppermute | solution.py:538
  43.0 3.3 %collective-permute-start.18 = (f32[4,64,128]{2,1,0:T(8,128)S(1)}, f32[4,64,128]{2,1,0:T(8,128)S(1)}, u32[]{:S(2)}, u32[]{:S(2)}) collective-permute-start(f32[4,64,128]{2,1,0:T(8,128)S(1)} %wave_halo.22.cur.prev), channel_id=1, source_target_pairs={{0,1},{1,0},{2,3},{3,2},{4,5},{5,4},{6,7},{7,6},{8,9},{9,8},{10,11... | collective-permute-start | bytes 393224 | tf_op jit(solution)/shard_map/ppermute | solution.py:542
  46.4 5.2 %collective-permute-start.19 = (f32[4,64,128]{2,1,0:T(8,128)S(1)}, f32[4,64,128]{2,1,0:T(8,128)S(1)}, u32[]{:S(2)}, u32[]{:S(2)}) collective-permute-start(f32[4,64,128]{2,1,0:T(8,128)S(1)} %wave_halo.23.cur.prev), channel_id=1, source_target_pairs={{0,4},{1,3},{2,6},{3,1},{4,0},{5,9},{6,2},{7,11},{8,12},{9,5},{10,... | collective-permute-start | bytes 393224 | tf_op jit(solution)/shard_map/ppermute | solution.py:538
  51.7 5.0 %collective-permute-start.21 = (f32[4,64,128]{2,1,0:T(8,128)S(1)}, f32[4,64,128]{2,1,0:T(8,128)S(1)}, u32[]{:S(2)}, u32[]{:S(2)}) collective-permute-start(f32[4,64,128]{2,1,0:T(8,128)S(1)} %wave_halo.24.cur.prev), channel_id=1, source_target_pairs={{0,4},{1,3},{2,6},{3,1},{4,0},{5,9},{6,2},{7,11},{8,12},{9,5},{10,... | collective-permute-start | bytes 393224 | tf_op jit(solution)/shard_map/ppermute | solution.py:538
  56.8 5.0 %collective-permute-start.23 = (f32[4,64,128]{2,1,0:T(8,128)S(1)}, f32[4,64,128]{2,1,0:T(8,128)S(1)}, u32[]{:S(2)}, u32[]{:S(2)}) collective-permute-start(f32[4,64,128]{2,1,0:T(8,128)S(1)} %wave_halo.25.cur.prev), channel_id=1, source_target_pairs={{0,4},{1,3},{2,6},{3,1},{4,0},{5,9},{6,2},{7,11},{8,12},{9,5},{10,... | collective-permute-start | bytes 393224 | tf_op jit(solution)/shard_map/ppermute | solution.py:538
  58.9 3.0 %collective-permute-start.24 = (f32[4,64,128]{2,1,0:T(8,128)S(1)}, f32[4,64,128]{2,1,0:T(8,128)S(1)}, u32[]{:S(2)}, u32[]{:S(2)}) collective-permute-start(f32[4,64,128]{2,1,0:T(8,128)S(1)} %wave_halo.25.cur.prev), channel_id=1, source_target_pairs={{0,1},{1,0},{2,3},{3,2},{4,5},{5,4},{6,7},{7,6},{8,9},{9,8},{10,11... | collective-permute-start | bytes 393224 | tf_op jit(solution)/shard_map/ppermute | solution.py:542
  61.9 6.3 %collective-permute-start.25 = (f32[4,64,128]{2,1,0:T(8,128)S(1)}, f32[4,64,128]{2,1,0:T(8,128)S(1)}, u32[]{:S(2)}, u32[]{:S(2)}) collective-permute-start(f32[4,64,128]{2,1,0:T(8,128)S(1)} %wave_halo.26.cur.prev), channel_id=1, source_target_pairs={{0,4},{1,3},{2,6},{3,1},{4,0},{5,9},{6,2},{7,11},{8,12},{9,5},{10,... | collective-permute-start | bytes 393224 | tf_op jit(solution)/shard_map/ppermute | solution.py:538
  64.0 4.2 %collective-permute-start.26 = (f32[4,64,128]{2,1,0:T(8,128)S(1)}, f32[4,64,128]{2,1,0:T(8,128)S(1)}, u32[]{:S(2)}, u32[]{:S(2)}) collective-permute-start(f32[4,64,128]{2,1,0:T(8,128)S(1)} %wave_halo.26.cur.prev), channel_id=1, source_target_pairs={{0,1},{1,0},{2,3},{3,2},{4,5},{5,4},{6,7},{7,6},{8,9},{9,8},{10,11... | collective-permute-start | bytes 393224 | tf_op jit(solution)/shard_map/ppermute | solution.py:542
  68.3 5.0 %collective-permute-start.27 = (f32[4,64,128]{2,1,0:T(8,128)S(1)}, f32[4,64,128]{2,1,0:T(8,128)S(1)}, u32[]{:S(2)}, u32[]{:S(2)}) collective-permute-start(f32[4,64,128]{2,1,0:T(8,128)S(1)} %wave_halo.27.cur.prev), channel_id=1, source_target_pairs={{0,4},{1,3},{2,6},{3,1},{4,0},{5,9},{6,2},{7,11},{8,12},{9,5},{10,... | collective-permute-start | bytes 393224 | tf_op jit(solution)/shard_map/ppermute | solution.py:538
  69.1 4.2 %collective-permute-start.28 = (f32[4,64,128]{2,1,0:T(8,128)S(1)}, f32[4,64,128]{2,1,0:T(8,128)S(1)}, u32[]{:S(2)}, u32[]{:S(2)}) collective-permute-start(f32[4,64,128]{2,1,0:T(8,128)S(1)} %wave_halo.27.cur.prev), channel_id=1, source_target_pairs={{0,1},{1,0},{2,3},{3,2},{4,5},{5,4},{6,7},{7,6},{8,9},{9,8},{10,11... | collective-permute-start | bytes 393224 | tf_op jit(solution)/shard_map/ppermute | solution.py:542
  73.4 5.2 %collective-permute-start.29 = (f32[4,64,128]{2,1,0:T(8,128)S(1)}, f32[4,64,128]{2,1,0:T(8,128)S(1)}, u32[]{:S(2)}, u32[]{:S(2)}) collective-permute-start(f32[4,64,128]{2,1,0:T(8,128)S(1)} %wave_halo.28.cur.prev), channel_id=1, source_target_pairs={{0,4},{1,3},{2,6},{3,1},{4,0},{5,9},{6,2},{7,11},{8,12},{9,5},{10,... | collective-permute-start | bytes 393224 | tf_op jit(solution)/shard_map/ppermute | solution.py:538
  75.6 3.0 %collective-permute-start.30 = (f32[4,64,128]{2,1,0:T(8,128)S(1)}, f32[4,64,128]{2,1,0:T(8,128)S(1)}, u32[]{:S(2)}, u32[]{:S(2)}) collective-permute-start(f32[4,64,128]{2,1,0:T(8,128)S(1)} %wave_halo.28.cur.prev), channel_id=1, source_target_pairs={{0,1},{1,0},{2,3},{3,2},{4,5},{5,4},{6,7},{7,6},{8,9},{9,8},{10,11... | collective-permute-start | bytes 393224 | tf_op jit(solution)/shard_map/ppermute | solution.py:542
  78.6 5.3 %collective-permute-start.31 = (f32[4,64,128]{2,1,0:T(8,128)S(1)}, f32[4,64,128]{2,1,0:T(8,128)S(1)}, u32[]{:S(2)}, u32[]{:S(2)}) collective-permute-start(f32[4,64,128]{2,1,0:T(8,128)S(1)} %wave_halo.29.cur.prev), channel_id=1, source_target_pairs={{0,4},{1,3},{2,6},{3,1},{4,0},{5,9},{6,2},{7,11},{8,12},{9,5},{10,... | collective-permute-start | bytes 393224 | tf_op jit(solution)/shard_map/ppermute | solution.py:538
  84.0 5.0 %collective-permute-start.33 = (f32[4,64,128]{2,1,0:T(8,128)S(1)}, f32[4,64,128]{2,1,0:T(8,128)S(1)}, u32[]{:S(2)}, u32[]{:S(2)}) collective-permute-start(f32[4,64,128]{2,1,0:T(8,128)S(1)} %wave_halo.30.cur), channel_id=1, source_target_pairs={{0,4},{1,3},{2,6},{3,1},{4,0},{5,9},{6,2},{7,11},{8,12},{9,5},{10,... | collective-permute-start | bytes 393224 | tf_op jit(solution)/shard_map/ppermute | solution.py:538
  89.1 4.0 %collective-permute-start.37 = (f32[4,64,128]{2,1,0:T(8,128)S(1)}, f32[4,64,128]{2,1,0:T(8,128)S(1)}, u32[]{:S(2)}, u32[]{:S(2)}) collective-permute-start(f32[4,64,128]{2,1,0:T(8,128)S(1)} %wave_halo.31.cur.own), channel_id=1, source_target_pairs={{0,1},{1,0},{2,3},{3,2},{4,5},{5,4},{6,7},{7,6},{8,9},{9,8},{10,11... | collective-permute-start | bytes 393224 | tf_op jit(solution)/shard_map/ppermute | solution.py:542
  91.1 5.1 %collective-permute-start.36 = (f32[36,128]{1,0:T(8,128)S(1)}, f32[36,128]{1,0:T(8,128)S(1)}, u32[]{:S(2)}, u32[]{:S(2)}) collective-permute-start(f32[36,128]{1,0:T(8,128)S(1)} %add.32), channel_id=1, source_target_pairs={{0,5},{1,4},{2,7},{3,6},{4,1},{5,0},{6,3},{7,2},{8,13},{9,12},{10,... | collective-permute-start | bytes 55304 | tf_op jit(solution)/shard_map/ppermute | solution.py:542
  96.2 3.7 %collective-permute-start.38 = (f32[36,128]{1,0:T(8,128)S(1)}, f32[36,128]{1,0:T(8,128)S(1)}, u32[]{:S(2)}, u32[]{:S(2)}) collective-permute-start(f32[36,128]{1,0:T(8,128)S(1)} %add.33), channel_id=1, source_target_pairs={{0,9},{1,8},{2,11},{3,10},{4,13},{5,12},{6,15},{7,14},{8,1},{9,0},... | collective-permute-start | bytes 55304 | tf_op jit(solution)/shard_map/ppermute | solution.py:542
  99.9 4.2 %collective-permute-start.39 = (f32[36,128]{1,0:T(8,128)S(1)}, f32[36,128]{1,0:T(8,128)S(1)}, u32[]{:S(2)}, u32[]{:S(2)}) collective-permute-start(f32[36,128]{1,0:T(8,128)S(1)} %add.34.packed), channel_id=1, source_target_pairs={{0,17},{1,16},{2,19},{3,18},{4,21},{5,20},{6,23},{7,22},{8,25},{9,... | collective-permute-start | bytes 55304 | tf_op jit(solution)/shard_map/ppermute | solution.py:542
  (17 other events, 118.3 us)

commit v6 on v5

--- a/solution.py
+++ b/solution.py
@@ -225,9 +225,9 @@
     )(base, cour, cour_outer, outer, inner)
 
 
-def trace_kernel(step, place, cur, surf, predicted, out):
+def trace_kernel(step, place, cur, surf, out):
     planes, rows, lanes = cur.shape
-    receivers = place.shape[0]
+    receivers = place.shape[1]
     steps = step + 1
     lane = lax.broadcasted_iota(jnp.int32, (rows, lanes), 1)
     columns = jnp.concatenate(
@@ -237,34 +237,31 @@
         ],
         0,
     )
-    where = lax.broadcasted_iota(jnp.int32, (receivers, planes * rows), 1)
-    pick = jnp.where(place[...] == where, 1.0, 0.0).astype(jnp.bfloat16)
+    columns = columns.T
+    spot = lax.broadcasted_iota(jnp.int32, (planes * rows, receivers), 0)
+    pick = jnp.where(place[...] == spot, 1.0, 0.0).astype(jnp.bfloat16)
     total = None
     for _ in range(3):
         part = columns.astype(jnp.bfloat16)
         columns = columns - part.astype(F32)
-        term = jnp.dot(pick, part, preferred_element_type=F32)
+        term = jnp.dot(part, pick, preferred_element_type=F32)
         total = term if total is None else total + term
-    total = total.T
     for b in range(receivers // 128):
         out[b * steps : (b + 1) * steps, :] = total[:steps, b * 128 : (b + 1) * 128]
-    out[steps * (receivers // 128) :, :] = predicted[...]
-
-
-def recorded_traces(step, place, cur, surf, predicted):
-    rows = (step + 1) * (place.shape[0] // 128) + predicted.shape[0]
+
+
+def recorded_traces(step, place, cur, surf):
     return pl.pallas_call(
         functools.partial(trace_kernel, step),
-        out_shape=shape((rows, 128)),
-        in_specs=[VMEM] * 4,
+        out_shape=shape(((step + 1) * (place.shape[1] // 128), 128)),
+        in_specs=[VMEM] * 3,
         out_specs=VMEM,
         compiler_params=room(4),
         name="traces",
-    )(place, cur, surf, predicted)
-
-
-def join_kernel(own, sibling, kept, out, sems):
-    del kept
+    )(place, cur, surf)
+
+
+def join_kernel(own, sibling, out, sems):
     slab = out.shape[0]
     _, upper = position()
     pairs = []
@@ -274,17 +271,17 @@
     run_copies(pairs, sems)
 
 
-def join(own, sibling, kept):
+def join(own, sibling):
     half, rows, lanes = own.shape
     return pl.pallas_call(
         join_kernel,
         out_shape=shape((2 * half, rows, lanes)),
-        in_specs=[VMEM] * 3,
+        in_specs=[VMEM] * 2,
         out_specs=HBM,
         scratch_shapes=[pltpu.SemaphoreType.DMA((2 * half,))],
         compiler_params=room(2),
         name="join",
-    )(own, sibling, kept)
+    )(own, sibling)
 
 
 def on_chip(value):
@@ -357,7 +354,7 @@
             accumulate()
         return carry
 
-    lax.fori_loop(0, count, one, 0, unroll=4)
+    lax.fori_loop(0, count, one, 0, unroll=8)
 
 
 def gravity_forward(first, count, guard, total_x, slab, lateral, head, table, dens):
@@ -375,16 +372,16 @@
     )(head, on_chip(table), dens)
 
 
-def spread_back(guard, total_x, lateral, row_low, head, weights, table, out):
+def adjoint_kernel(lines, guard, total_x, lateral, head, weights, table, start_at, out):
     slab, rows, lanes = out.shape
-    groups = (head.shape[0] - 1) // 128
     spread = 2 * lateral
     lead = total_x - 1 - head[0]
+    row_low = lax.axis_index("station") * rows
 
     def one(k, i, acc):
         sx, sy = divmod_static(head[1 + 128 * k + i], lateral)
         shift = lead - sx
-        weight = weights(k, i)
+        weight = weights[k, i]
         if guard:
             keep = (shift >= 0) & (shift < guard)
             shift = jnp.where(keep, shift, 0)
@@ -394,81 +391,73 @@
             acc[x] + weight * table[pl.ds(start + x * spread, rows), :] for x in range(slab)
         )
 
-    zero = jnp.zeros((rows, lanes), F32)
-    acc = (zero,) * slab
-    for k in range(groups):
-        acc = lax.fori_loop(0, 128, functools.partial(one, k), acc, unroll=4)
+    acc = tuple(start_at[x] for x in range(slab))
+    for k in lines:
+        acc = lax.fori_loop(0, 128, functools.partial(one, k), acc, unroll=8)
     for x in range(slab):
         out[x] = acc[x]
 
 
-def adjoint_kernel(guard, total_x, lateral, head, weights, table, out):
-    row_low = lax.axis_index("station") * out.shape[1]
-    spread_back(guard, total_x, lateral, row_low, head, lambda k, i: weights[128 * k + i], table, out)
-
-
-def gravity_adjoint(guard, total_x, slab, rows, lateral, head, weights, table):
-    return pl.pallas_call(
-        functools.partial(adjoint_kernel, guard, total_x, lateral),
-        out_shape=shape((slab, rows, table.shape[1])),
-        in_specs=[SMEM, SMEM, VMEM],
+def gravity_adjoint(lines, guard, total_x, lateral, head, weights, table, start_at):
+    return pl.pallas_call(
+        functools.partial(adjoint_kernel, lines, guard, total_x, lateral),
+        out_shape=shape(start_at.shape),
+        in_specs=[SMEM, SMEM, VMEM, VMEM],
         out_specs=VMEM,
+        cost_estimate=pl.CostEstimate(
+            flops=256 * len(lines) * start_at.size, bytes_accessed=8 * start_at.size, transcendentals=0
+        ),
         compiler_params=room(8),
         name="gravity_adjoint",
-    )(head, weights, table)
-
-
-def last_kernel(total_x, lateral, head, packed, other, observed, table, traces, own, out, held, scalars, sem):
-    steps, receivers = traces.shape
-    blocks = receivers // 128
-    total = packed[...] + other[...]
-    residual = total[steps * blocks :, :] - observed[...]
-    held[...] = residual.astype(jnp.bfloat16).astype(F32)
-    copy = pltpu.make_async_copy(held, scalars, sem)
-    copy.start()
-    for b in range(blocks):
-        traces[:, b * 128 : (b + 1) * 128] = total[b * steps : (b + 1) * steps, :]
-    s = lax.axis_index("station")
+    )(head, weights, table, start_at)
+
+
+def small_call(kernel, outs, name, *values):
+    single = not isinstance(outs, tuple)
+    return pl.pallas_call(
+        kernel,
+        out_shape=outs,
+        in_specs=[VMEM] * len(values),
+        out_specs=VMEM if single else (VMEM,) * len(outs),
+        compiler_params=room(2),
+        name=name,
+    )(*values)
+
+
+def sum_kernel(first, second, out):
+    out[...] = first[...] + second[...]
+
+
+def plus(first, second):
+    return small_call(sum_kernel, shape(first.shape), "sum", first, second)
+
+
+def unpack_kernel(packed, other, out):
+    steps, receivers = out.shape
+    for b in range(receivers // 128):
+        rows = slice(b * steps, (b + 1) * steps)
+        out[:, b * 128 : (b + 1) * 128] = packed[rows, :] + other[rows, :]
+
+
+def predict_kernel(*refs):
+    pieces, out = refs[:-1], refs[-1]
+    line = 0
+    for piece in pieces:
+        for k in range(piece.shape[0] // 128):
+            block = piece[k * 128 : (k + 1) * 128, :].T
+            out[line : line + 1, :] = jnp.sum(block, axis=0, keepdims=True)
+            line += 1
+
+
+def residual_kernel(packed, other, observed, weights, own):
+    residual = packed[...] + other[...] - observed[...]
+    weights[...] = residual.astype(jnp.bfloat16).astype(F32)
     mine = own.shape[0]
     for k in range(residual.shape[0] // mine):
 
-        @pl.when(s == k)
+        @pl.when(lax.axis_index("station") == k)
         def _(k=k):
             own[...] = residual[k * mine : (k + 1) * mine, :]
-
-    copy.wait()
-    spread_back(
-        0,
-        total_x,
-        lateral,
-        s * out.shape[1],
-        head,
-        lambda k, i: scalars[k, i],
-        table,
-        out,
-    )
-
-
-def gravity_last(steps, receivers, total_x, slab, rows, lateral, head, packed, other, observed, table):
-    count = lax.axis_size("station")
-    lines = observed.shape[0]
-    return pl.pallas_call(
-        functools.partial(last_kernel, total_x, lateral),
-        out_shape=(
-            shape((steps, receivers)),
-            shape((lines // count, 128)),
-            shape((slab, rows, table.shape[1])),
-        ),
-        in_specs=[SMEM] + [VMEM] * 4,
-        out_specs=(VMEM,) * 3,
-        scratch_shapes=[
-            pltpu.VMEM((lines, 128), F32),
-            pltpu.SMEM((lines, 128), F32),
-            pltpu.SemaphoreType.DMA,
-        ],
-        compiler_params=room(8),
-        name="gravity_last",
-    )(head, packed, other, observed, on_chip(table))
 
 
 def cross_kernel(count, velocity, density, outer, inner, out):
@@ -553,7 +542,7 @@
     receiver_j = receiver_x - m * slab
     receiver_j = jnp.where(upper, slab - 1 - receiver_j, receiver_j)
     inside = (receiver_j >= 0) & (receiver_j < half)
-    place = jnp.where(inside, receiver_j * lateral + receiver_y, -1)[:, None]
+    place = jnp.where(inside, receiver_j * lateral + receiver_y, -1)[None, :]
 
     reach = min(total_x, 64)
     chunks = -(-total_x // reach)
@@ -590,13 +579,20 @@
         state["cross"] = cross_gradient_of(count, velocity, density, edges, gate(state["inner"]))
         return "cross"
 
+    lines = n_stations // 128
+
     def build_table(gate):
-        cells = state["known"][0].reshape(-1).astype(jnp.int32)
-        state["head"] = head_of(0, cells)
-        state["table"] = table_of(gate(jnp.zeros((1,), jnp.int32)))
+        known = gate(state["known"])
+        cells = known[0].reshape(-1).astype(jnp.int32)
+        head = head_of(0, cells)
+        zero, head, observed_all, where = together(
+            (jnp.zeros((1,), jnp.int32), head, known[1].reshape(-1, 128), place)
+        )
+        state.update(head=head, observed=observed_all, place=where)
+        state["table"] = table_of(zero)
         return "table"
 
-    pieces = 8
+    pieces = 4
     part = n_stations // pieces
 
     def forward(i):
@@ -608,16 +604,55 @@
 
         return work
 
-    def gather_sums(gate):
-        sums = jnp.concatenate([state[i] for i in range(pieces)])
-        state["predicted"] = jnp.sum(gate(sums), axis=1).reshape(-1, 128)
-        return "predicted"
-
+    def predict(gate):
+        sums = [state[i] for i in range(pieces)]
+        sums[0] = gate(sums[0])
+        packed = small_call(predict_kernel, shape((lines, 128)), "predict", *sums)
+        state["packed"], state["other"] = packed, swap(packed, 0, 1)
+
+    def add_up(bit):
+        def work(gate):
+            packed = plus(gate(state["packed"]), state["other"])
+            state["packed"], state["other"] = packed, swap(packed, bit, 1)
+
+        return work
+
+    def residual(gate):
+        state["weights"], state["own"] = small_call(
+            residual_kernel,
+            (shape((lines, 128)), shape((lines // stations, 128))),
+            "residual",
+            gate(state["packed"]),
+            state["other"],
+            state["observed"],
+        )
+        state["gradient"] = jnp.zeros((slab, block, vertical), F32)
+        return "weights"
+
+    def adjoint(half_lines):
+        def work(gate):
+            state["gradient"] = gravity_adjoint(
+                half_lines,
+                0,
+                total_x,
+                lateral,
+                state["head"],
+                gate(state["weights"]),
+                state["table"],
+                state["gradient"],
+            )
+            return "gradient"
+
+        return work
+
+    hidden = chunks == 1 and count & (count - 1) == 0
     jobs = [exchange(1 << b) for b in range(stations.bit_length() - 1)]
+    if hidden:
+        jobs += [build_table] + [forward(i) for i in range(pieces)] + [predict]
+        jobs += [add_up(1 << b) for b in range(count.bit_length() - 1)] + [residual]
+        jobs += [adjoint(range(lines // 2)), adjoint(range(lines // 2, lines))]
     jobs.insert(1, share_edges)
-    jobs += [cross, None]
-    if chunks == 1:
-        jobs += [build_table] + [forward(i) for i in range(pieces)] + [gather_sums]
+    jobs.append(cross)
 
     surf = cour
     for step in range(steps):
@@ -625,26 +660,44 @@
             outer = across(cur)
             inner = swap(cur, 0, 1)
         base, surf = local_step(step, pulses, mask, cur, prev, cour, surf)
-        job = jobs.pop(0) if step and jobs else None
-        done = None
-        if job is not None:
-
-            def gate(value):
-                nonlocal base
-                base, value = together((base, value))
-                return value
-
-            done = job(gate)
+
+        def gate(value):
+            nonlocal base
+            base, value = together((base, value))
+            return value
+
+        ready = jobs.pop(0)(gate) if step and jobs else None
+        if step == steps - 1:
+            while jobs:
+                ready = jobs.pop(0)(gate)
         cur, prev = halo_step(base, cour, cour_outer, outer, inner), cur
-        if done is not None:
-            cur, state[done] = together((cur, state[done]))
-    assert not any(jobs)
-
-    all_observed = state["known"][1].reshape(-1, 128)
-    cells = state["known"][0].reshape(-1).astype(jnp.int32)
-    if chunks == 1:
-        predicted = state["predicted"]
+        if ready is not None:
+            cur, state[ready] = together((cur, state[ready]))
+
+    sibling = swap(cur, 0, 1)
+    packed = recorded_traces(steps - 1, state.get("place", place), cur, surf)
+    other = swap(packed, 0, 1)
+    if count & (count - 1) == 0:
+        bit = 1
+        while bit < count:
+            packed = plus(packed, other)
+            other = swap(packed, bit, 1)
+            if bit == 1:
+                wavefield = join(cur, sibling)
+                other, wavefield = together((other, wavefield))
+            bit *= 2
     else:
+        wavefield = join(cur, sibling)
+        packed = lax.psum(packed + other, "mp")
+        other = jnp.zeros_like(packed)
+    traces = small_call(
+        unpack_kernel, shape((steps, receiver_cells.shape[0])), "unpack", packed, other
+    )
+    if hidden:
+        gravity_residual = state["own"].reshape(-1)
+        density_gradient = state["gradient"]
+    else:
+        cells = state["known"][0].reshape(-1).astype(jnp.int32)
 
         def add_chunk(i, total):
             head = head_of(i * reach, cells)
@@ -653,56 +706,16 @@
             )
 
         sums = lax.fori_loop(0, chunks, add_chunk, jnp.zeros((n_stations, vertical), F32))
-        predicted = jnp.sum(sums, axis=1).reshape(-1, 128)
-
-    kept = state["table"] if chunks == 1 else predicted
-    sibling = swap(cur, 0, 1)
-    packed = recorded_traces(steps - 1, place, cur, surf, predicted)
-    other = swap(packed, 0, 1)
-    if count & (count - 1) == 0:
-        bit = 1
-        while bit < count:
-            packed = packed + other
-            other = swap(packed, bit, 1)
-            if bit == 1:
-                wavefield = join(cur, sibling, kept)
-                other, wavefield = together((other, wavefield))
-            bit *= 2
-    else:
-        wavefield = join(cur, sibling, kept)
-        packed = lax.psum(packed + other, "mp")
-        other = jnp.zeros_like(packed)
-
-    receivers = receiver_cells.shape[0]
-    if chunks == 1:
-        traces, own, density_gradient = gravity_last(
-            steps,
-            receivers,
-            total_x,
-            slab,
-            block,
-            lateral,
-            state["head"],
-            packed,
-            other,
-            all_observed,
-            state["table"],
-        )
-        gravity_residual = own.reshape(-1)
-    else:
-        packed = packed + other
-        blocks = receivers // 128
-        traces = jnp.concatenate(
-            [packed[b * steps : (b + 1) * steps] for b in range(blocks)], axis=1
-        )
-        residual = (packed[steps * blocks :] - all_observed).reshape(-1)
-        gravity_residual = lax.dynamic_slice(residual, (s * own_stations,), (own_stations,))
-        weights = residual.astype(jnp.bfloat16).astype(F32)
+        predicted = jnp.sum(sums, axis=1)
+        predicted = lax.psum(predicted + swap(predicted, 0, 1), "mp")
+        difference = predicted - state["known"][1].reshape(-1)
+        gravity_residual = lax.dynamic_slice(difference, (s * own_stations,), (own_stations,))
+        weights = difference.astype(jnp.bfloat16).astype(F32).reshape(-1, 128)
 
         def back_chunk(i, total):
             head = head_of(i * reach, cells)
-            return total + gravity_adjoint(
-                reach, total_x, slab, block, lateral, head, weights, table_of(head[:1])
+            return gravity_adjoint(
+                range(lines), reach, total_x, lateral, head, weights, table_of(head[:1]), total
             )
 
         density_gradient = lax.fori_loop(

time: 112 us -> 112 us (level)
  local copies, waits for them, and re-layouts: 7.79 us -> 0.67 us
  waiting for transfers between devices: 23.3 us -> 28.2 us
  starting transfers between devices: 44.9 us -> 49.4 us
  Pallas kernels: 32.4 us -> 30.1 us
    unnamed x25 -> x8, local copies, waits for them, and re-layouts: 7.65 us -> 0.67 us
    ppermute x24 -> x28, waiting for transfers between devices: 3.86 us -> 10.2 us  [swap(): return lax.ppermute(value, AXES, pairs)]
    ppermute x24 -> x28, starting transfers between devices: 11.1 us -> 14.3 us  [swap(): return lax.ppermute(value, AXES, pairs)]
    pallas_call x8 -> x4, Pallas kernels: 12 us -> 8.91 us  [gravity_forward(): pl.pallas_call(functools.partial(forward_kernel, first, guard, total_x, s...]
    ppermute x16, waiting for transfers between devices: 19.4 us -> 18 us  [across(): return lax.ppermute(value, AXES, chain)]
    ppermute x16, starting transfers between devices: 33.8 us -> 35.1 us  [across(): return lax.ppermute(value, AXES, chain)]
    pallas_call x2 -> x12, Pallas kernels: 5.69 us -> 6.34 us  [the longest x2 4.73 us: gravity_adjoint(): pl.pallas_call(functools.partial(adjoint_kernel, lines, guard, total_x, l...]
  transfers between devices with their start and end apart: 40 -> 44, of which waited for: 17 -> 20; matrix products, arithmetic and copies ran while one was open for 2% -> 1% of each run, Pallas kernels for 23% -> 24%
where the time goes in v6:
time: 112 us
  starting transfers between devices  49.4 us (44%)
  Pallas kernels  30.1 us (27%)
  waiting for transfers between devices  28.2 us (25%)
  between operations  1.75 us (2%)
  other arithmetic  1.44 us (1%)
    ppermute x16, starting transfers between devices, across(): return lax.ppermute(value, AXES, chain)  35.1 us
    ppermute x16, waiting for transfers between devices, across(): return lax.ppermute(value, AXES, chain)  18 us
    ppermute x28, starting transfers between devices, swap(): return lax.ppermute(value, AXES, pairs)  14.3 us
    ppermute x28, waiting for transfers between devices, swap(): return lax.ppermute(value, AXES, pairs)  10.2 us
    pallas_call x4, Pallas kernels, gravity_forward(): pl.pallas_call(functools.partial(forward_kernel, first, guard, total_x, s...  8.91 us
    pallas_call x16, Pallas kernels, local_step(): pl.pallas_call(functools.partial(local_kernel, step), out_shape=(shape(cu...  6.22 us
    pallas_call x2, Pallas kernels, gravity_adjoint(): pl.pallas_call(functools.partial(adjoint_kernel, lines, guard, total_x, l...  4.73 us
    pallas_call x1, Pallas kernels, gravity_table(): pl.pallas_call(functools.partial(table_kernel, total_x, slab, 2 * lateral...  2.81 us
  transfers between devices with their start and end apart: 44, of which 20 were waited for; matrix products, arithmetic and copies ran while one was open for 1% of the time, Pallas kernels for 24%

profile of v6, /device:TPU:0, one launch (start us, length us, event | category | flops | bytes accessed | tf_op | source)
XLA Modules:
  0.0 111.5 jit_solution(7412665185973288481)
XLA Ops:
  1.7 3.0 %collective-permute-start = (f32[6,64,128]{2,1,0:T(8,128)S(1)}, f32[6,64,128]{2,1,0:T(8,128)S(1)}, u32[]{:S(2)}, u32[]{:S(2)}) collective-permute-start(f32[6,64,128]{2,1,0:T(8,128)S(1)} %get-tuple-element.108), channel_id=1, source_target_pairs={{0,4},{1,3},{2,6},{3,1},{4,0},{5,9},{6,2},{7,11},{8,12},{9,5},{10,... | collective-permute-start | bytes 589832 | tf_op jit(solution)/shard_map/ppermute | solution.py:527
  9.8 2.5 %collective-permute-start.2 = (f32[4,64,128]{2,1,0:T(8,128)S(1)}, f32[4,64,128]{2,1,0:T(8,128)S(1)}, u32[]{:S(2)}, u32[]{:S(2)}) collective-permute-start(f32[4,64,128]{2,1,0:T(8,128)S(1)} %wave_halo.16.cur.prev), channel_id=1, source_target_pairs={{0,4},{1,3},{2,6},{3,1},{4,0},{5,9},{6,2},{7,11},{8,12},{9,5},{10,... | collective-permute-start | bytes 393224 | tf_op jit(solution)/shard_map/ppermute | solution.py:527
  15.4 2.1 %collective-permute-start.4 = (f32[4,64,128]{2,1,0:T(8,128)S(1)}, f32[4,64,128]{2,1,0:T(8,128)S(1)}, u32[]{:S(2)}, u32[]{:S(2)}) collective-permute-start(f32[4,64,128]{2,1,0:T(8,128)S(1)} %wave_halo.17.cur.prev), channel_id=1, source_target_pairs={{0,4},{1,3},{2,6},{3,1},{4,0},{5,9},{6,2},{7,11},{8,12},{9,5},{10,... | collective-permute-start | bytes 393224 | tf_op jit(solution)/shard_map/ppermute | solution.py:527
  17.9 2.5 %collective-permute-done.4.outer = f32[4,64,128]{2,1,0:T(8,128)S(1)} collective-permute-done((f32[4,64,128]{2,1,0:T(8,128)S(1)}, f32[4,64,128]{2,1,0:T(8,128)S(1)}, u32[]{:S(2)}, u32[]{:S(2)}) %collective-permute-start.4) | collective-permute-done | bytes 131104 | tf_op jit(solution)/shard_map/ppermute | solution.py:527
  22.5 2.1 %collective-permute-start.7 = (f32[4,64,128]{2,1,0:T(8,128)S(1)}, f32[4,64,128]{2,1,0:T(8,128)S(1)}, u32[]{:S(2)}, u32[]{:S(2)}) collective-permute-start(f32[4,64,128]{2,1,0:T(8,128)S(1)} %wave_halo.18.cur.prev), channel_id=1, source_target_pairs={{0,4},{1,3},{2,6},{3,1},{4,0},{5,9},{6,2},{7,11},{8,12},{9,5},{10,... | collective-permute-start | bytes 393224 | tf_op jit(solution)/shard_map/ppermute | solution.py:527
  24.6 2.9 %collective-permute-done.7.outer = f32[4,64,128]{2,1,0:T(8,128)S(1)} collective-permute-done((f32[4,64,128]{2,1,0:T(8,128)S(1)}, f32[4,64,128]{2,1,0:T(8,128)S(1)}, u32[]{:S(2)}, u32[]{:S(2)}) %collective-permute-start.7) | collective-permute-done | bytes 131104 | tf_op jit(solution)/shard_map/ppermute | solution.py:527
  27.6 2.1 %collective-permute-start.10 = (f32[4,64,128]{2,1,0:T(8,128)S(1)}, f32[4,64,128]{2,1,0:T(8,128)S(1)}, u32[]{:S(2)}, u32[]{:S(2)}) collective-permute-start(f32[4,64,128]{2,1,0:T(8,128)S(1)} %wave_halo.19.cur.prev), channel_id=1, source_target_pairs={{0,4},{1,3},{2,6},{3,1},{4,0},{5,9},{6,2},{7,11},{8,12},{9,5},{10,... | collective-permute-start | bytes 393224 | tf_op jit(solution)/shard_map/ppermute | solution.py:527
  30.2 2.8 %gravity_table.1.table = f32[9088,128]{1,0:T(8,128)S(1)} custom-call(s32[1]{0:T(128)} %constant.54.clone.1.head), custom_call_target="tpu_custom_call" | custom-call | flops 23265280 | bytes 4653056 | tf_op jit(solution)/shard_map/gravity_table/pallas_call | solution.py:317
  35.2 2.2 %gravity_forward.4.refs_0_ = f32[128,128]{1,0:T(8,128)S(1)} custom-call(s32[513]{0:T(1024)S(1)} %pad_add_fusion.head, f32[9088,128]{1,0:T(8,128)S(1)} %gravity_table.1.table, f32[4,64,128]{2,1,0:T(8,128)S(1)} %get-tuple-element.133.dens), custom_call_target="tpu_custom_call" | custom-call | flops 16777216 | bytes 131072 | tf_op jit(solution)/shard_map/gravity_forward/pallas_call | solution.py:362
  38.2 2.3 %collective-permute-start.14 = (f32[4,64,128]{2,1,0:T(8,128)S(1)}, f32[4,64,128]{2,1,0:T(8,128)S(1)}, u32[]{:S(2)}, u32[]{:S(2)}) collective-permute-start(f32[4,64,128]{2,1,0:T(8,128)S(1)} %wave_halo.21.cur.prev), channel_id=1, source_target_pairs={{0,4},{1,3},{2,6},{3,1},{4,0},{5,9},{6,2},{7,11},{8,12},{9,5},{10,... | collective-permute-start | bytes 393224 | tf_op jit(solution)/shard_map/ppermute | solution.py:527
  40.9 2.2 %gravity_forward.5.refs_1_ = f32[128,128]{1,0:T(8,128)S(1)} custom-call(s32[513]{0:T(1024)S(1)} %pad_add_fusion.head, f32[9088,128]{1,0:T(8,128)S(1)} %gravity_table.1.table, f32[4,64,128]{2,1,0:T(8,128)S(1)} %get-tuple-element.133.dens), custom_call_target="tpu_custom_call" | custom-call | flops 16777216 | bytes 131072 | tf_op jit(solution)/shard_map/gravity_forward/pallas_call | solution.py:362
  43.5 2.1 %collective-permute-start.16 = (f32[4,64,128]{2,1,0:T(8,128)S(1)}, f32[4,64,128]{2,1,0:T(8,128)S(1)}, u32[]{:S(2)}, u32[]{:S(2)}) collective-permute-start(f32[4,64,128]{2,1,0:T(8,128)S(1)} %wave_halo.22.cur.prev), channel_id=1, source_target_pairs={{0,4},{1,3},{2,6},{3,1},{4,0},{5,9},{6,2},{7,11},{8,12},{9,5},{10,... | collective-permute-start | bytes 393224 | tf_op jit(solution)/shard_map/ppermute | solution.py:527
  46.1 2.2 %gravity_forward.6.refs_2_ = f32[128,128]{1,0:T(8,128)S(1)} custom-call(s32[513]{0:T(1024)S(1)} %pad_add_fusion.head, f32[9088,128]{1,0:T(8,128)S(1)} %gravity_table.1.table, f32[4,64,128]{2,1,0:T(8,128)S(1)} %get-tuple-element.133.dens), custom_call_target="tpu_custom_call" | custom-call | flops 16777216 | bytes 131072 | tf_op jit(solution)/shard_map/gravity_forward/pallas_call | solution.py:362
  48.7 2.3 %collective-permute-start.18 = (f32[4,64,128]{2,1,0:T(8,128)S(1)}, f32[4,64,128]{2,1,0:T(8,128)S(1)}, u32[]{:S(2)}, u32[]{:S(2)}) collective-permute-start(f32[4,64,128]{2,1,0:T(8,128)S(1)} %wave_halo.23.cur.prev), channel_id=1, source_target_pairs={{0,4},{1,3},{2,6},{3,1},{4,0},{5,9},{6,2},{7,11},{8,12},{9,5},{10,... | collective-permute-start | bytes 393224 | tf_op jit(solution)/shard_map/ppermute | solution.py:527
  51.3 2.2 %gravity_forward.7.refs_3_ = f32[128,128]{1,0:T(8,128)S(1)} custom-call(s32[513]{0:T(1024)S(1)} %pad_add_fusion.head, f32[9088,128]{1,0:T(8,128)S(1)} %gravity_table.1.table, f32[4,64,128]{2,1,0:T(8,128)S(1)} %get-tuple-element.133.dens), custom_call_target="tpu_custom_call" | custom-call | flops 16777216 | bytes 131072 | tf_op jit(solution)/shard_map/gravity_forward/pallas_call | solution.py:362
  54.0 2.1 %collective-permute-start.20 = (f32[4,64,128]{2,1,0:T(8,128)S(1)}, f32[4,64,128]{2,1,0:T(8,128)S(1)}, u32[]{:S(2)}, u32[]{:S(2)}) collective-permute-start(f32[4,64,128]{2,1,0:T(8,128)S(1)} %wave_halo.24.cur.prev), channel_id=1, source_target_pairs={{0,4},{1,3},{2,6},{3,1},{4,0},{5,9},{6,2},{7,11},{8,12},{9,5},{10,... | collective-permute-start | bytes 393224 | tf_op jit(solution)/shard_map/ppermute | solution.py:527
  56.5 2.8 %collective-permute-done.20.outer = f32[4,64,128]{2,1,0:T(8,128)S(1)} collective-permute-done((f32[4,64,128]{2,1,0:T(8,128)S(1)}, f32[4,64,128]{2,1,0:T(8,128)S(1)}, u32[]{:S(2)}, u32[]{:S(2)}) %collective-permute-start.20) | collective-permute-done | bytes 131104 | tf_op jit(solution)/shard_map/ppermute | solution.py:527
  59.3 2.5 %collective-permute-start.22 = (f32[4,64,128]{2,1,0:T(8,128)S(1)}, f32[4,64,128]{2,1,0:T(8,128)S(1)}, u32[]{:S(2)}, u32[]{:S(2)}) collective-permute-start(f32[4,64,128]{2,1,0:T(8,128)S(1)} %wave_halo.25.cur.prev), channel_id=1, source_target_pairs={{0,4},{1,3},{2,6},{3,1},{4,0},{5,9},{6,2},{7,11},{8,12},{9,5},{10,... | collective-permute-start | bytes 393224 | tf_op jit(solution)/shard_map/ppermute | solution.py:527
  62.4 2.4 %collective-permute-done.22.outer = f32[4,64,128]{2,1,0:T(8,128)S(1)} collective-permute-done((f32[4,64,128]{2,1,0:T(8,128)S(1)}, f32[4,64,128]{2,1,0:T(8,128)S(1)}, u32[]{:S(2)}, u32[]{:S(2)}) %collective-permute-start.22) | collective-permute-done | bytes 131104 | tf_op jit(solution)/shard_map/ppermute | solution.py:527
  64.9 2.1 %collective-permute-start.25 = (f32[4,64,128]{2,1,0:T(8,128)S(1)}, f32[4,64,128]{2,1,0:T(8,128)S(1)}, u32[]{:S(2)}, u32[]{:S(2)}) collective-permute-start(f32[4,64,128]{2,1,0:T(8,128)S(1)} %wave_halo.26.cur.prev), channel_id=1, source_target_pairs={{0,4},{1,3},{2,6},{3,1},{4,0},{5,9},{6,2},{7,11},{8,12},{9,5},{10,... | collective-permute-start | bytes 393224 | tf_op jit(solution)/shard_map/ppermute | solution.py:527
  70.0 2.1 %collective-permute-start.28 = (f32[4,64,128]{2,1,0:T(8,128)S(1)}, f32[4,64,128]{2,1,0:T(8,128)S(1)}, u32[]{:S(2)}, u32[]{:S(2)}) collective-permute-start(f32[4,64,128]{2,1,0:T(8,128)S(1)} %wave_halo.27.cur.prev), channel_id=1, source_target_pairs={{0,4},{1,3},{2,6},{3,1},{4,0},{5,9},{6,2},{7,11},{8,12},{9,5},{10,... | collective-permute-start | bytes 393224 | tf_op jit(solution)/shard_map/ppermute | solution.py:527
  72.3 2.8 %collective-permute-done.27.second = f32[4,128]{1,0:T(4,128)S(1)} collective-permute-done((f32[4,128]{1,0:T(4,128)S(1)}, f32[4,128]{1,0:T(4,128)S(1)}, u32[]{:S(2)}, u32[]{:S(2)}) %collective-permute-start.27) | collective-permute-done | bytes 2080 | tf_op jit(solution)/shard_map/ppermute | solution.py:531
  77.2 2.1 %collective-permute-start.30 = (f32[4,128]{1,0:T(4,128)S(1)}, f32[4,128]{1,0:T(4,128)S(1)}, u32[]{:S(2)}, u32[]{:S(2)}) collective-permute-start(f32[4,128]{1,0:T(4,128)S(1)} %sum.7.first), channel_id=1, source_target_pairs={{0,9},{1,8},{2,11},{3,10},{4,13},{5,12},{6,15},{7,14},{8,1},{9,0},... | collective-permute-start | bytes 6152 | tf_op jit(solution)/shard_map/ppermute | solution.py:531
  79.3 2.0 %collective-permute-done.30.second = f32[4,128]{1,0:T(4,128)S(1)} collective-permute-done((f32[4,128]{1,0:T(4,128)S(1)}, f32[4,128]{1,0:T(4,128)S(1)}, u32[]{:S(2)}, u32[]{:S(2)}) %collective-permute-start.30) | collective-permute-done | bytes 2080 | tf_op jit(solution)/shard_map/ppermute | solution.py:531
  81.3 2.4 %collective-permute-start.33 = (f32[4,128]{1,0:T(4,128)S(1)}, f32[4,128]{1,0:T(4,128)S(1)}, u32[]{:S(2)}, u32[]{:S(2)}) collective-permute-start(f32[4,128]{1,0:T(4,128)S(1)} %sum.8.packed), channel_id=1, source_target_pairs={{0,17},{1,16},{2,19},{3,18},{4,21},{5,20},{6,23},{7,22},{8,25},{9,... | collective-permute-start | bytes 6152 | tf_op jit(solution)/shard_map/ppermute | solution.py:531
  85.8 1.9 %collective-permute-start.34 = (f32[4,64,128]{2,1,0:T(8,128)S(1)}, f32[4,64,128]{2,1,0:T(8,128)S(1)}, u32[]{:S(2)}, u32[]{:S(2)}) collective-permute-start(f32[4,64,128]{2,1,0:T(8,128)S(1)} %wave_halo.29.cur.prev), channel_id=1, source_target_pairs={{0,4},{1,3},{2,6},{3,1},{4,0},{5,9},{6,2},{7,11},{8,12},{9,5},{10,... | collective-permute-start | bytes 393224 | tf_op jit(solution)/shard_map/ppermute | solution.py:527
  88.6 2.0 %gravity_adjoint.2.start_at = f32[8,16,128]{2,1,0:T(8,128)S(1)} custom-call(s32[513]{0:T(1024)S(1)} %pad_add_fusion.head, f32[4,128]{1,0:T(4,128)S(1)} %get-tuple-element.194.weights, f32[9088,128]{1,0:T(8,128)S(1)} %gravity_table.1.table, f32[8,16,128]{2,1,0:T(8,128)S(1)} %broadcast_in_dim.16.start_at), custom_call_target="tpu_custom_call" | custom-call | flops 8388608 | bytes 131072 | tf_op jit(solution)/shard_map/gravity_adjoint/pallas_call | solution.py:402
  91.7 2.5 %collective-permute-start.37 = (f32[4,64,128]{2,1,0:T(8,128)S(1)}, f32[4,64,128]{2,1,0:T(8,128)S(1)}, u32[]{:S(2)}, u32[]{:S(2)}) collective-permute-start(f32[4,64,128]{2,1,0:T(8,128)S(1)} %wave_halo.30.cur), channel_id=1, source_target_pairs={{0,4},{1,3},{2,6},{3,1},{4,0},{5,9},{6,2},{7,11},{8,12},{9,5},{10,... | collective-permute-start | bytes 393224 | tf_op jit(solution)/shard_map/ppermute | solution.py:527
  99.1 2.0 %collective-permute-start.40 = (f32[32,128]{1,0:T(8,128)S(1)}, f32[32,128]{1,0:T(8,128)S(1)}, u32[]{:S(2)}, u32[]{:S(2)}) collective-permute-start(f32[32,128]{1,0:T(8,128)S(1)} %sum.9.first), channel_id=1, source_target_pairs={{0,5},{1,4},{2,7},{3,6},{4,1},{5,0},{6,3},{7,2},{8,13},{9,12},{10,... | collective-permute-start | bytes 49160 | tf_op jit(solution)/shard_map/ppermute | solution.py:531
  103.9 1.8 %collective-permute-done.42.second = f32[32,128]{1,0:T(8,128)S(1)} collective-permute-done((f32[32,128]{1,0:T(8,128)S(1)}, f32[32,128]{1,0:T(8,128)S(1)}, u32[]{:S(2)}, u32[]{:S(2)}) %collective-permute-start.42) | collective-permute-done | bytes 16416 | tf_op jit(solution)/shard_map/ppermute | solution.py:531
  105.7 2.5 %collective-permute-start.43 = (f32[32,128]{1,0:T(8,128)S(1)}, f32[32,128]{1,0:T(8,128)S(1)}, u32[]{:S(2)}, u32[]{:S(2)}) collective-permute-start(f32[32,128]{1,0:T(8,128)S(1)} %sum.11.packed), channel_id=1, source_target_pairs={{0,17},{1,16},{2,19},{3,18},{4,21},{5,20},{6,23},{7,22},{8,25},{9,... | collective-permute-start | bytes 49160 | tf_op jit(solution)/shard_map/ppermute | solution.py:531
  108.2 2.7 %gravity_adjoint.3 = f32[8,16,128]{2,1,0:T(8,128)} custom-call(s32[513]{0:T(1024)S(1)} %pad_add_fusion.head, f32[4,128]{1,0:T(4,128)S(1)} %get-tuple-element.194.weights, f32[9088,128]{1,0:T(8,128)S(1)} %gravity_table.1.table, f32[8,16,128]{2,1,0:T(8,128)S(1)} %gravity_adjoint.2.start_at), custom_call_target="tpu_custom_call" | custom-call | flops 8388608 | bytes 131072 | tf_op jit(solution)/shard_map/gravity_adjoint/pallas_call | solution.py:402
  (127 shorter events, 35.2 us)
Async XLA Ops:
  1.7 8.1 %collective-permute-start = (f32[6,64,128]{2,1,0:T(8,128)S(1)}, f32[6,64,128]{2,1,0:T(8,128)S(1)}, u32[]{:S(2)}, u32[]{:S(2)}) collective-permute-start(f32[6,64,128]{2,1,0:T(8,128)S(1)} %get-tuple-element.108), channel_id=1, source_target_pairs={{0,4},{1,3},{2,6},{3,1},{4,0},{5,9},{6,2},{7,11},{8,12},{9,5},{10,... | collective-permute-start | bytes 589832 | tf_op jit(solution)/shard_map/ppermute | solution.py:527
  4.7 3.4 %collective-permute-start.1 = (f32[4,64,128]{2,1,0:T(8,128)S(1)}, f32[4,64,128]{2,1,0:T(8,128)S(1)}, u32[]{:S(2)}, u32[]{:S(2)}) collective-permute-start(f32[4,64,128]{2,1,0:T(8,128)S(1)} %get-tuple-element.103.cur.prev), channel_id=1, source_target_pairs={{0,1},{1,0},{2,3},{3,2},{4,5},{5,4},{6,7},{7,6},{8,9},{9,8},{10,11... | collective-permute-start | bytes 393224 | tf_op jit(solution)/shard_map/ppermute | solution.py:531
  9.8 5.5 %collective-permute-start.2 = (f32[4,64,128]{2,1,0:T(8,128)S(1)}, f32[4,64,128]{2,1,0:T(8,128)S(1)}, u32[]{:S(2)}, u32[]{:S(2)}) collective-permute-start(f32[4,64,128]{2,1,0:T(8,128)S(1)} %wave_halo.16.cur.prev), channel_id=1, source_target_pairs={{0,4},{1,3},{2,6},{3,1},{4,0},{5,9},{6,2},{7,11},{8,12},{9,5},{10,... | collective-permute-start | bytes 393224 | tf_op jit(solution)/shard_map/ppermute | solution.py:527
  14.1 3.4 %collective-permute-start.6 = (f32[2,1,128]{2,1,0:T(1,128)S(1)}, f32[2,1,128]{2,1,0:T(1,128)S(1)}, u32[]{:S(2)}, u32[]{:S(2)}) collective-permute-start(f32[2,1,128]{2,1,0:T(1,128)S(1)} %bitcast.11), channel_id=1, source_target_pairs={{0,1},{1,0},{2,3},{3,2},{4,5},{5,4},{6,7},{7,6},{8,9},{9,8},{10,11... | collective-permute-start | bytes 3080 | tf_op jit(solution)/shard_map/ppermute | solution.py:531
  15.4 5.0 %collective-permute-start.4 = (f32[4,64,128]{2,1,0:T(8,128)S(1)}, f32[4,64,128]{2,1,0:T(8,128)S(1)}, u32[]{:S(2)}, u32[]{:S(2)}) collective-permute-start(f32[4,64,128]{2,1,0:T(8,128)S(1)} %wave_halo.17.cur.prev), channel_id=1, source_target_pairs={{0,4},{1,3},{2,6},{3,1},{4,0},{5,9},{6,2},{7,11},{8,12},{9,5},{10,... | collective-permute-start | bytes 393224 | tf_op jit(solution)/shard_map/ppermute | solution.py:527
  20.9 3.7 %collective-permute-start.9 = (f32[2,2,128]{2,1,0:T(2,128)S(1)}, f32[2,2,128]{2,1,0:T(2,128)S(1)}, u32[]{:S(2)}, u32[]{:S(2)}) collective-permute-start(f32[2,2,128]{2,1,0:T(2,128)S(1)} %pad_maximum_fusion.1), channel_id=1, source_target_pairs={{0,2},{1,3},{2,0},{3,1},{4,6},{5,7},{6,4},{7,5},{8,10},{9,11},{10,... | collective-permute-start | bytes 6152 | tf_op jit(solution)/shard_map/ppermute | solution.py:531
  22.5 5.0 %collective-permute-start.7 = (f32[4,64,128]{2,1,0:T(8,128)S(1)}, f32[4,64,128]{2,1,0:T(8,128)S(1)}, u32[]{:S(2)}, u32[]{:S(2)}) collective-permute-start(f32[4,64,128]{2,1,0:T(8,128)S(1)} %wave_halo.18.cur.prev), channel_id=1, source_target_pairs={{0,4},{1,3},{2,6},{3,1},{4,0},{5,9},{6,2},{7,11},{8,12},{9,5},{10,... | collective-permute-start | bytes 393224 | tf_op jit(solution)/shard_map/ppermute | solution.py:527
  27.6 5.4 %collective-permute-start.10 = (f32[4,64,128]{2,1,0:T(8,128)S(1)}, f32[4,64,128]{2,1,0:T(8,128)S(1)}, u32[]{:S(2)}, u32[]{:S(2)}) collective-permute-start(f32[4,64,128]{2,1,0:T(8,128)S(1)} %wave_halo.19.cur.prev), channel_id=1, source_target_pairs={{0,4},{1,3},{2,6},{3,1},{4,0},{5,9},{6,2},{7,11},{8,12},{9,5},{10,... | collective-permute-start | bytes 393224 | tf_op jit(solution)/shard_map/ppermute | solution.py:527
  29.7 3.3 %collective-permute-start.11 = (f32[4,64,128]{2,1,0:T(8,128)S(1)}, f32[4,64,128]{2,1,0:T(8,128)S(1)}, u32[]{:S(2)}, u32[]{:S(2)}) collective-permute-start(f32[4,64,128]{2,1,0:T(8,128)S(1)} %wave_halo.19.cur.prev), channel_id=1, source_target_pairs={{0,1},{1,0},{2,3},{3,2},{4,5},{5,4},{6,7},{7,6},{8,9},{9,8},{10,11... | collective-permute-start | bytes 393224 | tf_op jit(solution)/shard_map/ppermute | solution.py:531
  33.1 5.0 %collective-permute-start.12 = (f32[4,64,128]{2,1,0:T(8,128)S(1)}, f32[4,64,128]{2,1,0:T(8,128)S(1)}, u32[]{:S(2)}, u32[]{:S(2)}) collective-permute-start(f32[4,64,128]{2,1,0:T(8,128)S(1)} %wave_halo.20.cur.prev), channel_id=1, source_target_pairs={{0,4},{1,3},{2,6},{3,1},{4,0},{5,9},{6,2},{7,11},{8,12},{9,5},{10,... | collective-permute-start | bytes 393224 | tf_op jit(solution)/shard_map/ppermute | solution.py:527
  34.8 3.3 %collective-permute-start.13 = (f32[4,64,128]{2,1,0:T(8,128)S(1)}, f32[4,64,128]{2,1,0:T(8,128)S(1)}, u32[]{:S(2)}, u32[]{:S(2)}) collective-permute-start(f32[4,64,128]{2,1,0:T(8,128)S(1)} %wave_halo.20.cur.prev), channel_id=1, source_target_pairs={{0,1},{1,0},{2,3},{3,2},{4,5},{5,4},{6,7},{7,6},{8,9},{9,8},{10,11... | collective-permute-start | bytes 393224 | tf_op jit(solution)/shard_map/ppermute | solution.py:531
  38.2 5.3 %collective-permute-start.14 = (f32[4,64,128]{2,1,0:T(8,128)S(1)}, f32[4,64,128]{2,1,0:T(8,128)S(1)}, u32[]{:S(2)}, u32[]{:S(2)}) collective-permute-start(f32[4,64,128]{2,1,0:T(8,128)S(1)} %wave_halo.21.cur.prev), channel_id=1, source_target_pairs={{0,4},{1,3},{2,6},{3,1},{4,0},{5,9},{6,2},{7,11},{8,12},{9,5},{10,... | collective-permute-start | bytes 393224 | tf_op jit(solution)/shard_map/ppermute | solution.py:527
  43.5 5.1 %collective-permute-start.16 = (f32[4,64,128]{2,1,0:T(8,128)S(1)}, f32[4,64,128]{2,1,0:T(8,128)S(1)}, u32[]{:S(2)}, u32[]{:S(2)}) collective-permute-start(f32[4,64,128]{2,1,0:T(8,128)S(1)} %wave_halo.22.cur.prev), channel_id=1, source_target_pairs={{0,4},{1,3},{2,6},{3,1},{4,0},{5,9},{6,2},{7,11},{8,12},{9,5},{10,... | collective-permute-start | bytes 393224 | tf_op jit(solution)/shard_map/ppermute | solution.py:527
  48.7 5.2 %collective-permute-start.18 = (f32[4,64,128]{2,1,0:T(8,128)S(1)}, f32[4,64,128]{2,1,0:T(8,128)S(1)}, u32[]{:S(2)}, u32[]{:S(2)}) collective-permute-start(f32[4,64,128]{2,1,0:T(8,128)S(1)} %wave_halo.23.cur.prev), channel_id=1, source_target_pairs={{0,4},{1,3},{2,6},{3,1},{4,0},{5,9},{6,2},{7,11},{8,12},{9,5},{10,... | collective-permute-start | bytes 393224 | tf_op jit(solution)/shard_map/ppermute | solution.py:527
  54.0 5.3 %collective-permute-start.20 = (f32[4,64,128]{2,1,0:T(8,128)S(1)}, f32[4,64,128]{2,1,0:T(8,128)S(1)}, u32[]{:S(2)}, u32[]{:S(2)}) collective-permute-start(f32[4,64,128]{2,1,0:T(8,128)S(1)} %wave_halo.24.cur.prev), channel_id=1, source_target_pairs={{0,4},{1,3},{2,6},{3,1},{4,0},{5,9},{6,2},{7,11},{8,12},{9,5},{10,... | collective-permute-start | bytes 393224 | tf_op jit(solution)/shard_map/ppermute | solution.py:527
  56.1 3.2 %collective-permute-start.21 = (f32[4,64,128]{2,1,0:T(8,128)S(1)}, f32[4,64,128]{2,1,0:T(8,128)S(1)}, u32[]{:S(2)}, u32[]{:S(2)}) collective-permute-start(f32[4,64,128]{2,1,0:T(8,128)S(1)} %wave_halo.24.cur.prev), channel_id=1, source_target_pairs={{0,1},{1,0},{2,3},{3,2},{4,5},{5,4},{6,7},{7,6},{8,9},{9,8},{10,11... | collective-permute-start | bytes 393224 | tf_op jit(solution)/shard_map/ppermute | solution.py:531
  59.3 5.5 %collective-permute-start.22 = (f32[4,64,128]{2,1,0:T(8,128)S(1)}, f32[4,64,128]{2,1,0:T(8,128)S(1)}, u32[]{:S(2)}, u32[]{:S(2)}) collective-permute-start(f32[4,64,128]{2,1,0:T(8,128)S(1)} %wave_halo.25.cur.prev), channel_id=1, source_target_pairs={{0,4},{1,3},{2,6},{3,1},{4,0},{5,9},{6,2},{7,11},{8,12},{9,5},{10,... | collective-permute-start | bytes 393224 | tf_op jit(solution)/shard_map/ppermute | solution.py:527
  64.9 5.0 %collective-permute-start.25 = (f32[4,64,128]{2,1,0:T(8,128)S(1)}, f32[4,64,128]{2,1,0:T(8,128)S(1)}, u32[]{:S(2)}, u32[]{:S(2)}) collective-permute-start(f32[4,64,128]{2,1,0:T(8,128)S(1)} %wave_halo.26.cur.prev), channel_id=1, source_target_pairs={{0,4},{1,3},{2,6},{3,1},{4,0},{5,9},{6,2},{7,11},{8,12},{9,5},{10,... | collective-permute-start | bytes 393224 | tf_op jit(solution)/shard_map/ppermute | solution.py:527
  70.0 5.5 %collective-permute-start.28 = (f32[4,64,128]{2,1,0:T(8,128)S(1)}, f32[4,64,128]{2,1,0:T(8,128)S(1)}, u32[]{:S(2)}, u32[]{:S(2)}) collective-permute-start(f32[4,64,128]{2,1,0:T(8,128)S(1)} %wave_halo.27.cur.prev), channel_id=1, source_target_pairs={{0,4},{1,3},{2,6},{3,1},{4,0},{5,9},{6,2},{7,11},{8,12},{9,5},{10,... | collective-permute-start | bytes 393224 | tf_op jit(solution)/shard_map/ppermute | solution.py:527
  72.1 3.5 %collective-permute-start.29 = (f32[4,64,128]{2,1,0:T(8,128)S(1)}, f32[4,64,128]{2,1,0:T(8,128)S(1)}, u32[]{:S(2)}, u32[]{:S(2)}) collective-permute-start(f32[4,64,128]{2,1,0:T(8,128)S(1)} %wave_halo.27.cur.prev), channel_id=1, source_target_pairs={{0,1},{1,0},{2,3},{3,2},{4,5},{5,4},{6,7},{7,6},{8,9},{9,8},{10,11... | collective-permute-start | bytes 393224 | tf_op jit(solution)/shard_map/ppermute | solution.py:531
  75.6 10.1 %collective-permute-start.31 = (f32[4,64,128]{2,1,0:T(8,128)S(1)}, f32[4,64,128]{2,1,0:T(8,128)S(1)}, u32[]{:S(2)}, u32[]{:S(2)}) collective-permute-start(f32[4,64,128]{2,1,0:T(8,128)S(1)} %wave_halo.28.cur.prev), channel_id=1, source_target_pairs={{0,4},{1,3},{2,6},{3,1},{4,0},{5,9},{6,2},{7,11},{8,12},{9,5},{10,... | collective-permute-start | bytes 393224 | tf_op jit(solution)/shard_map/ppermute | solution.py:527
  77.2 8.5 %collective-permute-start.32 = (f32[4,64,128]{2,1,0:T(8,128)S(1)}, f32[4,64,128]{2,1,0:T(8,128)S(1)}, u32[]{:S(2)}, u32[]{:S(2)}) collective-permute-start(f32[4,64,128]{2,1,0:T(8,128)S(1)} %wave_halo.28.cur.prev), channel_id=1, source_target_pairs={{0,1},{1,0},{2,3},{3,2},{4,5},{5,4},{6,7},{7,6},{8,9},{9,8},{10,11... | collective-permute-start | bytes 393224 | tf_op jit(solution)/shard_map/ppermute | solution.py:531
  77.2 4.1 %collective-permute-start.30 = (f32[4,128]{1,0:T(4,128)S(1)}, f32[4,128]{1,0:T(4,128)S(1)}, u32[]{:S(2)}, u32[]{:S(2)}) collective-permute-start(f32[4,128]{1,0:T(4,128)S(1)} %sum.7.first), channel_id=1, source_target_pairs={{0,9},{1,8},{2,11},{3,10},{4,13},{5,12},{6,15},{7,14},{8,1},{9,0},... | collective-permute-start | bytes 6152 | tf_op jit(solution)/shard_map/ppermute | solution.py:531
  81.3 3.9 %collective-permute-start.33 = (f32[4,128]{1,0:T(4,128)S(1)}, f32[4,128]{1,0:T(4,128)S(1)}, u32[]{:S(2)}, u32[]{:S(2)}) collective-permute-start(f32[4,128]{1,0:T(4,128)S(1)} %sum.8.packed), channel_id=1, source_target_pairs={{0,17},{1,16},{2,19},{3,18},{4,21},{5,20},{6,23},{7,22},{8,25},{9,... | collective-permute-start | bytes 6152 | tf_op jit(solution)/shard_map/ppermute | solution.py:531
  85.8 5.8 %collective-permute-start.34 = (f32[4,64,128]{2,1,0:T(8,128)S(1)}, f32[4,64,128]{2,1,0:T(8,128)S(1)}, u32[]{:S(2)}, u32[]{:S(2)}) collective-permute-start(f32[4,64,128]{2,1,0:T(8,128)S(1)} %wave_halo.29.cur.prev), channel_id=1, source_target_pairs={{0,4},{1,3},{2,6},{3,1},{4,0},{5,9},{6,2},{7,11},{8,12},{9,5},{10,... | collective-permute-start | bytes 393224 | tf_op jit(solution)/shard_map/ppermute | solution.py:527
  87.7 3.9 %collective-permute-start.35 = (f32[4,64,128]{2,1,0:T(8,128)S(1)}, f32[4,64,128]{2,1,0:T(8,128)S(1)}, u32[]{:S(2)}, u32[]{:S(2)}) collective-permute-start(f32[4,64,128]{2,1,0:T(8,128)S(1)} %wave_halo.29.cur.prev), channel_id=1, source_target_pairs={{0,1},{1,0},{2,3},{3,2},{4,5},{5,4},{6,7},{7,6},{8,9},{9,8},{10,11... | collective-permute-start | bytes 393224 | tf_op jit(solution)/shard_map/ppermute | solution.py:531
  87.7 6.9 %collective-permute-start.36 = (f32[6,64,128]{2,1,0:T(8,128)S(1)}, f32[6,64,128]{2,1,0:T(8,128)S(1)}, u32[]{:S(2)}, u32[]{:S(2)}) collective-permute-start(f32[6,64,128]{2,1,0:T(8,128)S(1)} %collective-permute-done.outer), channel_id=1, source_target_pairs={{0,1},{1,0},{2,3},{3,2},{4,5},{5,4},{6,7},{7,6},{8,9},{9,8},{10,11... | collective-permute-start | bytes 589832 | tf_op jit(solution)/shard_map/ppermute | solution.py:531
  91.7 5.5 %collective-permute-start.37 = (f32[4,64,128]{2,1,0:T(8,128)S(1)}, f32[4,64,128]{2,1,0:T(8,128)S(1)}, u32[]{:S(2)}, u32[]{:S(2)}) collective-permute-start(f32[4,64,128]{2,1,0:T(8,128)S(1)} %wave_halo.30.cur), channel_id=1, source_target_pairs={{0,4},{1,3},{2,6},{3,1},{4,0},{5,9},{6,2},{7,11},{8,12},{9,5},{10,... | collective-permute-start | bytes 393224 | tf_op jit(solution)/shard_map/ppermute | solution.py:527
  97.2 3.9 %collective-permute-start.41 = (f32[4,64,128]{2,1,0:T(8,128)S(1)}, f32[4,64,128]{2,1,0:T(8,128)S(1)}, u32[]{:S(2)}, u32[]{:S(2)}) collective-permute-start(f32[4,64,128]{2,1,0:T(8,128)S(1)} %wave_halo.31.cur.own), channel_id=1, source_target_pairs={{0,1},{1,0},{2,3},{3,2},{4,5},{5,4},{6,7},{7,6},{8,9},{9,8},{10,11... | collective-permute-start | bytes 393224 | tf_op jit(solution)/shard_map/ppermute | solution.py:531
  99.1 3.5 %collective-permute-start.40 = (f32[32,128]{1,0:T(8,128)S(1)}, f32[32,128]{1,0:T(8,128)S(1)}, u32[]{:S(2)}, u32[]{:S(2)}) collective-permute-start(f32[32,128]{1,0:T(8,128)S(1)} %sum.9.first), channel_id=1, source_target_pairs={{0,5},{1,4},{2,7},{3,6},{4,1},{5,0},{6,3},{7,2},{8,13},{9,12},{10,... | collective-permute-start | bytes 49160 | tf_op jit(solution)/shard_map/ppermute | solution.py:531
  102.6 3.2 %collective-permute-start.42 = (f32[32,128]{1,0:T(8,128)S(1)}, f32[32,128]{1,0:T(8,128)S(1)}, u32[]{:S(2)}, u32[]{:S(2)}) collective-permute-start(f32[32,128]{1,0:T(8,128)S(1)} %sum.10.first), channel_id=1, source_target_pairs={{0,9},{1,8},{2,11},{3,10},{4,13},{5,12},{6,15},{7,14},{8,1},{9,0},... | collective-permute-start | bytes 49160 | tf_op jit(solution)/shard_map/ppermute | solution.py:531
  105.7 5.2 %collective-permute-start.43 = (f32[32,128]{1,0:T(8,128)S(1)}, f32[32,128]{1,0:T(8,128)S(1)}, u32[]{:S(2)}, u32[]{:S(2)}) collective-permute-start(f32[32,128]{1,0:T(8,128)S(1)} %sum.11.packed), channel_id=1, source_target_pairs={{0,17},{1,16},{2,19},{3,18},{4,21},{5,20},{6,23},{7,22},{8,25},{9,... | collective-permute-start | bytes 49160 | tf_op jit(solution)/shard_map/ppermute | solution.py:531
  (16 other events, 93.1 us)

commit v7 on v6

--- a/solution.py
+++ b/solution.py
@@ -6,6 +6,7 @@
 from jax.experimental import pallas as pl
 from jax.experimental.pallas import tpu as pltpu
 from jax.sharding import PartitionSpec as P
+
 
 STENCIL = (-205.0 / 72.0, 8.0 / 5.0, -1.0 / 5.0, 8.0 / 315.0, -1.0 / 560.0)
 TIME_RATIO = 0.1
@@ -327,8 +328,8 @@
     )(head)
 
 
-def forward_kernel(first, guard, total_x, slab, lateral, head, table, dens, out):
-    planes, rows, lanes = dens.shape
+def forward_kernel(first, guard, total_x, lateral, head, table, dens, out):
+    planes, rows, _ = dens.shape
     count = out.shape[0]
     spread = 2 * lateral
     core = lax.axis_index("station") % 2
@@ -357,10 +358,10 @@
     lax.fori_loop(0, count, one, 0, unroll=8)
 
 
-def gravity_forward(first, count, guard, total_x, slab, lateral, head, table, dens):
+def gravity_forward(first, count, guard, total_x, lateral, head, table, dens):
     work = count * dens.size
     return pl.pallas_call(
-        functools.partial(forward_kernel, first, guard, total_x, slab, lateral),
+        functools.partial(forward_kernel, first, guard, total_x, lateral),
         out_shape=shape((count, dens.shape[2])),
         in_specs=[SMEM, VMEM, VMEM],
         out_specs=VMEM,
@@ -373,7 +374,7 @@
 
 
 def adjoint_kernel(lines, guard, total_x, lateral, head, weights, table, start_at, out):
-    slab, rows, lanes = out.shape
+    slab, rows, _ = out.shape
     spread = 2 * lateral
     lead = total_x - 1 - head[0]
     row_low = lax.axis_index("station") * rows
@@ -412,7 +413,7 @@
     )(head, weights, table, start_at)
 
 
-def small_call(kernel, outs, name, *values):
+def small_call(kernel, outs, *values):
     single = not isinstance(outs, tuple)
     return pl.pallas_call(
         kernel,
@@ -420,7 +421,6 @@
         in_specs=[VMEM] * len(values),
         out_specs=VMEM if single else (VMEM,) * len(outs),
         compiler_params=room(2),
-        name=name,
     )(*values)
 
 
@@ -429,7 +429,7 @@
 
 
 def plus(first, second):
-    return small_call(sum_kernel, shape(first.shape), "sum", first, second)
+    return small_call(sum_kernel, shape(first.shape), first, second)
 
 
 def unpack_kernel(packed, other, out):
@@ -598,7 +598,7 @@
     def forward(i):
         def work(gate):
             state[i] = gravity_forward(
-                i * part, part, 0, total_x, slab, lateral, gate(state["head"]), state["table"], dens
+                i * part, part, 0, total_x, lateral, gate(state["head"]), state["table"], dens
             )
             return i
 
@@ -607,7 +607,7 @@
     def predict(gate):
         sums = [state[i] for i in range(pieces)]
         sums[0] = gate(sums[0])
-        packed = small_call(predict_kernel, shape((lines, 128)), "predict", *sums)
+        packed = small_call(predict_kernel, shape((lines, 128)), *sums)
         state["packed"], state["other"] = packed, swap(packed, 0, 1)
 
     def add_up(bit):
@@ -621,7 +621,6 @@
         state["weights"], state["own"] = small_call(
             residual_kernel,
             (shape((lines, 128)), shape((lines // stations, 128))),
-            "residual",
             gate(state["packed"]),
             state["other"],
             state["observed"],
@@ -645,14 +644,22 @@
 
         return work
 
+    def both(first, second):
+        def work(gate):
+            first(gate)
+            return second(gate)
+
+        return work
+
     hidden = chunks == 1 and count & (count - 1) == 0
     jobs = [exchange(1 << b) for b in range(stations.bit_length() - 1)]
     if hidden:
         jobs += [build_table] + [forward(i) for i in range(pieces)] + [predict]
         jobs += [add_up(1 << b) for b in range(count.bit_length() - 1)] + [residual]
         jobs += [adjoint(range(lines // 2)), adjoint(range(lines // 2, lines))]
-    jobs.insert(1, share_edges)
-    jobs.append(cross)
+    jobs[0] = both(share_edges, jobs[0])
+    jobs.insert(2, cross)
+    assert len(jobs) < steps
 
     surf = cour
     for step in range(steps):
@@ -666,10 +673,9 @@
             base, value = together((base, value))
             return value
 
-        ready = jobs.pop(0)(gate) if step and jobs else None
-        if step == steps - 1:
-            while jobs:
-                ready = jobs.pop(0)(gate)
+        ready = None
+        if step and jobs:
+            ready = jobs.pop(0)(gate)
         cur, prev = halo_step(base, cour, cour_outer, outer, inner), cur
         if ready is not None:
             cur, state[ready] = together((cur, state[ready]))
@@ -690,9 +696,7 @@
         wavefield = join(cur, sibling)
         packed = lax.psum(packed + other, "mp")
         other = jnp.zeros_like(packed)
-    traces = small_call(
-        unpack_kernel, shape((steps, receiver_cells.shape[0])), "unpack", packed, other
-    )
+    traces = small_call(unpack_kernel, shape((steps, receiver_cells.shape[0])), packed, other)
     if hidden:
         gravity_residual = state["own"].reshape(-1)
         density_gradient = state["gradient"]
@@ -702,7 +706,7 @@
         def add_chunk(i, total):
             head = head_of(i * reach, cells)
             return total + gravity_forward(
-                0, n_stations, reach, total_x, slab, lateral, head, table_of(head[:1]), dens
+                0, n_stations, reach, total_x, lateral, head, table_of(head[:1]), dens
             )
 
         sums = lax.fori_loop(0, chunks, add_chunk, jnp.zeros((n_stations, vertical), F32))
@@ -743,6 +747,7 @@
         P("mp", "station", None),
         P(None, "mp", None, None),
     )
+
     return jax.shard_map(
         per_device, mesh=mesh, in_specs=in_specs, out_specs=out_specs, check_vma=False
     )

time: 112 us -> 112 us (level)
    ppermute x28, waiting for transfers between devices: 10.2 us -> 12.3 us  [swap(): return lax.ppermute(value, AXES, pairs)]
    ppermute x16, waiting for transfers between devices: 18 us -> 16.8 us  [across(): return lax.ppermute(value, AXES, chain)]
    ppermute x28, starting transfers between devices: 14.3 us -> 13.2 us  [swap(): return lax.ppermute(value, AXES, pairs)]
  transfers between devices with their start and end apart: 44 -> 44, of which waited for: 20 -> 20; matrix products, arithmetic and copies ran while one was open for 1% -> 0% of each run, Pallas kernels for 24% -> 24%
where the time goes in v7:
time: 112 us
  starting transfers between devices  49 us (44%)
  Pallas kernels  30 us (27%)
  waiting for transfers between devices  29.1 us (26%)
  between operations  1.77 us (2%)
  other arithmetic  1.44 us (1%)
    ppermute x16, starting transfers between devices, across(): return lax.ppermute(value, AXES, chain)  35.9 us
    ppermute x16, waiting for transfers between devices, across(): return lax.ppermute(value, AXES, chain)  16.8 us
    ppermute x28, starting transfers between devices, swap(): return lax.ppermute(value, AXES, pairs)  13.2 us
    ppermute x28, waiting for transfers between devices, swap(): return lax.ppermute(value, AXES, pairs)  12.3 us
    pallas_call x4, Pallas kernels, gravity_forward(): pl.pallas_call(functools.partial(forward_kernel, first, guard, total_x, l...  8.9 us
    pallas_call x16, Pallas kernels, local_step(): pl.pallas_call(functools.partial(local_kernel, step), out_shape=(shape(cu...  6.09 us
    pallas_call x2, Pallas kernels, gravity_adjoint(): pl.pallas_call(functools.partial(adjoint_kernel, lines, guard, total_x, l...  4.73 us
    pallas_call x1, Pallas kernels, gravity_table(): pl.pallas_call(functools.partial(table_kernel, total_x, slab, 2 * lateral...  2.81 us
  transfers between devices with their start and end apart: 44, of which 20 were waited for; matrix products, arithmetic and copies ran while one was open for 0% of the time, Pallas kernels for 24%

profile of v7, /device:TPU:0, one launch (start us, length us, event | category | flops | bytes accessed | tf_op | source)
XLA Modules:
  0.0 112.0 jit_solution(1734850599702187916)
XLA Ops:
  1.7 3.0 %collective-permute-start = (f32[6,64,128]{2,1,0:T(8,128)S(1)}, f32[6,64,128]{2,1,0:T(8,128)S(1)}, u32[]{:S(2)}, u32[]{:S(2)}) collective-permute-start(f32[6,64,128]{2,1,0:T(8,128)S(1)} %get-tuple-element.110), channel_id=1, source_target_pairs={{0,4},{1,3},{2,6},{3,1},{4,0},{5,9},{6,2},{7,11},{8,12},{9,5},{10,... | collective-permute-start | bytes 589832 | tf_op jit(solution)/shard_map/ppermute | solution.py:527
  6.1 1.7 %setup.1 = (f32[4,64,128]{2,1,0:T(8,128)S(1)}, f32[4,64,128]{2,1,0:T(8,128)S(1)}, f32[4,64,128]{2,1,0:T(8,128)S(1)}, f32[4,64,128]{2,1,0:T(8,128)S(1)}, f32[4,64...) custom-call(s32[1]{0:T(128)S(6)} %copy.14.source, f32[16]{0:T(128)S(1)} %copy-done.2, f32[8,64,128]{2,1,0:T(8,128)} %p_prev.1, ...), custom_call_target="tpu_custom_call" | custom-call | flops 655360 | bytes 1048576 | tf_op jit(solution)/shard_map/setup/pallas_call | solution.py:141
  11.6 2.5 %collective-permute-start.2 = (f32[4,64,128]{2,1,0:T(8,128)S(1)}, f32[4,64,128]{2,1,0:T(8,128)S(1)}, u32[]{:S(2)}, u32[]{:S(2)}) collective-permute-start(f32[4,64,128]{2,1,0:T(8,128)S(1)} %wave_halo.16.cur.prev), channel_id=1, source_target_pairs={{0,4},{1,3},{2,6},{3,1},{4,0},{5,9},{6,2},{7,11},{8,12},{9,5},{10,... | collective-permute-start | bytes 393224 | tf_op jit(solution)/shard_map/ppermute | solution.py:527
  14.2 3.9 %collective-permute-done.2.outer = f32[4,64,128]{2,1,0:T(8,128)S(1)} collective-permute-done((f32[4,64,128]{2,1,0:T(8,128)S(1)}, f32[4,64,128]{2,1,0:T(8,128)S(1)}, u32[]{:S(2)}, u32[]{:S(2)}) %collective-permute-start.2) | collective-permute-done | bytes 131104 | tf_op jit(solution)/shard_map/ppermute | solution.py:527
  18.2 2.5 %collective-permute-start.5 = (f32[4,64,128]{2,1,0:T(8,128)S(1)}, f32[4,64,128]{2,1,0:T(8,128)S(1)}, u32[]{:S(2)}, u32[]{:S(2)}) collective-permute-start(f32[4,64,128]{2,1,0:T(8,128)S(1)} %wave_halo.17.cur.prev), channel_id=1, source_target_pairs={{0,4},{1,3},{2,6},{3,1},{4,0},{5,9},{6,2},{7,11},{8,12},{9,5},{10,... | collective-permute-start | bytes 393224 | tf_op jit(solution)/shard_map/ppermute | solution.py:527
  23.7 2.3 %collective-permute-start.8 = (f32[4,64,128]{2,1,0:T(8,128)S(1)}, f32[4,64,128]{2,1,0:T(8,128)S(1)}, u32[]{:S(2)}, u32[]{:S(2)}) collective-permute-start(f32[4,64,128]{2,1,0:T(8,128)S(1)} %wave_halo.18.cur.prev), channel_id=1, source_target_pairs={{0,4},{1,3},{2,6},{3,1},{4,0},{5,9},{6,2},{7,11},{8,12},{9,5},{10,... | collective-permute-start | bytes 393224 | tf_op jit(solution)/shard_map/ppermute | solution.py:527
  29.0 2.1 %collective-permute-start.11 = (f32[4,64,128]{2,1,0:T(8,128)S(1)}, f32[4,64,128]{2,1,0:T(8,128)S(1)}, u32[]{:S(2)}, u32[]{:S(2)}) collective-permute-start(f32[4,64,128]{2,1,0:T(8,128)S(1)} %wave_halo.19.cur.prev), channel_id=1, source_target_pairs={{0,4},{1,3},{2,6},{3,1},{4,0},{5,9},{6,2},{7,11},{8,12},{9,5},{10,... | collective-permute-start | bytes 393224 | tf_op jit(solution)/shard_map/ppermute | solution.py:527
  31.6 2.8 %gravity_table.1.table = f32[9088,128]{1,0:T(8,128)S(1)} custom-call(s32[1]{0:T(128)} %constant.54.clone.1.head), custom_call_target="tpu_custom_call" | custom-call | flops 23265280 | bytes 4653056 | tf_op jit(solution)/shard_map/gravity_table/pallas_call | solution.py:318
  34.5 1.7 %collective-permute-start.13 = (f32[4,64,128]{2,1,0:T(8,128)S(1)}, f32[4,64,128]{2,1,0:T(8,128)S(1)}, u32[]{:S(2)}, u32[]{:S(2)}) collective-permute-start(f32[4,64,128]{2,1,0:T(8,128)S(1)} %wave_halo.20.cur.prev), channel_id=1, source_target_pairs={{0,4},{1,3},{2,6},{3,1},{4,0},{5,9},{6,2},{7,11},{8,12},{9,5},{10,... | collective-permute-start | bytes 393224 | tf_op jit(solution)/shard_map/ppermute | solution.py:527
  36.7 2.2 %gravity_forward.4.refs_0_ = f32[128,128]{1,0:T(8,128)S(1)} custom-call(s32[513]{0:T(1024)S(1)} %pad_add_fusion.head, f32[9088,128]{1,0:T(8,128)S(1)} %gravity_table.1.table, f32[4,64,128]{2,1,0:T(8,128)S(1)} %get-tuple-element.139.dens), custom_call_target="tpu_custom_call" | custom-call | flops 16777216 | bytes 131072 | tf_op jit(solution)/shard_map/gravity_forward/pallas_call | solution.py:363
  39.6 2.3 %collective-permute-start.15 = (f32[4,64,128]{2,1,0:T(8,128)S(1)}, f32[4,64,128]{2,1,0:T(8,128)S(1)}, u32[]{:S(2)}, u32[]{:S(2)}) collective-permute-start(f32[4,64,128]{2,1,0:T(8,128)S(1)} %wave_halo.21.cur.prev), channel_id=1, source_target_pairs={{0,4},{1,3},{2,6},{3,1},{4,0},{5,9},{6,2},{7,11},{8,12},{9,5},{10,... | collective-permute-start | bytes 393224 | tf_op jit(solution)/shard_map/ppermute | solution.py:527
  42.3 2.2 %gravity_forward.5.refs_1_ = f32[128,128]{1,0:T(8,128)S(1)} custom-call(s32[513]{0:T(1024)S(1)} %pad_add_fusion.head, f32[9088,128]{1,0:T(8,128)S(1)} %gravity_table.1.table, f32[4,64,128]{2,1,0:T(8,128)S(1)} %get-tuple-element.139.dens), custom_call_target="tpu_custom_call" | custom-call | flops 16777216 | bytes 131072 | tf_op jit(solution)/shard_map/gravity_forward/pallas_call | solution.py:363
  44.9 2.1 %collective-permute-start.17 = (f32[4,64,128]{2,1,0:T(8,128)S(1)}, f32[4,64,128]{2,1,0:T(8,128)S(1)}, u32[]{:S(2)}, u32[]{:S(2)}) collective-permute-start(f32[4,64,128]{2,1,0:T(8,128)S(1)} %wave_halo.22.cur.prev), channel_id=1, source_target_pairs={{0,4},{1,3},{2,6},{3,1},{4,0},{5,9},{6,2},{7,11},{8,12},{9,5},{10,... | collective-permute-start | bytes 393224 | tf_op jit(solution)/shard_map/ppermute | solution.py:527
  47.4 2.2 %gravity_forward.6.refs_2_ = f32[128,128]{1,0:T(8,128)S(1)} custom-call(s32[513]{0:T(1024)S(1)} %pad_add_fusion.head, f32[9088,128]{1,0:T(8,128)S(1)} %gravity_table.1.table, f32[4,64,128]{2,1,0:T(8,128)S(1)} %get-tuple-element.139.dens), custom_call_target="tpu_custom_call" | custom-call | flops 16777216 | bytes 131072 | tf_op jit(solution)/shard_map/gravity_forward/pallas_call | solution.py:363
  50.1 2.4 %collective-permute-start.19 = (f32[4,64,128]{2,1,0:T(8,128)S(1)}, f32[4,64,128]{2,1,0:T(8,128)S(1)}, u32[]{:S(2)}, u32[]{:S(2)}) collective-permute-start(f32[4,64,128]{2,1,0:T(8,128)S(1)} %wave_halo.23.cur.prev), channel_id=1, source_target_pairs={{0,4},{1,3},{2,6},{3,1},{4,0},{5,9},{6,2},{7,11},{8,12},{9,5},{10,... | collective-permute-start | bytes 393224 | tf_op jit(solution)/shard_map/ppermute | solution.py:527
  52.8 2.2 %gravity_forward.7.refs_3_ = f32[128,128]{1,0:T(8,128)S(1)} custom-call(s32[513]{0:T(1024)S(1)} %pad_add_fusion.head, f32[9088,128]{1,0:T(8,128)S(1)} %gravity_table.1.table, f32[4,64,128]{2,1,0:T(8,128)S(1)} %get-tuple-element.139.dens), custom_call_target="tpu_custom_call" | custom-call | flops 16777216 | bytes 131072 | tf_op jit(solution)/shard_map/gravity_forward/pallas_call | solution.py:363
  55.4 2.1 %collective-permute-start.21 = (f32[4,64,128]{2,1,0:T(8,128)S(1)}, f32[4,64,128]{2,1,0:T(8,128)S(1)}, u32[]{:S(2)}, u32[]{:S(2)}) collective-permute-start(f32[4,64,128]{2,1,0:T(8,128)S(1)} %wave_halo.24.cur.prev), channel_id=1, source_target_pairs={{0,4},{1,3},{2,6},{3,1},{4,0},{5,9},{6,2},{7,11},{8,12},{9,5},{10,... | collective-permute-start | bytes 393224 | tf_op jit(solution)/shard_map/ppermute | solution.py:527
  57.9 2.8 %collective-permute-done.21.outer = f32[4,64,128]{2,1,0:T(8,128)S(1)} collective-permute-done((f32[4,64,128]{2,1,0:T(8,128)S(1)}, f32[4,64,128]{2,1,0:T(8,128)S(1)}, u32[]{:S(2)}, u32[]{:S(2)}) %collective-permute-start.21) | collective-permute-done | bytes 131104 | tf_op jit(solution)/shard_map/ppermute | solution.py:527
  60.8 2.5 %collective-permute-start.23 = (f32[4,64,128]{2,1,0:T(8,128)S(1)}, f32[4,64,128]{2,1,0:T(8,128)S(1)}, u32[]{:S(2)}, u32[]{:S(2)}) collective-permute-start(f32[4,64,128]{2,1,0:T(8,128)S(1)} %wave_halo.25.cur.prev), channel_id=1, source_target_pairs={{0,4},{1,3},{2,6},{3,1},{4,0},{5,9},{6,2},{7,11},{8,12},{9,5},{10,... | collective-permute-start | bytes 393224 | tf_op jit(solution)/shard_map/ppermute | solution.py:527
  63.9 2.4 %collective-permute-done.23.outer = f32[4,64,128]{2,1,0:T(8,128)S(1)} collective-permute-done((f32[4,64,128]{2,1,0:T(8,128)S(1)}, f32[4,64,128]{2,1,0:T(8,128)S(1)}, u32[]{:S(2)}, u32[]{:S(2)}) %collective-permute-start.23) | collective-permute-done | bytes 131104 | tf_op jit(solution)/shard_map/ppermute | solution.py:527
  66.4 2.1 %collective-permute-start.26 = (f32[4,64,128]{2,1,0:T(8,128)S(1)}, f32[4,64,128]{2,1,0:T(8,128)S(1)}, u32[]{:S(2)}, u32[]{:S(2)}) collective-permute-start(f32[4,64,128]{2,1,0:T(8,128)S(1)} %wave_halo.26.cur.prev), channel_id=1, source_target_pairs={{0,4},{1,3},{2,6},{3,1},{4,0},{5,9},{6,2},{7,11},{8,12},{9,5},{10,... | collective-permute-start | bytes 393224 | tf_op jit(solution)/shard_map/ppermute | solution.py:527
  71.5 2.1 %collective-permute-start.29 = (f32[4,64,128]{2,1,0:T(8,128)S(1)}, f32[4,64,128]{2,1,0:T(8,128)S(1)}, u32[]{:S(2)}, u32[]{:S(2)}) collective-permute-start(f32[4,64,128]{2,1,0:T(8,128)S(1)} %wave_halo.27.cur.prev), channel_id=1, source_target_pairs={{0,4},{1,3},{2,6},{3,1},{4,0},{5,9},{6,2},{7,11},{8,12},{9,5},{10,... | collective-permute-start | bytes 393224 | tf_op jit(solution)/shard_map/ppermute | solution.py:527
  73.7 2.8 %collective-permute-done.28.second = f32[4,128]{1,0:T(4,128)S(1)} collective-permute-done((f32[4,128]{1,0:T(4,128)S(1)}, f32[4,128]{1,0:T(4,128)S(1)}, u32[]{:S(2)}, u32[]{:S(2)}) %collective-permute-start.28) | collective-permute-done | bytes 2080 | tf_op jit(solution)/shard_map/ppermute | solution.py:531
  78.7 2.1 %collective-permute-start.31 = (f32[4,128]{1,0:T(4,128)S(1)}, f32[4,128]{1,0:T(4,128)S(1)}, u32[]{:S(2)}, u32[]{:S(2)}) collective-permute-start(f32[4,128]{1,0:T(4,128)S(1)} %shard_map.130.first), channel_id=1, source_target_pairs={{0,9},{1,8},{2,11},{3,10},{4,13},{5,12},{6,15},{7,14},{8,1},{9,0},... | collective-permute-start | bytes 6152 | tf_op jit(solution)/shard_map/ppermute | solution.py:531
  80.8 2.0 %collective-permute-done.31.second = f32[4,128]{1,0:T(4,128)S(1)} collective-permute-done((f32[4,128]{1,0:T(4,128)S(1)}, f32[4,128]{1,0:T(4,128)S(1)}, u32[]{:S(2)}, u32[]{:S(2)}) %collective-permute-start.31) | collective-permute-done | bytes 2080 | tf_op jit(solution)/shard_map/ppermute | solution.py:531
  82.7 2.4 %collective-permute-start.34 = (f32[4,128]{1,0:T(4,128)S(1)}, f32[4,128]{1,0:T(4,128)S(1)}, u32[]{:S(2)}, u32[]{:S(2)}) collective-permute-start(f32[4,128]{1,0:T(4,128)S(1)} %shard_map.131.packed), channel_id=1, source_target_pairs={{0,17},{1,16},{2,19},{3,18},{4,21},{5,20},{6,23},{7,22},{8,25},{9,... | collective-permute-start | bytes 6152 | tf_op jit(solution)/shard_map/ppermute | solution.py:531
  87.2 1.9 %collective-permute-start.35 = (f32[4,64,128]{2,1,0:T(8,128)S(1)}, f32[4,64,128]{2,1,0:T(8,128)S(1)}, u32[]{:S(2)}, u32[]{:S(2)}) collective-permute-start(f32[4,64,128]{2,1,0:T(8,128)S(1)} %wave_halo.29.cur.prev), channel_id=1, source_target_pairs={{0,4},{1,3},{2,6},{3,1},{4,0},{5,9},{6,2},{7,11},{8,12},{9,5},{10,... | collective-permute-start | bytes 393224 | tf_op jit(solution)/shard_map/ppermute | solution.py:527
  89.5 2.0 %gravity_adjoint.2.start_at = f32[8,16,128]{2,1,0:T(8,128)S(1)} custom-call(s32[513]{0:T(1024)S(1)} %pad_add_fusion.head, f32[4,128]{1,0:T(4,128)S(1)} %get-tuple-element.192.weights, f32[9088,128]{1,0:T(8,128)S(1)} %gravity_table.1.table, f32[8,16,128]{2,1,0:T(8,128)S(1)} %broadcast_in_dim.16.start_at), custom_call_target="tpu_custom_call" | custom-call | flops 8388608 | bytes 131072 | tf_op jit(solution)/shard_map/gravity_adjoint/pallas_call | solution.py:403
  93.1 2.5 %collective-permute-start.37 = (f32[4,64,128]{2,1,0:T(8,128)S(1)}, f32[4,64,128]{2,1,0:T(8,128)S(1)}, u32[]{:S(2)}, u32[]{:S(2)}) collective-permute-start(f32[4,64,128]{2,1,0:T(8,128)S(1)} %wave_halo.30.cur), channel_id=1, source_target_pairs={{0,4},{1,3},{2,6},{3,1},{4,0},{5,9},{6,2},{7,11},{8,12},{9,5},{10,... | collective-permute-start | bytes 393224 | tf_op jit(solution)/shard_map/ppermute | solution.py:527
  96.0 2.7 %gravity_adjoint.3 = f32[8,16,128]{2,1,0:T(8,128)} custom-call(s32[513]{0:T(1024)S(1)} %pad_add_fusion.head, f32[4,128]{1,0:T(4,128)S(1)} %get-tuple-element.192.weights, f32[9088,128]{1,0:T(8,128)S(1)} %gravity_table.1.table, f32[8,16,128]{2,1,0:T(8,128)S(1)} %gravity_adjoint.2.start_at), custom_call_target="tpu_custom_call" | custom-call | flops 8388608 | bytes 131072 | tf_op jit(solution)/shard_map/gravity_adjoint/pallas_call | solution.py:403
  105.5 1.8 %collective-permute-done.42.second = f32[32,128]{1,0:T(8,128)S(1)} collective-permute-done((f32[32,128]{1,0:T(8,128)S(1)}, f32[32,128]{1,0:T(8,128)S(1)}, u32[]{:S(2)}, u32[]{:S(2)}) %collective-permute-start.42) | collective-permute-done | bytes 16416 | tf_op jit(solution)/shard_map/ppermute | solution.py:531
  107.3 2.4 %collective-permute-start.43 = (f32[32,128]{1,0:T(8,128)S(1)}, f32[32,128]{1,0:T(8,128)S(1)}, u32[]{:S(2)}, u32[]{:S(2)}) collective-permute-start(f32[32,128]{1,0:T(8,128)S(1)} %shard_map.135.packed), channel_id=1, source_target_pairs={{0,17},{1,16},{2,19},{3,18},{4,21},{5,20},{6,23},{7,22},{8,25},{9,... | collective-permute-start | bytes 49160 | tf_op jit(solution)/shard_map/ppermute | solution.py:531
  (127 shorter events, 35.2 us)
Async XLA Ops:
  1.7 8.1 %collective-permute-start = (f32[6,64,128]{2,1,0:T(8,128)S(1)}, f32[6,64,128]{2,1,0:T(8,128)S(1)}, u32[]{:S(2)}, u32[]{:S(2)}) collective-permute-start(f32[6,64,128]{2,1,0:T(8,128)S(1)} %get-tuple-element.110), channel_id=1, source_target_pairs={{0,4},{1,3},{2,6},{3,1},{4,0},{5,9},{6,2},{7,11},{8,12},{9,5},{10,... | collective-permute-start | bytes 589832 | tf_op jit(solution)/shard_map/ppermute | solution.py:527
  4.8 3.4 %collective-permute-start.1 = (f32[4,64,128]{2,1,0:T(8,128)S(1)}, f32[4,64,128]{2,1,0:T(8,128)S(1)}, u32[]{:S(2)}, u32[]{:S(2)}) collective-permute-start(f32[4,64,128]{2,1,0:T(8,128)S(1)} %get-tuple-element.105.cur.prev), channel_id=1, source_target_pairs={{0,1},{1,0},{2,3},{3,2},{4,5},{5,4},{6,7},{7,6},{8,9},{9,8},{10,11... | collective-permute-start | bytes 393224 | tf_op jit(solution)/shard_map/ppermute | solution.py:531
  11.6 6.4 %collective-permute-start.2 = (f32[4,64,128]{2,1,0:T(8,128)S(1)}, f32[4,64,128]{2,1,0:T(8,128)S(1)}, u32[]{:S(2)}, u32[]{:S(2)}) collective-permute-start(f32[4,64,128]{2,1,0:T(8,128)S(1)} %wave_halo.16.cur.prev), channel_id=1, source_target_pairs={{0,4},{1,3},{2,6},{3,1},{4,0},{5,9},{6,2},{7,11},{8,12},{9,5},{10,... | collective-permute-start | bytes 393224 | tf_op jit(solution)/shard_map/ppermute | solution.py:527
  14.2 3.9 %collective-permute-start.3 = (f32[4,64,128]{2,1,0:T(8,128)S(1)}, f32[4,64,128]{2,1,0:T(8,128)S(1)}, u32[]{:S(2)}, u32[]{:S(2)}) collective-permute-start(f32[4,64,128]{2,1,0:T(8,128)S(1)} %wave_halo.16.cur.prev), channel_id=1, source_target_pairs={{0,1},{1,0},{2,3},{3,2},{4,5},{5,4},{6,7},{7,6},{8,9},{9,8},{10,11... | collective-permute-start | bytes 393224 | tf_op jit(solution)/shard_map/ppermute | solution.py:531
  18.2 5.5 %collective-permute-start.5 = (f32[4,64,128]{2,1,0:T(8,128)S(1)}, f32[4,64,128]{2,1,0:T(8,128)S(1)}, u32[]{:S(2)}, u32[]{:S(2)}) collective-permute-start(f32[4,64,128]{2,1,0:T(8,128)S(1)} %wave_halo.17.cur.prev), channel_id=1, source_target_pairs={{0,4},{1,3},{2,6},{3,1},{4,0},{5,9},{6,2},{7,11},{8,12},{9,5},{10,... | collective-permute-start | bytes 393224 | tf_op jit(solution)/shard_map/ppermute | solution.py:527
  21.1 4.9 %collective-permute-start.10 = (f32[2,2,128]{2,1,0:T(2,128)S(1)}, f32[2,2,128]{2,1,0:T(2,128)S(1)}, u32[]{:S(2)}, u32[]{:S(2)}) collective-permute-start(f32[2,2,128]{2,1,0:T(2,128)S(1)} %pad_maximum_fusion.1), channel_id=1, source_target_pairs={{0,2},{1,3},{2,0},{3,1},{4,6},{5,7},{6,4},{7,5},{8,10},{9,11},{10,... | collective-permute-start | bytes 6152 | tf_op jit(solution)/shard_map/ppermute | solution.py:531
  22.7 3.7 %collective-permute-start.7 = (f32[6,64,128]{2,1,0:T(8,128)S(1)}, f32[6,64,128]{2,1,0:T(8,128)S(1)}, u32[]{:S(2)}, u32[]{:S(2)}) collective-permute-start(f32[6,64,128]{2,1,0:T(8,128)S(1)} %collective-permute-done.outer), channel_id=1, source_target_pairs={{0,1},{1,0},{2,3},{3,2},{4,5},{5,4},{6,7},{7,6},{8,9},{9,8},{10,11... | collective-permute-start | bytes 589832 | tf_op jit(solution)/shard_map/ppermute | solution.py:531
  23.7 5.2 %collective-permute-start.8 = (f32[4,64,128]{2,1,0:T(8,128)S(1)}, f32[4,64,128]{2,1,0:T(8,128)S(1)}, u32[]{:S(2)}, u32[]{:S(2)}) collective-permute-start(f32[4,64,128]{2,1,0:T(8,128)S(1)} %wave_halo.18.cur.prev), channel_id=1, source_target_pairs={{0,4},{1,3},{2,6},{3,1},{4,0},{5,9},{6,2},{7,11},{8,12},{9,5},{10,... | collective-permute-start | bytes 393224 | tf_op jit(solution)/shard_map/ppermute | solution.py:527
  29.0 5.4 %collective-permute-start.11 = (f32[4,64,128]{2,1,0:T(8,128)S(1)}, f32[4,64,128]{2,1,0:T(8,128)S(1)}, u32[]{:S(2)}, u32[]{:S(2)}) collective-permute-start(f32[4,64,128]{2,1,0:T(8,128)S(1)} %wave_halo.19.cur.prev), channel_id=1, source_target_pairs={{0,4},{1,3},{2,6},{3,1},{4,0},{5,9},{6,2},{7,11},{8,12},{9,5},{10,... | collective-permute-start | bytes 393224 | tf_op jit(solution)/shard_map/ppermute | solution.py:527
  31.1 3.3 %collective-permute-start.12 = (f32[4,64,128]{2,1,0:T(8,128)S(1)}, f32[4,64,128]{2,1,0:T(8,128)S(1)}, u32[]{:S(2)}, u32[]{:S(2)}) collective-permute-start(f32[4,64,128]{2,1,0:T(8,128)S(1)} %wave_halo.19.cur.prev), channel_id=1, source_target_pairs={{0,1},{1,0},{2,3},{3,2},{4,5},{5,4},{6,7},{7,6},{8,9},{9,8},{10,11... | collective-permute-start | bytes 393224 | tf_op jit(solution)/shard_map/ppermute | solution.py:531
  34.5 5.0 %collective-permute-start.13 = (f32[4,64,128]{2,1,0:T(8,128)S(1)}, f32[4,64,128]{2,1,0:T(8,128)S(1)}, u32[]{:S(2)}, u32[]{:S(2)}) collective-permute-start(f32[4,64,128]{2,1,0:T(8,128)S(1)} %wave_halo.20.cur.prev), channel_id=1, source_target_pairs={{0,4},{1,3},{2,6},{3,1},{4,0},{5,9},{6,2},{7,11},{8,12},{9,5},{10,... | collective-permute-start | bytes 393224 | tf_op jit(solution)/shard_map/ppermute | solution.py:527
  36.2 3.3 %collective-permute-start.14 = (f32[4,64,128]{2,1,0:T(8,128)S(1)}, f32[4,64,128]{2,1,0:T(8,128)S(1)}, u32[]{:S(2)}, u32[]{:S(2)}) collective-permute-start(f32[4,64,128]{2,1,0:T(8,128)S(1)} %wave_halo.20.cur.prev), channel_id=1, source_target_pairs={{0,1},{1,0},{2,3},{3,2},{4,5},{5,4},{6,7},{7,6},{8,9},{9,8},{10,11... | collective-permute-start | bytes 393224 | tf_op jit(solution)/shard_map/ppermute | solution.py:531
  39.6 5.3 %collective-permute-start.15 = (f32[4,64,128]{2,1,0:T(8,128)S(1)}, f32[4,64,128]{2,1,0:T(8,128)S(1)}, u32[]{:S(2)}, u32[]{:S(2)}) collective-permute-start(f32[4,64,128]{2,1,0:T(8,128)S(1)} %wave_halo.21.cur.prev), channel_id=1, source_target_pairs={{0,4},{1,3},{2,6},{3,1},{4,0},{5,9},{6,2},{7,11},{8,12},{9,5},{10,... | collective-permute-start | bytes 393224 | tf_op jit(solution)/shard_map/ppermute | solution.py:527
  44.9 5.1 %collective-permute-start.17 = (f32[4,64,128]{2,1,0:T(8,128)S(1)}, f32[4,64,128]{2,1,0:T(8,128)S(1)}, u32[]{:S(2)}, u32[]{:S(2)}) collective-permute-start(f32[4,64,128]{2,1,0:T(8,128)S(1)} %wave_halo.22.cur.prev), channel_id=1, source_target_pairs={{0,4},{1,3},{2,6},{3,1},{4,0},{5,9},{6,2},{7,11},{8,12},{9,5},{10,... | collective-permute-start | bytes 393224 | tf_op jit(solution)/shard_map/ppermute | solution.py:527
  50.1 5.3 %collective-permute-start.19 = (f32[4,64,128]{2,1,0:T(8,128)S(1)}, f32[4,64,128]{2,1,0:T(8,128)S(1)}, u32[]{:S(2)}, u32[]{:S(2)}) collective-permute-start(f32[4,64,128]{2,1,0:T(8,128)S(1)} %wave_halo.23.cur.prev), channel_id=1, source_target_pairs={{0,4},{1,3},{2,6},{3,1},{4,0},{5,9},{6,2},{7,11},{8,12},{9,5},{10,... | collective-permute-start | bytes 393224 | tf_op jit(solution)/shard_map/ppermute | solution.py:527
  55.4 5.3 %collective-permute-start.21 = (f32[4,64,128]{2,1,0:T(8,128)S(1)}, f32[4,64,128]{2,1,0:T(8,128)S(1)}, u32[]{:S(2)}, u32[]{:S(2)}) collective-permute-start(f32[4,64,128]{2,1,0:T(8,128)S(1)} %wave_halo.24.cur.prev), channel_id=1, source_target_pairs={{0,4},{1,3},{2,6},{3,1},{4,0},{5,9},{6,2},{7,11},{8,12},{9,5},{10,... | collective-permute-start | bytes 393224 | tf_op jit(solution)/shard_map/ppermute | solution.py:527
  57.5 3.2 %collective-permute-start.22 = (f32[4,64,128]{2,1,0:T(8,128)S(1)}, f32[4,64,128]{2,1,0:T(8,128)S(1)}, u32[]{:S(2)}, u32[]{:S(2)}) collective-permute-start(f32[4,64,128]{2,1,0:T(8,128)S(1)} %wave_halo.24.cur.prev), channel_id=1, source_target_pairs={{0,1},{1,0},{2,3},{3,2},{4,5},{5,4},{6,7},{7,6},{8,9},{9,8},{10,11... | collective-permute-start | bytes 393224 | tf_op jit(solution)/shard_map/ppermute | solution.py:531
  60.8 5.5 %collective-permute-start.23 = (f32[4,64,128]{2,1,0:T(8,128)S(1)}, f32[4,64,128]{2,1,0:T(8,128)S(1)}, u32[]{:S(2)}, u32[]{:S(2)}) collective-permute-start(f32[4,64,128]{2,1,0:T(8,128)S(1)} %wave_halo.25.cur.prev), channel_id=1, source_target_pairs={{0,4},{1,3},{2,6},{3,1},{4,0},{5,9},{6,2},{7,11},{8,12},{9,5},{10,... | collective-permute-start | bytes 393224 | tf_op jit(solution)/shard_map/ppermute | solution.py:527
  66.4 5.0 %collective-permute-start.26 = (f32[4,64,128]{2,1,0:T(8,128)S(1)}, f32[4,64,128]{2,1,0:T(8,128)S(1)}, u32[]{:S(2)}, u32[]{:S(2)}) collective-permute-start(f32[4,64,128]{2,1,0:T(8,128)S(1)} %wave_halo.26.cur.prev), channel_id=1, source_target_pairs={{0,4},{1,3},{2,6},{3,1},{4,0},{5,9},{6,2},{7,11},{8,12},{9,5},{10,... | collective-permute-start | bytes 393224 | tf_op jit(solution)/shard_map/ppermute | solution.py:527
  71.5 5.5 %collective-permute-start.29 = (f32[4,64,128]{2,1,0:T(8,128)S(1)}, f32[4,64,128]{2,1,0:T(8,128)S(1)}, u32[]{:S(2)}, u32[]{:S(2)}) collective-permute-start(f32[4,64,128]{2,1,0:T(8,128)S(1)} %wave_halo.27.cur.prev), channel_id=1, source_target_pairs={{0,4},{1,3},{2,6},{3,1},{4,0},{5,9},{6,2},{7,11},{8,12},{9,5},{10,... | collective-permute-start | bytes 393224 | tf_op jit(solution)/shard_map/ppermute | solution.py:527
  73.5 3.4 %collective-permute-start.30 = (f32[4,64,128]{2,1,0:T(8,128)S(1)}, f32[4,64,128]{2,1,0:T(8,128)S(1)}, u32[]{:S(2)}, u32[]{:S(2)}) collective-permute-start(f32[4,64,128]{2,1,0:T(8,128)S(1)} %wave_halo.27.cur.prev), channel_id=1, source_target_pairs={{0,1},{1,0},{2,3},{3,2},{4,5},{5,4},{6,7},{7,6},{8,9},{9,8},{10,11... | collective-permute-start | bytes 393224 | tf_op jit(solution)/shard_map/ppermute | solution.py:531
  77.0 10.1 %collective-permute-start.32 = (f32[4,64,128]{2,1,0:T(8,128)S(1)}, f32[4,64,128]{2,1,0:T(8,128)S(1)}, u32[]{:S(2)}, u32[]{:S(2)}) collective-permute-start(f32[4,64,128]{2,1,0:T(8,128)S(1)} %wave_halo.28.cur.prev), channel_id=1, source_target_pairs={{0,4},{1,3},{2,6},{3,1},{4,0},{5,9},{6,2},{7,11},{8,12},{9,5},{10,... | collective-permute-start | bytes 393224 | tf_op jit(solution)/shard_map/ppermute | solution.py:527
  78.6 8.5 %collective-permute-start.33 = (f32[4,64,128]{2,1,0:T(8,128)S(1)}, f32[4,64,128]{2,1,0:T(8,128)S(1)}, u32[]{:S(2)}, u32[]{:S(2)}) collective-permute-start(f32[4,64,128]{2,1,0:T(8,128)S(1)} %wave_halo.28.cur.prev), channel_id=1, source_target_pairs={{0,1},{1,0},{2,3},{3,2},{4,5},{5,4},{6,7},{7,6},{8,9},{9,8},{10,11... | collective-permute-start | bytes 393224 | tf_op jit(solution)/shard_map/ppermute | solution.py:531
  78.7 4.0 %collective-permute-start.31 = (f32[4,128]{1,0:T(4,128)S(1)}, f32[4,128]{1,0:T(4,128)S(1)}, u32[]{:S(2)}, u32[]{:S(2)}) collective-permute-start(f32[4,128]{1,0:T(4,128)S(1)} %shard_map.130.first), channel_id=1, source_target_pairs={{0,9},{1,8},{2,11},{3,10},{4,13},{5,12},{6,15},{7,14},{8,1},{9,0},... | collective-permute-start | bytes 6152 | tf_op jit(solution)/shard_map/ppermute | solution.py:531
  82.7 3.9 %collective-permute-start.34 = (f32[4,128]{1,0:T(4,128)S(1)}, f32[4,128]{1,0:T(4,128)S(1)}, u32[]{:S(2)}, u32[]{:S(2)}) collective-permute-start(f32[4,128]{1,0:T(4,128)S(1)} %shard_map.131.packed), channel_id=1, source_target_pairs={{0,17},{1,16},{2,19},{3,18},{4,21},{5,20},{6,23},{7,22},{8,25},{9,... | collective-permute-start | bytes 6152 | tf_op jit(solution)/shard_map/ppermute | solution.py:531
  87.2 5.8 %collective-permute-start.35 = (f32[4,64,128]{2,1,0:T(8,128)S(1)}, f32[4,64,128]{2,1,0:T(8,128)S(1)}, u32[]{:S(2)}, u32[]{:S(2)}) collective-permute-start(f32[4,64,128]{2,1,0:T(8,128)S(1)} %wave_halo.29.cur.prev), channel_id=1, source_target_pairs={{0,4},{1,3},{2,6},{3,1},{4,0},{5,9},{6,2},{7,11},{8,12},{9,5},{10,... | collective-permute-start | bytes 393224 | tf_op jit(solution)/shard_map/ppermute | solution.py:527
  89.1 3.9 %collective-permute-start.36 = (f32[4,64,128]{2,1,0:T(8,128)S(1)}, f32[4,64,128]{2,1,0:T(8,128)S(1)}, u32[]{:S(2)}, u32[]{:S(2)}) collective-permute-start(f32[4,64,128]{2,1,0:T(8,128)S(1)} %wave_halo.29.cur.prev), channel_id=1, source_target_pairs={{0,1},{1,0},{2,3},{3,2},{4,5},{5,4},{6,7},{7,6},{8,9},{9,8},{10,11... | collective-permute-start | bytes 393224 | tf_op jit(solution)/shard_map/ppermute | solution.py:531
  93.1 5.6 %collective-permute-start.37 = (f32[4,64,128]{2,1,0:T(8,128)S(1)}, f32[4,64,128]{2,1,0:T(8,128)S(1)}, u32[]{:S(2)}, u32[]{:S(2)}) collective-permute-start(f32[4,64,128]{2,1,0:T(8,128)S(1)} %wave_halo.30.cur), channel_id=1, source_target_pairs={{0,4},{1,3},{2,6},{3,1},{4,0},{5,9},{6,2},{7,11},{8,12},{9,5},{10,... | collective-permute-start | bytes 393224 | tf_op jit(solution)/shard_map/ppermute | solution.py:527
  98.8 3.7 %collective-permute-start.41 = (f32[4,64,128]{2,1,0:T(8,128)S(1)}, f32[4,64,128]{2,1,0:T(8,128)S(1)}, u32[]{:S(2)}, u32[]{:S(2)}) collective-permute-start(f32[4,64,128]{2,1,0:T(8,128)S(1)} %wave_halo.31.cur.own), channel_id=1, source_target_pairs={{0,1},{1,0},{2,3},{3,2},{4,5},{5,4},{6,7},{7,6},{8,9},{9,8},{10,11... | collective-permute-start | bytes 393224 | tf_op jit(solution)/shard_map/ppermute | solution.py:531
  101.0 3.2 %collective-permute-start.40 = (f32[32,128]{1,0:T(8,128)S(1)}, f32[32,128]{1,0:T(8,128)S(1)}, u32[]{:S(2)}, u32[]{:S(2)}) collective-permute-start(f32[32,128]{1,0:T(8,128)S(1)} %shard_map.133.first), channel_id=1, source_target_pairs={{0,5},{1,4},{2,7},{3,6},{4,1},{5,0},{6,3},{7,2},{8,13},{9,12},{10,... | collective-permute-start | bytes 49160 | tf_op jit(solution)/shard_map/ppermute | solution.py:531
  104.1 3.2 %collective-permute-start.42 = (f32[32,128]{1,0:T(8,128)S(1)}, f32[32,128]{1,0:T(8,128)S(1)}, u32[]{:S(2)}, u32[]{:S(2)}) collective-permute-start(f32[32,128]{1,0:T(8,128)S(1)} %shard_map.134.first), channel_id=1, source_target_pairs={{0,9},{1,8},{2,11},{3,10},{4,13},{5,12},{6,15},{7,14},{8,1},{9,0},... | collective-permute-start | bytes 49160 | tf_op jit(solution)/shard_map/ppermute | solution.py:531
  107.3 4.1 %collective-permute-start.43 = (f32[32,128]{1,0:T(8,128)S(1)}, f32[32,128]{1,0:T(8,128)S(1)}, u32[]{:S(2)}, u32[]{:S(2)}) collective-permute-start(f32[32,128]{1,0:T(8,128)S(1)} %shard_map.135.packed), channel_id=1, source_target_pairs={{0,17},{1,16},{2,19},{3,18},{4,21},{5,20},{6,23},{7,22},{8,25},{9,... | collective-permute-start | bytes 49160 | tf_op jit(solution)/shard_map/ppermute | solution.py:531
  (16 other events, 106.3 us)

commit v8 on v7

--- a/solution.py
+++ b/solution.py
@@ -74,35 +74,46 @@
     return jnp.where(upper, slab - 1 - j, j)
 
 
-def first_kernel(now, velocity, density, cur, message, sems):
+def first_kernel(now, cur, sems):
     slab = now.shape[0]
-    half = slab // 2
     _, upper = position()
-    pairs = []
-    for j in range(half):
-        plane = plane_of(upper, j, slab)
-        pairs += [(now.at[plane], cur.at[j]), (now.at[plane], message.at[j])]
-    edge = plane_of(upper, 0, slab)
-    pairs += [(velocity.at[edge], message.at[half]), (density.at[edge], message.at[half + 1])]
-    run_copies(pairs, sems)
-
-
-def first_message(p_now, velocity, density):
+    run_copies([(now.at[plane_of(upper, j, slab)], cur.at[j]) for j in range(slab // 2)], sems)
+
+
+def first_planes(p_now):
     slab, rows, lanes = p_now.shape
     half = slab // 2
     return pl.pallas_call(
         first_kernel,
-        out_shape=(shape((half, rows, lanes)), shape((half + 2, rows, lanes))),
-        in_specs=[HBM] * 3,
-        out_specs=(VMEM, VMEM),
-        scratch_shapes=[pltpu.SemaphoreType.DMA((2 * half + 2,))],
+        out_shape=shape((half, rows, lanes)),
+        in_specs=[HBM],
+        out_specs=VMEM,
+        scratch_shapes=[pltpu.SemaphoreType.DMA((half,))],
         compiler_params=room(2),
-        name="first_message",
-    )(*in_place(p_now, velocity, density))
+        name="first_planes",
+    )(*in_place(p_now))
 
 
 def setup_kernel(
-    count, source, wavelet, p_prev, velocity, density, prev, cour, cour_outer, mask, dens, pulses, vel, raw, sems
+    count,
+    source,
+    wavelet,
+    cells,
+    observed,
+    p_prev,
+    velocity,
+    density,
+    prev,
+    cour,
+    cour_outer,
+    mask,
+    dens,
+    pulses,
+    known,
+    edges,
+    vel,
+    raw,
+    sems,
 ):
     slab = p_prev.shape[0]
     half, rows, lanes = prev.shape
@@ -113,7 +124,11 @@
         pairs += [(p_prev.at[plane], prev.at[j]), (velocity.at[plane], vel.at[j])]
     low = half * (lax.axis_index("station") % 2)
     pairs += [(density.at[pl.ds(low, half)], raw)]
+    edge = plane_of(upper, 0, slab)
+    pairs += [(velocity.at[edge], edges.at[0]), (density.at[edge], edges.at[1])]
     run_copies(pairs, sems)
+    known[0] = cells[...].astype(F32)
+    known[1] = observed[...]
     for n in range(pulses.shape[0]):
         pulses[n : n + 1, :] = jnp.full((1, lanes), wavelet[n], F32)
     outer_ok = jnp.where(upper, m < count - 1, m > 0)
@@ -133,23 +148,28 @@
         dens[j] = raw[j].astype(jnp.bfloat16).astype(F32)
 
 
-def setup(count, source_cell, wavelet, p_prev, velocity, density):
+def setup(count, source_cell, wavelet, cells, observed, p_prev, velocity, density):
     slab, rows, lanes = p_prev.shape
     half = slab // 2
     part = shape((half, rows, lanes))
     held = pltpu.VMEM((half, rows, lanes), F32)
     return pl.pallas_call(
         functools.partial(setup_kernel, count),
-        out_shape=(part,) * 5 + (shape((wavelet.shape[0], lanes)),),
-        in_specs=[SMEM, SMEM] + [HBM] * 3,
-        out_specs=(VMEM,) * 6,
-        scratch_shapes=[held, held, pltpu.SemaphoreType.DMA((2 * half + 1,))],
+        out_shape=(part,) * 5
+        + (
+            shape((wavelet.shape[0], lanes)),
+            shape((2,) + cells.shape),
+            shape((2, rows, lanes)),
+        ),
+        in_specs=[SMEM, SMEM, VMEM, VMEM] + [HBM] * 3,
+        out_specs=(VMEM,) * 8,
+        scratch_shapes=[held, held, pltpu.SemaphoreType.DMA((2 * half + 3,))],
         compiler_params=room(4),
         cost_estimate=pl.CostEstimate(
             flops=20 * half * rows * lanes, bytes_accessed=32 * half * rows * lanes, transcendentals=0
         ),
         name="setup",
-    )(source_cell, wavelet, *in_place(p_prev, velocity, density))
+    )(source_cell, wavelet, cells, observed, *in_place(p_prev, velocity, density))
 
 
 def local_kernel(step, pulses, mask, cur, prev, cour, surf_in, base, surf, pad):
@@ -304,8 +324,8 @@
 
     def one(t, carry):
         dx = (t + low).astype(F32)
-        square = dx * dx + side + deep
-        value = dz / (square * jnp.sqrt(square))
+        inverse = lax.rsqrt(dx * dx + side + deep)
+        value = dz * (inverse * inverse * inverse)
         start = pl.multiple_of(t * spread, spread)
         out[pl.ds(start, spread), :] = value.astype(jnp.bfloat16).astype(F32)
         return carry
@@ -337,25 +357,34 @@
     if guard:
         out[...] = jnp.zeros_like(out)
 
-    def one(s, carry):
+    def window(s):
         sx, sy = divmod_static(head[1 + first + s], lateral)
         shift = lead - sx
-        start = (shift + core * planes) * spread + (lateral - 1 - sy)
-
-        def accumulate():
-            acc = None
-            for p in range(planes):
-                term = table[pl.ds(start + p * spread, rows), :] * dens[p]
-                acc = term if acc is None else acc + term
-            out[pl.ds(s, 1), :] = jnp.sum(acc, axis=0, keepdims=True)
-
+        return shift, (shift + core * planes) * spread + (lateral - 1 - sy)
+
+    def several(s, starts):
+        totals = [None] * len(starts)
+        for p in range(planes):
+            for r in range(0, rows, 8):
+                value = dens[p, r : r + 8, :]
+                for q, start in enumerate(starts):
+                    term = table[pl.ds(start + (p * spread + r), 8), :] * value
+                    totals[q] = term if totals[q] is None else totals[q] + term
+        for q, total in enumerate(totals):
+            out[pl.ds(s + q, 1), :] = jnp.sum(total, axis=0, keepdims=True)
+
+    def one(g, carry):
         if guard:
-            pl.when((shift >= 0) & (shift < guard))(accumulate)
+            shift, start = window(g)
+            pl.when((shift >= 0) & (shift < guard))(lambda: several(g, [start]))
         else:
-            accumulate()
+            several(4 * g, [window(4 * g + q)[1] for q in range(4)])
         return carry
 
-    lax.fori_loop(0, count, one, 0, unroll=8)
+    if guard:
+        lax.fori_loop(0, count, one, 0)
+    else:
+        lax.fori_loop(0, count // 4, one, 0, unroll=2)
 
 
 def gravity_forward(first, count, guard, total_x, lateral, head, table, dens):
@@ -462,7 +491,6 @@
 
 def cross_kernel(count, velocity, density, outer, inner, out):
     slab, rows, lanes = velocity.shape
-    half = slab // 2
     lane = lax.broadcasted_iota(jnp.int32, (rows, lanes), 1)
     row = lax.broadcasted_iota(jnp.int32, (rows, lanes), 0)
     m, flipped = position()
@@ -486,8 +514,8 @@
         return above - below, (up - down) * 0.5, (ahead - back) * 0.5
 
     for x in range(slab):
-        v = slopes(velocity, half, x)
-        q = slopes(density, half + 1, x)
+        v = slopes(velocity, 0, x)
+        q = slopes(density, 1, x)
         out[0, x] = v[1] * q[2] - v[2] * q[1]
         out[1, x] = v[2] * q[0] - v[0] * q[2]
         out[2, x] = v[0] * q[1] - v[1] * q[0]
@@ -530,12 +558,18 @@
         pairs = pairs_of(count, stations, lambda i, k: (i ^ slab_bit, k ^ station_bit))
         return lax.ppermute(value, AXES, pairs)
 
-    cur, message = first_message(p_now, velocity, density)
-    outer = across(message)
+    cur = first_planes(p_now)
+    outer = across(cur)
     inner = swap(cur, 0, 1)
-    edges = outer
-    prev, cour, cour_outer, mask, dens, pulses = setup(
-        count, source_cell, wavelet, p_prev, velocity, density
+    prev, cour, cour_outer, mask, dens, pulses, known, edges = setup(
+        count,
+        source_cell,
+        wavelet,
+        station_cells.reshape(-1, 128),
+        observed.reshape(-1, 128),
+        p_prev,
+        velocity,
+        density,
     )
 
     receiver_x, receiver_y = divmod_static(receiver_cells, lateral)
@@ -556,14 +590,11 @@
     def table_of(head):
         return gravity_table(total_x, slab, span, lateral, vertical, head)
 
-    state = {}
+    state = {"known": known, "edges": edges}
 
     def exchange(bit):
         def work(gate):
-            if bit == 1:
-                known = jnp.stack([gate(station_cells).astype(F32), observed])[:, None, :]
-            else:
-                known = gate(state["known"])
+            known = gate(state["known"])
             other = swap(known, 0, bit)
             upper = (s // bit) % 2 == 1
             state["known"] = jnp.concatenate(
@@ -572,11 +603,16 @@
 
         return work
 
+    def send_edges(gate):
+        state["outer"] = across(gate(state["edges"]))
+
     def share_edges(gate):
-        state["inner"] = swap(gate(edges), 0, 1)
+        state["inner"] = swap(gate(state["outer"]), 0, 1)
 
     def cross(gate):
-        state["cross"] = cross_gradient_of(count, velocity, density, edges, gate(state["inner"]))
+        state["cross"] = cross_gradient_of(
+            count, velocity, density, state["outer"], gate(state["inner"])
+        )
         return "cross"
 
     lines = n_stations // 128
@@ -657,7 +693,8 @@
         jobs += [build_table] + [forward(i) for i in range(pieces)] + [predict]
         jobs += [add_up(1 << b) for b in range(count.bit_length() - 1)] + [residual]
         jobs += [adjoint(range(lines // 2)), adjoint(range(lines // 2, lines))]
-    jobs[0] = both(share_edges, jobs[0])
+    jobs[0] = both(send_edges, jobs[0])
+    jobs[1] = both(share_edges, jobs[1])
     jobs.insert(2, cross)
     assert len(jobs) < steps
 
@@ -690,6 +727,7 @@
             other = swap(packed, bit, 1)
             if bit == 1:
                 wavefield = join(cur, sibling)
+            if bit == 2:
                 other, wavefield = together((other, wavefield))
             bit *= 2
     else:

time: 112 us -> 112 us (level)
  waiting for transfers between devices: 29.1 us -> 26.2 us
  local copies, waits for them, and re-layouts: 0.67 us -> 1.98 us
  Pallas kernels: 30 us -> 31.2 us
    ppermute x16 -> x17, waiting for transfers between devices: 16.8 us -> 13.2 us  [across(): return lax.ppermute(value, AXES, chain)]
    pallas_call x4, Pallas kernels: 8.9 us -> 11.1 us  [gravity_forward(): pl.pallas_call(functools.partial(forward_kernel, first, guard, total_x, l...]
    another operation x2 -> x0, other arithmetic: 1.32 us -> none  [work(): known = jnp.stack([gate(station_cells).astype(F32), observed])[:, None, :]]
    unnamed x8 -> x10, local copies, waits for them, and re-layouts: 0.67 us -> 1.97 us
    ppermute x16 -> x17, starting transfers between devices: 35.9 us -> 35.9 us  [across(): return lax.ppermute(value, AXES, chain)]
  transfers between devices with their start and end apart: 44 -> 45, of which waited for: 20 -> 15; matrix products, arithmetic and copies ran while one was open for 0% -> 1% of each run, Pallas kernels for 24% -> 25%
where the time goes in v8:
time: 112 us; the launch traced here: 111 us
  starting transfers between devices  49.6 us (44%)
  Pallas kernels  31.2 us (28%)
  waiting for transfers between devices  26.2 us (23%)
  local copies, waits for them, and re-layouts  1.98 us (2%)
  between operations  1.73 us (2%)
    ppermute x17, starting transfers between devices, across(): return lax.ppermute(value, AXES, chain)  35.9 us
    ppermute x28, starting transfers between devices, swap(): return lax.ppermute(value, AXES, pairs)  13.7 us
    ppermute x17, waiting for transfers between devices, across(): return lax.ppermute(value, AXES, chain)  13.2 us
    ppermute x28, waiting for transfers between devices, swap(): return lax.ppermute(value, AXES, pairs)  13 us
    pallas_call x4, Pallas kernels, gravity_forward(): pl.pallas_call(functools.partial(forward_kernel, first, guard, total_x, l...  11.1 us
    pallas_call x16, Pallas kernels, local_step(): pl.pallas_call(functools.partial(local_kernel, step), out_shape=(shape(cu...  6.2 us
    pallas_call x2, Pallas kernels, gravity_adjoint(): pl.pallas_call(functools.partial(adjoint_kernel, lines, guard, total_x, l...  4.73 us
  transfers between devices with their start and end apart: 45, of which 15 were waited for; matrix products, arithmetic and copies ran while one was open for 1% of the time, Pallas kernels for 25%

profile of v8, /device:TPU:0, one launch (start us, length us, event | category | flops | bytes accessed | tf_op | source)
XLA Modules:
  0.0 111.4 jit_solution(10887467961094390484)
XLA Ops:
  1.6 3.0 %collective-permute-start = (f32[4,64,128]{2,1,0:T(8,128)S(1)}, f32[4,64,128]{2,1,0:T(8,128)S(1)}, u32[]{:S(2)}, u32[]{:S(2)}) collective-permute-start(f32[4,64,128]{2,1,0:T(8,128)S(1)} %first_planes.1.cur.prev), channel_id=1, source_target_pairs={{0,4},{1,3},{2,6},{3,1},{4,0},{5,9},{6,2},{7,11},{8,12},{9,5},{10,... | collective-permute-start | bytes 393224 | tf_op jit(solution)/shard_map/ppermute | solution.py:555
  7.2 1.8 %setup.1 = (f32[4,64,128]{2,1,0:T(8,128)S(1)}, f32[4,64,128]{2,1,0:T(8,128)S(1)}, f32[4,64,128]{2,1,0:T(8,128)S(1)}, f32[4,64,128]{2,1,0:T(8,128)S(1)}, f32[4,64...) custom-call(s32[1]{0:T(128)S(6)} %copy.14.source, ...), custom_call_target="tpu_custom_call" | custom-call | flops 655360 | bytes 1048576 | tf_op jit(solution)/shard_map/setup/pallas_call | solution.py:156
  13.3 2.6 %collective-permute-done.2.outer = f32[4,64,128]{2,1,0:T(8,128)S(1)} collective-permute-done((f32[4,64,128]{2,1,0:T(8,128)S(1)}, f32[4,64,128]{2,1,0:T(8,128)S(1)}, u32[]{:S(2)}, u32[]{:S(2)}) %collective-permute-start.2) | collective-permute-done | bytes 131104 | tf_op jit(solution)/shard_map/ppermute | solution.py:555
  16.1 2.5 %collective-permute-start.6 = (f32[4,64,128]{2,1,0:T(8,128)S(1)}, f32[4,64,128]{2,1,0:T(8,128)S(1)}, u32[]{:S(2)}, u32[]{:S(2)}) collective-permute-start(f32[4,64,128]{2,1,0:T(8,128)S(1)} %wave_halo.17.cur.prev), channel_id=1, source_target_pairs={{0,4},{1,3},{2,6},{3,1},{4,0},{5,9},{6,2},{7,11},{8,12},{9,5},{10,... | collective-permute-start | bytes 393224 | tf_op jit(solution)/shard_map/ppermute | solution.py:555
  19.0 1.6 %collective-permute-start.11 = (f32[2,2,128]{2,1,0:T(2,128)S(1)}, f32[2,2,128]{2,1,0:T(2,128)S(1)}, u32[]{:S(2)}, u32[]{:S(2)}) collective-permute-start(f32[2,2,128]{2,1,0:T(2,128)S(1)} %pad_maximum_fusion.1), channel_id=1, source_target_pairs={{0,2},{1,3},{2,0},{3,1},{4,6},{5,7},{6,4},{7,5},{8,10},{9,11},{10,... | collective-permute-start | bytes 6152 | tf_op jit(solution)/shard_map/ppermute | solution.py:559
  22.0 1.8 %collective-permute-start.9 = (f32[4,64,128]{2,1,0:T(8,128)S(1)}, f32[4,64,128]{2,1,0:T(8,128)S(1)}, u32[]{:S(2)}, u32[]{:S(2)}) collective-permute-start(f32[4,64,128]{2,1,0:T(8,128)S(1)} %wave_halo.18.cur.prev), channel_id=1, source_target_pairs={{0,4},{1,3},{2,6},{3,1},{4,0},{5,9},{6,2},{7,11},{8,12},{9,5},{10,... | collective-permute-start | bytes 393224 | tf_op jit(solution)/shard_map/ppermute | solution.py:555
  25.5 2.1 %collective-permute-done.9.outer = f32[4,64,128]{2,1,0:T(8,128)S(1)} collective-permute-done((f32[4,64,128]{2,1,0:T(8,128)S(1)}, f32[4,64,128]{2,1,0:T(8,128)S(1)}, u32[]{:S(2)}, u32[]{:S(2)}) %collective-permute-start.9) | collective-permute-done | bytes 131104 | tf_op jit(solution)/shard_map/ppermute | solution.py:555
  27.7 2.5 %collective-permute-start.12 = (f32[4,64,128]{2,1,0:T(8,128)S(1)}, f32[4,64,128]{2,1,0:T(8,128)S(1)}, u32[]{:S(2)}, u32[]{:S(2)}) collective-permute-start(f32[4,64,128]{2,1,0:T(8,128)S(1)} %wave_halo.19.cur.prev), channel_id=1, source_target_pairs={{0,4},{1,3},{2,6},{3,1},{4,0},{5,9},{6,2},{7,11},{8,12},{9,5},{10,... | collective-permute-start | bytes 393224 | tf_op jit(solution)/shard_map/ppermute | solution.py:555
  30.8 1.8 %gravity_table.1.table = f32[9088,128]{1,0:T(8,128)S(1)} custom-call(s32[1]{0:T(128)} %constant.54.clone.1.head), custom_call_target="tpu_custom_call" | custom-call | flops 23265280 | bytes 4653056 | tf_op jit(solution)/shard_map/gravity_table/pallas_call | solution.py:338
  33.3 2.3 %collective-permute-start.14 = (f32[4,64,128]{2,1,0:T(8,128)S(1)}, f32[4,64,128]{2,1,0:T(8,128)S(1)}, u32[]{:S(2)}, u32[]{:S(2)}) collective-permute-start(f32[4,64,128]{2,1,0:T(8,128)S(1)} %wave_halo.20.cur.prev), channel_id=1, source_target_pairs={{0,4},{1,3},{2,6},{3,1},{4,0},{5,9},{6,2},{7,11},{8,12},{9,5},{10,... | collective-permute-start | bytes 393224 | tf_op jit(solution)/shard_map/ppermute | solution.py:555
  36.0 2.8 %gravity_forward.4.refs_0_ = f32[128,128]{1,0:T(8,128)S(1)} custom-call(s32[513]{0:T(1024)S(1)} %pad_add_fusion.head, f32[9088,128]{1,0:T(8,128)S(1)} %gravity_table.1.table, f32[4,64,128]{2,1,0:T(8,128)S(1)} %get-tuple-element.143.dens), custom_call_target="tpu_custom_call" | custom-call | flops 16777216 | bytes 131072 | tf_op jit(solution)/shard_map/gravity_forward/pallas_call | solution.py:392
  38.9 1.8 %collective-permute-start.16 = (f32[4,64,128]{2,1,0:T(8,128)S(1)}, f32[4,64,128]{2,1,0:T(8,128)S(1)}, u32[]{:S(2)}, u32[]{:S(2)}) collective-permute-start(f32[4,64,128]{2,1,0:T(8,128)S(1)} %wave_halo.21.cur.prev), channel_id=1, source_target_pairs={{0,4},{1,3},{2,6},{3,1},{4,0},{5,9},{6,2},{7,11},{8,12},{9,5},{10,... | collective-permute-start | bytes 393224 | tf_op jit(solution)/shard_map/ppermute | solution.py:555
  41.1 2.8 %gravity_forward.5.refs_1_ = f32[128,128]{1,0:T(8,128)S(1)} custom-call(s32[513]{0:T(1024)S(1)} %pad_add_fusion.head, f32[9088,128]{1,0:T(8,128)S(1)} %gravity_table.1.table, f32[4,64,128]{2,1,0:T(8,128)S(1)} %get-tuple-element.143.dens), custom_call_target="tpu_custom_call" | custom-call | flops 16777216 | bytes 131072 | tf_op jit(solution)/shard_map/gravity_forward/pallas_call | solution.py:392
  44.0 2.3 %collective-permute-start.18 = (f32[4,64,128]{2,1,0:T(8,128)S(1)}, f32[4,64,128]{2,1,0:T(8,128)S(1)}, u32[]{:S(2)}, u32[]{:S(2)}) collective-permute-start(f32[4,64,128]{2,1,0:T(8,128)S(1)} %wave_halo.22.cur.prev), channel_id=1, source_target_pairs={{0,4},{1,3},{2,6},{3,1},{4,0},{5,9},{6,2},{7,11},{8,12},{9,5},{10,... | collective-permute-start | bytes 393224 | tf_op jit(solution)/shard_map/ppermute | solution.py:555
  46.7 2.8 %gravity_forward.6.refs_2_ = f32[128,128]{1,0:T(8,128)S(1)} custom-call(s32[513]{0:T(1024)S(1)} %pad_add_fusion.head, f32[9088,128]{1,0:T(8,128)S(1)} %gravity_table.1.table, f32[4,64,128]{2,1,0:T(8,128)S(1)} %get-tuple-element.143.dens), custom_call_target="tpu_custom_call" | custom-call | flops 16777216 | bytes 131072 | tf_op jit(solution)/shard_map/gravity_forward/pallas_call | solution.py:392
  49.6 2.4 %collective-permute-start.20 = (f32[4,64,128]{2,1,0:T(8,128)S(1)}, f32[4,64,128]{2,1,0:T(8,128)S(1)}, u32[]{:S(2)}, u32[]{:S(2)}) collective-permute-start(f32[4,64,128]{2,1,0:T(8,128)S(1)} %wave_halo.23.cur.prev), channel_id=1, source_target_pairs={{0,4},{1,3},{2,6},{3,1},{4,0},{5,9},{6,2},{7,11},{8,12},{9,5},{10,... | collective-permute-start | bytes 393224 | tf_op jit(solution)/shard_map/ppermute | solution.py:555
  52.4 2.8 %gravity_forward.7.refs_3_ = f32[128,128]{1,0:T(8,128)S(1)} custom-call(s32[513]{0:T(1024)S(1)} %pad_add_fusion.head, f32[9088,128]{1,0:T(8,128)S(1)} %gravity_table.1.table, f32[4,64,128]{2,1,0:T(8,128)S(1)} %get-tuple-element.143.dens), custom_call_target="tpu_custom_call" | custom-call | flops 16777216 | bytes 131072 | tf_op jit(solution)/shard_map/gravity_forward/pallas_call | solution.py:392
  55.3 2.4 %collective-permute-start.22 = (f32[4,64,128]{2,1,0:T(8,128)S(1)}, f32[4,64,128]{2,1,0:T(8,128)S(1)}, u32[]{:S(2)}, u32[]{:S(2)}) collective-permute-start(f32[4,64,128]{2,1,0:T(8,128)S(1)} %wave_halo.24.cur.prev), channel_id=1, source_target_pairs={{0,4},{1,3},{2,6},{3,1},{4,0},{5,9},{6,2},{7,11},{8,12},{9,5},{10,... | collective-permute-start | bytes 393224 | tf_op jit(solution)/shard_map/ppermute | solution.py:555
  58.1 2.7 %collective-permute-done.22.outer = f32[4,64,128]{2,1,0:T(8,128)S(1)} collective-permute-done((f32[4,64,128]{2,1,0:T(8,128)S(1)}, f32[4,64,128]{2,1,0:T(8,128)S(1)}, u32[]{:S(2)}, u32[]{:S(2)}) %collective-permute-start.22) | collective-permute-done | bytes 131104 | tf_op jit(solution)/shard_map/ppermute | solution.py:555
  60.8 2.5 %collective-permute-start.24 = (f32[4,64,128]{2,1,0:T(8,128)S(1)}, f32[4,64,128]{2,1,0:T(8,128)S(1)}, u32[]{:S(2)}, u32[]{:S(2)}) collective-permute-start(f32[4,64,128]{2,1,0:T(8,128)S(1)} %wave_halo.25.cur.prev), channel_id=1, source_target_pairs={{0,4},{1,3},{2,6},{3,1},{4,0},{5,9},{6,2},{7,11},{8,12},{9,5},{10,... | collective-permute-start | bytes 393224 | tf_op jit(solution)/shard_map/ppermute | solution.py:555
  63.9 2.4 %collective-permute-done.24.outer = f32[4,64,128]{2,1,0:T(8,128)S(1)} collective-permute-done((f32[4,64,128]{2,1,0:T(8,128)S(1)}, f32[4,64,128]{2,1,0:T(8,128)S(1)}, u32[]{:S(2)}, u32[]{:S(2)}) %collective-permute-start.24) | collective-permute-done | bytes 131104 | tf_op jit(solution)/shard_map/ppermute | solution.py:555
  66.4 2.1 %collective-permute-start.27 = (f32[4,64,128]{2,1,0:T(8,128)S(1)}, f32[4,64,128]{2,1,0:T(8,128)S(1)}, u32[]{:S(2)}, u32[]{:S(2)}) collective-permute-start(f32[4,64,128]{2,1,0:T(8,128)S(1)} %wave_halo.26.cur.prev), channel_id=1, source_target_pairs={{0,4},{1,3},{2,6},{3,1},{4,0},{5,9},{6,2},{7,11},{8,12},{9,5},{10,... | collective-permute-start | bytes 393224 | tf_op jit(solution)/shard_map/ppermute | solution.py:555
  71.5 2.1 %collective-permute-start.30 = (f32[4,64,128]{2,1,0:T(8,128)S(1)}, f32[4,64,128]{2,1,0:T(8,128)S(1)}, u32[]{:S(2)}, u32[]{:S(2)}) collective-permute-start(f32[4,64,128]{2,1,0:T(8,128)S(1)} %wave_halo.27.cur.prev), channel_id=1, source_target_pairs={{0,4},{1,3},{2,6},{3,1},{4,0},{5,9},{6,2},{7,11},{8,12},{9,5},{10,... | collective-permute-start | bytes 393224 | tf_op jit(solution)/shard_map/ppermute | solution.py:555
  73.8 2.8 %collective-permute-done.29.second = f32[4,128]{1,0:T(4,128)S(1)} collective-permute-done((f32[4,128]{1,0:T(4,128)S(1)}, f32[4,128]{1,0:T(4,128)S(1)}, u32[]{:S(2)}, u32[]{:S(2)}) %collective-permute-start.29) | collective-permute-done | bytes 2080 | tf_op jit(solution)/shard_map/ppermute | solution.py:559
  77.1 1.6 %collective-permute-start.33 = (f32[4,64,128]{2,1,0:T(8,128)S(1)}, f32[4,64,128]{2,1,0:T(8,128)S(1)}, u32[]{:S(2)}, u32[]{:S(2)}) collective-permute-start(f32[4,64,128]{2,1,0:T(8,128)S(1)} %wave_halo.28.cur.prev), channel_id=1, source_target_pairs={{0,4},{1,3},{2,6},{3,1},{4,0},{5,9},{6,2},{7,11},{8,12},{9,5},{10,... | collective-permute-start | bytes 393224 | tf_op jit(solution)/shard_map/ppermute | solution.py:555
  80.4 2.3 %collective-permute-done.32.second = f32[4,128]{1,0:T(4,128)S(1)} collective-permute-done((f32[4,128]{1,0:T(4,128)S(1)}, f32[4,128]{1,0:T(4,128)S(1)}, u32[]{:S(2)}, u32[]{:S(2)}) %collective-permute-start.32) | collective-permute-done | bytes 2080 | tf_op jit(solution)/shard_map/ppermute | solution.py:559
  82.7 2.0 %collective-permute-start.35 = (f32[4,128]{1,0:T(4,128)S(1)}, f32[4,128]{1,0:T(4,128)S(1)}, u32[]{:S(2)}, u32[]{:S(2)}) collective-permute-start(f32[4,128]{1,0:T(4,128)S(1)} %shard_map.131.packed), channel_id=1, source_target_pairs={{0,17},{1,16},{2,19},{3,18},{4,21},{5,20},{6,23},{7,22},{8,25},{9,... | collective-permute-start | bytes 6152 | tf_op jit(solution)/shard_map/ppermute | solution.py:559
  89.0 2.0 %gravity_adjoint.2.start_at = f32[8,16,128]{2,1,0:T(8,128)S(1)} custom-call(s32[513]{0:T(1024)S(1)} %pad_add_fusion.head, f32[4,128]{1,0:T(4,128)S(1)} %get-tuple-element.196.weights, f32[9088,128]{1,0:T(8,128)S(1)} %gravity_table.1.table, f32[8,16,128]{2,1,0:T(8,128)S(1)} %broadcast_in_dim.12.start_at), custom_call_target="tpu_custom_call" | custom-call | flops 8388608 | bytes 131072 | tf_op jit(solution)/shard_map/gravity_adjoint/pallas_call | solution.py:432
  92.5 2.5 %collective-permute-start.38 = (f32[4,64,128]{2,1,0:T(8,128)S(1)}, f32[4,64,128]{2,1,0:T(8,128)S(1)}, u32[]{:S(2)}, u32[]{:S(2)}) collective-permute-start(f32[4,64,128]{2,1,0:T(8,128)S(1)} %wave_halo.30.cur), channel_id=1, source_target_pairs={{0,4},{1,3},{2,6},{3,1},{4,0},{5,9},{6,2},{7,11},{8,12},{9,5},{10,... | collective-permute-start | bytes 393224 | tf_op jit(solution)/shard_map/ppermute | solution.py:555
  95.5 2.7 %gravity_adjoint.3 = f32[8,16,128]{2,1,0:T(8,128)} custom-call(s32[513]{0:T(1024)S(1)} %pad_add_fusion.head, f32[4,128]{1,0:T(4,128)S(1)} %get-tuple-element.196.weights, f32[9088,128]{1,0:T(8,128)S(1)} %gravity_table.1.table, f32[8,16,128]{2,1,0:T(8,128)S(1)} %gravity_adjoint.2.start_at), custom_call_target="tpu_custom_call" | custom-call | flops 8388608 | bytes 131072 | tf_op jit(solution)/shard_map/gravity_adjoint/pallas_call | solution.py:432
  102.0 1.6 %collective-permute-done.41.second = f32[32,128]{1,0:T(8,128)S(1)} collective-permute-done((f32[32,128]{1,0:T(8,128)S(1)}, f32[32,128]{1,0:T(8,128)S(1)}, u32[]{:S(2)}, u32[]{:S(2)}) %collective-permute-start.41) | collective-permute-done | bytes 16416 | tf_op jit(solution)/shard_map/ppermute | solution.py:559
  106.7 2.5 %collective-permute-start.44 = (f32[32,128]{1,0:T(8,128)S(1)}, f32[32,128]{1,0:T(8,128)S(1)}, u32[]{:S(2)}, u32[]{:S(2)}) collective-permute-start(f32[32,128]{1,0:T(8,128)S(1)} %shard_map.135.packed), channel_id=1, source_target_pairs={{0,17},{1,16},{2,19},{3,18},{4,21},{5,20},{6,23},{7,22},{8,25},{9,... | collective-permute-start | bytes 49160 | tf_op jit(solution)/shard_map/ppermute | solution.py:559
  (129 shorter events, 35.5 us)
Async XLA Ops:
  1.6 7.8 %collective-permute-start = (f32[4,64,128]{2,1,0:T(8,128)S(1)}, f32[4,64,128]{2,1,0:T(8,128)S(1)}, u32[]{:S(2)}, u32[]{:S(2)}) collective-permute-start(f32[4,64,128]{2,1,0:T(8,128)S(1)} %first_planes.1.cur.prev), channel_id=1, source_target_pairs={{0,4},{1,3},{2,6},{3,1},{4,0},{5,9},{6,2},{7,11},{8,12},{9,5},{10,... | collective-permute-start | bytes 393224 | tf_op jit(solution)/shard_map/ppermute | solution.py:555
  4.6 4.8 %collective-permute-start.1 = (f32[4,64,128]{2,1,0:T(8,128)S(1)}, f32[4,64,128]{2,1,0:T(8,128)S(1)}, u32[]{:S(2)}, u32[]{:S(2)}) collective-permute-start(f32[4,64,128]{2,1,0:T(8,128)S(1)} %first_planes.1.cur.prev), channel_id=1, source_target_pairs={{0,1},{1,0},{2,3},{3,2},{4,5},{5,4},{6,7},{7,6},{8,9},{9,8},{10,11... | collective-permute-start | bytes 393224 | tf_op jit(solution)/shard_map/ppermute | solution.py:559
  9.9 3.4 %collective-permute-start.5 = (f32[2,1,128]{2,1,0:T(1,128)S(1)}, f32[2,1,128]{2,1,0:T(1,128)S(1)}, u32[]{:S(2)}, u32[]{:S(2)}) collective-permute-start(f32[2,1,128]{2,1,0:T(1,128)S(1)} %get-tuple-element.121), channel_id=1, source_target_pairs={{0,1},{1,0},{2,3},{3,2},{4,5},{5,4},{6,7},{7,6},{8,9},{9,8},{10,11... | collective-permute-start | bytes 3080 | tf_op jit(solution)/shard_map/ppermute | solution.py:559
  10.5 5.5 %collective-permute-start.2 = (f32[4,64,128]{2,1,0:T(8,128)S(1)}, f32[4,64,128]{2,1,0:T(8,128)S(1)}, u32[]{:S(2)}, u32[]{:S(2)}) collective-permute-start(f32[4,64,128]{2,1,0:T(8,128)S(1)} %wave_halo.16.cur.prev), channel_id=1, source_target_pairs={{0,4},{1,3},{2,6},{3,1},{4,0},{5,9},{6,2},{7,11},{8,12},{9,5},{10,... | collective-permute-start | bytes 393224 | tf_op jit(solution)/shard_map/ppermute | solution.py:555
  11.4 4.6 %collective-permute-start.3 = (f32[4,64,128]{2,1,0:T(8,128)S(1)}, f32[4,64,128]{2,1,0:T(8,128)S(1)}, u32[]{:S(2)}, u32[]{:S(2)}) collective-permute-start(f32[4,64,128]{2,1,0:T(8,128)S(1)} %wave_halo.16.cur.prev), channel_id=1, source_target_pairs={{0,1},{1,0},{2,3},{3,2},{4,5},{5,4},{6,7},{7,6},{8,9},{9,8},{10,11... | collective-permute-start | bytes 393224 | tf_op jit(solution)/shard_map/ppermute | solution.py:559
  11.8 7.2 %collective-permute-start.4 = (f32[2,64,128]{2,1,0:T(8,128)S(1)}, f32[2,64,128]{2,1,0:T(8,128)S(1)}, u32[]{:S(2)}, u32[]{:S(2)}) collective-permute-start(f32[2,64,128]{2,1,0:T(8,128)S(1)} %get-tuple-element.119), channel_id=1, source_target_pairs={{0,4},{1,3},{2,6},{3,1},{4,0},{5,9},{6,2},{7,11},{8,12},{9,5},{10,... | collective-permute-start | bytes 196616 | tf_op jit(solution)/shard_map/ppermute | solution.py:555
  16.1 5.5 %collective-permute-start.6 = (f32[4,64,128]{2,1,0:T(8,128)S(1)}, f32[4,64,128]{2,1,0:T(8,128)S(1)}, u32[]{:S(2)}, u32[]{:S(2)}) collective-permute-start(f32[4,64,128]{2,1,0:T(8,128)S(1)} %wave_halo.17.cur.prev), channel_id=1, source_target_pairs={{0,4},{1,3},{2,6},{3,1},{4,0},{5,9},{6,2},{7,11},{8,12},{9,5},{10,... | collective-permute-start | bytes 393224 | tf_op jit(solution)/shard_map/ppermute | solution.py:555
  19.0 4.8 %collective-permute-start.11 = (f32[2,2,128]{2,1,0:T(2,128)S(1)}, f32[2,2,128]{2,1,0:T(2,128)S(1)}, u32[]{:S(2)}, u32[]{:S(2)}) collective-permute-start(f32[2,2,128]{2,1,0:T(2,128)S(1)} %pad_maximum_fusion.1), channel_id=1, source_target_pairs={{0,2},{1,3},{2,0},{3,1},{4,6},{5,7},{6,4},{7,5},{8,10},{9,11},{10,... | collective-permute-start | bytes 6152 | tf_op jit(solution)/shard_map/ppermute | solution.py:559
  21.6 3.9 %collective-permute-start.10 = (f32[4,64,128]{2,1,0:T(8,128)S(1)}, f32[4,64,128]{2,1,0:T(8,128)S(1)}, u32[]{:S(2)}, u32[]{:S(2)}) collective-permute-start(f32[4,64,128]{2,1,0:T(8,128)S(1)} %wave_halo.18.cur.prev), channel_id=1, source_target_pairs={{0,1},{1,0},{2,3},{3,2},{4,5},{5,4},{6,7},{7,6},{8,9},{9,8},{10,11... | collective-permute-start | bytes 393224 | tf_op jit(solution)/shard_map/ppermute | solution.py:559
  22.0 5.7 %collective-permute-start.9 = (f32[4,64,128]{2,1,0:T(8,128)S(1)}, f32[4,64,128]{2,1,0:T(8,128)S(1)}, u32[]{:S(2)}, u32[]{:S(2)}) collective-permute-start(f32[4,64,128]{2,1,0:T(8,128)S(1)} %wave_halo.18.cur.prev), channel_id=1, source_target_pairs={{0,4},{1,3},{2,6},{3,1},{4,0},{5,9},{6,2},{7,11},{8,12},{9,5},{10,... | collective-permute-start | bytes 393224 | tf_op jit(solution)/shard_map/ppermute | solution.py:555
  27.7 5.5 %collective-permute-start.12 = (f32[4,64,128]{2,1,0:T(8,128)S(1)}, f32[4,64,128]{2,1,0:T(8,128)S(1)}, u32[]{:S(2)}, u32[]{:S(2)}) collective-permute-start(f32[4,64,128]{2,1,0:T(8,128)S(1)} %wave_halo.19.cur.prev), channel_id=1, source_target_pairs={{0,4},{1,3},{2,6},{3,1},{4,0},{5,9},{6,2},{7,11},{8,12},{9,5},{10,... | collective-permute-start | bytes 393224 | tf_op jit(solution)/shard_map/ppermute | solution.py:555
  33.3 5.5 %collective-permute-start.14 = (f32[4,64,128]{2,1,0:T(8,128)S(1)}, f32[4,64,128]{2,1,0:T(8,128)S(1)}, u32[]{:S(2)}, u32[]{:S(2)}) collective-permute-start(f32[4,64,128]{2,1,0:T(8,128)S(1)} %wave_halo.20.cur.prev), channel_id=1, source_target_pairs={{0,4},{1,3},{2,6},{3,1},{4,0},{5,9},{6,2},{7,11},{8,12},{9,5},{10,... | collective-permute-start | bytes 393224 | tf_op jit(solution)/shard_map/ppermute | solution.py:555
  35.6 3.2 %collective-permute-start.15 = (f32[4,64,128]{2,1,0:T(8,128)S(1)}, f32[4,64,128]{2,1,0:T(8,128)S(1)}, u32[]{:S(2)}, u32[]{:S(2)}) collective-permute-start(f32[4,64,128]{2,1,0:T(8,128)S(1)} %wave_halo.20.cur.prev), channel_id=1, source_target_pairs={{0,1},{1,0},{2,3},{3,2},{4,5},{5,4},{6,7},{7,6},{8,9},{9,8},{10,11... | collective-permute-start | bytes 393224 | tf_op jit(solution)/shard_map/ppermute | solution.py:559
  38.9 5.0 %collective-permute-start.16 = (f32[4,64,128]{2,1,0:T(8,128)S(1)}, f32[4,64,128]{2,1,0:T(8,128)S(1)}, u32[]{:S(2)}, u32[]{:S(2)}) collective-permute-start(f32[4,64,128]{2,1,0:T(8,128)S(1)} %wave_halo.21.cur.prev), channel_id=1, source_target_pairs={{0,4},{1,3},{2,6},{3,1},{4,0},{5,9},{6,2},{7,11},{8,12},{9,5},{10,... | collective-permute-start | bytes 393224 | tf_op jit(solution)/shard_map/ppermute | solution.py:555
  40.7 3.2 %collective-permute-start.17 = (f32[4,64,128]{2,1,0:T(8,128)S(1)}, f32[4,64,128]{2,1,0:T(8,128)S(1)}, u32[]{:S(2)}, u32[]{:S(2)}) collective-permute-start(f32[4,64,128]{2,1,0:T(8,128)S(1)} %wave_halo.21.cur.prev), channel_id=1, source_target_pairs={{0,1},{1,0},{2,3},{3,2},{4,5},{5,4},{6,7},{7,6},{8,9},{9,8},{10,11... | collective-permute-start | bytes 393224 | tf_op jit(solution)/shard_map/ppermute | solution.py:559
  44.0 5.5 %collective-permute-start.18 = (f32[4,64,128]{2,1,0:T(8,128)S(1)}, f32[4,64,128]{2,1,0:T(8,128)S(1)}, u32[]{:S(2)}, u32[]{:S(2)}) collective-permute-start(f32[4,64,128]{2,1,0:T(8,128)S(1)} %wave_halo.22.cur.prev), channel_id=1, source_target_pairs={{0,4},{1,3},{2,6},{3,1},{4,0},{5,9},{6,2},{7,11},{8,12},{9,5},{10,... | collective-permute-start | bytes 393224 | tf_op jit(solution)/shard_map/ppermute | solution.py:555
  49.6 5.6 %collective-permute-start.20 = (f32[4,64,128]{2,1,0:T(8,128)S(1)}, f32[4,64,128]{2,1,0:T(8,128)S(1)}, u32[]{:S(2)}, u32[]{:S(2)}) collective-permute-start(f32[4,64,128]{2,1,0:T(8,128)S(1)} %wave_halo.23.cur.prev), channel_id=1, source_target_pairs={{0,4},{1,3},{2,6},{3,1},{4,0},{5,9},{6,2},{7,11},{8,12},{9,5},{10,... | collective-permute-start | bytes 393224 | tf_op jit(solution)/shard_map/ppermute | solution.py:555
  52.0 3.2 %collective-permute-start.21 = (f32[4,64,128]{2,1,0:T(8,128)S(1)}, f32[4,64,128]{2,1,0:T(8,128)S(1)}, u32[]{:S(2)}, u32[]{:S(2)}) collective-permute-start(f32[4,64,128]{2,1,0:T(8,128)S(1)} %wave_halo.23.cur.prev), channel_id=1, source_target_pairs={{0,1},{1,0},{2,3},{3,2},{4,5},{5,4},{6,7},{7,6},{8,9},{9,8},{10,11... | collective-permute-start | bytes 393224 | tf_op jit(solution)/shard_map/ppermute | solution.py:559
  55.3 5.5 %collective-permute-start.22 = (f32[4,64,128]{2,1,0:T(8,128)S(1)}, f32[4,64,128]{2,1,0:T(8,128)S(1)}, u32[]{:S(2)}, u32[]{:S(2)}) collective-permute-start(f32[4,64,128]{2,1,0:T(8,128)S(1)} %wave_halo.24.cur.prev), channel_id=1, source_target_pairs={{0,4},{1,3},{2,6},{3,1},{4,0},{5,9},{6,2},{7,11},{8,12},{9,5},{10,... | collective-permute-start | bytes 393224 | tf_op jit(solution)/shard_map/ppermute | solution.py:555
  60.8 5.5 %collective-permute-start.24 = (f32[4,64,128]{2,1,0:T(8,128)S(1)}, f32[4,64,128]{2,1,0:T(8,128)S(1)}, u32[]{:S(2)}, u32[]{:S(2)}) collective-permute-start(f32[4,64,128]{2,1,0:T(8,128)S(1)} %wave_halo.25.cur.prev), channel_id=1, source_target_pairs={{0,4},{1,3},{2,6},{3,1},{4,0},{5,9},{6,2},{7,11},{8,12},{9,5},{10,... | collective-permute-start | bytes 393224 | tf_op jit(solution)/shard_map/ppermute | solution.py:555
  66.4 5.0 %collective-permute-start.27 = (f32[4,64,128]{2,1,0:T(8,128)S(1)}, f32[4,64,128]{2,1,0:T(8,128)S(1)}, u32[]{:S(2)}, u32[]{:S(2)}) collective-permute-start(f32[4,64,128]{2,1,0:T(8,128)S(1)} %wave_halo.26.cur.prev), channel_id=1, source_target_pairs={{0,4},{1,3},{2,6},{3,1},{4,0},{5,9},{6,2},{7,11},{8,12},{9,5},{10,... | collective-permute-start | bytes 393224 | tf_op jit(solution)/shard_map/ppermute | solution.py:555
  71.5 5.5 %collective-permute-start.30 = (f32[4,64,128]{2,1,0:T(8,128)S(1)}, f32[4,64,128]{2,1,0:T(8,128)S(1)}, u32[]{:S(2)}, u32[]{:S(2)}) collective-permute-start(f32[4,64,128]{2,1,0:T(8,128)S(1)} %wave_halo.27.cur.prev), channel_id=1, source_target_pairs={{0,4},{1,3},{2,6},{3,1},{4,0},{5,9},{6,2},{7,11},{8,12},{9,5},{10,... | collective-permute-start | bytes 393224 | tf_op jit(solution)/shard_map/ppermute | solution.py:555
  73.6 3.4 %collective-permute-start.31 = (f32[4,64,128]{2,1,0:T(8,128)S(1)}, f32[4,64,128]{2,1,0:T(8,128)S(1)}, u32[]{:S(2)}, u32[]{:S(2)}) collective-permute-start(f32[4,64,128]{2,1,0:T(8,128)S(1)} %wave_halo.27.cur.prev), channel_id=1, source_target_pairs={{0,1},{1,0},{2,3},{3,2},{4,5},{5,4},{6,7},{7,6},{8,9},{9,8},{10,11... | collective-permute-start | bytes 393224 | tf_op jit(solution)/shard_map/ppermute | solution.py:559
  77.1 10.1 %collective-permute-start.33 = (f32[4,64,128]{2,1,0:T(8,128)S(1)}, f32[4,64,128]{2,1,0:T(8,128)S(1)}, u32[]{:S(2)}, u32[]{:S(2)}) collective-permute-start(f32[4,64,128]{2,1,0:T(8,128)S(1)} %wave_halo.28.cur.prev), channel_id=1, source_target_pairs={{0,4},{1,3},{2,6},{3,1},{4,0},{5,9},{6,2},{7,11},{8,12},{9,5},{10,... | collective-permute-start | bytes 393224 | tf_op jit(solution)/shard_map/ppermute | solution.py:555
  78.7 8.5 %collective-permute-start.34 = (f32[4,64,128]{2,1,0:T(8,128)S(1)}, f32[4,64,128]{2,1,0:T(8,128)S(1)}, u32[]{:S(2)}, u32[]{:S(2)}) collective-permute-start(f32[4,64,128]{2,1,0:T(8,128)S(1)} %wave_halo.28.cur.prev), channel_id=1, source_target_pairs={{0,1},{1,0},{2,3},{3,2},{4,5},{5,4},{6,7},{7,6},{8,9},{9,8},{10,11... | collective-permute-start | bytes 393224 | tf_op jit(solution)/shard_map/ppermute | solution.py:559
  78.9 3.8 %collective-permute-start.32 = (f32[4,128]{1,0:T(4,128)S(1)}, f32[4,128]{1,0:T(4,128)S(1)}, u32[]{:S(2)}, u32[]{:S(2)}) collective-permute-start(f32[4,128]{1,0:T(4,128)S(1)} %shard_map.130.first), channel_id=1, source_target_pairs={{0,9},{1,8},{2,11},{3,10},{4,13},{5,12},{6,15},{7,14},{8,1},{9,0},... | collective-permute-start | bytes 6152 | tf_op jit(solution)/shard_map/ppermute | solution.py:559
  82.7 3.9 %collective-permute-start.35 = (f32[4,128]{1,0:T(4,128)S(1)}, f32[4,128]{1,0:T(4,128)S(1)}, u32[]{:S(2)}, u32[]{:S(2)}) collective-permute-start(f32[4,128]{1,0:T(4,128)S(1)} %shard_map.131.packed), channel_id=1, source_target_pairs={{0,17},{1,16},{2,19},{3,18},{4,21},{5,20},{6,23},{7,22},{8,25},{9,... | collective-permute-start | bytes 6152 | tf_op jit(solution)/shard_map/ppermute | solution.py:559
  87.2 5.2 %collective-permute-start.36 = (f32[4,64,128]{2,1,0:T(8,128)S(1)}, f32[4,64,128]{2,1,0:T(8,128)S(1)}, u32[]{:S(2)}, u32[]{:S(2)}) collective-permute-start(f32[4,64,128]{2,1,0:T(8,128)S(1)} %wave_halo.29.cur.prev), channel_id=1, source_target_pairs={{0,4},{1,3},{2,6},{3,1},{4,0},{5,9},{6,2},{7,11},{8,12},{9,5},{10,... | collective-permute-start | bytes 393224 | tf_op jit(solution)/shard_map/ppermute | solution.py:555
  88.6 3.9 %collective-permute-start.37 = (f32[4,64,128]{2,1,0:T(8,128)S(1)}, f32[4,64,128]{2,1,0:T(8,128)S(1)}, u32[]{:S(2)}, u32[]{:S(2)}) collective-permute-start(f32[4,64,128]{2,1,0:T(8,128)S(1)} %wave_halo.29.cur.prev), channel_id=1, source_target_pairs={{0,1},{1,0},{2,3},{3,2},{4,5},{5,4},{6,7},{7,6},{8,9},{9,8},{10,11... | collective-permute-start | bytes 393224 | tf_op jit(solution)/shard_map/ppermute | solution.py:559
  92.5 5.6 %collective-permute-start.38 = (f32[4,64,128]{2,1,0:T(8,128)S(1)}, f32[4,64,128]{2,1,0:T(8,128)S(1)}, u32[]{:S(2)}, u32[]{:S(2)}) collective-permute-start(f32[4,64,128]{2,1,0:T(8,128)S(1)} %wave_halo.30.cur), channel_id=1, source_target_pairs={{0,4},{1,3},{2,6},{3,1},{4,0},{5,9},{6,2},{7,11},{8,12},{9,5},{10,... | collective-permute-start | bytes 393224 | tf_op jit(solution)/shard_map/ppermute | solution.py:555
  98.2 6.7 %collective-permute-start.43 = (f32[4,64,128]{2,1,0:T(8,128)S(1)}, f32[4,64,128]{2,1,0:T(8,128)S(1)}, u32[]{:S(2)}, u32[]{:S(2)}) collective-permute-start(f32[4,64,128]{2,1,0:T(8,128)S(1)} %wave_halo.31.cur.own), channel_id=1, source_target_pairs={{0,1},{1,0},{2,3},{3,2},{4,5},{5,4},{6,7},{7,6},{8,9},{9,8},{10,11... | collective-permute-start | bytes 393224 | tf_op jit(solution)/shard_map/ppermute | solution.py:559
  106.7 4.1 %collective-permute-start.44 = (f32[32,128]{1,0:T(8,128)S(1)}, f32[32,128]{1,0:T(8,128)S(1)}, u32[]{:S(2)}, u32[]{:S(2)}) collective-permute-start(f32[32,128]{1,0:T(8,128)S(1)} %shard_map.135.packed), channel_id=1, source_target_pairs={{0,17},{1,16},{2,19},{3,18},{4,21},{5,20},{6,23},{7,22},{8,25},{9,... | collective-permute-start | bytes 49160 | tf_op jit(solution)/shard_map/ppermute | solution.py:559
  (18 other events, 85.2 us)
